TPU v7x, 32 devices: a whole 2x2x4 slice. The times are simulated.
32 devices in a mesh: seq: 8 (over z, y), mlp: 4 (over x, core).
Axes of the slice: x: 2, y: 2, z: 4, core: 2. Of those that a mesh axis runs over, the one named last changes fastest.
Arguments:
- inputs: bfloat16 [1024, 2048], P('seq'), may hold values from -6 to 6
- first_gain: float32 [3, 2048], replicated, may hold values from 0.1 to 1.9
- query_weight: bfloat16 [2048, 2048], P(None, 'mlp'), may hold values from -0.1875 to 0.1875
- key_weight: bfloat16 [2048, 2048], P(None, 'mlp'), may hold values from -0.125 to 0.125
- value_weight: bfloat16 [2048, 2048], P(None, 'mlp'), may hold values from -0.125 to 0.125
- output_weight: bfloat16 [2048, 2048], P('mlp'), may hold values from -0.75 to 0.75
- second_gain: float32 [3, 2048], replicated, may hold values from 0.1 to 1.9
- up_weight: bfloat16 [2048, 8192], P(None, 'mlp'), may hold values from -0.125 to 0.125
- down_weight: bfloat16 [8192, 2048], P('mlp'), may hold values from -0.0625 to 0.0625
- frame_sizes: int32 [1, 8], replicated, may hold values from 144 to 576, as said below
- text_counts: int32 [1, 8], replicated, may hold values from 1 to 32
- action_counts: int32 [1, 8], replicated, may hold values from 1 to 2
- cotangent: bfloat16 [1024, 2048], P('seq'), may hold values from -6 to 6
Outputs:
- outputs: bfloat16 [1024, 2048], P('seq')
- input_grad: bfloat16 [1024, 2048], P('seq')
- first_gain_grad: float32 [3, 2048], P(None, 'seq')
- query_grad: float32 [2048, 2048], P('seq', 'mlp')
- key_grad: float32 [2048, 2048], P('seq', 'mlp')
- value_grad: float32 [2048, 2048], P('seq', 'mlp')
- output_grad: float32 [2048, 2048], P('mlp', 'seq')
- second_gain_grad: float32 [3, 2048], P(None, 'seq')
- up_grad: float32 [2048, 8192], P('seq', 'mlp')
- down_grad: float32 [8192, 2048], P('mlp', 'seq')
Inputs may be any that keep to these rules, and one draw needn't show every extreme that they name: `frame_sizes`: each entry is 144 or 576; in every clip frame 0 has 576 and frame 1 has 144.
All inputs are finite; a program needn't handle non-finite values.
Results may differ from a plain program's by a relative error of at most 0.024.
Values may be sent and summed in bfloat16 or wider, within the bound.
No kernel may reach another device: no remote copies, remote signals or barrier semaphores. Data moves between devices by JAX's collectives and lax.ppermute only.
A program may use at most 192 MiB of HBM per device.

v0:
```python
from functools import partial
import math

import jax
import jax.numpy as jnp
from jax import lax
from jax.experimental import pallas as pl
from jax.experimental.pallas import tpu as pltpu
from jax.sharding import PartitionSpec as P

HEAD_DIM = 128
epsilon = 1e-05
bf16 = jnp.bfloat16
f32 = jnp.float32
NEGATIVE = -1e30
VMEM_LIMIT = 60 * 1024 * 1024

NN = ((1,), (0,))
NT = ((1,), (1,))
TN = ((0,), (0,))


def dot(a, b, dims):
    return lax.dot_general(a, b, (dims, ((), ())), preferred_element_type=f32)


def params():
    return pltpu.CompilerParams(vmem_limit_bytes=VMEM_LIMIT)


def cost(flops, moved, transcendentals=0):
    return pl.CostEstimate(
        flops=int(flops), bytes_accessed=int(moved), transcendentals=int(transcendentals)
    )


def swap(value, axis, bit):
    size = lax.axis_size(axis)
    return lax.ppermute(value, axis, [(i, i ^ bit) for i in range(size)])


def inner_size():
    return 1 << (int(math.log2(lax.axis_size("seq"))) // 2)


def x_size():
    return lax.axis_size("mlp") // 2


def own_quarter(half):
    rows = half.shape[0] // x_size()
    return lax.dynamic_slice_in_dim(half, (lax.axis_index("mlp") // 2) * rows, rows, 0)


def join_x(quarter):
    bit = 1
    while bit < x_size():
        quarter = jnp.concatenate([quarter, swap(quarter, "mlp", 2 * bit)], axis=0)
        bit *= 2
    return quarter


def gather_early(half):
    size, inner = lax.axis_size("seq"), inner_size()
    quarter = own_quarter(half)
    pieces = {0: half}
    far = {outer: swap(quarter, "seq", outer) for outer in range(inner, size, inner)}
    for bit in range(1, inner):
        pieces[bit] = swap(half, "seq", bit)
    for outer in range(inner, size, inner):
        pieces[outer] = join_x(far[outer])
        for bit in range(1, inner):
            pieces[outer | bit] = swap(pieces[outer], "seq", bit)
    return [pieces[d] for d in range(size)]


def gather_late(half, after=None):
    size, inner = lax.axis_size("seq"), inner_size()
    quarter = own_quarter(half)
    if after is not None:
        quarter, half, _ = lax.optimization_barrier((quarter, half, after))
    far = [swap(quarter, "seq", outer) for outer in range(inner, size, inner)]
    near = jnp.concatenate([half, join_x(jnp.concatenate(far, axis=0))], axis=0)
    rows = [near] + [swap(near, "seq", bit) for bit in range(1, inner)]
    return rows, [swap(array, "mlp", 1) for array in rows]


def gather_pieces(piece):
    size, inner = lax.axis_size("seq"), inner_size()
    pieces = {0: piece}
    for outer in range(inner, size, inner):
        pieces[outer] = swap(piece, "seq", outer)
    for outer in range(0, size, inner):
        for bit in range(1, inner):
            pieces[outer | bit] = swap(pieces[outer], "seq", bit)
    return [pieces[d] for d in range(size)]


def rounded(value):
    return lax.optimization_barrier(value.astype(bf16))


def pair_mlp(partial_sum):
    half = partial_sum.shape[0] // 2
    came = swap(partial_sum[half:].astype(bf16), "mlp", 1)
    total = partial_sum[:half] + came.astype(f32)
    low, other = rounded(total), None
    bit = 2
    while bit < lax.axis_size("mlp"):
        if other is not None:
            low = rounded(low.astype(f32) + other.astype(f32))
        other = swap(low, "mlp", bit)
        bit *= 2
    if other is None:
        other = jnp.zeros_like(low)
    return low, other


def both(half):
    return jnp.concatenate([half, swap(half, "mlp", 1)], axis=0)


def tables_kernel(index, frames, texts, actions, *outs, shards, length, groups, clip_length):
    place_a, place_b, kind_a, kind_b, query_place, own_place, own_kind = outs
    shard_index, core = index[0], index[1]
    shape = (shards, length)
    place = lax.broadcasted_iota(jnp.int32, shape, 0) * length + lax.broadcasted_iota(
        jnp.int32, shape, 1
    )
    kinds = jnp.full(shape, 2, jnp.int32)
    for clip in range(frames.shape[0]):
        start = jnp.int32(clip * clip_length)
        within = (place >= clip * clip_length) & (place < (clip + 1) * clip_length)
        for frame in range(frames.shape[1]):
            text_end = start + texts[clip, frame]
            action_end = text_end + actions[clip, frame]
            kinds = jnp.where(within & (place >= start) & (place < text_end), 0, kinds)
            kinds = jnp.where(within & (place >= text_end) & (place < action_end), 1, kinds)
            start = action_end + frames[clip, frame]
    square = (length, length)
    down = lax.broadcasted_iota(jnp.int32, square, 0)
    across = lax.broadcasted_iota(jnp.int32, square, 1)
    earlier = (down < across).astype(f32).astype(bf16)
    rank = jnp.zeros(shape, f32)
    before = jnp.zeros((shards, 1), f32)
    for kind in range(3):
        chosen = (kinds == kind).astype(f32)
        rank += chosen * (dot(chosen.astype(bf16), earlier, NN) + before)
        before += chosen.sum(axis=1, keepdims=True)
    rank_low, kinds_low = rank.astype(bf16), kinds.astype(f32).astype(bf16)
    piece = length // shards // 2
    lane = lax.broadcasted_iota(jnp.int32, (1, length), 1).astype(f32)

    def find(shard, offset, side, row):
        wanted = (shard_index ^ offset) * (2 * piece) + (core ^ side) * piece + row
        pick = shard == lax.broadcasted_iota(jnp.int32, (length, shards), 1)
        pick = pick.astype(f32).astype(bf16)
        hit = dot(pick, rank_low, NN) == wanted.astype(f32)
        where = jnp.sum(jnp.where(hit, lane, 0.0), axis=1, keepdims=True).astype(jnp.int32)
        kind = jnp.sum(jnp.where(hit, dot(pick, kinds_low, NN), 0.0), axis=1, keepdims=True)
        return where + shard * length, kind.astype(jnp.int32)

    def as_row(column):
        return jnp.sum(jnp.where(down == across, column, 0), axis=0, keepdims=True)

    step = lax.broadcasted_iota(jnp.int32, (length, 1), 0)
    half = length // 2
    for side, (place_out, kind_out) in enumerate(((place_a, kind_a), (place_b, kind_b))):
        for block in range(shards // 2):
            token = step + block * length
            if groups > 1:
                shard, offset = token // (shards * piece), (token // piece) % shards
            else:
                offset, shard = token // half, (token % half) // piece
            where, kind = find(shard, offset, side, token % piece)
            at = pl.ds(block * length, length)
            place_out[at, :] = where
            kind_out[at, :] = kind
            query_place[:, pl.ds((2 * block + side) * length, length)] = as_row(where)
    where, kind = find((step % half) // piece, step * 0, step // half, step % piece)
    own_place[...] = as_row(where)
    own_kind[...] = kind


def tables(frames, texts, actions, shards, length, groups):
    index = jnp.stack([lax.axis_index("seq"), lax.axis_index("mlp") % 2]).astype(jnp.int32)
    total = shards * length
    column = jax.ShapeDtypeStruct((total // 2, 1), jnp.int32)
    return pl.pallas_call(
        partial(
            tables_kernel,
            shards=shards,
            length=length,
            groups=groups,
            clip_length=total // frames.shape[0],
        ),
        in_specs=[pl.BlockSpec(memory_space=pltpu.SMEM)] * 4,
        out_shape=[column] * 4
        + [
            jax.ShapeDtypeStruct((1, total), jnp.int32),
            jax.ShapeDtypeStruct((1, length), jnp.int32),
            jax.ShapeDtypeStruct((length, 1), jnp.int32),
        ],
        cost_estimate=cost(8 * total * length, 8 * 128 * total),
        name="tables",
    )(index, frames, texts, actions)


def gain_rows(gain, column):
    return jnp.where(
        column == 0, gain[0:1, :], jnp.where(column == 1, gain[1:2, :], gain[2:3, :])
    )


def normalize(values):
    mean = jnp.mean(values, axis=1, keepdims=True)
    centered = values - mean
    inverse = lax.rsqrt(jnp.mean(centered * centered, axis=1, keepdims=True) + epsilon)
    return (centered * inverse, inverse)


def norm_back(grad, normal, inverse, gains):
    scaled = grad * gains
    return inverse * (
        scaled
        - jnp.mean(scaled, axis=1, keepdims=True)
        - normal * jnp.mean(scaled * normal, axis=1, keepdims=True)
    )


def norm_kernel(*refs, groups, inner, parts):
    index, gain, kind, out = refs[0], refs[-3], refs[-2], refs[-1]
    pieces = refs[1:-3]
    rows, width = pieces[0].shape
    count = len(pieces)
    step = rows // parts
    for d, piece in enumerate(pieces):
        for part in range(parts):
            normal, _ = normalize(piece[pl.ds(part * step, step), :].astype(f32))
            place = part if d < inner else part ^ index[0]
            if groups > 1:
                each = groups // parts
                at = pl.ds(place * each, each)
                column = kind[at, d].reshape(step, 1)
                normed = (normal * gain_rows(gain, column)).astype(bf16)
                out[at, d] = normed.reshape(each, rows // groups, width)
            else:
                column = kind[d, place]
                out[d, place] = (normal * gain_rows(gain, column)).astype(bf16)


def norm_pieces(pieces, gain, kind, groups):
    rows, width = pieces[0].shape
    count = len(pieces)
    parts = x_size()
    if groups > 1:
        shape = (groups, count, rows // groups)
    else:
        shape = (count, parts, rows // parts)
    memory = [pl.BlockSpec(memory_space=pltpu.SMEM)]
    index = (lax.axis_index("mlp") // 2).astype(jnp.int32).reshape(1)
    out = pl.pallas_call(
        partial(norm_kernel, groups=groups, inner=inner_size(), parts=parts),
        in_specs=memory + [pl.BlockSpec(memory_space=pltpu.VMEM)] * (count + 2),
        out_shape=jax.ShapeDtypeStruct(shape + (width,), bf16),
        compiler_params=params(),
        cost_estimate=cost(10 * count * rows * width, 4 * count * rows * width),
        name="norm_pieces",
    )(index, *pieces, gain, kind.reshape(shape + (1,)))
    return out.reshape(count * rows, width)


def own_norm_kernel(rows, gain, kind, out):
    normal, _ = normalize(rows[...].astype(f32))
    out[...] = (normal * gain_rows(gain, kind[...])).astype(bf16)


def own_norm(rows, gain, kind):
    return pl.pallas_call(
        own_norm_kernel,
        out_shape=jax.ShapeDtypeStruct(rows.shape, bf16),
        compiler_params=params(),
        cost_estimate=cost(10 * rows.size, 4 * rows.size),
        name="own_norm",
    )(rows, gain, kind)


def lift_kernel(rows, low, other, gain, kind, residual, lifted):
    value = rows[...].astype(f32) + (low[...].astype(f32) + other[...].astype(f32))
    residual[...] = value
    normal, _ = normalize(value)
    lifted[...] = (normal * gain_rows(gain, kind[...])).astype(bf16)


def lift(rows, low, other, gain, kind):
    return pl.pallas_call(
        lift_kernel,
        out_shape=[jax.ShapeDtypeStruct(rows.shape, f32), jax.ShapeDtypeStruct(rows.shape, bf16)],
        compiler_params=params(),
        cost_estimate=cost(10 * rows.size, 12 * rows.size),
        name="lift",
    )(rows, low, other, gain, kind)


def kind_sums(term, kind):
    sums = [jnp.sum(jnp.where(kind == k, term, 0.0), axis=0, keepdims=True) for k in range(3)]
    high = [value.astype(bf16) for value in sums]
    low = [(value - part.astype(f32)).astype(bf16) for value, part in zip(sums, high)]
    zero = jnp.zeros((1, term.shape[1]), bf16)
    return jnp.concatenate(high + low + [zero, zero], axis=0)


def middle_kernel(residual, low, other, grad, gain, kind, grad_residual, mixed, sums):
    lifted_grad = low[...].astype(f32) + other[...].astype(f32)
    normal, inverse = normalize(residual[...])
    column = kind[...]
    back = norm_back(lifted_grad, normal, inverse, gain_rows(gain, column))
    value = grad[...].astype(f32) + back
    grad_residual[...] = value
    mixed[...] = value.astype(bf16)
    sums[...] = kind_sums(lifted_grad * normal, column)


def middle(residual, low, other, grad, gain, kind):
    width = residual.shape[1]
    return pl.pallas_call(
        middle_kernel,
        out_shape=[
            jax.ShapeDtypeStruct(residual.shape, f32),
            jax.ShapeDtypeStruct(residual.shape, bf16),
            jax.ShapeDtypeStruct((8, width), bf16),
        ],
        compiler_params=params(),
        cost_estimate=cost(20 * residual.size, 16 * residual.size),
        name="middle",
    )(residual, low, other, grad, gain, kind)


def last_kernel(rows, low, other, grad_residual, gain, kind, out):
    grad = low[...].astype(f32) + other[...].astype(f32)
    normal, inverse = normalize(rows[...].astype(f32))
    back = norm_back(grad, normal, inverse, gain_rows(gain, kind[...]))
    out[...] = (grad_residual[...] + back).astype(bf16)


def last(rows, low, other, grad_residual, gain, kind):
    return pl.pallas_call(
        last_kernel,
        out_shape=jax.ShapeDtypeStruct(rows.shape, bf16),
        compiler_params=params(),
        cost_estimate=cost(20 * rows.size, 12 * rows.size),
        name="last",
    )(rows, low, other, grad_residual, gain, kind)


def gelu_parts(value):
    rate = math.sqrt(2 / math.pi)
    square = value * value
    bent = jnp.tanh(value * (rate + (rate * 0.044715) * square))
    upper = 0.5 * (1 + bent)
    slope = upper + (0.5 * value) * (1 - bent * bent) * (rate + (rate * 3 * 0.044715) * square)
    return value * upper, slope


def own_kernel(lifted, up, grad_activated, activated, lifted_grad):
    value, slope = gelu_parts(dot(lifted[...], up[...], NN))
    activated[...] = value.astype(bf16)
    hidden_grad = (grad_activated[...] * slope).astype(bf16)
    term = dot(hidden_grad, up[...], NT)

    @pl.when(pl.program_id(0) == 0)
    def _():
        lifted_grad[...] = term

    @pl.when(pl.program_id(0) > 0)
    def _():
        lifted_grad[...] += term


def feed_own(lifted, up, grad_activated):
    rows, width = lifted.shape
    hidden = up.shape[1]
    tile = math.gcd(hidden, 512)
    across = lambda t: (0, t)
    whole = lambda t: (0, 0)
    return pl.pallas_call(
        own_kernel,
        grid=(hidden // tile,),
        in_specs=[
            pl.BlockSpec((rows, width), whole),
            pl.BlockSpec((width, tile), across),
            pl.BlockSpec((rows, tile), across),
        ],
        out_specs=[pl.BlockSpec((rows, tile), across), pl.BlockSpec((rows, width), whole)],
        out_shape=[
            jax.ShapeDtypeStruct((rows, hidden), bf16),
            jax.ShapeDtypeStruct((rows, width), f32),
        ],
        compiler_params=params(),
        cost_estimate=cost(4 * rows * width * hidden, 2 * width * hidden),
        name="feed_own",
    )(lifted, up, grad_activated)


def all_kernel(index, *refs, count, first):
    lifted, grad = refs[:count], refs[count : 2 * count]
    lifted_part, grad_part = refs[2 * count : 3 * count], refs[3 * count : 4 * count]
    up, down = refs[4 * count : 4 * count + 2]
    up_grad, down_grad = refs[-2:]
    up_sum = None if first else refs[4 * count + 2][...]
    down_sum = None if first else refs[4 * count + 3][...]
    for k in range(count):
        value, slope = gelu_parts(dot(lifted[k][...], up[...], NN))
        hidden_grad = (dot(grad[k][...], down[...], NT) * slope).astype(bf16)
        down_term = dot(value.astype(bf16), grad_part[k][...], TN)
        up_term = dot(lifted_part[k][...], hidden_grad, TN)
        up_sum = up_term if up_sum is None else up_sum + up_term
        down_sum = down_term if down_sum is None else down_sum + down_term
    up_grad[...] = up_sum
    down_grad[...] = down_sum


def feed_all(lifted, grad, up, down, shards, sums=()):
    rows, width = lifted[0].shape
    count = len(lifted)
    part = width // shards
    hidden = up.shape[1]
    tile = math.gcd(hidden, 256)
    across = lambda t, index: (0, t)
    below = lambda t, index: (t, 0)
    whole = lambda t, index: (0, 0)
    mine = lambda t, index: (0, index[0])
    sum_specs = [pl.BlockSpec((part, tile), across), pl.BlockSpec((tile, part), below)]
    index = lax.axis_index("seq").astype(jnp.int32).reshape(1)
    return pl.pallas_call(
        partial(all_kernel, count=count, first=not sums),
        grid_spec=pltpu.PrefetchScalarGridSpec(
            num_scalar_prefetch=1,
            grid=(hidden // tile,),
            in_specs=[pl.BlockSpec((rows, width), whole)] * (2 * count)
            + [pl.BlockSpec((rows, part), mine)] * (2 * count)
            + [pl.BlockSpec((width, tile), across), pl.BlockSpec((tile, width), below)]
            + (sum_specs if sums else []),
            out_specs=sum_specs,
        ),
        out_shape=[
            jax.ShapeDtypeStruct((part, hidden), f32),
            jax.ShapeDtypeStruct((hidden, part), f32),
        ],
        compiler_params=params(),
        cost_estimate=cost(
            4 * count * rows * hidden * (width + part), 4 * width * hidden + 4 * count * rows * width
        ),
        name="feed_all",
    )(index, *lifted, *grad, *lifted, *grad, up, down, *sums)


def project_kernel(index, *refs):
    normed, lows, weights = refs[0:2], refs[2:8], refs[8:11]
    gain, kinds = refs[11], refs[12:14]
    outs, gain_grad = refs[14:17], refs[17]
    for k in range(3):
        outs[k][...] = sum(dot(normed[side][...], lows[2 * k + side][...], TN) for side in range(2))
    gain_sum = [0.0, 0.0, 0.0]
    for side in range(2):
        column = kinds[side][...]
        term = sum(dot(lows[2 * k + side][...], weights[k][...], NT) for k in range(3))
        term = term * (normed[side][...].astype(f32) / gain_rows(gain, column))
        for k in range(3):
            gain_sum[k] += jnp.sum(jnp.where(column == k, term, 0.0), axis=0, keepdims=True)
    gain_grad[...] = jnp.concatenate(gain_sum, axis=0)


def project(normed, lows, weights, gain, kinds, shards):
    rows, width = normed[0].shape
    across = lows[0][0].shape[1]
    part = width // shards
    whole = lambda t, index: (0, 0)
    mine = lambda t, index: (0, index[0])
    below = lambda t, index: (index[0], 0)
    index = lax.axis_index("seq").astype(jnp.int32).reshape(1)
    return pl.pallas_call(
        project_kernel,
        grid_spec=pltpu.PrefetchScalarGridSpec(
            num_scalar_prefetch=1,
            grid=(1,),
            in_specs=[pl.BlockSpec((rows, part), mine)] * 2
            + [pl.BlockSpec((rows, across), whole)] * 6
            + [pl.BlockSpec((part, across), below)] * 3
            + [pl.BlockSpec((gain.shape[0], part), mine)]
            + [pl.BlockSpec((rows, 1), whole)] * 2,
            out_specs=[pl.BlockSpec((part, across), whole)] * 3
            + [pl.BlockSpec((gain.shape[0], part), whole)],
        ),
        out_shape=[jax.ShapeDtypeStruct((part, across), f32)] * 3
        + [jax.ShapeDtypeStruct((gain.shape[0], part), f32)],
        compiler_params=params(),
        cost_estimate=cost(24 * rows * part * across, 12 * rows * across + 12 * part * across),
        name="project",
    )(index, *normed, *[low for pair in lows for low in pair], *weights, gain, *kinds)


def mask_of(key_place, query_place, clip_length, clips):
    allowed = key_place <= query_place
    if clips > 1:
        allowed = allowed & (key_place // clip_length == query_place // clip_length)
    return allowed


def probabilities(scores, scale):
    top = scores[0].max(axis=0, keepdims=True)
    for block in scores[1:]:
        top = jnp.maximum(top, block.max(axis=0, keepdims=True))
    rate = scale * math.log2(math.e)
    weights = [jnp.exp2((block - top) * rate) for block in scores]
    total = weights[0].sum(axis=0, keepdims=True)
    for block in weights[1:]:
        total = total + block.sum(axis=0, keepdims=True)
    inverse = 1.0 / total
    return [block * inverse for block in weights]


def forward_kernel(query, key_a, key_b, value_a, value_b, place_a, place_b, query_place, out, **opts):
    scale = opts["scale"]
    query_place = query_place[...]
    allowed = [
        mask_of(place[...], query_place, opts["clip_length"], opts["clips"])
        for place in (place_a, place_b)
    ]
    for head in range(query.shape[1] // HEAD_DIM):
        at = pl.ds(head * HEAD_DIM, HEAD_DIM)
        scores = [
            jnp.where(mask, dot(key[:, at], query[:, at], NT), NEGATIVE)
            for mask, key in zip(allowed, (key_a, key_b))
        ]
        prob = [block.astype(bf16) for block in probabilities(scores, scale)]
        result = dot(prob[0], value_a[:, at], TN) + dot(prob[1], value_b[:, at], TN)
        out[:, at] = result.astype(bf16)


def attend(query, keys, values, places, query_place, clip_length, clips):
    rows, width = query.shape
    total = 2 * keys[0].shape[0]
    return pl.pallas_call(
        partial(
            forward_kernel, scale=1.0 / math.sqrt(HEAD_DIM), clip_length=clip_length, clips=clips
        ),
        out_shape=jax.ShapeDtypeStruct((rows, width), bf16),
        compiler_params=params(),
        cost_estimate=cost(
            4 * rows * total * width, 4 * total * width, rows * total * (width // HEAD_DIM)
        ),
        name="attend",
    )(query, *keys, *values, *places, query_place)


def backward_kernel(*refs, count, groups, scale, clip_length, clips):
    grads = refs[:count]
    query_a, query_b, key_a, key_b, value_a, value_b, place_a, place_b, query_place = refs[
        count : count + 9
    ]
    outs = refs[count + 9 : count + 20]
    attended, grad_query, grad_key, grad_value = outs[0:2], outs[2:4], outs[4:6], outs[6:8]
    own_query, own_key, own_value = outs[8:11]
    sums = refs[count + 20 :]
    half = key_a.shape[0]
    rows = half // count
    group_rows = rows // groups
    block = min(128, half)
    blocks = half // block

    def sources(index):
        found = []
        if groups == 1:
            for d in range(index * block // rows, (index + 1) * block // rows):
                found.append((d, 0, rows))
            return found
        each = count * group_rows
        for j in range(index * block // each, (index + 1) * block // each):
            for d in range(count):
                found.append((d, j * group_rows, group_rows))
        return found

    def keep_own(target, values, index):
        for side in range(2):
            at = side * block
            for d, start, size in sources(index):
                if d == 0:
                    target[pl.ds(side * rows + start, size), :] = values[at : at + size]
                at += size

    for ref in sums:
        ref[...] = jnp.zeros_like(ref)
    for index in range(blocks):
        mine = pl.ds(index * block, block)
        reach = (index + 1) * block if groups > 1 else half
        free = index * block if groups > 1 else 0
        query = jnp.concatenate([query_a[mine, :], query_b[mine, :]], axis=0)
        grad = jnp.concatenate(
            [
                grads[d][pl.ds(side * rows + start, size), :]
                for side in range(2)
                for d, start, size in sources(index)
            ],
            axis=0,
        )
        at_place = query_place[:, pl.ds(index * 2 * block, 2 * block)]
        spans = []
        for side in range(2):
            if free:
                spans.append((side, 0, free, False))
            spans.append((side, free, reach, True))
        keys, values, places = (key_a, key_b), (value_a, value_b), (place_a, place_b)
        scores = []
        for side, low, high, masked in spans:
            score = dot(keys[side][pl.ds(low, high - low), :], query, NT)
            if masked:
                place = places[side][pl.ds(low, high - low), :]
                score = jnp.where(mask_of(place, at_place, clip_length, clips), score, NEGATIVE)
            scores.append(score)
        prob = probabilities(scores, scale)
        lows = [part.astype(bf16) for part in prob]
        grad_prob = [
            dot(values[side][pl.ds(low, high - low), :], grad, NT) for side, low, high, _ in spans
        ]
        delta = sum((p * g).sum(axis=0, keepdims=True) for p, g in zip(prob, grad_prob))
        grad_score = [(p * (g - delta)).astype(bf16) for p, g in zip(prob, grad_prob)]
        result = sum(
            dot(part, values[side][pl.ds(low, high - low), :], TN)
            for part, (side, low, high, _) in zip(lows, spans)
        ).astype(bf16)
        back = (
            sum(
                dot(part, keys[side][pl.ds(low, high - low), :], TN)
                for part, (side, low, high, _) in zip(grad_score, spans)
            )
            * scale
        ).astype(bf16)
        for side in range(2):
            attended[side][mine, :] = result[side * block : (side + 1) * block]
            grad_query[side][mine, :] = back[side * block : (side + 1) * block]
        keep_own(own_query, back, index)
        for (side, low, high, _), score, part in zip(spans, grad_score, lows):
            at = pl.ds(low, high - low)
            sums[side][at, :] += dot(score, query, NN)
            sums[2 + side][at, :] += dot(part, grad, NN)
    low_key = [(sums[side][...] * scale).astype(bf16) for side in range(2)]
    low_value = [sums[2 + side][...].astype(bf16) for side in range(2)]
    for side in range(2):
        grad_key[side][...] = low_key[side]
        grad_value[side][...] = low_value[side]
    for index in range(blocks):
        cut = slice(index * block, (index + 1) * block)
        keep_own(own_key, jnp.concatenate([low[cut] for low in low_key], axis=0), index)
        keep_own(own_value, jnp.concatenate([low[cut] for low in low_value], axis=0), index)


def attend_back(grads, queries, keys, values, places, query_place, groups, clip_length, clips):
    half, width = keys[0].shape
    count = len(grads)
    heads = width // HEAD_DIM
    rows = grads[0].shape[0]
    by_head = lambda h: (0, h)
    whole = lambda h: (0, 0)
    tall = pl.BlockSpec((half, HEAD_DIM), by_head)
    short = pl.BlockSpec((rows, HEAD_DIM), by_head)
    outs = pl.pallas_call(
        partial(
            backward_kernel,
            count=count,
            groups=groups,
            scale=1.0 / math.sqrt(HEAD_DIM),
            clip_length=clip_length,
            clips=clips,
        ),
        grid=(heads,),
        in_specs=[short] * count
        + [tall] * 6
        + [pl.BlockSpec((half, 1), whole)] * 2
        + [pl.BlockSpec((1, 2 * half), whole)],
        out_specs=[tall] * 8 + [short] * 3,
        out_shape=[jax.ShapeDtypeStruct((half, width), bf16)] * 8
        + [jax.ShapeDtypeStruct((rows, width), bf16)] * 3,
        scratch_shapes=[pltpu.VMEM((half, HEAD_DIM), f32)] * 4,
        compiler_params=params(),
        cost_estimate=cost(
            12 * 4 * half * half * width, 32 * half * width, 4 * half * half * heads
        ),
        name="attend_back",
    )(*grads, *queries, *keys, *values, *places, query_place)
    return outs[0:2], outs[2:4], outs[4:6], outs[6:8], outs[8:11]


def body(
    inputs,
    first_gain,
    query_weight,
    key_weight,
    value_weight,
    output_weight,
    second_gain,
    up_weight,
    down_weight,
    frame_sizes,
    text_counts,
    action_counts,
    cotangent,
):
    shards = lax.axis_size("seq")
    shard_index = lax.axis_index("seq")
    core = lax.axis_index("mlp") % 2
    length, width = inputs.shape
    total = length * shards
    half = length // 2
    piece = half // shards
    clips = frame_sizes.shape[0]
    clip_length = total // clips
    part = width // shards
    groups = shards if piece % 8 == 0 else 1

    def halves(rows):
        cut = rows.reshape(2, piece, shards, width)
        mine = lax.dynamic_index_in_dim(cut, core, 0, keepdims=False)
        other = lax.dynamic_index_in_dim(cut, 1 - core, 0, keepdims=False)
        return (
            mine.transpose(1, 0, 2).reshape(half, width),
            other.transpose(1, 0, 2).reshape(half, width),
        )

    def restore(mine):
        other = swap(mine, "mlp", 1)
        upper = jnp.where(core == 0, mine, other)
        lower = jnp.where(core == 0, other, mine)
        rows = jnp.stack([upper, lower]).reshape(2, shards, piece, width)
        return rows.transpose(0, 2, 1, 3).reshape(length, width)

    inputs_half, inputs_other = halves(inputs)
    pieces = gather_early(inputs_half)
    grad_half, grad_other = halves(cotangent)
    grad_own = jnp.concatenate([grad_half, grad_other], axis=0)

    place_a, place_b, kind_a, kind_b, query_place, own_place, own_kind = tables(
        frame_sizes, text_counts, action_counts, shards, length, groups
    )
    places, kinds = (place_a, place_b), (kind_a, kind_b)
    half_kind = own_kind[:half]
    own_normed = own_norm(
        jnp.concatenate([inputs_half, inputs_other], axis=0), first_gain, own_kind
    )
    query_own = dot(own_normed, query_weight, NN).astype(bf16)
    own_activated_grad = dot(grad_own, down_weight, NT)

    normed = [norm_pieces(pieces, first_gain, kind_a, groups)]
    normed.append(swap(normed[0], "mlp", 1))
    keys = [dot(rows, key_weight, NN).astype(bf16) for rows in normed]
    values = [dot(rows, value_weight, NN).astype(bf16) for rows in normed]
    heads_own = attend(query_own, keys, values, places, own_place, clip_length, clips)
    low, other = pair_mlp(dot(heads_own, output_weight, NN))
    residual, lifted_half = lift(inputs_half, low, other, second_gain, half_kind)
    queries = [dot(rows, query_weight, NN).astype(bf16) for rows in normed]
    grads = gather_late(grad_half, after=pieces[-1])

    lifted = gather_late(lifted_half)
    activated_own, lifted_term = feed_own(both(lifted_half), up_weight, own_activated_grad)
    low, other = pair_mlp(lifted_term)
    grad_residual, mixed_half, second_sums = middle(
        residual, low, other, grad_half, second_gain, half_kind
    )
    heads_grad = dot(both(mixed_half), output_weight, NT).astype(bf16)
    low, other = pair_mlp(dot(activated_own, down_weight, NN))
    outputs = restore((residual + (low.astype(f32) + other.astype(f32))).astype(bf16))

    attended, query_low, key_low, value_low, own_low = attend_back(
        gather_pieces(heads_grad),
        queries,
        keys,
        values,
        places,
        query_place,
        groups,
        clip_length,
        clips,
    )
    attention_weights = (query_weight, key_weight, value_weight)
    normed_term = sum(dot(low, weight, NT) for low, weight in zip(own_low, attention_weights))
    low, other = pair_mlp(normed_term)
    input_grad = restore(last(inputs_half, low, other, grad_residual, first_gain, half_kind))

    query_grad, key_grad, value_grad, first_gain_grad = project(
        normed, (query_low, key_low, value_low), attention_weights, first_gain, kinds, shards
    )
    bit = 1
    while bit < lax.axis_size("mlp"):
        first_gain_grad = first_gain_grad + swap(first_gain_grad, "mlp", bit)
        bit *= 2

    came = lax.all_to_all(
        jnp.concatenate([mixed_half, second_sums], axis=0).reshape(half + 8, shards, part),
        "seq",
        split_axis=1,
        concat_axis=0,
        tiled=False,
    )
    second_sums = jnp.sum(came[:, half : half + 6].astype(f32), axis=0)
    second_sums = second_sums[:3] + second_sums[3:]
    second_gain_grad = second_sums + swap(second_sums, "mlp", 1)
    came = came[shard_index ^ jnp.arange(shards, dtype=jnp.int32), :half]
    if groups > 1:
        came = came.reshape(shards, shards, piece, part).transpose(1, 0, 2, 3)
    mixed_part = [came.reshape(-1, part)]
    mixed_part.append(swap(mixed_part[0], "mlp", 1))
    output_grad = sum(dot(rows, mixed, TN) for rows, mixed in zip(attended, mixed_part))

    sums = ()
    for side in range(2):
        sums = feed_all(lifted[side], grads[side], up_weight, down_weight, shards, sums)
    up_grad, down_grad = sums

    return (
        outputs,
        input_grad,
        first_gain_grad,
        query_grad,
        key_grad,
        value_grad,
        output_grad,
        second_gain_grad,
        up_grad,
        down_grad,
    )


def solution(mesh):
    return jax.shard_map(
        body,
        mesh=mesh,
        in_specs=(
            P("seq", None),
            P(),
            P(None, "mlp"),
            P(None, "mlp"),
            P(None, "mlp"),
            P("mlp", None),
            P(),
            P(None, "mlp"),
            P("mlp", None),
            P(),
            P(),
            P(),
            P("seq", None),
        ),
        out_specs=(
            P("seq", None),
            P("seq", None),
            P(None, "seq"),
            P("seq", "mlp"),
            P("seq", "mlp"),
            P("seq", "mlp"),
            P("mlp", "seq"),
            P(None, "seq"),
            P("seq", "mlp"),
            P("mlp", "seq"),
        ),
        check_vma=False,
    )
```

profile of v0, /device:TPU:0, one launch (start us, length us, event | category | flops | bytes accessed | tf_op | source)
XLA Modules:
  0.0 268.9 jit_solution(10679478136030727301)
XLA Ops:
  2.3 3.0 %collective-permute-start = (bf16[64,2048]{1,0:T(8,128)(2,1)S(1)}, bf16[64,2048]{1,0:T(8,128)(2,1)S(1)}, u32[]{:S(2)}, u32[]{:S(2)}) collective-permute-start(bf16[64,2048]{1,0:T(8,128)(2,1)S(1)} %bitcast.102), channel_id=1, source_target_pairs={{0,4},{4,0},{8,12},{12,8},{16,20},{20,16},{24,28},{28,24},{1,5},{5... | collective-permute-start | bytes 786440 | tf_op jit(solution)/shard_map/ppermute | solution.py:39
  6.0 1.6 collective-permute-start.1
  7.5 2.6 collective-permute-start.4
  11.7 7.3 %fusion.4.grad_activated = f32[128,2048]{1,0:T(8,128)} fusion(bf16[2048,2048]{1,0:T(8,128)(2,1)} %refs_9_.7, bf16[64,2048]{1,0:T(8,128)(2,1)S(1)} %bitcast.117, bf16[64,2048]{1,0:T(8,128)(2,1)S(1)} %bitcast.109), kind=kOutput, calls=%fused_computation.24 | convolution fusion | flops 1074790400 | bytes 9961472 | tf_op jit(solution)/shard_map/dot_general | solution.py:24
  19.6 2.4 tables.1
  23.4 2.4 own_norm.1
  25.7 1.6 collective-permute-start.2
  29.8 1.6 collective-permute-start.8
  32.9 2.2 collective-permute-done.5
  37.3 2.9 %convolution_convert_fusion.7.query = bf16[128,512]{1,0:T(8,128)(2,1)} fusion(bf16[128,2048]{1,0:T(8,128)(2,1)} %own_norm.1, bf16[2048,512]{1,0:T(8,128)(2,1)} %refs_8_.3), kind=kOutput, calls=%fused_computation.11 | convolution fusion | flops 268500992 | bytes 2752512 | tf_op jit(solution)/shard_map/dot_general | solution.py:24
  40.2 9.7 %collective-permute-done.9.refs_8_ = bf16[64,2048]{1,0:T(8,128)(2,1)} collective-permute-done((bf16[64,2048]{1,0:T(8,128)(2,1)S(1)}, bf16[64,2048]{1,0:T(8,128)(2,1)}, u32[]{:S(2)}, u32[]{:S(2)}) %collective-permute-start.9) | collective-permute-done | bytes 262176 | tf_op jit(solution)/shard_map/ppermute | solution.py:39
  50.5 3.5 %collective-permute-start.42 = (bf16[32,2048]{1,0:T(8,128)(2,1)S(1)}, bf16[32,2048]{1,0:T(8,128)(2,1)S(1)}, u32[]{:S(2)}, u32[]{:S(2)}) collective-permute-start(bf16[32,2048]{1,0:T(8,128)(2,1)S(1)} %constant_dynamic-slice_fusion.1), channel_id=1, source_target_pairs={{0,16},{4,20},{8,24},{12,28},{16,0},{20,4},{24,8},{28,12},{1,17},{... | collective-permute-start | bytes 393224 | tf_op jit(solution)/shard_map/ppermute | solution.py:39
  55.7 5.3 %norm_pieces.1 = bf16[8,8,8,2048]{3,2,1,0:T(8,128)(2,1)} custom-call(s32[1]{0:T(128)} %bitcast.11.refs_0_, bf16[64,2048]{1,0:T(8,128)(2,1)} %bitcast.105, bf16[64,2048]{1,0:T(8,128)(2,1)} %copy-done.24, bf16[64,2048]{1,0:T(8,128)(2,1)} %copy-done.20, bf16[64,2048]{1,0:T(8,128)(2,1)} %copy-done.25, bf16[64,2048]{1,0:T(8,128)(2,1)} %copy-done.19, ...), custom_call_target="tpu_custom_call" | custom-call | flops 10485760 | bytes 4194304 | tf_op jit(solution)/shard_map/norm_pieces/pallas_call | solution.py:262
  61.1 4.4 %convolution_convert_fusion.1.refs_8_ = bf16[512,512]{1,0:T(8,128)(2,1)} fusion(bf16[512,2048]{1,0:T(8,128)(2,1)} %bitcast.98, bf16[2048,512]{1,0:T(8,128)(2,1)} %refs_8_.3), kind=kOutput, calls=%fused_computation.4 | convolution fusion | flops 1074003968 | bytes 4718592 | tf_op jit(solution)/shard_map/dot_general | solution.py:24
  65.5 2.0 convolution_convert_fusion.5.key_a.refs_10_
  67.5 2.0 convolution_convert_fusion.3.value_a.refs_12_
  72.3 2.0 convolution_convert_fusion.4.key_b.refs_11_
  74.4 2.0 convolution_convert_fusion.2.value_b.refs_13_
  76.4 4.5 %attend.1 = bf16[128,512]{1,0:T(8,128)(2,1)} custom-call(bf16[128,512]{1,0:T(8,128)(2,1)} %convolution_convert_fusion.7.query, bf16[512,512]{1,0:T(8,128)(2,1)} %convolution_convert_fusion.5.key_a.refs_10_, bf16[512,512]{1,0:T(8,128)(2,1)} %convolution_convert_fusion.4.key_b.refs_11_, bf16[512,512]{1,0:T(8,128)(2,1)} %convolution_convert_fusion.3.value_a.refs_12_, ...), custom_call_target="tpu_custom_call" | custom-call | flops 268435456 | bytes 2097152 | tf_op jit(solution)/shard_map/attend/pallas_call | solution.py:544
  84.6 1.6 collective-permute-start.12
  86.2 2.1 convolution_convert_fusion.refs_9_
  88.3 4.8 %collective-permute-done.12.other = bf16[64,2048]{1,0:T(8,128)(2,1)S(1)} collective-permute-done((bf16[64,2048]{1,0:T(8,128)(2,1)S(1)}, bf16[64,2048]{1,0:T(8,128)(2,1)S(1)}, u32[]{:S(2)}, u32[]{:S(2)}) %collective-permute-start.12) | collective-permute-done | bytes 262176 | tf_op jit(solution)/shard_map/ppermute | solution.py:39
  93.8 2.2 lift.1
  97.3 3.8 %collective-permute-start.35 = (bf16[32,2048]{1,0:T(8,128)(2,1)S(1)}, bf16[32,2048]{1,0:T(8,128)(2,1)S(1)}, u32[]{:S(2)}, u32[]{:S(2)}) collective-permute-start(bf16[32,2048]{1,0:T(8,128)(2,1)S(1)} %constant_dynamic-slice_fusion), channel_id=1, source_target_pairs={{0,16},{4,20},{8,24},{12,28},{16,0},{20,4},{24,8},{28,12},{1,17},{... | collective-permute-start | bytes 393224 | tf_op jit(solution)/shard_map/ppermute | solution.py:39
  101.3 1.7 constant_dynamic-update-slice_fusion.10
  103.0 2.4 collective-permute-done.34
  105.4 5.6 %collective-permute-done.35 = bf16[32,2048]{1,0:T(8,128)(2,1)S(1)} collective-permute-done((bf16[32,2048]{1,0:T(8,128)(2,1)S(1)}, bf16[32,2048]{1,0:T(8,128)(2,1)S(1)}, u32[]{:S(2)}, u32[]{:S(2)}) %collective-permute-start.35) | collective-permute-done | bytes 131104 | tf_op jit(solution)/shard_map/ppermute | solution.py:39
  111.0 1.6 collective-permute-start.37
  112.6 1.8 pad_maximum_fusion.1.lifted
  114.4 9.2 %feed_own.1 = (bf16[128,2048]{1,0:T(8,128)(2,1)}, f32[128,2048]{1,0:T(8,128)}) custom-call(bf16[128,2048]{1,0:T(8,128)(2,1)} %pad_maximum_fusion.1.lifted, bf16[2048,2048]{1,0:T(8,128)(2,1)} %refs_8_.5, f32[128,2048]{1,0:T(8,128)} %fusion.4.grad_activated), custom_call_target="tpu_custom_call" | custom-call | flops 2147483648 | bytes 8388608 | tf_op jit(solution)/shard_map/feed_own/pallas_call | solution.py:386
  123.6 4.9 %fusion.17 = f32[128,2048]{1,0:T(8,128)S(1)} fusion(bf16[128,2048]{1,0:T(8,128)(2,1)} %get-tuple-element.52, bf16[2048,2048]{1,0:T(8,128)(2,1)} %refs_9_.7), kind=kOutput, calls=%fused_computation.80 | convolution fusion | flops 1073741824 | bytes 9961472 | tf_op jit(solution)/shard_map/dot_general | solution.py:24
  132.5 11.7 %collective-permute-done.18.other = bf16[64,2048]{1,0:T(8,128)(2,1)S(1)} collective-permute-done((bf16[64,2048]{1,0:T(8,128)(2,1)S(1)}, bf16[64,2048]{1,0:T(8,128)(2,1)S(1)}, u32[]{:S(2)}, u32[]{:S(2)}) %collective-permute-start.18) | collective-permute-done | bytes 262176 | tf_op jit(solution)/shard_map/ppermute | solution.py:39
  145.0 2.9 %middle.1 = (f32[64,2048]{1,0:T(8,128)}, bf16[64,2048]{1,0:T(8,128)(2,1)}, bf16[8,2048]{1,0:T(8,128)(2,1)}) custom-call(f32[64,2048]{1,0:T(8,128)} %get-tuple-element.50.residual, bf16[64,2048]{1,0:T(8,128)(2,1)} %copy-done.17, bf16[64,2048]{1,0:T(8,128)(2,1)} %copy-done.30, bf16[64,2048]{1,0:T(8,128)(2,1)} %bitcast.111, f32[3,2048]{1,0:T(4,128)} %gain.6, ...), custom_call_target="tpu_custom_call" | custom-call | flops 2621440 | bytes 2097152 | tf_op jit(solution)/shard_map/middle/pallas_call | solution.py:326
  151.4 6.2 %all-to-all-start = ((bf16[1,72,8,256]{3,1,0,2:T(8,128)(2,1)}), bf16[1,72,8,256]{3,1,0,2:T(8,128)(2,1)S(1)}, u32[]{:S(2)}, u32[]{:S(2)}) async-start(bf16[1,72,8,256]{3,1,0,2:T(8,128)(2,1)} %copy.42), calls=%async_computation | async-start | bytes 589824 | tf_op jit(solution)/shard_map/all_to_all | solution.py:797
  159.1 2.0 collective-permute-start.20
  162.5 2.4 collective-permute-start.23
  166.7 3.1 %collective-permute-done.21.refs_2_ = bf16[128,512]{1,0:T(8,128)(2,1)S(1)} collective-permute-done((bf16[128,512]{1,0:T(8,128)(2,1)}, bf16[128,512]{1,0:T(8,128)(2,1)S(1)}, u32[]{:S(2)}, u32[]{:S(2)}) %collective-permute-start.21) | collective-permute-done | bytes 131104 | tf_op jit(solution)/shard_map/ppermute | solution.py:39
  170.6 6.0 %collective-permute-done.23.refs_4_ = bf16[128,512]{1,0:T(8,128)(2,1)S(1)} collective-permute-done((bf16[128,512]{1,0:T(8,128)(2,1)}, bf16[128,512]{1,0:T(8,128)(2,1)S(1)}, u32[]{:S(2)}, u32[]{:S(2)}) %collective-permute-start.23) | collective-permute-done | bytes 131104 | tf_op jit(solution)/shard_map/ppermute | solution.py:39
  176.6 1.7 collective-permute-start.24
  180.1 1.8 collective-permute-start.39
  182.9 2.8 %collective-permute-done.26.refs_7_ = bf16[128,512]{1,0:T(8,128)(2,1)S(1)} collective-permute-done((bf16[128,512]{1,0:T(8,128)(2,1)S(1)}, bf16[128,512]{1,0:T(8,128)(2,1)S(1)}, u32[]{:S(2)}, u32[]{:S(2)}) %collective-permute-start.26) | collective-permute-done | bytes 131104 | tf_op jit(solution)/shard_map/ppermute | solution.py:39
  186.4 17.5 %attend_back.1 = (bf16[512,512]{1,0:T(8,128)(2,1)}, bf16[512,512]{1,0:T(8,128)(2,1)}, bf16[512,512]{1,0:T(8,128)(2,1)}, bf16[512,512]{1,0:T(8,128)(2,1)}, bf16[5...) custom-call(bf16[128,512]{1,0:T(8,128)(2,1)} %convolution_convert_fu, ...), custom_call_target="tpu_custom_call" | custom-call | flops 6442450944 | bytes 8388608 | tf_op jit(solution)/shard_map/attend_back/pallas_call | solution.py:667
  203.9 5.2 %project.1 = (f32[256,512]{1,0:T(8,128)}, f32[256,512]{1,0:T(8,128)}, f32[256,512]{1,0:T(8,128)}, f32[3,256]{1,0:T(4,128)}) custom-call(s32[1]{0:T(128)} %bitcast.9.index, bf16[512,2048]{1,0:T(8,128)(2,1)} %bitcast.99, bf16[512,2048]{1,0:T(8,128)(2,1)} %copy-done.12, bf16[512,512]{1,0:T(8,128)(2,1)} %get-tuple-element.60.refs_2_, ...), custom_call_target="tpu_custom_call" | custom-call | flops 1610612736 | bytes 4718592 | tf_op jit(solution)/shard_map/project/pallas_call | solution.py:482
  214.2 2.5 collective-permute-done.31
  220.0 6.5 %collective-permute-done.28.other = bf16[64,2048]{1,0:T(8,128)(2,1)S(1)} collective-permute-done((bf16[64,2048]{1,0:T(8,128)(2,1)S(1)}, bf16[64,2048]{1,0:T(8,128)(2,1)S(1)}, u32[]{:S(2)}, u32[]{:S(2)}) %collective-permute-start.28) | collective-permute-done | bytes 262176 | tf_op jit(solution)/shard_map/ppermute | solution.py:39
  227.2 2.5 last.1
  229.7 18.1 %feed_all.2 = (f32[256,2048]{1,0:T(8,128)}, f32[2048,256]{1,0:T(8,128)}) custom-call(s32[1]{0:T(128)} %bitcast.9.index, bf16[256,2048]{1,0:T(8,128)(2,1)} %copy-done.35, bf16[256,2048]{1,0:T(8,128)(2,1)} %collective-permute-done.39.refs_1_.refs_5_, bf16[256,2048]{1,0:T(8,128)(2,1)} %constant_dynamic-update-slice_fusion.11.refs_2_.refs_6_, ...), custom_call_target="tpu_custom_call" | custom-call | flops 9663676416 | bytes 20971520 | tf_op jit(solution)/shard_map/feed_all/pallas_call | solution.py:435
  249.0 19.6 %feed_all.3 = (f32[256,2048]{1,0:T(8,128)}, f32[2048,256]{1,0:T(8,128)}) custom-call(s32[1]{0:T(128)} %bitcast.9.index, bf16[256,2048]{1,0:T(8,128)(2,1)} %collective-permute-done.38.refs_0_.refs_4_, bf16[256,2048]{1,0:T(8,128)(2,1)} %collective-permute-done.40.refs_1_.refs_5_, bf16[256,2048]{1,0:T(8,128)(2,1)} %collective-permute-done.45.refs_2_.refs_6_, ...), custom_call_target="tpu_custom_call" | custom-call | flops 9663676416 | bytes 20971520 | tf_op jit(solution)/shard_map/feed_all/pallas_call | solution.py:435
  (225 shorter events, 50.3 us)
Async XLA Ops:
  2.3 51.7 %collective-permute-start = (bf16[64,2048]{1,0:T(8,128)(2,1)S(1)}, bf16[64,2048]{1,0:T(8,128)(2,1)S(1)}, u32[]{:S(2)}, u32[]{:S(2)}) collective-permute-start(bf16[64,2048]{1,0:T(8,128)(2,1)S(1)} %bitcast.102), channel_id=1, source_target_pairs={{0,4},{4,0},{8,12},{12,8},{16,20},{20,16},{24,28},{28,24},{1,5},{5... | collective-permute-start | bytes 786440 | tf_op jit(solution)/shard_map/ppermute | solution.py:39
  6.0 19.8 %collective-permute-start.1 = (bf16[32,2048]{1,0:T(8,128)(2,1)}, bf16[32,2048]{1,0:T(8,128)(2,1)}, u32[]{:S(2)}, u32[]{:S(2)}) collective-permute-start(bf16[32,2048]{1,0:T(8,128)(2,1)} %constant_dynamic-slice_fusion.4), channel_id=1, source_target_pairs={{0,8},{4,12},{8,0},{12,4},{16,24},{20,28},{24,16},{28,20},{1,9},{5... | collective-permute-start | bytes 393224 | tf_op jit(solution)/shard_map/ppermute | solution.py:39
  7.5 20.7 %collective-permute-start.4 = (bf16[32,2048]{1,0:T(8,128)(2,1)}, bf16[32,2048]{1,0:T(8,128)(2,1)}, u32[]{:S(2)}, u32[]{:S(2)}) collective-permute-start(bf16[32,2048]{1,0:T(8,128)(2,1)} %constant_dynamic-slice_fusion.4), channel_id=1, source_target_pairs={{0,16},{4,20},{8,24},{12,28},{16,0},{20,4},{24,8},{28,12},{1,17},{... | collective-permute-start | bytes 393224 | tf_op jit(solution)/shard_map/ppermute | solution.py:39
  10.1 19.7 %collective-permute-start.7 = (bf16[32,2048]{1,0:T(8,128)(2,1)}, bf16[32,2048]{1,0:T(8,128)(2,1)}, u32[]{:S(2)}, u32[]{:S(2)}) collective-permute-start(bf16[32,2048]{1,0:T(8,128)(2,1)} %constant_dynamic-slice_fusion.4), channel_id=1, source_target_pairs={{0,24},{4,28},{8,16},{12,20},{16,8},{20,12},{24,0},{28,4},{1,25},{... | collective-permute-start | bytes 393224 | tf_op jit(solution)/shard_map/ppermute | solution.py:39
  25.7 6.6 %collective-permute-start.2 = (bf16[32,2048]{1,0:T(8,128)(2,1)}, bf16[32,2048]{1,0:T(8,128)(2,1)S(1)}, u32[]{:S(2)}, u32[]{:S(2)}) collective-permute-start(bf16[32,2048]{1,0:T(8,128)(2,1)} %collective-permute-done.1), channel_id=1, source_target_pairs={{0,2},{1,3},{2,0},{3,1},{4,6},{5,7},{6,4},{7,5},{8,10},{9,11},{10,... | collective-permute-start | bytes 393224 | tf_op jit(solution)/shard_map/ppermute | solution.py:39
  28.2 6.9 %collective-permute-start.5 = (bf16[32,2048]{1,0:T(8,128)(2,1)}, bf16[32,2048]{1,0:T(8,128)(2,1)S(1)}, u32[]{:S(2)}, u32[]{:S(2)}) collective-permute-start(bf16[32,2048]{1,0:T(8,128)(2,1)} %collective-permute-done.4), channel_id=1, source_target_pairs={{0,2},{1,3},{2,0},{3,1},{4,6},{5,7},{6,4},{7,5},{8,10},{9,11},{10,... | collective-permute-start | bytes 393224 | tf_op jit(solution)/shard_map/ppermute | solution.py:39
  29.8 6.8 %collective-permute-start.8 = (bf16[32,2048]{1,0:T(8,128)(2,1)}, bf16[32,2048]{1,0:T(8,128)(2,1)S(1)}, u32[]{:S(2)}, u32[]{:S(2)}) collective-permute-start(bf16[32,2048]{1,0:T(8,128)(2,1)} %collective-permute-done.7), channel_id=1, source_target_pairs={{0,2},{1,3},{2,0},{3,1},{4,6},{5,7},{6,4},{7,5},{8,10},{9,11},{10,... | collective-permute-start | bytes 393224 | tf_op jit(solution)/shard_map/ppermute | solution.py:39
  32.4 21.9 %collective-permute-start.3 = (bf16[64,2048]{1,0:T(8,128)(2,1)S(1)}, bf16[64,2048]{1,0:T(8,128)(2,1)S(1)}, u32[]{:S(2)}, u32[]{:S(2)}) collective-permute-start(bf16[64,2048]{1,0:T(8,128)(2,1)S(1)} %constant_dynamic-update-slice_fusion.refs_3_), channel_id=1, source_target_pairs={{0,4},{4,0},{8,12},{12,8},{16,20},{20,16},{24,28},{28,24},{1,5},{5... | collective-permute-start | bytes 786440 | tf_op jit(solution)/shard_map/ppermute | solution.py:39
  35.2 19.2 %collective-permute-start.6 = (bf16[64,2048]{1,0:T(8,128)(2,1)S(1)}, bf16[64,2048]{1,0:T(8,128)(2,1)S(1)}, u32[]{:S(2)}, u32[]{:S(2)}) collective-permute-start(bf16[64,2048]{1,0:T(8,128)(2,1)S(1)} %constant_dynamic-update-slice_fusion.2.refs_5_), channel_id=1, source_target_pairs={{0,4},{4,0},{8,12},{12,8},{16,20},{20,16},{24,28},{28,24},{1,5},{5... | collective-permute-start | bytes 786440 | tf_op jit(solution)/shard_map/ppermute | solution.py:39
  36.6 13.3 %collective-permute-start.9 = (bf16[64,2048]{1,0:T(8,128)(2,1)S(1)}, bf16[64,2048]{1,0:T(8,128)(2,1)}, u32[]{:S(2)}, u32[]{:S(2)}) collective-permute-start(bf16[64,2048]{1,0:T(8,128)(2,1)S(1)} %constant_dynamic-update-slice_fusion.4.refs_7_), channel_id=1, source_target_pairs={{0,4},{4,0},{8,12},{12,8},{16,20},{20,16},{24,28},{28,24},{1,5},{5... | collective-permute-start | bytes 786440 | tf_op jit(solution)/shard_map/ppermute | solution.py:39
  49.9 20.4 %collective-permute-start.41 = (bf16[32,2048]{1,0:T(8,128)(2,1)S(1)}, bf16[32,2048]{1,0:T(8,128)(2,1)S(1)}, u32[]{:S(2)}, u32[]{:S(2)}) collective-permute-start(bf16[32,2048]{1,0:T(8,128)(2,1)S(1)} %constant_dynamic-slice_fusion.1), channel_id=1, source_target_pairs={{0,8},{4,12},{8,0},{12,4},{16,24},{20,28},{24,16},{28,20},{1,9},{5... | collective-permute-start | bytes 393224 | tf_op jit(solution)/shard_map/ppermute | solution.py:39
  50.5 19.8 %collective-permute-start.42 = (bf16[32,2048]{1,0:T(8,128)(2,1)S(1)}, bf16[32,2048]{1,0:T(8,128)(2,1)S(1)}, u32[]{:S(2)}, u32[]{:S(2)}) collective-permute-start(bf16[32,2048]{1,0:T(8,128)(2,1)S(1)} %constant_dynamic-slice_fusion.1), channel_id=1, source_target_pairs={{0,16},{4,20},{8,24},{12,28},{16,0},{20,4},{24,8},{28,12},{1,17},{... | collective-permute-start | bytes 393224 | tf_op jit(solution)/shard_map/ppermute | solution.py:39
  54.0 16.3 %collective-permute-start.43 = (bf16[32,2048]{1,0:T(8,128)(2,1)S(1)}, bf16[32,2048]{1,0:T(8,128)(2,1)S(1)}, u32[]{:S(2)}, u32[]{:S(2)}) collective-permute-start(bf16[32,2048]{1,0:T(8,128)(2,1)S(1)} %constant_dynamic-slice_fusion.1), channel_id=1, source_target_pairs={{0,24},{4,28},{8,16},{12,20},{16,8},{20,12},{24,0},{28,4},{1,25},{... | collective-permute-start | bytes 393224 | tf_op jit(solution)/shard_map/ppermute | solution.py:39
  61.1 11.2 %collective-permute-start.10 = (bf16[512,2048]{1,0:T(8,128)(2,1)}, bf16[512,2048]{1,0:T(8,128)(2,1)S(1)}, u32[]{:S(2)}, u32[]{:S(2)}) collective-permute-start(bf16[512,2048]{1,0:T(8,128)(2,1)} %bitcast.97), channel_id=1, source_target_pairs={{0,1},{1,0},{2,3},{3,2},{4,5},{5,4},{6,7},{7,6},{8,9},{9,8},{10,11... | collective-permute-start | bytes 6291464 | tf_op jit(solution)/shard_map/ppermute | solution.py:39
  70.4 12.9 %collective-permute-start.44 = (bf16[96,2048]{1,0:T(8,128)(2,1)S(1)}, bf16[96,2048]{1,0:T(8,128)(2,1)S(1)}, u32[]{:S(2)}, u32[]{:S(2)}) collective-permute-start(bf16[96,2048]{1,0:T(8,128)(2,1)S(1)} %pad_maximum_fusion.3), channel_id=1, source_target_pairs={{0,2},{1,3},{2,0},{3,1},{4,6},{5,7},{6,4},{7,5},{8,10},{9,11},{10,... | collective-permute-start | bytes 1179656 | tf_op jit(solution)/shard_map/ppermute | solution.py:39
  82.5 2.1 collective-permute-start.11
  84.1 130.2 %collective-permute-start.46 = (bf16[256,2048]{1,0:T(8,128)(2,1)}, bf16[256,2048]{1,0:T(8,128)(2,1)}, u32[]{:S(2)}, u32[]{:S(2)}) collective-permute-start(bf16[256,2048]{1,0:T(8,128)(2,1)} %constant_dynamic-update-slice_fusion.11.refs_2_.refs_6_), channel_id=1, source_target_pairs={{0,4},{4,0},{8,12},{12,8},{16,20},{20,16},{24,28},{28,24},{1,5},{5... | collective-permute-start | bytes 3145736 | tf_op jit(solution)/shard_map/ppermute | solution.py:39
  84.6 8.4 %collective-permute-start.12 = (bf16[64,2048]{1,0:T(8,128)(2,1)S(1)}, bf16[64,2048]{1,0:T(8,128)(2,1)S(1)}, u32[]{:S(2)}, u32[]{:S(2)}) collective-permute-start(bf16[64,2048]{1,0:T(8,128)(2,1)S(1)} %fusion.3.low), channel_id=1, source_target_pairs={{0,2},{1,3},{2,0},{3,1},{4,6},{5,7},{6,4},{7,5},{8,10},{9,11},{10,... | collective-permute-start | bytes 786440 | tf_op jit(solution)/shard_map/ppermute | solution.py:39
  96.0 16.6 %collective-permute-start.13 = (bf16[64,2048]{1,0:T(8,128)(2,1)}, bf16[64,2048]{1,0:T(8,128)(2,1)S(1)}, u32[]{:S(2)}, u32[]{:S(2)}) collective-permute-start(bf16[64,2048]{1,0:T(8,128)(2,1)} %get-tuple-element.51), channel_id=1, source_target_pairs={{0,1},{1,0},{2,3},{3,2},{4,5},{5,4},{6,7},{7,6},{8,9},{9,8},{10,11... | collective-permute-start | bytes 786440 | tf_op jit(solution)/shard_map/ppermute | solution.py:39
  96.9 8.5 %collective-permute-start.34 = (bf16[32,2048]{1,0:T(8,128)(2,1)S(1)}, bf16[32,2048]{1,0:T(8,128)(2,1)S(1)}, u32[]{:S(2)}, u32[]{:S(2)}) collective-permute-start(bf16[32,2048]{1,0:T(8,128)(2,1)S(1)} %constant_dynamic-slice_fusion), channel_id=1, source_target_pairs={{0,8},{4,12},{8,0},{12,4},{16,24},{20,28},{24,16},{28,20},{1,9},{5... | collective-permute-start | bytes 393224 | tf_op jit(solution)/shard_map/ppermute | solution.py:39
  97.3 13.7 %collective-permute-start.35 = (bf16[32,2048]{1,0:T(8,128)(2,1)S(1)}, bf16[32,2048]{1,0:T(8,128)(2,1)S(1)}, u32[]{:S(2)}, u32[]{:S(2)}) collective-permute-start(bf16[32,2048]{1,0:T(8,128)(2,1)S(1)} %constant_dynamic-slice_fusion), channel_id=1, source_target_pairs={{0,16},{4,20},{8,24},{12,28},{16,0},{20,4},{24,8},{28,12},{1,17},{... | collective-permute-start | bytes 393224 | tf_op jit(solution)/shard_map/ppermute | solution.py:39
  101.1 9.9 %collective-permute-start.36 = (bf16[32,2048]{1,0:T(8,128)(2,1)S(1)}, bf16[32,2048]{1,0:T(8,128)(2,1)S(1)}, u32[]{:S(2)}, u32[]{:S(2)}) collective-permute-start(bf16[32,2048]{1,0:T(8,128)(2,1)S(1)} %constant_dynamic-slice_fusion), channel_id=1, source_target_pairs={{0,24},{4,28},{8,16},{12,20},{16,8},{20,12},{24,0},{28,4},{1,25},{... | collective-permute-start | bytes 393224 | tf_op jit(solution)/shard_map/ppermute | solution.py:39
  111.0 21.5 %collective-permute-start.37 = (bf16[96,2048]{1,0:T(8,128)(2,1)S(1)}, bf16[96,2048]{1,0:T(8,128)(2,1)S(1)}, u32[]{:S(2)}, u32[]{:S(2)}) collective-permute-start(bf16[96,2048]{1,0:T(8,128)(2,1)S(1)} %pad_maximum_fusion.2), channel_id=1, source_target_pairs={{0,2},{1,3},{2,0},{3,1},{4,6},{5,7},{6,4},{7,5},{8,10},{9,11},{10,... | collective-permute-start | bytes 1179656 | tf_op jit(solution)/shard_map/ppermute | solution.py:39
  128.8 2.1 collective-permute-start.17
  130.2 17.7 %collective-permute-start.15 = (bf16[64,2048]{1,0:T(8,128)(2,1)S(1)}, bf16[64,2048]{1,0:T(8,128)(2,1)}, u32[]{:S(2)}, u32[]{:S(2)}) collective-permute-start(bf16[64,2048]{1,0:T(8,128)(2,1)S(1)} %fusion.2), channel_id=1, source_target_pairs={{0,2},{1,3},{2,0},{3,1},{4,6},{5,7},{6,4},{7,5},{8,10},{9,11},{10,... | collective-permute-start | bytes 786440 | tf_op jit(solution)/shard_map/ppermute | solution.py:39
  130.9 13.3 %collective-permute-start.18 = (bf16[64,2048]{1,0:T(8,128)(2,1)S(1)}, bf16[64,2048]{1,0:T(8,128)(2,1)S(1)}, u32[]{:S(2)}, u32[]{:S(2)}) collective-permute-start(bf16[64,2048]{1,0:T(8,128)(2,1)S(1)} %add_convert_fusion.low), channel_id=1, source_target_pairs={{0,2},{1,3},{2,0},{3,1},{4,6},{5,7},{6,4},{7,5},{8,10},{9,11},{10,... | collective-permute-start | bytes 786440 | tf_op jit(solution)/shard_map/ppermute | solution.py:39
  147.9 9.6 %collective-permute-start.19 = (bf16[64,2048]{1,0:T(8,128)(2,1)}, bf16[64,2048]{1,0:T(8,128)(2,1)S(1)}, u32[]{:S(2)}, u32[]{:S(2)}) collective-permute-start(bf16[64,2048]{1,0:T(8,128)(2,1)} %get-tuple-element.54), channel_id=1, source_target_pairs={{0,1},{1,0},{2,3},{3,2},{4,5},{5,4},{6,7},{7,6},{8,9},{9,8},{10,11... | collective-permute-start | bytes 786440 | tf_op jit(solution)/shard_map/ppermute | solution.py:39
  149.0 15.9 %collective-permute-start.16 = (bf16[64,2048]{1,0:T(8,128)(2,1)S(1)}, bf16[64,2048]{1,0:T(8,128)(2,1)S(1)}, u32[]{:S(2)}, u32[]{:S(2)}) collective-permute-start(bf16[64,2048]{1,0:T(8,128)(2,1)S(1)} %add_convert_fusion.1), channel_id=1, source_target_pairs={{0,1},{1,0},{2,3},{3,2},{4,5},{5,4},{6,7},{7,6},{8,9},{9,8},{10,11... | collective-permute-start | bytes 786440 | tf_op jit(solution)/shard_map/ppermute | solution.py:39
  151.4 27.2 %all-to-all-start = ((bf16[1,72,8,256]{3,1,0,2:T(8,128)(2,1)}), bf16[1,72,8,256]{3,1,0,2:T(8,128)(2,1)S(1)}, u32[]{:S(2)}, u32[]{:S(2)}) async-start(bf16[1,72,8,256]{3,1,0,2:T(8,128)(2,1)} %copy.42), calls=%async_computation | async-start | bytes 589824 | tf_op jit(solution)/shard_map/all_to_all | solution.py:797
  159.1 21.0 %collective-permute-start.20 = (bf16[128,512]{1,0:T(8,128)(2,1)}, bf16[128,512]{1,0:T(8,128)(2,1)S(1)}, u32[]{:S(2)}, u32[]{:S(2)}) collective-permute-start(bf16[128,512]{1,0:T(8,128)(2,1)} %convolution_convert_fusion.6.refs_0_), channel_id=1, source_target_pairs={{0,4},{4,0},{8,12},{12,8},{16,20},{20,16},{24,28},{28,24},{1,5},{5... | collective-permute-start | bytes 393224 | tf_op jit(solution)/shard_map/ppermute | solution.py:39
  161.1 8.6 %collective-permute-start.21 = (bf16[128,512]{1,0:T(8,128)(2,1)}, bf16[128,512]{1,0:T(8,128)(2,1)S(1)}, u32[]{:S(2)}, u32[]{:S(2)}) collective-permute-start(bf16[128,512]{1,0:T(8,128)(2,1)} %convolution_convert_fusion.6.refs_0_), channel_id=1, source_target_pairs={{0,8},{4,12},{8,0},{12,4},{16,24},{20,28},{24,16},{28,20},{1,9},{5... | collective-permute-start | bytes 393224 | tf_op jit(solution)/shard_map/ppermute | solution.py:39
  162.5 14.0 %collective-permute-start.23 = (bf16[128,512]{1,0:T(8,128)(2,1)}, bf16[128,512]{1,0:T(8,128)(2,1)S(1)}, u32[]{:S(2)}, u32[]{:S(2)}) collective-permute-start(bf16[128,512]{1,0:T(8,128)(2,1)} %convolution_convert_fusion.6.refs_0_), channel_id=1, source_target_pairs={{0,16},{4,20},{8,24},{12,28},{16,0},{20,4},{24,8},{28,12},{1,17},{... | collective-permute-start | bytes 393224 | tf_op jit(solution)/shard_map/ppermute | solution.py:39
  164.9 13.4 %collective-permute-start.25 = (bf16[128,512]{1,0:T(8,128)(2,1)}, bf16[128,512]{1,0:T(8,128)(2,1)S(1)}, u32[]{:S(2)}, u32[]{:S(2)}) collective-permute-start(bf16[128,512]{1,0:T(8,128)(2,1)} %convolution_convert_fusion.6.refs_0_), channel_id=1, source_target_pairs={{0,24},{4,28},{8,16},{12,20},{16,8},{20,12},{24,0},{28,4},{1,25},{... | collective-permute-start | bytes 393224 | tf_op jit(solution)/shard_map/ppermute | solution.py:39
  169.7 12.1 %collective-permute-start.22 = (bf16[128,512]{1,0:T(8,128)(2,1)S(1)}, bf16[128,512]{1,0:T(8,128)(2,1)S(1)}, u32[]{:S(2)}, u32[]{:S(2)}) collective-permute-start(bf16[128,512]{1,0:T(8,128)(2,1)S(1)} %collective-permute-done.21.refs_2_), channel_id=1, source_target_pairs={{0,4},{4,0},{8,12},{12,8},{16,20},{20,16},{24,28},{28,24},{1,5},{5... | collective-permute-start | bytes 393224 | tf_op jit(solution)/shard_map/ppermute | solution.py:39
  176.6 6.3 %collective-permute-start.24 = (bf16[128,512]{1,0:T(8,128)(2,1)S(1)}, bf16[128,512]{1,0:T(8,128)(2,1)S(1)}, u32[]{:S(2)}, u32[]{:S(2)}) collective-permute-start(bf16[128,512]{1,0:T(8,128)(2,1)S(1)} %collective-permute-done.23.refs_4_), channel_id=1, source_target_pairs={{0,4},{4,0},{8,12},{12,8},{16,20},{20,16},{24,28},{28,24},{1,5},{5... | collective-permute-start | bytes 393224 | tf_op jit(solution)/shard_map/ppermute | solution.py:39
  178.3 7.4 %collective-permute-start.26 = (bf16[128,512]{1,0:T(8,128)(2,1)S(1)}, bf16[128,512]{1,0:T(8,128)(2,1)S(1)}, u32[]{:S(2)}, u32[]{:S(2)}) collective-permute-start(bf16[128,512]{1,0:T(8,128)(2,1)S(1)} %collective-permute-done.25.refs_6_), channel_id=1, source_target_pairs={{0,4},{4,0},{8,12},{12,8},{16,20},{20,16},{24,28},{28,24},{1,5},{5... | collective-permute-start | bytes 393224 | tf_op jit(solution)/shard_map/ppermute | solution.py:39
  180.1 39.9 %collective-permute-start.39 = (bf16[256,2048]{1,0:T(8,128)(2,1)S(1)}, bf16[256,2048]{1,0:T(8,128)(2,1)}, u32[]{:S(2)}, u32[]{:S(2)}) collective-permute-start(bf16[256,2048]{1,0:T(8,128)(2,1)S(1)} %copy-done.36), channel_id=1, source_target_pairs={{0,4},{4,0},{8,12},{12,8},{16,20},{20,16},{24,28},{28,24},{1,5},{5... | collective-permute-start | bytes 3145736 | tf_op jit(solution)/shard_map/ppermute | solution.py:39
  181.9 35.4 %collective-permute-start.32 = (bf16[512,256]{1,0:T(8,128)(2,1)S(1)}, bf16[512,256]{1,0:T(8,128)(2,1)S(1)}, u32[]{:S(2)}, u32[]{:S(2)}) collective-permute-start(bf16[512,256]{1,0:T(8,128)(2,1)S(1)} %bitcast.115), channel_id=1, source_target_pairs={{0,1},{1,0},{2,3},{3,2},{4,5},{5,4},{6,7},{7,6},{8,9},{9,8},{10,11... | collective-permute-start | bytes 786440 | tf_op jit(solution)/shard_map/ppermute | solution.py:39
  182.9 30.1 %collective-permute-start.33 = (f32[3,256]{1,0:T(4,128)S(1)}, f32[3,256]{1,0:T(4,128)S(1)}, u32[]{:S(2)}, u32[]{:S(2)}) collective-permute-start(f32[3,256]{1,0:T(4,128)S(1)} %slice_add_fusion.3), channel_id=1, source_target_pairs={{0,1},{1,0},{2,3},{3,2},{4,5},{5,4},{6,7},{7,6},{8,9},{9,8},{10,11... | collective-permute-start | bytes 9224 | tf_op jit(solution)/shard_map/ppermute | solution.py:39
  209.1 3.5 %collective-permute-start.30 = (f32[3,256]{1,0:T(4,128)}, f32[3,256]{1,0:T(4,128)S(1)}, u32[]{:S(2)}, u32[]{:S(2)}) collective-permute-start(f32[3,256]{1,0:T(4,128)} %get-tuple-element.67), channel_id=1, source_target_pairs={{0,1},{1,0},{2,3},{3,2},{4,5},{5,4},{6,7},{7,6},{8,9},{9,8},{10,11... | collective-permute-start | bytes 9224 | tf_op jit(solution)/shard_map/ppermute | solution.py:39
  212.6 5.5 %collective-permute-start.27 = (bf16[64,2048]{1,0:T(8,128)(2,1)S(1)}, bf16[64,2048]{1,0:T(8,128)(2,1)S(1)}, u32[]{:S(2)}, u32[]{:S(2)}) collective-permute-start(bf16[64,2048]{1,0:T(8,128)(2,1)S(1)} %slice.81), channel_id=1, source_target_pairs={{0,1},{1,0},{2,3},{3,2},{4,5},{5,4},{6,7},{7,6},{8,9},{9,8},{10,11... | collective-permute-start | bytes 786440 | tf_op jit(solution)/shard_map/ppermute | solution.py:39
  213.0 3.7 %collective-permute-start.31 = (f32[3,256]{1,0:T(4,128)S(1)}, f32[3,256]{1,0:T(4,128)S(1)}, u32[]{:S(2)}, u32[]{:S(2)}) collective-permute-start(f32[3,256]{1,0:T(4,128)S(1)} %add.84), channel_id=1, source_target_pairs={{0,2},{1,3},{2,0},{3,1},{4,6},{5,7},{6,4},{7,5},{8,10},{9,11},{10,... | collective-permute-start | bytes 9224 | tf_op jit(solution)/shard_map/ppermute | solution.py:39
  214.2 34.8 %collective-permute-start.45 = (bf16[256,2048]{1,0:T(8,128)(2,1)}, bf16[256,2048]{1,0:T(8,128)(2,1)}, u32[]{:S(2)}, u32[]{:S(2)}) collective-permute-start(bf16[256,2048]{1,0:T(8,128)(2,1)} %constant_dynamic-update-slice_fusion.11.refs_2_.refs_6_), channel_id=1, source_target_pairs={{0,1},{1,0},{2,3},{3,2},{4,5},{5,4},{6,7},{7,6},{8,9},{9,8},{10,11... | collective-permute-start | bytes 3145736 | tf_op jit(solution)/shard_map/ppermute | solution.py:39
  216.7 32.3 %collective-permute-start.47 = (bf16[256,2048]{1,0:T(8,128)(2,1)}, bf16[256,2048]{1,0:T(8,128)(2,1)}, u32[]{:S(2)}, u32[]{:S(2)}) collective-permute-start(bf16[256,2048]{1,0:T(8,128)(2,1)} %collective-permute-done.46.refs_3_.refs_7_), channel_id=1, source_target_pairs={{0,1},{1,0},{2,3},{3,2},{4,5},{5,4},{6,7},{7,6},{8,9},{9,8},{10,11... | collective-permute-start | bytes 3145736 | tf_op jit(solution)/shard_map/ppermute | solution.py:39
  217.3 31.7 %collective-permute-start.38 = (bf16[256,2048]{1,0:T(8,128)(2,1)S(1)}, bf16[256,2048]{1,0:T(8,128)(2,1)}, u32[]{:S(2)}, u32[]{:S(2)}) collective-permute-start(bf16[256,2048]{1,0:T(8,128)(2,1)S(1)} %copy-done.36), channel_id=1, source_target_pairs={{0,1},{1,0},{2,3},{3,2},{4,5},{5,4},{6,7},{7,6},{8,9},{9,8},{10,11... | collective-permute-start | bytes 3145736 | tf_op jit(solution)/shard_map/ppermute | solution.py:39
  218.2 8.3 %collective-permute-start.28 = (bf16[64,2048]{1,0:T(8,128)(2,1)S(1)}, bf16[64,2048]{1,0:T(8,128)(2,1)S(1)}, u32[]{:S(2)}, u32[]{:S(2)}) collective-permute-start(bf16[64,2048]{1,0:T(8,128)(2,1)S(1)} %fusion.1.low), channel_id=1, source_target_pairs={{0,2},{1,3},{2,0},{3,1},{4,6},{5,7},{6,4},{7,5},{8,10},{9,11},{10,... | collective-permute-start | bytes 786440 | tf_op jit(solution)/shard_map/ppermute | solution.py:39
  220.0 29.0 %collective-permute-start.40 = (bf16[256,2048]{1,0:T(8,128)(2,1)}, bf16[256,2048]{1,0:T(8,128)(2,1)}, u32[]{:S(2)}, u32[]{:S(2)}) collective-permute-start(bf16[256,2048]{1,0:T(8,128)(2,1)} %collective-permute-done.39.refs_1_.refs_5_), channel_id=1, source_target_pairs={{0,1},{1,0},{2,3},{3,2},{4,5},{5,4},{6,7},{7,6},{8,9},{9,8},{10,11... | collective-permute-start | bytes 3145736 | tf_op jit(solution)/shard_map/ppermute | solution.py:39
  229.7 18.1 %collective-permute-start.29 = (bf16[64,2048]{1,0:T(8,128)(2,1)}, bf16[64,2048]{1,0:T(8,128)(2,1)S(1)}, u32[]{:S(2)}, u32[]{:S(2)}) collective-permute-start(bf16[64,2048]{1,0:T(8,128)(2,1)} %last.1), channel_id=1, source_target_pairs={{0,1},{1,0},{2,3},{3,2},{4,5},{5,4},{6,7},{7,6},{8,9},{9,8},{10,11... | collective-permute-start | bytes 786440 | tf_op jit(solution)/shard_map/ppermute | solution.py:39
  (46 other events, 452.3 us)
where the time goes:
time: 270 us; the launch traced here: 269 us
  Pallas kernels  91.8 us (34%)
  waiting for transfers between devices  60.2 us (22%)
  starting transfers between devices  48.8 us (18%)
  matrix products  36.7 us (14%)
  local copies, waits for them, and re-layouts  22.8 us (8%)
  other arithmetic  7 us (3%)
    ppermute x48, waiting for transfers between devices, swap(): return lax.ppermute(value, axis, [(i, i ^ bit) for i in range(size)])  60.2 us
    ppermute x48, starting transfers between devices, swap(): return lax.ppermute(value, axis, [(i, i ^ bit) for i in range(size)])  42.6 us
    pallas_call x2, Pallas kernels, feed_all(): pl.pallas_call(partial(all_kernel, count=count, first=not sums), grid_spe...  37.7 us
    dot_general x16, matrix products, dot(): return lax.dot_general(a, b, (dims, ((), ())), preferred_element_type=f32)  36.7 us
    pallas_call x1, Pallas kernels, attend_back(): pl.pallas_call(partial(backward_kernel, count=count, groups=groups, scale...  17.5 us
    unnamed x102, local copies, waits for them, and re-layouts  12.5 us
    pallas_call x1, Pallas kernels, feed_own(): pl.pallas_call(own_kernel, grid=(hidden // tile,), in_specs=[pl.BlockSpec...  9.2 us
    all_to_all x1, starting transfers between devices, body(): lax.all_to_all(jnp.concatenate([mixed_half, second_sums], axis=0).reshape...  6.2 us
  transfers between devices with their start and end apart: 49, of which 14 were waited for; matrix products, arithmetic and copies ran while one was open for 22% of the time, Pallas kernels for 27%

commit v1 on v0

--- a/solution.py
+++ b/solution.py
@@ -13,7 +13,6 @@
 bf16 = jnp.bfloat16
 f32 = jnp.float32
 NEGATIVE = -1e30
-VMEM_LIMIT = 60 * 1024 * 1024
 
 NN = ((1,), (0,))
 NT = ((1,), (1,))
@@ -24,13 +23,15 @@
     return lax.dot_general(a, b, (dims, ((), ())), preferred_element_type=f32)
 
 
-def params():
-    return pltpu.CompilerParams(vmem_limit_bytes=VMEM_LIMIT)
-
-
-def cost(flops, moved, transcendentals=0):
+def params(mebibytes):
+    return pltpu.CompilerParams(vmem_limit_bytes=mebibytes * 1024 * 1024)
+
+
+def cost(flops, moved, transcendentals=0, share=100):
     return pl.CostEstimate(
-        flops=int(flops), bytes_accessed=int(moved), transcendentals=int(transcendentals)
+        flops=int(flops) // share,
+        bytes_accessed=int(moved) // share,
+        transcendentals=int(transcendentals) // share,
     )
 
 
@@ -47,15 +48,24 @@
     return lax.axis_size("mlp") // 2
 
 
+def after(values, *earlier):
+    return lax.optimization_barrier((values, earlier))[0]
+
+
+def in_hbm(array):
+    return pltpu.with_memory_space_constraint(array, pltpu.HBM)
+
+
 def own_quarter(half):
     rows = half.shape[0] // x_size()
     return lax.dynamic_slice_in_dim(half, (lax.axis_index("mlp") // 2) * rows, rows, 0)
 
 
-def join_x(quarter):
+def join_x(quarter, *earlier):
     bit = 1
     while bit < x_size():
-        quarter = jnp.concatenate([quarter, swap(quarter, "mlp", 2 * bit)], axis=0)
+        came = after(swap(quarter, "mlp", 2 * bit), earlier)
+        quarter = jnp.concatenate([quarter, came], axis=0)
         bit *= 2
     return quarter
 
@@ -74,25 +84,34 @@
     return [pieces[d] for d in range(size)]
 
 
-def gather_late(half, after=None):
+def gather_outer(half):
     size, inner = lax.axis_size("seq"), inner_size()
     quarter = own_quarter(half)
-    if after is not None:
-        quarter, half, _ = lax.optimization_barrier((quarter, half, after))
-    far = [swap(quarter, "seq", outer) for outer in range(inner, size, inner)]
-    near = jnp.concatenate([half, join_x(jnp.concatenate(far, axis=0))], axis=0)
-    rows = [near] + [swap(near, "seq", bit) for bit in range(1, inner)]
-    return rows, [swap(array, "mlp", 1) for array in rows]
-
-
-def gather_pieces(piece):
+    return [swap(quarter, "seq", outer) for outer in range(inner, size, inner)]
+
+
+def gather_inner(array):
+    return [swap(array, "seq", bit) for bit in range(1, inner_size())]
+
+
+def with_core(arrays):
+    return [each for array in arrays for each in (array, swap(array, "mlp", 1))]
+
+
+def gather_first(piece):
     size, inner = lax.axis_size("seq"), inner_size()
     pieces = {0: piece}
-    for outer in range(inner, size, inner):
-        pieces[outer] = swap(piece, "seq", outer)
-    for outer in range(0, size, inner):
+    for bit in range(1, inner):
+        pieces[bit] = swap(piece, "seq", bit)
+    return pieces, [swap(piece, "seq", outer) for outer in range(inner, size, inner)]
+
+
+def gather_pieces(pieces, far):
+    size, inner = lax.axis_size("seq"), inner_size()
+    for outer, came in zip(range(inner, size, inner), far):
+        pieces[outer] = came
         for bit in range(1, inner):
-            pieces[outer | bit] = swap(pieces[outer], "seq", bit)
+            pieces[outer | bit] = swap(came, "seq", bit)
     return [pieces[d] for d in range(size)]
 
 
@@ -100,11 +119,8 @@
     return lax.optimization_barrier(value.astype(bf16))
 
 
-def pair_mlp(partial_sum):
-    half = partial_sum.shape[0] // 2
-    came = swap(partial_sum[half:].astype(bf16), "mlp", 1)
-    total = partial_sum[:half] + came.astype(f32)
-    low, other = rounded(total), None
+def pair_mlp(mine, other_half):
+    low, other = rounded(mine + swap(other_half, "mlp", 1).astype(f32)), None
     bit = 2
     while bit < lax.axis_size("mlp"):
         if other is not None:
@@ -206,6 +222,99 @@
     )(index, frames, texts, actions)
 
 
+def rows_kernel(*refs, count):
+    rows, weights, outs = refs[0], refs[1 : 1 + count], refs[1 + count :]
+    for weight, out in zip(weights, outs):
+        out[...] = dot(rows[...], weight[...], NN).astype(bf16)
+
+
+def project_rows(rows, *weights):
+    across = weights[0].shape[1]
+    return pl.pallas_call(
+        partial(rows_kernel, count=len(weights)),
+        out_shape=[jax.ShapeDtypeStruct((rows.shape[0], across), bf16)] * len(weights),
+        compiler_params=params(16),
+        cost_estimate=cost(2 * rows.size * across * len(weights), 2 * rows.size),
+        name="project_rows",
+    )(rows, *weights)
+
+
+def one_kernel(rows, weight, out):
+    out[...] = dot(rows[...], weight[...], NT).astype(bf16)
+
+
+def product_back(rows, weight):
+    return pl.pallas_call(
+        one_kernel,
+        out_shape=jax.ShapeDtypeStruct((rows.shape[0], weight.shape[0]), bf16),
+        compiler_params=params(10),
+        cost_estimate=cost(2 * rows.size * weight.shape[0], 2 * weight.size),
+        name="product_back",
+    )(rows, weight)
+
+
+def halves_kernel(*refs, count, dims):
+    mine, other = refs[-2:]
+    half = mine.shape[0]
+    total = sum(dot(refs[k][...], refs[count + k][...], dims) for k in range(count))
+    mine[...] = total[:half]
+    other[...] = total[half:].astype(bf16)
+
+
+def product_halves(rows, weights, dims):
+    count = len(rows)
+    half = rows[0].shape[0] // 2
+    across = weights[0].shape[1 - dims[1][0]]
+    shape = (half, across)
+    return pl.pallas_call(
+        partial(halves_kernel, count=count, dims=dims),
+        out_shape=[jax.ShapeDtypeStruct(shape, f32), jax.ShapeDtypeStruct(shape, bf16)],
+        compiler_params=params(16),
+        cost_estimate=cost(2 * count * rows[0].size * across, 2 * count * weights[0].size),
+        name="product_halves",
+    )(*rows, *weights)
+
+
+def down_own_kernel(rows, weight, mine, other, total):
+    term = dot(rows[...], weight[...], NN)
+
+    @pl.when(pl.program_id(0) == 0)
+    def _():
+        total[...] = term
+
+    @pl.when(pl.program_id(0) > 0)
+    def _():
+        total[...] += term
+
+    @pl.when(pl.program_id(0) == pl.num_programs(0) - 1)
+    def _():
+        half = mine.shape[0]
+        mine[...] = total[:half]
+        other[...] = total[half:].astype(bf16)
+
+
+def down_own(rows, weight):
+    count, deep = rows.shape
+    across = weight.shape[1]
+    tile = math.gcd(deep, 512)
+    shape = (count // 2, across)
+    whole = pl.BlockSpec(shape, lambda t: (0, 0))
+    return pl.pallas_call(
+        down_own_kernel,
+        grid=(deep // tile,),
+        in_specs=[
+            pl.BlockSpec((count, tile), lambda t: (0, t)),
+            pl.BlockSpec((tile, across), lambda t: (t, 0)),
+        ],
+        out_specs=[whole, whole],
+        out_shape=[jax.ShapeDtypeStruct(shape, f32), jax.ShapeDtypeStruct(shape, bf16)],
+        scratch_shapes=[pltpu.VMEM((count, across), f32)],
+        compiler_params=params(12),
+        cost_estimate=cost(2 * rows.size * across, 2 * weight.size),
+        name="down_own",
+    )(rows, in_hbm(weight))
+
+
 def gain_rows(gain, column):
     return jnp.where(
         column == 0, gain[0:1, :], jnp.where(column == 1, gain[1:2, :], gain[2:3, :])
@@ -263,7 +372,7 @@
         partial(norm_kernel, groups=groups, inner=inner_size(), parts=parts),
         in_specs=memory + [pl.BlockSpec(memory_space=pltpu.VMEM)] * (count + 2),
         out_shape=jax.ShapeDtypeStruct(shape + (width,), bf16),
-        compiler_params=params(),
+        compiler_params=params(20),
         cost_estimate=cost(10 * count * rows * width, 4 * count * rows * width),
         name="norm_pieces",
     )(index, *pieces, gain, kind.reshape(shape + (1,)))
@@ -279,7 +388,7 @@
     return pl.pallas_call(
         own_norm_kernel,
         out_shape=jax.ShapeDtypeStruct(rows.shape, bf16),
-        compiler_params=params(),
+        compiler_params=params(8),
         cost_estimate=cost(10 * rows.size, 4 * rows.size),
         name="own_norm",
     )(rows, gain, kind)
@@ -296,7 +405,7 @@
     return pl.pallas_call(
         lift_kernel,
         out_shape=[jax.ShapeDtypeStruct(rows.shape, f32), jax.ShapeDtypeStruct(rows.shape, bf16)],
-        compiler_params=params(),
+        compiler_params=params(8),
         cost_estimate=cost(10 * rows.size, 12 * rows.size),
         name="lift",
     )(rows, low, other, gain, kind)
@@ -330,7 +439,7 @@
             jax.ShapeDtypeStruct(residual.shape, bf16),
             jax.ShapeDtypeStruct((8, width), bf16),
         ],
-        compiler_params=params(),
+        compiler_params=params(10),
         cost_estimate=cost(20 * residual.size, 16 * residual.size),
         name="middle",
     )(residual, low, other, grad, gain, kind)
@@ -347,7 +456,7 @@
     return pl.pallas_call(
         last_kernel,
         out_shape=jax.ShapeDtypeStruct(rows.shape, bf16),
-        compiler_params=params(),
+        compiler_params=params(8),
         cost_estimate=cost(20 * rows.size, 12 * rows.size),
         name="last",
     )(rows, low, other, grad_residual, gain, kind)
@@ -362,7 +471,7 @@
     return value * upper, slope
 
 
-def own_kernel(lifted, up, grad_activated, activated, lifted_grad):
+def own_kernel(lifted, up, grad_activated, activated, mine, other, lifted_grad):
     value, slope = gelu_parts(dot(lifted[...], up[...], NN))
     activated[...] = value.astype(bf16)
     hidden_grad = (grad_activated[...] * slope).astype(bf16)
@@ -375,6 +484,12 @@
     @pl.when(pl.program_id(0) > 0)
     def _():
         lifted_grad[...] += term
+
+    @pl.when(pl.program_id(0) == pl.num_programs(0) - 1)
+    def _():
+        half = mine.shape[0]
+        mine[...] = lifted_grad[:half]
+        other[...] = lifted_grad[half:].astype(bf16)
 
 
 def feed_own(lifted, up, grad_activated):
@@ -391,68 +506,116 @@
             pl.BlockSpec((width, tile), across),
             pl.BlockSpec((rows, tile), across),
         ],
-        out_specs=[pl.BlockSpec((rows, tile), across), pl.BlockSpec((rows, width), whole)],
+        out_specs=[pl.BlockSpec((rows, tile), across)]
+        + [pl.BlockSpec((rows // 2, width), whole)] * 2,
         out_shape=[
             jax.ShapeDtypeStruct((rows, hidden), bf16),
-            jax.ShapeDtypeStruct((rows, width), f32),
+            jax.ShapeDtypeStruct((rows // 2, width), f32),
+            jax.ShapeDtypeStruct((rows // 2, width), bf16),
         ],
-        compiler_params=params(),
+        scratch_shapes=[pltpu.VMEM((rows, width), f32)],
+        compiler_params=params(16),
         cost_estimate=cost(4 * rows * width * hidden, 2 * width * hidden),
         name="feed_own",
     )(lifted, up, grad_activated)
 
 
-def all_kernel(index, *refs, count, first):
-    lifted, grad = refs[:count], refs[count : 2 * count]
-    lifted_part, grad_part = refs[2 * count : 3 * count], refs[3 * count : 4 * count]
-    up, down = refs[4 * count : 4 * count + 2]
-    up_grad, down_grad = refs[-2:]
-    up_sum = None if first else refs[4 * count + 2][...]
-    down_sum = None if first else refs[4 * count + 3][...]
-    for k in range(count):
-        value, slope = gelu_parts(dot(lifted[k][...], up[...], NN))
-        hidden_grad = (dot(grad[k][...], down[...], NT) * slope).astype(bf16)
-        down_term = dot(value.astype(bf16), grad_part[k][...], TN)
-        up_term = dot(lifted_part[k][...], hidden_grad, TN)
-        up_sum = up_term if up_sum is None else up_sum + up_term
-        down_sum = down_term if down_sum is None else down_sum + down_term
-    up_grad[...] = up_sum
-    down_grad[...] = down_sum
-
-
-def feed_all(lifted, grad, up, down, shards, sums=()):
-    rows, width = lifted[0].shape
-    count = len(lifted)
+def down_kernel(grad, down, out):
+    out[...] = dot(grad[...], down[...], NT)
+
+
+def grad_activated(grad, down):
+    rows, width = grad.shape
+    hidden = down.shape[0]
+    tile = math.gcd(hidden, 512)
+    return pl.pallas_call(
+        down_kernel,
+        grid=(hidden // tile,),
+        in_specs=[
+            pl.BlockSpec((rows, width), lambda t: (0, 0)),
+            pl.BlockSpec((tile, width), lambda t: (t, 0)),
+        ],
+        out_specs=pl.BlockSpec((rows, tile), lambda t: (0, t)),
+        out_shape=jax.ShapeDtypeStruct((rows, hidden), f32),
+        compiler_params=params(12),
+        cost_estimate=cost(2 * rows * width * hidden, 2 * width * hidden),
+        name="grad_activated",
+    )(grad, down)
+
+
+def all_kernel(index, *refs, counts, add):
+    count = len(counts)
+    lifted_parts, grad_parts = refs[:count], refs[count : 2 * count]
+    up, down = refs[2 * count : 2 * count + 2]
+    up_grad, down_grad, lifted, grad, sems = refs[-5:]
+
+    @pl.when(pl.program_id(0) == 0)
+    def _():
+        copies = []
+        for k, (source, target) in enumerate(((lifted_parts, lifted), (grad_parts, grad))):
+            start = 0
+            for j, rows in enumerate(counts):
+                here = target.at[pl.ds(start, rows)]
+                copies.append(pltpu.make_async_copy(source[j], here, sems.at[k * count + j]))
+                start += rows
+        for copy in copies:
+            copy.start()
+        for copy in copies:
+            copy.wait()
+
+    part = up_grad.shape[0]
+    mine = pl.ds(pl.multiple_of(index[0] * part, part), part)
+    value, slope = gelu_parts(dot(lifted[...], up[...], NN))
+    hidden_grad = (dot(grad[...], down[...], NT) * slope).astype(bf16)
+    down_term = dot(value.astype(bf16), grad[:, mine], TN)
+    up_term = dot(lifted[:, mine], hidden_grad, TN)
+    if add:
+        up_term += refs[2 * count + 2][...]
+        down_term += refs[2 * count + 3][...]
+    up_grad[...] = up_term
+    down_grad[...] = down_term
+
+
+def feed_all(lifted, grad, up, down, shards, place, places, sums, add):
+    counts = [array.shape[0] for array in lifted]
+    rows, width = sum(counts), lifted[0].shape[1]
+    count = len(counts)
     part = width // shards
     hidden = up.shape[1]
-    tile = math.gcd(hidden, 256)
-    across = lambda t, index: (0, t)
-    below = lambda t, index: (t, 0)
-    whole = lambda t, index: (0, 0)
-    mine = lambda t, index: (0, index[0])
+    tile = math.gcd(hidden // places, 256)
+    steps = hidden // places // tile
+    first = place * steps
+    across = lambda t, index: (0, first + t)
+    below = lambda t, index: (first + t, 0)
+    anywhere = pl.BlockSpec(memory_space=pl.ANY)
     sum_specs = [pl.BlockSpec((part, tile), across), pl.BlockSpec((tile, part), below)]
     index = lax.axis_index("seq").astype(jnp.int32).reshape(1)
-    return pl.pallas_call(
-        partial(all_kernel, count=count, first=not sums),
+    at = 1 + 2 * count + 2
+    return pl.pallas_call(
+        partial(all_kernel, counts=counts, add=add),
         grid_spec=pltpu.PrefetchScalarGridSpec(
             num_scalar_prefetch=1,
-            grid=(hidden // tile,),
-            in_specs=[pl.BlockSpec((rows, width), whole)] * (2 * count)
-            + [pl.BlockSpec((rows, part), mine)] * (2 * count)
+            grid=(steps,),
+            in_specs=[anywhere] * (2 * count)
             + [pl.BlockSpec((width, tile), across), pl.BlockSpec((tile, width), below)]
-            + (sum_specs if sums else []),
+            + ((sum_specs if add else [anywhere] * 2) if sums else []),
             out_specs=sum_specs,
+            scratch_shapes=[pltpu.VMEM((rows, width), bf16)] * 2
+            + [pltpu.SemaphoreType.DMA((2 * count,))],
         ),
         out_shape=[
             jax.ShapeDtypeStruct((part, hidden), f32),
             jax.ShapeDtypeStruct((hidden, part), f32),
         ],
-        compiler_params=params(),
+        input_output_aliases={at: 0, at + 1: 1} if sums else {},
+        compiler_params=params(10 + 20 * rows // 640),
         cost_estimate=cost(
-            4 * count * rows * hidden * (width + part), 4 * width * hidden + 4 * count * rows * width
+            4 * rows * hidden // places * (width + part),
+            4 * width * hidden // places + 4 * rows * width,
+            share=4,
         ),
         name="feed_all",
-    )(index, *lifted, *grad, *lifted, *grad, up, down, *sums)
+    )(index, *lifted, *grad, in_hbm(up), in_hbm(down), *sums)
 
 
 def project_kernel(index, *refs):
@@ -494,10 +657,40 @@
         ),
         out_shape=[jax.ShapeDtypeStruct((part, across), f32)] * 3
         + [jax.ShapeDtypeStruct((gain.shape[0], part), f32)],
-        compiler_params=params(),
+        compiler_params=params(20),
         cost_estimate=cost(24 * rows * part * across, 12 * rows * across + 12 * part * across),
         name="project",
     )(index, *normed, *[low for pair in lows for low in pair], *weights, gain, *kinds)
+
+
+def output_kernel(index, attended_a, attended_b, mixed_a, mixed_b, out, *, groups):
+    total = 0.0
+    shards, half, part = mixed_a.shape
+    each = half // groups
+    for attended, mixed in ((attended_a, mixed_a), (attended_b, mixed_b)):
+        rows = [
+            mixed[index[0] ^ d, pl.ds(group * each, each), :]
+            for group in range(groups)
+            for d in range(shards)
+        ]
+        total += dot(attended[...], jnp.concatenate(rows, axis=0), TN)
+    out[...] = total
+
+
+def output_part(attended, mixed, groups):
+    index = lax.axis_index("seq").astype(jnp.int32).reshape(1)
+    across, part = attended[0].shape[1], mixed[0].shape[2]
+    return pl.pallas_call(
+        partial(output_kernel, groups=groups),
+        in_specs=[pl.BlockSpec(memory_space=pltpu.SMEM)]
+        + [pl.BlockSpec(memory_space=pltpu.VMEM)] * 4,
+        out_shape=jax.ShapeDtypeStruct((across, part), f32),
+        compiler_params=params(10),
+        cost_estimate=cost(
+            4 * attended[0].shape[0] * across * part, 4 * attended[0].shape[0] * (across + part)
+        ),
+        name="output_part",
+    )(index, *attended, *mixed)
 
 
 def mask_of(key_place, query_place, clip_length, clips):
@@ -546,7 +739,7 @@
             forward_kernel, scale=1.0 / math.sqrt(HEAD_DIM), clip_length=clip_length, clips=clips
         ),
         out_shape=jax.ShapeDtypeStruct((rows, width), bf16),
-        compiler_params=params(),
+        compiler_params=params(16),
         cost_estimate=cost(
             4 * rows * total * width, 4 * total * width, rows * total * (width // HEAD_DIM)
         ),
@@ -682,12 +875,12 @@
         out_shape=[jax.ShapeDtypeStruct((half, width), bf16)] * 8
         + [jax.ShapeDtypeStruct((rows, width), bf16)] * 3,
         scratch_shapes=[pltpu.VMEM((half, HEAD_DIM), f32)] * 4,
-        compiler_params=params(),
+        compiler_params=params(32),
         cost_estimate=cost(
             12 * 4 * half * half * width, 32 * half * width, 4 * half * half * heads
         ),
         name="attend_back",
-    )(*grads, *queries, *keys, *values, *places, query_place)
+    )(*[in_hbm(grad) for grad in grads], *queries, *keys, *values, *places, query_place)
     return outs[0:2], outs[2:4], outs[4:6], outs[6:8], outs[8:11]
 
 
@@ -736,8 +929,7 @@
 
     inputs_half, inputs_other = halves(inputs)
     pieces = gather_early(inputs_half)
-    grad_half, grad_other = halves(cotangent)
-    grad_own = jnp.concatenate([grad_half, grad_other], axis=0)
+    arrived = pieces[inner_size() :: inner_size()]
 
     place_a, place_b, kind_a, kind_b, query_place, own_place, own_kind = tables(
         frame_sizes, text_counts, action_counts, shards, length, groups
@@ -747,31 +939,60 @@
     own_normed = own_norm(
         jnp.concatenate([inputs_half, inputs_other], axis=0), first_gain, own_kind
     )
-    query_own = dot(own_normed, query_weight, NN).astype(bf16)
-    own_activated_grad = dot(grad_own, down_weight, NT)
+    grad_half, grad_other = halves(cotangent)
+    grad_own = jnp.concatenate([grad_half, grad_other], axis=0)
+    (query_own,) = project_rows(after(own_normed, arrived), query_weight)
+    own_activated_grad = grad_activated(after(grad_own, query_own), down_weight)
+    grad_far = gather_outer(after(grad_half, arrived))
+    pieces, grad_far = after((pieces, grad_far), own_activated_grad)
 
     normed = [norm_pieces(pieces, first_gain, kind_a, groups)]
     normed.append(swap(normed[0], "mlp", 1))
-    keys = [dot(rows, key_weight, NN).astype(bf16) for rows in normed]
-    values = [dot(rows, value_weight, NN).astype(bf16) for rows in normed]
+    keys, values = zip(*[project_rows(rows, key_weight, value_weight) for rows in normed])
     heads_own = attend(query_own, keys, values, places, own_place, clip_length, clips)
-    low, other = pair_mlp(dot(heads_own, output_weight, NN))
+    grad_far = join_x(jnp.concatenate(after(grad_far, normed[0]), axis=0), heads_own)
+    mine, other = product_halves([heads_own], [output_weight], NN)
+    other, grad_far = after((other, grad_far), other)
+    grad_inner = gather_inner(grad_half) + gather_inner(grad_far)
+    low, other = pair_mlp(mine, other)
+    queries = [project_rows(rows, query_weight)[0] for rows in after(normed, low)]
+    other = after(other, queries)
     residual, lifted_half = lift(inputs_half, low, other, second_gain, half_kind)
-    queries = [dot(rows, query_weight, NN).astype(bf16) for rows in normed]
-    grads = gather_late(grad_half, after=pieces[-1])
-
-    lifted = gather_late(lifted_half)
-    activated_own, lifted_term = feed_own(both(lifted_half), up_weight, own_activated_grad)
-    low, other = pair_mlp(lifted_term)
+
+    lifted_own = both(lifted_half)
+    activated_own, mine, other = feed_own(lifted_own, up_weight, own_activated_grad)
+    lifted_far = gather_outer(after(lifted_half, other))
+    other, grad_inner = after((other, grad_inner), other)
+    low, other = pair_mlp(mine, other)
+    down_mine, down_other = down_own(after(activated_own, low), down_weight)
+    other, lifted_far = after((other, lifted_far), down_other)
     grad_residual, mixed_half, second_sums = middle(
         residual, low, other, grad_half, second_gain, half_kind
     )
-    heads_grad = dot(both(mixed_half), output_weight, NT).astype(bf16)
-    low, other = pair_mlp(dot(activated_own, down_weight, NN))
-    outputs = restore((residual + (low.astype(f32) + other.astype(f32))).astype(bf16))
+    heads_grad = product_back(both(mixed_half), output_weight)
+
+    places_up = 2
+    sums = ()
+
+    def feed(lifted, grads, place, add, *earlier):
+        return feed_all(
+            after(lifted, earlier), grads, up_weight, down_weight, shards, place, places_up, sums, add
+        )
+
+    heads_first = gather_first(heads_grad)
+    lifted_far = join_x(jnp.concatenate(lifted_far, axis=0), heads_first)
+    heads_grads = gather_pieces(*heads_first)
+    first_lifted = [lifted_own] + with_core([lifted_far])
+    first_grads = [grad_own] + with_core([grad_far])
+    sums = feed(first_lifted, first_grads, 0, False, heads_grads[inner_size() + 1])
+    sums = feed(first_lifted, first_grads, 1, False)
+    down_low, down_other = pair_mlp(down_mine, after(down_other, heads_grad))
+    heads_grads, down_low = after((heads_grads, down_low), sums)
+    lifted_inner = gather_inner(after(lifted_half, heads_grads))
+    lifted_inner += gather_inner(after(lifted_far, heads_grads))
 
     attended, query_low, key_low, value_low, own_low = attend_back(
-        gather_pieces(heads_grad),
+        heads_grads,
         queries,
         keys,
         values,
@@ -781,40 +1002,46 @@
         clip_length,
         clips,
     )
+    own_low, lifted_inner, down_other = after((own_low, lifted_inner, down_other), own_low)
+    rest_lifted, rest_grads = with_core(lifted_inner), with_core(grad_inner)
     attention_weights = (query_weight, key_weight, value_weight)
-    normed_term = sum(dot(low, weight, NT) for low, weight in zip(own_low, attention_weights))
-    low, other = pair_mlp(normed_term)
-    input_grad = restore(last(inputs_half, low, other, grad_residual, first_gain, half_kind))
+    low, other = pair_mlp(*product_halves(own_low, attention_weights, NT))
+    sums = feed(rest_lifted, rest_grads, 0, True, low)
+    other = after(other, sums)
+    input_grad_half = last(inputs_half, low, other, grad_residual, first_gain, half_kind)
+    input_grad = restore(input_grad_half)
+
+    mixed_part = lax.all_to_all(
+        after(jnp.concatenate([mixed_half, second_sums], axis=0), other).reshape(
+            half + 8, shards, part
+        ),
+        "seq",
+        split_axis=1,
+        concat_axis=0,
+        tiled=False,
+    )
+    down_total = down_low.astype(f32) + after(down_other, input_grad_half).astype(f32)
+    outputs = restore((residual + down_total).astype(bf16))
 
     query_grad, key_grad, value_grad, first_gain_grad = project(
-        normed, (query_low, key_low, value_low), attention_weights, first_gain, kinds, shards
+        normed,
+        after((query_low, key_low, value_low), other),
+        attention_weights,
+        first_gain,
+        kinds,
+        shards,
     )
     bit = 1
     while bit < lax.axis_size("mlp"):
         first_gain_grad = first_gain_grad + swap(first_gain_grad, "mlp", bit)
         bit *= 2
-
-    came = lax.all_to_all(
-        jnp.concatenate([mixed_half, second_sums], axis=0).reshape(half + 8, shards, part),
-        "seq",
-        split_axis=1,
-        concat_axis=0,
-        tiled=False,
-    )
-    second_sums = jnp.sum(came[:, half : half + 6].astype(f32), axis=0)
+    up_grad, down_grad = feed(rest_lifted, rest_grads, 1, True, query_grad)
+
+    second_sums = jnp.sum(mixed_part[:, half : half + 6].astype(f32), axis=0)
     second_sums = second_sums[:3] + second_sums[3:]
     second_gain_grad = second_sums + swap(second_sums, "mlp", 1)
-    came = came[shard_index ^ jnp.arange(shards, dtype=jnp.int32), :half]
-    if groups > 1:
-        came = came.reshape(shards, shards, piece, part).transpose(1, 0, 2, 3)
-    mixed_part = [came.reshape(-1, part)]
-    mixed_part.append(swap(mixed_part[0], "mlp", 1))
-    output_grad = sum(dot(rows, mixed, TN) for rows, mixed in zip(attended, mixed_part))
-
-    sums = ()
-    for side in range(2):
-        sums = feed_all(lifted[side], grads[side], up_weight, down_weight, shards, sums)
-    up_grad, down_grad = sums
+    mixed_part = after(mixed_part[:, :half], up_grad)
+    output_grad = output_part(attended, (mixed_part, swap(mixed_part, "mlp", 1)), groups)
 
     return (
         outputs,

time: 270 us -> 233 us (0.86)
  matrix products: 36.7 us -> 0 us
  Pallas kernels: 91.8 us -> 103 us
  local copies, waits for them, and re-layouts: 22.8 us -> 12.9 us
  waiting for transfers between devices: 60.2 us -> 52.1 us
  starting transfers between devices: 48.8 us -> 52.1 us
  other arithmetic: 7 us -> 10.2 us
    dot_general x16 -> x0, matrix products: 36.7 us -> none  [dot(): return lax.dot_general(a, b, (dims, ((), ())), preferred_element_type=f32)]
    pallas_call x2 -> x15, Pallas kernels: 37.7 us -> 64.4 us  [the longest x4 43.3 us: feed_all(): pl.pallas_call(partial(all_kernel, counts=counts, add=add), grid_spec=plt...]
    ppermute x48 -> x52, waiting for transfers between devices: 60.2 us -> 52.1 us  [swap(): return lax.ppermute(value, axis, [(i, i ^ bit) for i in range(size)])]
    unnamed x102 -> x125, local copies, waits for them, and re-layouts: 12.5 us -> 4.61 us
    ppermute x48 -> x52, starting transfers between devices: 42.6 us -> 47.2 us  [swap(): return lax.ppermute(value, axis, [(i, i ^ bit) for i in range(size)])]
    concatenate x3 -> x7, other arithmetic: 0.06 us -> 3.58 us  [the longest x4 2.43 us: join_x(): quarter = jnp.concatenate([quarter, came], axis=0)]
    pallas_call x1, Pallas kernels: 9.2 us -> 6.2 us  [feed_own(): pl.pallas_call(own_kernel, grid=(hidden // tile,), in_specs=[pl.BlockSpec...]
    dynamic_slice x2 -> x3, local copies, waits for them, and re-layouts: 0.3 us -> 3.24 us  [halves(): other = lax.dynamic_index_in_dim(cut, 1 - core, 0, keepdims=False)]
  transfers between devices with their start and end apart: 49 -> 53, of which waited for: 14 -> 20; matrix products, arithmetic and copies ran while one was open for 22% -> 6% of each run, Pallas kernels for 27% -> 40%
where the time goes in v1:
time: 233 us; the launch traced here: 232 us
  Pallas kernels  103 us (44%)
  starting transfers between devices  52.1 us (22%)
  waiting for transfers between devices  52.1 us (22%)
  local copies, waits for them, and re-layouts  12.9 us (6%)
  other arithmetic  10.2 us (4%)
    ppermute x52, waiting for transfers between devices, swap(): return lax.ppermute(value, axis, [(i, i ^ bit) for i in range(size)])  52.1 us
    ppermute x52, starting transfers between devices, swap(): return lax.ppermute(value, axis, [(i, i ^ bit) for i in range(size)])  47.2 us
    pallas_call x4, Pallas kernels, feed_all(): pl.pallas_call(partial(all_kernel, counts=counts, add=add), grid_spec=plt...  43.3 us
    pallas_call x1, Pallas kernels, attend_back(): pl.pallas_call(partial(backward_kernel, count=count, groups=groups, scale...  17.2 us
    pallas_call x5, Pallas kernels, project_rows(): pl.pallas_call(partial(rows_kernel, count=len(weights)), out_shape=[jax.S...  7.58 us
    pallas_call x1, Pallas kernels, feed_own(): pl.pallas_call(own_kernel, grid=(hidden // tile,), in_specs=[pl.BlockSpec...  6.2 us
    pallas_call x1, Pallas kernels, down_own(): pl.pallas_call(down_own_kernel, grid=(deep // tile,), in_specs=[pl.BlockS...  5.42 us
    all_to_all x1, starting transfers between devices, body(): lax.all_to_all(after(jnp.concatenate([mixed_half, second_sums], axis=0),...  4.87 us
  transfers between devices with their start and end apart: 53, of which 20 were waited for; matrix products, arithmetic and copies ran while one was open for 6% of the time, Pallas kernels for 40%

profile of v1, /device:TPU:0, one launch (start us, length us, event | category | flops | bytes accessed | tf_op | source)
XLA Modules:
  0.0 231.8 jit_solution(3437108041053389173)
XLA Ops:
  0.7 2.0 constant_dynamic-slice_fusion.1
  2.9 3.1 %collective-permute-start = (bf16[32,2048]{1,0:T(8,128)(2,1)S(1)}, bf16[32,2048]{1,0:T(8,128)(2,1)S(1)}, u32[]{:S(2)}, u32[]{:S(2)}) collective-permute-start(bf16[32,2048]{1,0:T(8,128)(2,1)S(1)} %constant_dynamic-slice_fusion.4), channel_id=1, source_target_pairs={{0,8},{4,12},{8,0},{12,4},{16,24},{20,28},{24,16},{28,20},{1,9},{5... | collective-permute-start | bytes 393224 | tf_op jit(solution)/shard_map/ppermute | solution.py:40
  6.0 2.6 %collective-permute-start.2 = (bf16[32,2048]{1,0:T(8,128)(2,1)S(1)}, bf16[32,2048]{1,0:T(8,128)(2,1)S(1)}, u32[]{:S(2)}, u32[]{:S(2)}) collective-permute-start(bf16[32,2048]{1,0:T(8,128)(2,1)S(1)} %constant_dynamic-slice_fusion.4), channel_id=1, source_target_pairs={{0,16},{4,20},{8,24},{12,28},{16,0},{20,4},{24,8},{28,12},{1,17},{... | collective-permute-start | bytes 393224 | tf_op jit(solution)/shard_map/ppermute | solution.py:40
  8.6 2.4 %collective-permute-done = bf16[32,2048]{1,0:T(8,128)(2,1)S(1)} collective-permute-done((bf16[32,2048]{1,0:T(8,128)(2,1)S(1)}, bf16[32,2048]{1,0:T(8,128)(2,1)S(1)}, u32[]{:S(2)}, u32[]{:S(2)}) %collective-permute-start) | collective-permute-done | bytes 131104 | tf_op jit(solution)/shard_map/ppermute | solution.py:40
  11.0 1.7 collective-permute-start.1
  12.7 1.5 collective-permute-start.6
  14.5 4.4 %collective-permute-done.2 = bf16[32,2048]{1,0:T(8,128)(2,1)S(1)} collective-permute-done((bf16[32,2048]{1,0:T(8,128)(2,1)S(1)}, bf16[32,2048]{1,0:T(8,128)(2,1)S(1)}, u32[]{:S(2)}, u32[]{:S(2)}) %collective-permute-start.2) | collective-permute-done | bytes 131104 | tf_op jit(solution)/shard_map/ppermute | solution.py:40
  18.9 1.5 collective-permute-start.3
  20.9 2.9 %collective-permute-done.3 = bf16[32,2048]{1,0:T(8,128)(2,1)S(1)} collective-permute-done((bf16[32,2048]{1,0:T(8,128)(2,1)S(1)}, bf16[32,2048]{1,0:T(8,128)(2,1)S(1)}, u32[]{:S(2)}, u32[]{:S(2)}) %collective-permute-start.3) | collective-permute-done | bytes 131104 | tf_op jit(solution)/shard_map/ppermute | solution.py:40
  27.6 1.6 collective-permute-start.7
  29.7 1.5 collective-permute-start.9
  31.8 2.4 %tables.1 = (s32[512,1]{1,0:T(8,128)}, s32[512,1]{1,0:T(8,128)}, s32[512,1]{1,0:T(8,128)}, s32[512,1]{1,0:T(8,128)}, s32[1,1024]{1,0:T(1,128)}, /*index=5*/s32[1,128]{1,0:T(1,128)}, s32[128,1]{1,0:T(8,128)}) custom-call(s32[2]{0:T(128)} %pad_add_fusion.index, s32[1,8]{1,0:T(1,128)} %frames.1, s32[1,8]{1,0:T(1,128)} %texts.1, s32[1,8]{1,0:T(1,128)} %actions.1), custom_call_target="tpu_custom_call" | custom-call | flops 10485 | bytes 10485 | tf_op jit(solution)/shard_map/tables/pallas_call | solution.py:205
  36.6 2.1 collective-permute-start.11
  38.7 1.5 collective-permute-start.12
  40.8 3.4 %copy-done = bf16[2048,2048]{1,0:T(8,128)(2,1)S(1)} copy-done((bf16[2048,2048]{1,0:T(8,128)(2,1)S(1)}, bf16[2048,2048]{1,0:T(8,128)(2,1)}, u32[]{:S(2)}) %copy-start) | copy-done | bytes 8388632
  44.2 3.4 %grad_activated.1 = f32[128,2048]{1,0:T(8,128)S(1)} custom-call(bf16[128,2048]{1,0:T(8,128)(2,1)S(1)} %pad_maximum_fusion.2.grad.refs_3_, bf16[2048,2048]{1,0:T(8,128)(2,1)S(1)} %copy-done), custom_call_target="tpu_custom_call" | custom-call | flops 10737418 | bytes 83886 | tf_op jit(solution)/shard_map/grad_activated/pallas_call | solution.py:531
  47.7 3.8 %norm_pieces.1 = bf16[8,8,8,2048]{3,2,1,0:T(8,128)(2,1)S(1)} custom-call(s32[1]{0:T(128)} %bitcast.11.refs_0_, bf16[64,2048]{1,0:T(8,128)(2,1)S(1)} %bitcast.66, bf16[64,2048]{1,0:T(8,128)(2,1)} %collective-permute-done.6.refs_2_, bf16[64,2048]{1,0:T(8,128)(2,1)S(1)} %pad_maximum_fusion.7.refs_3_, bf16[64,2048]{1,0:T(8,128)(2,1)} %collective-permute-done.7.refs_4_, ...), custom_call_target="tpu_custom_call" | custom-call | flops 104857 | bytes 41943 | tf_op jit(solution)/shard_map/norm_pieces/pallas_call | solution.py:371
  52.6 1.5 collective-permute-start.14
  54.1 2.3 %project_rows.6 = (bf16[512,512]{1,0:T(8,128)(2,1)S(1)}, bf16[512,512]{1,0:T(8,128)(2,1)S(1)}) custom-call(bf16[512,2048]{1,0:T(8,128)(2,1)S(1)} %bitcast.60, bf16[2048,512]{1,0:T(8,128)(2,1)S(1)} %copy-done.2, bf16[2048,512]{1,0:T(8,128)(2,1)S(1)} %copy-done.4), custom_call_target="tpu_custom_call" | custom-call | flops 21474836 | bytes 20971 | tf_op jit(solution)/shard_map/project_rows/pallas_call | solution.py:233
  56.5 2.3 %project_rows.7 = (bf16[512,512]{1,0:T(8,128)(2,1)S(1)}, bf16[512,512]{1,0:T(8,128)(2,1)S(1)}) custom-call(bf16[512,2048]{1,0:T(8,128)(2,1)S(1)} %collective-permute-done.13.refs_0_.refs_1_, bf16[2048,512]{1,0:T(8,128)(2,1)S(1)} %copy-done.2, bf16[2048,512]{1,0:T(8,128)(2,1)S(1)} %copy-done.4), custom_call_target="tpu_custom_call" | custom-call | flops 21474836 | bytes 20971 | tf_op jit(solution)/shard_map/project_rows/pallas_call | solution.py:233
  58.9 2.0 attend.1.refs_0_
  61.4 2.7 %collective-permute-done.14 = bf16[96,2048]{1,0:T(8,128)(2,1)S(1)} collective-permute-done((bf16[96,2048]{1,0:T(8,128)(2,1)S(1)}, bf16[96,2048]{1,0:T(8,128)(2,1)S(1)}, u32[]{:S(2)}, u32[]{:S(2)}) %collective-permute-start.14) | collective-permute-done | bytes 393248 | tf_op jit(solution)/shard_map/ppermute | solution.py:40
  70.7 4.4 %collective-permute-done.16.other = bf16[64,2048]{1,0:T(8,128)(2,1)S(1)} collective-permute-done((bf16[64,2048]{1,0:T(8,128)(2,1)S(1)}, bf16[64,2048]{1,0:T(8,128)(2,1)S(1)}, u32[]{:S(2)}, u32[]{:S(2)}) %collective-permute-start.16) | collective-permute-done | bytes 262176 | tf_op jit(solution)/shard_map/ppermute | solution.py:40
  77.1 6.2 %feed_own.1 = (bf16[128,2048]{1,0:T(8,128)(2,1)S(1)}, f32[64,2048]{1,0:T(8,128)S(1)}, bf16[64,2048]{1,0:T(8,128)(2,1)S(1)}) custom-call(bf16[128,2048]{1,0:T(8,128)(2,1)S(1)} %constant_dynamic-update-slice_fusion.lifted.refs_0_, bf16[2048,2048]{1,0:T(8,128)(2,1)S(1)} %bitcast.58, f32[128,2048]{1,0:T(8,128)S(1)} %grad_activated.1), custom_call_target="tpu_custom_call" | custom-call | flops 21474836 | bytes 83886 | tf_op jit(solution)/shard_map/feed_own/pallas_call | solution.py:501
  83.3 7.5 %collective-permute-done.18.refs_4_ = bf16[64,2048]{1,0:T(8,128)(2,1)} collective-permute-done((bf16[64,2048]{1,0:T(8,128)(2,1)S(1)}, bf16[64,2048]{1,0:T(8,128)(2,1)}, u32[]{:S(2)}, u32[]{:S(2)}) %collective-permute-start.18) | collective-permute-done | bytes 262176 | tf_op jit(solution)/shard_map/ppermute | solution.py:40
  90.8 1.5 collective-permute-done.20
  93.9 1.9 collective-permute-start.22
  96.8 1.5 collective-permute-start.24
  98.3 5.4 %down_own.1 = (f32[64,2048]{1,0:T(8,128)S(1)}, bf16[64,2048]{1,0:T(8,128)(2,1)S(1)}) custom-call(bf16[128,2048]{1,0:T(8,128)(2,1)S(1)} %get-tuple-element.174.rows, bf16[2048,2048]{1,0:T(8,128)(2,1)} %refs_9_.7), custom_call_target="tpu_custom_call" | custom-call | flops 10737418 | bytes 83886 | tf_op jit(solution)/shard_map/down_own/pallas_call | solution.py:302
  103.8 4.5 %collective-permute-done.23 = bf16[32,2048]{1,0:T(8,128)(2,1)S(1)} collective-permute-done((bf16[32,2048]{1,0:T(8,128)(2,1)S(1)}, bf16[32,2048]{1,0:T(8,128)(2,1)S(1)}, u32[]{:S(2)}, u32[]{:S(2)}) %collective-permute-start.23) | collective-permute-done | bytes 131104 | tf_op jit(solution)/shard_map/ppermute | solution.py:40
  112.1 2.4 %collective-permute-start.27 = (bf16[128,512]{1,0:T(8,128)(2,1)S(1)}, bf16[128,512]{1,0:T(8,128)(2,1)S(1)}, u32[]{:S(2)}, u32[]{:S(2)}) collective-permute-start(bf16[128,512]{1,0:T(8,128)(2,1)S(1)} %product_back.1.refs_0_), channel_id=1, source_target_pairs={{0,8},{4,12},{8,0},{12,4},{16,24},{20,28},{24,16},{28,20},{1,9},{5... | collective-permute-start | bytes 393224 | tf_op jit(solution)/shard_map/ppermute | solution.py:40
  114.5 2.3 collective-permute-start.31
  117.1 1.8 collective-permute-done.27.refs_2_
  118.9 8.0 %collective-permute-done.29.refs_4_ = bf16[128,512]{1,0:T(8,128)(2,1)S(1)} collective-permute-done((bf16[128,512]{1,0:T(8,128)(2,1)S(1)}, bf16[128,512]{1,0:T(8,128)(2,1)S(1)}, u32[]{:S(2)}, u32[]{:S(2)}) %collective-permute-start.29) | collective-permute-done | bytes 131104 | tf_op jit(solution)/shard_map/ppermute | solution.py:40
  127.6 1.5 collective-permute-start.28
  130.8 1.5 collective-permute-start.32
  132.4 1.5 collective-permute-done.28.refs_3_
  134.0 9.5 %feed_all.4 = (f32[256,2048]{1,0:T(8,128)}, f32[2048,256]{1,0:T(8,128)}) custom-call(s32[1]{0:T(128)} %bitcast.9.index, bf16[128,2048]{1,0:T(8,128)(2,1)S(1)} %constant_dynamic-update-slice_fusion.lifted.refs_0_, bf16[192,2048]{1,0:T(8,128)(2,1)S(1)} %constant_dynamic-update-slice_fusion.2.refs_1_, bf16[192,2048]{1,0:T(8,128)(2,1)S(1)} %collective-permute-done.35.refs_2_, ...), custom_call_target="tpu_custom_call" | custom-call | flops 1207959552 | bytes 3145728 | tf_op jit(solution)/shard_map/feed_all/pallas_call | solution.py:594
  143.6 9.5 %feed_all.5 = (f32[256,2048]{1,0:T(8,128)}, f32[2048,256]{1,0:T(8,128)}) custom-call(s32[1]{0:T(128)} %bitcast.9.index, bf16[128,2048]{1,0:T(8,128)(2,1)S(1)} %constant_dynamic-update-slice_fusion.lifted.refs_0_, bf16[192,2048]{1,0:T(8,128)(2,1)S(1)} %constant_dynamic-update-slice_fusion.2.refs_1_, ...), custom_call_target="tpu_custom_call", output_to_operand_aliasing={{0}: (9, {}), {1}: (10, {})} | custom-call | flops 1207959552 | bytes 3145728 | tf_op jit(solution)/shard_map/feed_all/pallas_call | solution.py:594
  153.1 1.7 collective-permute-start.38
  156.1 17.2 %attend_back.1 = (bf16[512,512]{1,0:T(8,128)(2,1)S(1)}, bf16[512,512]{1,0:T(8,128)(2,1)S(1)}, bf16[512,512]{1,0:T(8,128)(2,1)S(1)}, bf16[512,512]{1,0:T(8,128)(2...) custom-call(bf16[128,512]{1,0:T(8,128)(2,1)} %copy-done.40, ...), custom_call_target="tpu_custom_call" | custom-call | flops 64424508 | bytes 83886 | tf_op jit(solution)/shard_map/attend_back/pallas_call | solution.py:860
  173.4 4.1 %collective-permute-done.37.refs_0_ = bf16[64,2048]{1,0:T(8,128)(2,1)S(1)} collective-permute-done((bf16[64,2048]{1,0:T(8,128)(2,1)S(1)}, bf16[64,2048]{1,0:T(8,128)(2,1)S(1)}, u32[]{:S(2)}, u32[]{:S(2)}) %collective-permute-start.37) | collective-permute-done | bytes 262176 | tf_op jit(solution)/shard_map/ppermute | solution.py:40
  177.4 2.1 product_halves.3
  184.5 12.8 %feed_all.6 = (f32[256,2048]{1,0:T(8,128)}, f32[2048,256]{1,0:T(8,128)}) custom-call(s32[1]{0:T(128)} %bitcast.9.index, bf16[64,2048]{1,0:T(8,128)(2,1)S(1)} %collective-permute-done.37.refs_0_, bf16[64,2048]{1,0:T(8,128)(2,1)} %collective-permute-done.42.refs_1_, ...), custom_call_target="tpu_custom_call", output_to_operand_aliasing={{0}: (11, {}), {1}: (12, {})} | custom-call | flops 1207959552 | bytes 3145728 | tf_op jit(solution)/shard_map/feed_all/pallas_call | solution.py:594
  197.3 2.4 %last.1 = bf16[64,2048]{1,0:T(8,128)(2,1)} custom-call(bf16[64,2048]{1,0:T(8,128)(2,1)S(1)} %bitcast.68, bf16[64,2048]{1,0:T(8,128)(2,1)} %add_convert_fusion.1.low, bf16[64,2048]{1,0:T(8,128)(2,1)} %collective-permute-done.41.other, f32[64,2048]{1,0:T(8,128)S(1)} %copy-done.23, f32[3,2048]{1,0:T(4,128)S(1)} %copy-done.21, s32[64,1]{1,0:T(8,128)S(1)} %slice.15.kind), custom_call_target="tpu_custom_call" | custom-call | flops 26214 | bytes 15728 | tf_op jit(solution)/shard_map/last/pallas_call | solution.py:456
  200.8 2.8 %project.1 = (f32[256,512]{1,0:T(8,128)}, f32[256,512]{1,0:T(8,128)}, f32[256,512]{1,0:T(8,128)}, f32[3,256]{1,0:T(4,128)S(1)}) custom-call(s32[1]{0:T(128)} %bitcast.9.index, bf16[512,2048]{1,0:T(8,128)(2,1)S(1)} %bitcast.62, bf16[512,2048]{1,0:T(8,128)(2,1)S(1)} %copy-done.9, bf16[512,512]{1,0:T(8,128)(2,1)S(1)} %copy-done.29, ...), custom_call_target="tpu_custom_call" | custom-call | flops 16106127 | bytes 47185 | tf_op jit(solution)/shard_map/project/pallas_call | solution.py:645
  205.0 4.9 %all-to-all-start = ((bf16[1,72,8,256]{3,1,0,2:T(8,128)(2,1)}), bf16[1,72,8,256]{3,1,0,2:T(8,128)(2,1)}, u32[]{:S(2)}, u32[]{:S(2)}) async-start(bf16[1,72,8,256]{3,1,0,2:T(8,128)(2,1)} %copy.48), calls=%async_computation | async-start | bytes 589824 | tf_op jit(solution)/shard_map/all_to_all | solution.py:1014
  210.9 11.5 %feed_all.7 = (f32[256,2048]{1,0:T(8,128)}, f32[2048,256]{1,0:T(8,128)}) custom-call(s32[1]{0:T(128)} %bitcast.9.index, bf16[64,2048]{1,0:T(8,128)(2,1)S(1)} %collective-permute-done.37.refs_0_, bf16[64,2048]{1,0:T(8,128)(2,1)} %collective-permute-done.42.refs_1_, ...), custom_call_target="tpu_custom_call", output_to_operand_aliasing={{0}: (11, {}), {1}: (12, {})} | custom-call | flops 1207959552 | bytes 3145728 | tf_op jit(solution)/shard_map/feed_all/pallas_call | solution.py:594
  (249 shorter events, 47.0 us)
Async XLA Ops:
  2.9 8.1 %collective-permute-start = (bf16[32,2048]{1,0:T(8,128)(2,1)S(1)}, bf16[32,2048]{1,0:T(8,128)(2,1)S(1)}, u32[]{:S(2)}, u32[]{:S(2)}) collective-permute-start(bf16[32,2048]{1,0:T(8,128)(2,1)S(1)} %constant_dynamic-slice_fusion.4), channel_id=1, source_target_pairs={{0,8},{4,12},{8,0},{12,4},{16,24},{20,28},{24,16},{28,20},{1,9},{5... | collective-permute-start | bytes 393224 | tf_op jit(solution)/shard_map/ppermute | solution.py:40
  6.0 12.9 %collective-permute-start.2 = (bf16[32,2048]{1,0:T(8,128)(2,1)S(1)}, bf16[32,2048]{1,0:T(8,128)(2,1)S(1)}, u32[]{:S(2)}, u32[]{:S(2)}) collective-permute-start(bf16[32,2048]{1,0:T(8,128)(2,1)S(1)} %constant_dynamic-slice_fusion.4), channel_id=1, source_target_pairs={{0,16},{4,20},{8,24},{12,28},{16,0},{20,4},{24,8},{28,12},{1,17},{... | collective-permute-start | bytes 393224 | tf_op jit(solution)/shard_map/ppermute | solution.py:40
  8.5 11.8 %collective-permute-start.4 = (bf16[32,2048]{1,0:T(8,128)(2,1)S(1)}, bf16[32,2048]{1,0:T(8,128)(2,1)S(1)}, u32[]{:S(2)}, u32[]{:S(2)}) collective-permute-start(bf16[32,2048]{1,0:T(8,128)(2,1)S(1)} %constant_dynamic-slice_fusion.4), channel_id=1, source_target_pairs={{0,24},{4,28},{8,16},{12,20},{16,8},{20,12},{24,0},{28,4},{1,25},{... | collective-permute-start | bytes 393224 | tf_op jit(solution)/shard_map/ppermute | solution.py:40
  11.0 9.9 %collective-permute-start.1 = (bf16[32,2048]{1,0:T(8,128)(2,1)S(1)}, bf16[32,2048]{1,0:T(8,128)(2,1)S(1)}, u32[]{:S(2)}, u32[]{:S(2)}) collective-permute-start(bf16[32,2048]{1,0:T(8,128)(2,1)S(1)} %collective-permute-done), channel_id=1, source_target_pairs={{0,2},{1,3},{2,0},{3,1},{4,6},{5,7},{6,4},{7,5},{8,10},{9,11},{10,... | collective-permute-start | bytes 393224 | tf_op jit(solution)/shard_map/ppermute | solution.py:40
  12.7 23.9 %collective-permute-start.6 = (bf16[64,2048]{1,0:T(8,128)(2,1)S(1)}, bf16[64,2048]{1,0:T(8,128)(2,1)}, u32[]{:S(2)}, u32[]{:S(2)}) collective-permute-start(bf16[64,2048]{1,0:T(8,128)(2,1)S(1)} %bitcast.64), channel_id=1, source_target_pairs={{0,4},{4,0},{8,12},{12,8},{16,20},{20,16},{24,28},{28,24},{1,5},{5... | collective-permute-start | bytes 786440 | tf_op jit(solution)/shard_map/ppermute | solution.py:40
  18.9 5.0 %collective-permute-start.3 = (bf16[32,2048]{1,0:T(8,128)(2,1)S(1)}, bf16[32,2048]{1,0:T(8,128)(2,1)S(1)}, u32[]{:S(2)}, u32[]{:S(2)}) collective-permute-start(bf16[32,2048]{1,0:T(8,128)(2,1)S(1)} %collective-permute-done.2), channel_id=1, source_target_pairs={{0,2},{1,3},{2,0},{3,1},{4,6},{5,7},{6,4},{7,5},{8,10},{9,11},{10,... | collective-permute-start | bytes 393224 | tf_op jit(solution)/shard_map/ppermute | solution.py:40
  20.4 5.0 %collective-permute-start.5 = (bf16[32,2048]{1,0:T(8,128)(2,1)S(1)}, bf16[32,2048]{1,0:T(8,128)(2,1)S(1)}, u32[]{:S(2)}, u32[]{:S(2)}) collective-permute-start(bf16[32,2048]{1,0:T(8,128)(2,1)S(1)} %collective-permute-done.4), channel_id=1, source_target_pairs={{0,2},{1,3},{2,0},{3,1},{4,6},{5,7},{6,4},{7,5},{8,10},{9,11},{10,... | collective-permute-start | bytes 393224 | tf_op jit(solution)/shard_map/ppermute | solution.py:40
  26.7 12.0 %collective-permute-start.10 = (bf16[32,2048]{1,0:T(8,128)(2,1)}, bf16[32,2048]{1,0:T(8,128)(2,1)}, u32[]{:S(2)}, u32[]{:S(2)}) collective-permute-start(bf16[32,2048]{1,0:T(8,128)(2,1)} %constant_dynamic-slice_fusion.2), channel_id=1, source_target_pairs={{0,8},{4,12},{8,0},{12,4},{16,24},{20,28},{24,16},{28,20},{1,9},{5... | collective-permute-start | bytes 393224 | tf_op jit(solution)/shard_map/ppermute | solution.py:40
  27.6 20.0 %collective-permute-start.7 = (bf16[64,2048]{1,0:T(8,128)(2,1)S(1)}, bf16[64,2048]{1,0:T(8,128)(2,1)}, u32[]{:S(2)}, u32[]{:S(2)}) collective-permute-start(bf16[64,2048]{1,0:T(8,128)(2,1)S(1)} %pad_maximum_fusion.7.refs_3_), channel_id=1, source_target_pairs={{0,4},{4,0},{8,12},{12,8},{16,20},{20,16},{24,28},{28,24},{1,5},{5... | collective-permute-start | bytes 786440 | tf_op jit(solution)/shard_map/ppermute | solution.py:40
  29.2 18.5 %collective-permute-start.8 = (bf16[64,2048]{1,0:T(8,128)(2,1)}, bf16[64,2048]{1,0:T(8,128)(2,1)}, u32[]{:S(2)}, u32[]{:S(2)}) collective-permute-start(bf16[64,2048]{1,0:T(8,128)(2,1)} %pad_maximum_fusion.8.refs_5_), channel_id=1, source_target_pairs={{0,4},{4,0},{8,12},{12,8},{16,20},{20,16},{24,28},{28,24},{1,5},{5... | collective-permute-start | bytes 786440 | tf_op jit(solution)/shard_map/ppermute | solution.py:40
  29.7 18.0 %collective-permute-start.9 = (bf16[64,2048]{1,0:T(8,128)(2,1)}, bf16[64,2048]{1,0:T(8,128)(2,1)}, u32[]{:S(2)}, u32[]{:S(2)}) collective-permute-start(bf16[64,2048]{1,0:T(8,128)(2,1)} %pad_maximum_fusion.9.refs_7_), channel_id=1, source_target_pairs={{0,4},{4,0},{8,12},{12,8},{16,20},{20,16},{24,28},{28,24},{1,5},{5... | collective-permute-start | bytes 786440 | tf_op jit(solution)/shard_map/ppermute | solution.py:40
  36.6 11.0 %collective-permute-start.11 = (bf16[32,2048]{1,0:T(8,128)(2,1)}, bf16[32,2048]{1,0:T(8,128)(2,1)S(1)}, u32[]{:S(2)}, u32[]{:S(2)}) collective-permute-start(bf16[32,2048]{1,0:T(8,128)(2,1)} %constant_dynamic-slice_fusion.2), channel_id=1, source_target_pairs={{0,16},{4,20},{8,24},{12,28},{16,0},{20,4},{24,8},{28,12},{1,17},{... | collective-permute-start | bytes 393224 | tf_op jit(solution)/shard_map/ppermute | solution.py:40
  38.7 8.8 %collective-permute-start.12 = (bf16[32,2048]{1,0:T(8,128)(2,1)}, bf16[32,2048]{1,0:T(8,128)(2,1)S(1)}, u32[]{:S(2)}, u32[]{:S(2)}) collective-permute-start(bf16[32,2048]{1,0:T(8,128)(2,1)} %constant_dynamic-slice_fusion.2), channel_id=1, source_target_pairs={{0,24},{4,28},{8,16},{12,20},{16,8},{20,12},{24,0},{28,4},{1,25},{... | collective-permute-start | bytes 393224 | tf_op jit(solution)/shard_map/ppermute | solution.py:40
  51.5 5.0 %collective-permute-start.13 = (bf16[512,2048]{1,0:T(8,128)(2,1)S(1)}, bf16[512,2048]{1,0:T(8,128)(2,1)S(1)}, u32[]{:S(2)}, u32[]{:S(2)}) collective-permute-start(bf16[512,2048]{1,0:T(8,128)(2,1)S(1)} %bitcast.59), channel_id=1, source_target_pairs={{0,1},{1,0},{2,3},{3,2},{4,5},{5,4},{6,7},{7,6},{8,9},{9,8},{10,11... | collective-permute-start | bytes 6291464 | tf_op jit(solution)/shard_map/ppermute | solution.py:40
  52.6 11.4 %collective-permute-start.14 = (bf16[96,2048]{1,0:T(8,128)(2,1)S(1)}, bf16[96,2048]{1,0:T(8,128)(2,1)S(1)}, u32[]{:S(2)}, u32[]{:S(2)}) collective-permute-start(bf16[96,2048]{1,0:T(8,128)(2,1)S(1)} %pad_maximum_fusion.4), channel_id=1, source_target_pairs={{0,2},{1,3},{2,0},{3,1},{4,6},{5,7},{6,4},{7,5},{8,10},{9,11},{10,... | collective-permute-start | bytes 1179656 | tf_op jit(solution)/shard_map/ppermute | solution.py:40
  65.1 25.7 %collective-permute-start.19 = (bf16[192,2048]{1,0:T(8,128)(2,1)S(1)}, bf16[192,2048]{1,0:T(8,128)(2,1)S(1)}, u32[]{:S(2)}, u32[]{:S(2)}) collective-permute-start(bf16[192,2048]{1,0:T(8,128)(2,1)S(1)} %pad_maximum_fusion.refs_4_), channel_id=1, source_target_pairs={{0,4},{4,0},{8,12},{12,8},{16,20},{20,16},{24,28},{28,24},{1,5},{5... | collective-permute-start | bytes 2359304 | tf_op jit(solution)/shard_map/ppermute | solution.py:40
  66.7 8.4 %collective-permute-start.16 = (bf16[64,2048]{1,0:T(8,128)(2,1)S(1)}, bf16[64,2048]{1,0:T(8,128)(2,1)S(1)}, u32[]{:S(2)}, u32[]{:S(2)}) collective-permute-start(bf16[64,2048]{1,0:T(8,128)(2,1)S(1)} %add_convert_fusion.4.low), channel_id=1, source_target_pairs={{0,2},{1,3},{2,0},{3,1},{4,6},{5,7},{6,4},{7,5},{8,10},{9,11},{10,... | collective-permute-start | bytes 786440 | tf_op jit(solution)/shard_map/ppermute | solution.py:40
  75.6 15.2 %collective-permute-start.18 = (bf16[64,2048]{1,0:T(8,128)(2,1)S(1)}, bf16[64,2048]{1,0:T(8,128)(2,1)}, u32[]{:S(2)}, u32[]{:S(2)}) collective-permute-start(bf16[64,2048]{1,0:T(8,128)(2,1)S(1)} %bitcast.71), channel_id=1, source_target_pairs={{0,4},{4,0},{8,12},{12,8},{16,20},{20,16},{24,28},{28,24},{1,5},{5... | collective-permute-start | bytes 786440 | tf_op jit(solution)/shard_map/ppermute | solution.py:40
  92.4 15.8 %collective-permute-start.21 = (bf16[64,2048]{1,0:T(8,128)(2,1)S(1)}, bf16[64,2048]{1,0:T(8,128)(2,1)S(1)}, u32[]{:S(2)}, u32[]{:S(2)}) collective-permute-start(bf16[64,2048]{1,0:T(8,128)(2,1)S(1)} %add_convert_fusion.3.low), channel_id=1, source_target_pairs={{0,2},{1,3},{2,0},{3,1},{4,6},{5,7},{6,4},{7,5},{8,10},{9,11},{10,... | collective-permute-start | bytes 786440 | tf_op jit(solution)/shard_map/ppermute | solution.py:40
  93.9 9.9 %collective-permute-start.22 = (bf16[32,2048]{1,0:T(8,128)(2,1)S(1)}, bf16[32,2048]{1,0:T(8,128)(2,1)S(1)}, u32[]{:S(2)}, u32[]{:S(2)}) collective-permute-start(bf16[32,2048]{1,0:T(8,128)(2,1)S(1)} %constant_dynamic-slice_fusion), channel_id=1, source_target_pairs={{0,8},{4,12},{8,0},{12,4},{16,24},{20,28},{24,16},{28,20},{1,9},{5... | collective-permute-start | bytes 393224 | tf_op jit(solution)/shard_map/ppermute | solution.py:40
  95.7 12.5 %collective-permute-start.23 = (bf16[32,2048]{1,0:T(8,128)(2,1)S(1)}, bf16[32,2048]{1,0:T(8,128)(2,1)S(1)}, u32[]{:S(2)}, u32[]{:S(2)}) collective-permute-start(bf16[32,2048]{1,0:T(8,128)(2,1)S(1)} %constant_dynamic-slice_fusion), channel_id=1, source_target_pairs={{0,16},{4,20},{8,24},{12,28},{16,0},{20,4},{24,8},{28,12},{1,17},{... | collective-permute-start | bytes 393224 | tf_op jit(solution)/shard_map/ppermute | solution.py:40
  96.8 11.4 %collective-permute-start.24 = (bf16[32,2048]{1,0:T(8,128)(2,1)S(1)}, bf16[32,2048]{1,0:T(8,128)(2,1)S(1)}, u32[]{:S(2)}, u32[]{:S(2)}) collective-permute-start(bf16[32,2048]{1,0:T(8,128)(2,1)S(1)} %constant_dynamic-slice_fusion), channel_id=1, source_target_pairs={{0,24},{4,28},{8,16},{12,20},{16,8},{20,12},{24,0},{28,4},{1,25},{... | collective-permute-start | bytes 393224 | tf_op jit(solution)/shard_map/ppermute | solution.py:40
  109.1 17.8 %collective-permute-start.34 = (bf16[96,2048]{1,0:T(8,128)(2,1)S(1)}, bf16[96,2048]{1,0:T(8,128)(2,1)S(1)}, u32[]{:S(2)}, u32[]{:S(2)}) collective-permute-start(bf16[96,2048]{1,0:T(8,128)(2,1)S(1)} %pad_maximum_fusion.5), channel_id=1, source_target_pairs={{0,2},{1,3},{2,0},{3,1},{4,6},{5,7},{6,4},{7,5},{8,10},{9,11},{10,... | collective-permute-start | bytes 1179656 | tf_op jit(solution)/shard_map/ppermute | solution.py:40
  111.5 5.6 %collective-permute-start.26 = (bf16[128,512]{1,0:T(8,128)(2,1)S(1)}, bf16[128,512]{1,0:T(8,128)(2,1)S(1)}, u32[]{:S(2)}, u32[]{:S(2)}) collective-permute-start(bf16[128,512]{1,0:T(8,128)(2,1)S(1)} %product_back.1.refs_0_), channel_id=1, source_target_pairs={{0,4},{4,0},{8,12},{12,8},{16,20},{20,16},{24,28},{28,24},{1,5},{5... | collective-permute-start | bytes 393224 | tf_op jit(solution)/shard_map/ppermute | solution.py:40
  112.1 6.9 %collective-permute-start.27 = (bf16[128,512]{1,0:T(8,128)(2,1)S(1)}, bf16[128,512]{1,0:T(8,128)(2,1)S(1)}, u32[]{:S(2)}, u32[]{:S(2)}) collective-permute-start(bf16[128,512]{1,0:T(8,128)(2,1)S(1)} %product_back.1.refs_0_), channel_id=1, source_target_pairs={{0,8},{4,12},{8,0},{12,4},{16,24},{20,28},{24,16},{28,20},{1,9},{5... | collective-permute-start | bytes 393224 | tf_op jit(solution)/shard_map/ppermute | solution.py:40
  114.4 12.5 %collective-permute-start.29 = (bf16[128,512]{1,0:T(8,128)(2,1)S(1)}, bf16[128,512]{1,0:T(8,128)(2,1)S(1)}, u32[]{:S(2)}, u32[]{:S(2)}) collective-permute-start(bf16[128,512]{1,0:T(8,128)(2,1)S(1)} %product_back.1.refs_0_), channel_id=1, source_target_pairs={{0,16},{4,20},{8,24},{12,28},{16,0},{20,4},{24,8},{28,12},{1,17},{... | collective-permute-start | bytes 393224 | tf_op jit(solution)/shard_map/ppermute | solution.py:40
  114.5 12.4 %collective-permute-start.31 = (bf16[128,512]{1,0:T(8,128)(2,1)S(1)}, bf16[128,512]{1,0:T(8,128)(2,1)S(1)}, u32[]{:S(2)}, u32[]{:S(2)}) collective-permute-start(bf16[128,512]{1,0:T(8,128)(2,1)S(1)} %product_back.1.refs_0_), channel_id=1, source_target_pairs={{0,24},{4,28},{8,16},{12,20},{16,8},{20,12},{24,0},{28,4},{1,25},{... | collective-permute-start | bytes 393224 | tf_op jit(solution)/shard_map/ppermute | solution.py:40
  127.0 7.0 %collective-permute-start.35 = (bf16[192,2048]{1,0:T(8,128)(2,1)S(1)}, bf16[192,2048]{1,0:T(8,128)(2,1)S(1)}, u32[]{:S(2)}, u32[]{:S(2)}) collective-permute-start(bf16[192,2048]{1,0:T(8,128)(2,1)S(1)} %constant_dynamic-update-slice_fusion.2.refs_1_), channel_id=1, source_target_pairs={{0,1},{1,0},{2,3},{3,2},{4,5},{5,4},{6,7},{7,6},{8,9},{9,8},{10,11... | collective-permute-start | bytes 2359304 | tf_op jit(solution)/shard_map/ppermute | solution.py:40
  127.1 6.9 %collective-permute-start.36 = (bf16[192,2048]{1,0:T(8,128)(2,1)S(1)}, bf16[192,2048]{1,0:T(8,128)(2,1)S(1)}, u32[]{:S(2)}, u32[]{:S(2)}) collective-permute-start(bf16[192,2048]{1,0:T(8,128)(2,1)S(1)} %pad_maximum_fusion.refs_4_), channel_id=1, source_target_pairs={{0,1},{1,0},{2,3},{3,2},{4,5},{5,4},{6,7},{7,6},{8,9},{9,8},{10,11... | collective-permute-start | bytes 2359304 | tf_op jit(solution)/shard_map/ppermute | solution.py:40
  127.6 3.3 %collective-permute-start.33 = (bf16[64,2048]{1,0:T(8,128)(2,1)S(1)}, bf16[64,2048]{1,0:T(8,128)(2,1)S(1)}, u32[]{:S(2)}, u32[]{:S(2)}) collective-permute-start(bf16[64,2048]{1,0:T(8,128)(2,1)S(1)} %get-tuple-element.179), channel_id=1, source_target_pairs={{0,1},{1,0},{2,3},{3,2},{4,5},{5,4},{6,7},{7,6},{8,9},{9,8},{10,11... | collective-permute-start | bytes 786440 | tf_op jit(solution)/shard_map/ppermute | solution.py:40
  127.6 6.3 %collective-permute-start.28 = (bf16[128,512]{1,0:T(8,128)(2,1)S(1)}, bf16[128,512]{1,0:T(8,128)(2,1)S(1)}, u32[]{:S(2)}, u32[]{:S(2)}) collective-permute-start(bf16[128,512]{1,0:T(8,128)(2,1)S(1)} %collective-permute-done.27.refs_2_), channel_id=1, source_target_pairs={{0,4},{4,0},{8,12},{12,8},{16,20},{20,16},{24,28},{28,24},{1,5},{5... | collective-permute-start | bytes 393224 | tf_op jit(solution)/shard_map/ppermute | solution.py:40
  129.2 23.9 %collective-permute-start.30 = (bf16[128,512]{1,0:T(8,128)(2,1)S(1)}, bf16[128,512]{1,0:T(8,128)(2,1)S(1)}, u32[]{:S(2)}, u32[]{:S(2)}) collective-permute-start(bf16[128,512]{1,0:T(8,128)(2,1)S(1)} %collective-permute-done.29.refs_4_), channel_id=1, source_target_pairs={{0,4},{4,0},{8,12},{12,8},{16,20},{20,16},{24,28},{28,24},{1,5},{5... | collective-permute-start | bytes 393224 | tf_op jit(solution)/shard_map/ppermute | solution.py:40
  130.8 22.2 %collective-permute-start.32 = (bf16[128,512]{1,0:T(8,128)(2,1)S(1)}, bf16[128,512]{1,0:T(8,128)(2,1)S(1)}, u32[]{:S(2)}, u32[]{:S(2)}) collective-permute-start(bf16[128,512]{1,0:T(8,128)(2,1)S(1)} %collective-permute-done.31.refs_6_), channel_id=1, source_target_pairs={{0,4},{4,0},{8,12},{12,8},{16,20},{20,16},{24,28},{28,24},{1,5},{5... | collective-permute-start | bytes 393224 | tf_op jit(solution)/shard_map/ppermute | solution.py:40
  153.1 24.3 %collective-permute-start.38 = (bf16[192,2048]{1,0:T(8,128)(2,1)S(1)}, bf16[192,2048]{1,0:T(8,128)(2,1)}, u32[]{:S(2)}, u32[]{:S(2)}) collective-permute-start(bf16[192,2048]{1,0:T(8,128)(2,1)S(1)} %constant_dynamic-update-slice_fusion.2.refs_1_), channel_id=1, source_target_pairs={{0,4},{4,0},{8,12},{12,8},{16,20},{20,16},{24,28},{28,24},{1,5},{5... | collective-permute-start | bytes 2359304 | tf_op jit(solution)/shard_map/ppermute | solution.py:40
  154.8 18.5 %collective-permute-start.39 = (bf16[64,2048]{1,0:T(8,128)(2,1)S(1)}, bf16[64,2048]{1,0:T(8,128)(2,1)S(1)}, u32[]{:S(2)}, u32[]{:S(2)}) collective-permute-start(bf16[64,2048]{1,0:T(8,128)(2,1)S(1)} %add_convert_fusion.2), channel_id=1, source_target_pairs={{0,2},{1,3},{2,0},{3,1},{4,6},{5,7},{6,4},{7,5},{8,10},{9,11},{10,... | collective-permute-start | bytes 786440 | tf_op jit(solution)/shard_map/ppermute | solution.py:40
  155.7 21.7 %collective-permute-start.37 = (bf16[64,2048]{1,0:T(8,128)(2,1)S(1)}, bf16[64,2048]{1,0:T(8,128)(2,1)S(1)}, u32[]{:S(2)}, u32[]{:S(2)}) collective-permute-start(bf16[64,2048]{1,0:T(8,128)(2,1)S(1)} %get-tuple-element.207), channel_id=1, source_target_pairs={{0,4},{4,0},{8,12},{12,8},{16,20},{20,16},{24,28},{28,24},{1,5},{5... | collective-permute-start | bytes 786440 | tf_op jit(solution)/shard_map/ppermute | solution.py:40
  179.7 4.7 %collective-permute-start.43 = (bf16[192,2048]{1,0:T(8,128)(2,1)}, bf16[192,2048]{1,0:T(8,128)(2,1)}, u32[]{:S(2)}, u32[]{:S(2)}) collective-permute-start(bf16[192,2048]{1,0:T(8,128)(2,1)} %collective-permute-done.38.refs_2_), channel_id=1, source_target_pairs={{0,1},{1,0},{2,3},{3,2},{4,5},{5,4},{6,7},{7,6},{8,9},{9,8},{10,11... | collective-permute-start | bytes 2359304 | tf_op jit(solution)/shard_map/ppermute | solution.py:40
  180.2 4.2 %collective-permute-start.45 = (bf16[192,2048]{1,0:T(8,128)(2,1)S(1)}, bf16[192,2048]{1,0:T(8,128)(2,1)}, u32[]{:S(2)}, u32[]{:S(2)}) collective-permute-start(bf16[192,2048]{1,0:T(8,128)(2,1)S(1)} %collective-permute-done.19.refs_6_), channel_id=1, source_target_pairs={{0,1},{1,0},{2,3},{3,2},{4,5},{5,4},{6,7},{7,6},{8,9},{9,8},{10,11... | collective-permute-start | bytes 2359304 | tf_op jit(solution)/shard_map/ppermute | solution.py:40
  180.3 4.1 %collective-permute-start.44 = (bf16[64,2048]{1,0:T(8,128)(2,1)}, bf16[64,2048]{1,0:T(8,128)(2,1)}, u32[]{:S(2)}, u32[]{:S(2)}) collective-permute-start(bf16[64,2048]{1,0:T(8,128)(2,1)} %collective-permute-done.18.refs_4_), channel_id=1, source_target_pairs={{0,1},{1,0},{2,3},{3,2},{4,5},{5,4},{6,7},{7,6},{8,9},{9,8},{10,11... | collective-permute-start | bytes 786440 | tf_op jit(solution)/shard_map/ppermute | solution.py:40
  180.7 3.6 %collective-permute-start.42 = (bf16[64,2048]{1,0:T(8,128)(2,1)S(1)}, bf16[64,2048]{1,0:T(8,128)(2,1)}, u32[]{:S(2)}, u32[]{:S(2)}) collective-permute-start(bf16[64,2048]{1,0:T(8,128)(2,1)S(1)} %collective-permute-done.37.refs_0_), channel_id=1, source_target_pairs={{0,1},{1,0},{2,3},{3,2},{4,5},{5,4},{6,7},{7,6},{8,9},{9,8},{10,11... | collective-permute-start | bytes 786440 | tf_op jit(solution)/shard_map/ppermute | solution.py:40
  182.0 15.3 %collective-permute-start.41 = (bf16[64,2048]{1,0:T(8,128)(2,1)}, bf16[64,2048]{1,0:T(8,128)(2,1)}, u32[]{:S(2)}, u32[]{:S(2)}) collective-permute-start(bf16[64,2048]{1,0:T(8,128)(2,1)} %add_convert_fusion.1.low), channel_id=1, source_target_pairs={{0,2},{1,3},{2,0},{3,1},{4,6},{5,7},{6,4},{7,5},{8,10},{9,11},{10,... | collective-permute-start | bytes 786440 | tf_op jit(solution)/shard_map/ppermute | solution.py:40
  200.5 22.5 %collective-permute-start.46 = (bf16[64,2048]{1,0:T(8,128)(2,1)}, bf16[64,2048]{1,0:T(8,128)(2,1)}, u32[]{:S(2)}, u32[]{:S(2)}) collective-permute-start(bf16[64,2048]{1,0:T(8,128)(2,1)} %add_convert_fusion), channel_id=1, source_target_pairs={{0,1},{1,0},{2,3},{3,2},{4,5},{5,4},{6,7},{7,6},{8,9},{9,8},{10,11... | collective-permute-start | bytes 786440 | tf_op jit(solution)/shard_map/ppermute | solution.py:40
  203.6 6.3 %collective-permute-start.48 = (f32[3,256]{1,0:T(4,128)S(1)}, f32[3,256]{1,0:T(4,128)S(1)}, u32[]{:S(2)}, u32[]{:S(2)}) collective-permute-start(f32[3,256]{1,0:T(4,128)S(1)} %get-tuple-element.241), channel_id=1, source_target_pairs={{0,1},{1,0},{2,3},{3,2},{4,5},{5,4},{6,7},{7,6},{8,9},{9,8},{10,11... | collective-permute-start | bytes 9224 | tf_op jit(solution)/shard_map/ppermute | solution.py:40
  204.0 20.2 %collective-permute-start.47 = (bf16[64,2048]{1,0:T(8,128)(2,1)}, bf16[64,2048]{1,0:T(8,128)(2,1)}, u32[]{:S(2)}, u32[]{:S(2)}) collective-permute-start(bf16[64,2048]{1,0:T(8,128)(2,1)} %last.1), channel_id=1, source_target_pairs={{0,1},{1,0},{2,3},{3,2},{4,5},{5,4},{6,7},{7,6},{8,9},{9,8},{10,11... | collective-permute-start | bytes 786440 | tf_op jit(solution)/shard_map/ppermute | solution.py:40
  205.0 20.3 %all-to-all-start = ((bf16[1,72,8,256]{3,1,0,2:T(8,128)(2,1)}), bf16[1,72,8,256]{3,1,0,2:T(8,128)(2,1)}, u32[]{:S(2)}, u32[]{:S(2)}) async-start(bf16[1,72,8,256]{3,1,0,2:T(8,128)(2,1)} %copy.48), calls=%async_computation | async-start | bytes 589824 | tf_op jit(solution)/shard_map/all_to_all | solution.py:1014
  209.9 12.5 %collective-permute-start.49 = (f32[3,256]{1,0:T(4,128)S(1)}, f32[3,256]{1,0:T(4,128)S(1)}, u32[]{:S(2)}, u32[]{:S(2)}) collective-permute-start(f32[3,256]{1,0:T(4,128)S(1)} %add.61), channel_id=1, source_target_pairs={{0,2},{1,3},{2,0},{3,1},{4,6},{5,7},{6,4},{7,5},{8,10},{9,11},{10,... | collective-permute-start | bytes 9224 | tf_op jit(solution)/shard_map/ppermute | solution.py:40
  227.1 3.4 %collective-permute-start.50 = (bf16[8,64,256]{2,1,0:T(8,128)(2,1)S(1)}, bf16[8,64,256]{2,1,0:T(8,128)(2,1)S(1)}, u32[]{:S(2)}, u32[]{:S(2)}) collective-permute-start(bf16[8,64,256]{2,1,0:T(8,128)(2,1)S(1)} %slice.20.mixed_a), channel_id=1, source_target_pairs={{0,1},{1,0},{2,3},{3,2},{4,5},{5,4},{6,7},{7,6},{8,9},{9,8},{10,11... | collective-permute-start | bytes 786440 | tf_op jit(solution)/shard_map/ppermute | solution.py:40
  227.2 2.7 %collective-permute-start.51 = (f32[3,256]{1,0:T(4,128)S(1)}, f32[3,256]{1,0:T(4,128)S(1)}, u32[]{:S(2)}, u32[]{:S(2)}) collective-permute-start(f32[3,256]{1,0:T(4,128)S(1)} %slice_add_fusion), channel_id=1, source_target_pairs={{0,1},{1,0},{2,3},{3,2},{4,5},{5,4},{6,7},{7,6},{8,9},{9,8},{10,11... | collective-permute-start | bytes 9224 | tf_op jit(solution)/shard_map/ppermute | solution.py:40
  (65 other events, 653.3 us)

commit v2 on v1

--- a/solution.py
+++ b/solution.py
@@ -233,7 +233,7 @@
     return pl.pallas_call(
         partial(rows_kernel, count=len(weights)),
         out_shape=[jax.ShapeDtypeStruct((rows.shape[0], across), bf16)] * len(weights),
-        compiler_params=params(16),
+        compiler_params=params(10),
         cost_estimate=cost(2 * rows.size * across * len(weights), 2 * rows.size),
         name="project_rows",
     )(rows, *weights)
@@ -247,7 +247,7 @@
     return pl.pallas_call(
         one_kernel,
         out_shape=jax.ShapeDtypeStruct((rows.shape[0], weight.shape[0]), bf16),
-        compiler_params=params(10),
+        compiler_params=params(6),
         cost_estimate=cost(2 * rows.size * weight.shape[0], 2 * weight.size),
         name="product_back",
     )(rows, weight)
@@ -269,50 +269,38 @@
     return pl.pallas_call(
         partial(halves_kernel, count=count, dims=dims),
         out_shape=[jax.ShapeDtypeStruct(shape, f32), jax.ShapeDtypeStruct(shape, bf16)],
-        compiler_params=params(16),
+        compiler_params=params(10),
         cost_estimate=cost(2 * count * rows[0].size * across, 2 * count * weights[0].size),
         name="product_halves",
     )(*rows, *weights)
 
 
 def down_own_kernel(rows, weight, mine, other, total):
-    term = dot(rows[...], weight[...], NN)
-
-    @pl.when(pl.program_id(0) == 0)
-    def _():
-        total[...] = term
-
-    @pl.when(pl.program_id(0) > 0)
-    def _():
-        total[...] += term
-
-    @pl.when(pl.program_id(0) == pl.num_programs(0) - 1)
-    def _():
-        half = mine.shape[0]
-        mine[...] = total[:half]
-        other[...] = total[half:].astype(bf16)
+    total[...] = jnp.zeros_like(total)
+
+    def step(at):
+        total[...] += dot(rows[:, at], weight[at, :], NN)
+
+    tiles_of(weight.shape[0], math.gcd(weight.shape[0], 512), step)
+    half = mine.shape[0]
+    mine[...] = total[:half]
+    other[...] = total[half:].astype(bf16)
 
 
 def down_own(rows, weight):
     count, deep = rows.shape
     across = weight.shape[1]
-    tile = math.gcd(deep, 512)
     shape = (count // 2, across)
-    whole = pl.BlockSpec(shape, lambda t: (0, 0))
     return pl.pallas_call(
         down_own_kernel,
-        grid=(deep // tile,),
-        in_specs=[
-            pl.BlockSpec((count, tile), lambda t: (0, t)),
-            pl.BlockSpec((tile, across), lambda t: (t, 0)),
-        ],
-        out_specs=[whole, whole],
+        in_specs=[WHOLE] * 2,
+        out_specs=[WHOLE] * 2,
         out_shape=[jax.ShapeDtypeStruct(shape, f32), jax.ShapeDtypeStruct(shape, bf16)],
         scratch_shapes=[pltpu.VMEM((count, across), f32)],
-        compiler_params=params(12),
+        compiler_params=params(6),
         cost_estimate=cost(2 * rows.size * across, 2 * weight.size),
         name="down_own",
-    )(rows, in_hbm(weight))
+    )(rows, weight)
 
 
 def gain_rows(gain, column):
@@ -372,7 +360,7 @@
         partial(norm_kernel, groups=groups, inner=inner_size(), parts=parts),
         in_specs=memory + [pl.BlockSpec(memory_space=pltpu.VMEM)] * (count + 2),
         out_shape=jax.ShapeDtypeStruct(shape + (width,), bf16),
-        compiler_params=params(20),
+        compiler_params=params(4 + count),
         cost_estimate=cost(10 * count * rows * width, 4 * count * rows * width),
         name="norm_pieces",
     )(index, *pieces, gain, kind.reshape(shape + (1,)))
@@ -388,7 +376,7 @@
     return pl.pallas_call(
         own_norm_kernel,
         out_shape=jax.ShapeDtypeStruct(rows.shape, bf16),
-        compiler_params=params(8),
+        compiler_params=params(4),
         cost_estimate=cost(10 * rows.size, 4 * rows.size),
         name="own_norm",
     )(rows, gain, kind)
@@ -405,7 +393,7 @@
     return pl.pallas_call(
         lift_kernel,
         out_shape=[jax.ShapeDtypeStruct(rows.shape, f32), jax.ShapeDtypeStruct(rows.shape, bf16)],
-        compiler_params=params(8),
+        compiler_params=params(4),
         cost_estimate=cost(10 * rows.size, 12 * rows.size),
         name="lift",
     )(rows, low, other, gain, kind)
@@ -419,44 +407,93 @@
     return jnp.concatenate(high + low + [zero, zero], axis=0)
 
 
-def middle_kernel(residual, low, other, grad, gain, kind, grad_residual, mixed, sums):
+def middle_kernel(residual, low, other, grad, gain, kind, grad_residual, mixed, parts):
     lifted_grad = low[...].astype(f32) + other[...].astype(f32)
     normal, inverse = normalize(residual[...])
     column = kind[...]
     back = norm_back(lifted_grad, normal, inverse, gain_rows(gain, column))
     value = grad[...].astype(f32) + back
     grad_residual[...] = value
-    mixed[...] = value.astype(bf16)
-    sums[...] = kind_sums(lifted_grad * normal, column)
-
-
-def middle(residual, low, other, grad, gain, kind):
-    width = residual.shape[1]
+    rounded_value = value.astype(bf16)
+    mixed[...] = rounded_value
+    sums = kind_sums(lifted_grad * normal, column)
+    shards, rows, part = parts.shape
+    for k in range(shards):
+        parts[k, pl.ds(0, rows - 8), :] = rounded_value[:, k * part : (k + 1) * part]
+        parts[k, pl.ds(rows - 8, 8), :] = sums[:, k * part : (k + 1) * part]
+
+
+def middle(residual, low, other, grad, gain, kind, shards):
+    rows, width = residual.shape
     return pl.pallas_call(
         middle_kernel,
         out_shape=[
             jax.ShapeDtypeStruct(residual.shape, f32),
             jax.ShapeDtypeStruct(residual.shape, bf16),
-            jax.ShapeDtypeStruct((8, width), bf16),
+            jax.ShapeDtypeStruct((shards, rows + 8, width // shards), bf16),
         ],
-        compiler_params=params(10),
+        compiler_params=params(6),
         cost_estimate=cost(20 * residual.size, 16 * residual.size),
         name="middle",
     )(residual, low, other, grad, gain, kind)
 
 
-def last_kernel(rows, low, other, grad_residual, gain, kind, out):
+def reordered(values, shards):
+    count = values.shape[0]
+    piece = count // shards
+    to = lax.broadcasted_iota(jnp.int32, (count, count), 0)
+    source = lax.broadcasted_iota(jnp.int32, (count, count), 1)
+    pick = (source == (to % shards) * piece + to // shards).astype(f32).astype(bf16)
+    return dot(pick, values, NN).astype(bf16)
+
+
+def finish_kernel(residual, low, other, out, *, shards):
+    value = residual[...] + (low[...].astype(f32) + other[...].astype(f32))
+    out[...] = reordered(value.astype(bf16), shards)
+
+
+def finish(residual, low, other, shards):
+    return pl.pallas_call(
+        partial(finish_kernel, shards=shards),
+        out_shape=jax.ShapeDtypeStruct(residual.shape, bf16),
+        compiler_params=params(4),
+        cost_estimate=cost(2 * residual.size, 10 * residual.size),
+        name="finish",
+    )(residual, low, other)
+
+
+def place_kernel(index, mine, other, out):
+    half = mine.shape[0]
+    out[pl.ds(pl.multiple_of(index[0] * half, half), half), :] = mine[...]
+    out[pl.ds(pl.multiple_of((1 - index[0]) * half, half), half), :] = other[...]
+
+
+def place_halves(mine):
+    half, width = mine.shape
+    index = (lax.axis_index("mlp") % 2).astype(jnp.int32).reshape(1)
+    return pl.pallas_call(
+        place_kernel,
+        in_specs=[pl.BlockSpec(memory_space=pltpu.SMEM)]
+        + [pl.BlockSpec(memory_space=pltpu.VMEM)] * 2,
+        out_shape=jax.ShapeDtypeStruct((2 * half, width), bf16),
+        compiler_params=params(4),
+        cost_estimate=cost(mine.size, 8 * mine.size),
+        name="place_halves",
+    )(index, mine, swap(mine, "mlp", 1))
+
+
+def last_kernel(rows, low, other, grad_residual, gain, kind, out, *, shards):
     grad = low[...].astype(f32) + other[...].astype(f32)
     normal, inverse = normalize(rows[...].astype(f32))
     back = norm_back(grad, normal, inverse, gain_rows(gain, kind[...]))
-    out[...] = (grad_residual[...] + back).astype(bf16)
-
-
-def last(rows, low, other, grad_residual, gain, kind):
-    return pl.pallas_call(
-        last_kernel,
+    out[...] = reordered((grad_residual[...] + back).astype(bf16), shards)
+
+
+def last(rows, low, other, grad_residual, gain, kind, shards):
+    return pl.pallas_call(
+        partial(last_kernel, shards=shards),
         out_shape=jax.ShapeDtypeStruct(rows.shape, bf16),
-        compiler_params=params(8),
+        compiler_params=params(6),
         cost_estimate=cost(20 * rows.size, 12 * rows.size),
         name="last",
     )(rows, low, other, grad_residual, gain, kind)
@@ -471,83 +508,81 @@
     return value * upper, slope
 
 
-def own_kernel(lifted, up, grad_activated, activated, mine, other, lifted_grad):
-    value, slope = gelu_parts(dot(lifted[...], up[...], NN))
-    activated[...] = value.astype(bf16)
-    hidden_grad = (grad_activated[...] * slope).astype(bf16)
-    term = dot(hidden_grad, up[...], NT)
-
-    @pl.when(pl.program_id(0) == 0)
-    def _():
-        lifted_grad[...] = term
-
-    @pl.when(pl.program_id(0) > 0)
-    def _():
-        lifted_grad[...] += term
-
-    @pl.when(pl.program_id(0) == pl.num_programs(0) - 1)
-    def _():
-        half = mine.shape[0]
-        mine[...] = lifted_grad[:half]
-        other[...] = lifted_grad[half:].astype(bf16)
+WHOLE = pl.BlockSpec(memory_space=pltpu.VMEM)
+
+
+def tiles_of(extent, tile, step):
+    def at(t, _):
+        step(pl.ds(pl.multiple_of(t * tile, tile), tile))
+        return 0
+
+    lax.fori_loop(0, extent // tile, at, 0)
+
+
+def own_kernel(lifted, up, grad_activated, activated, hidden_grads, mine, other, total):
+    total[...] = jnp.zeros_like(total)
+
+    def step(at):
+        value, slope = gelu_parts(dot(lifted[...], up[:, at], NN))
+        activated[:, at] = value.astype(bf16)
+        hidden_grad = (grad_activated[:, at] * slope).astype(bf16)
+        hidden_grads[:, at] = hidden_grad
+        total[...] += dot(hidden_grad, up[:, at], NT)
+
+    tiles_of(up.shape[1], math.gcd(up.shape[1], 512), step)
+    half = mine.shape[0]
+    mine[...] = total[:half]
+    other[...] = total[half:].astype(bf16)
 
 
 def feed_own(lifted, up, grad_activated):
     rows, width = lifted.shape
     hidden = up.shape[1]
-    tile = math.gcd(hidden, 512)
-    across = lambda t: (0, t)
-    whole = lambda t: (0, 0)
     return pl.pallas_call(
         own_kernel,
-        grid=(hidden // tile,),
-        in_specs=[
-            pl.BlockSpec((rows, width), whole),
-            pl.BlockSpec((width, tile), across),
-            pl.BlockSpec((rows, tile), across),
-        ],
-        out_specs=[pl.BlockSpec((rows, tile), across)]
-        + [pl.BlockSpec((rows // 2, width), whole)] * 2,
-        out_shape=[
-            jax.ShapeDtypeStruct((rows, hidden), bf16),
+        in_specs=[WHOLE] * 3,
+        out_specs=[WHOLE] * 4,
+        out_shape=[jax.ShapeDtypeStruct((rows, hidden), bf16)] * 2
+        + [
             jax.ShapeDtypeStruct((rows // 2, width), f32),
             jax.ShapeDtypeStruct((rows // 2, width), bf16),
         ],
         scratch_shapes=[pltpu.VMEM((rows, width), f32)],
-        compiler_params=params(16),
+        compiler_params=params(8),
         cost_estimate=cost(4 * rows * width * hidden, 2 * width * hidden),
         name="feed_own",
     )(lifted, up, grad_activated)
 
 
 def down_kernel(grad, down, out):
-    out[...] = dot(grad[...], down[...], NT)
+    def step(at):
+        out[:, at] = dot(grad[...], down[at, :], NT)
+
+    tiles_of(down.shape[0], math.gcd(down.shape[0], 512), step)
 
 
 def grad_activated(grad, down):
     rows, width = grad.shape
     hidden = down.shape[0]
-    tile = math.gcd(hidden, 512)
     return pl.pallas_call(
         down_kernel,
-        grid=(hidden // tile,),
-        in_specs=[
-            pl.BlockSpec((rows, width), lambda t: (0, 0)),
-            pl.BlockSpec((tile, width), lambda t: (t, 0)),
-        ],
-        out_specs=pl.BlockSpec((rows, tile), lambda t: (0, t)),
+        in_specs=[WHOLE] * 2,
+        out_specs=WHOLE,
         out_shape=jax.ShapeDtypeStruct((rows, hidden), f32),
-        compiler_params=params(12),
+        compiler_params=params(6),
         cost_estimate=cost(2 * rows * width * hidden, 2 * width * hidden),
         name="grad_activated",
     )(grad, down)
 
 
-def all_kernel(index, *refs, counts, add):
+def all_kernel(index, *refs, counts):
     count = len(counts)
     lifted_parts, grad_parts = refs[:count], refs[count : 2 * count]
     up, down = refs[2 * count : 2 * count + 2]
-    up_grad, down_grad, lifted, grad, sems = refs[-5:]
+    before = refs[2 * count + 2 : -8]
+    up_grad, down_grad, lifted, grad, lifted_across, hidden_kept, grad_kept, sems = refs[-8:]
+    part = up_grad.shape[0]
+    mine = pl.ds(pl.multiple_of(index[0] * part, part), part)
 
     @pl.when(pl.program_id(0) == 0)
     def _():
@@ -562,60 +597,96 @@
             copy.start()
         for copy in copies:
             copy.wait()
-
-    part = up_grad.shape[0]
-    mine = pl.ds(pl.multiple_of(index[0] * part, part), part)
-    value, slope = gelu_parts(dot(lifted[...], up[...], NN))
-    hidden_grad = (dot(grad[...], down[...], NT) * slope).astype(bf16)
-    down_term = dot(value.astype(bf16), grad[:, mine], TN)
-    up_term = dot(lifted[:, mine], hidden_grad, TN)
-    if add:
-        up_term += refs[2 * count + 2][...]
-        down_term += refs[2 * count + 3][...]
-    up_grad[...] = up_term
-    down_grad[...] = down_term
-
-
-def feed_all(lifted, grad, up, down, shards, place, places, sums, add):
+        lifted_across[...] = lifted[:, mine].T
+
+    first = pl.program_id(0) == 0
+    last_step = pl.num_programs(0) - 1
+
+    def products():
+        return dot(lifted[...], up[...], NN), dot(grad[...], down[...], NT)
+
+    def finish_tile(hidden_value, activated_grad):
+        value, slope = gelu_parts(hidden_value)
+        hidden_grad = (activated_grad * slope).astype(bf16)
+        down_term = dot(value.astype(bf16), grad[:, mine], TN)
+        up_term = dot(lifted_across[...], hidden_grad, NN)
+        if len(before) == 2:
+            up_term += before[0][...]
+            down_term += before[1][...]
+        else:
+            lifted_own, grad_own, activated, hidden_own = before
+            up_term += dot(lifted_own[...], hidden_own[...], TN)
+            down_term += dot(activated[...], grad_own[...], TN)
+        up_grad[...] = up_term
+        down_grad[...] = down_term
+
+    @pl.when(first)
+    def _():
+        hidden_kept[...], grad_kept[...] = products()
+
+    @pl.when((pl.program_id(0) > 0) & (pl.program_id(0) < last_step))
+    def _():
+        kept = hidden_kept[...], grad_kept[...]
+        fresh = products()
+        finish_tile(*kept)
+        hidden_kept[...], grad_kept[...] = fresh
+
+    @pl.when(pl.program_id(0) == last_step)
+    def _():
+        finish_tile(hidden_kept[...], grad_kept[...])
+
+
+def feed_all(lifted, grad, up, down, shards, sums=(), own=()):
     counts = [array.shape[0] for array in lifted]
     rows, width = sum(counts), lifted[0].shape[1]
     count = len(counts)
     part = width // shards
     hidden = up.shape[1]
-    tile = math.gcd(hidden // places, 256)
-    steps = hidden // places // tile
-    first = place * steps
-    across = lambda t, index: (0, first + t)
-    below = lambda t, index: (first + t, 0)
+    tile = math.gcd(hidden, 256)
+    steps = hidden // tile
+    wide = lambda t, index: (0, jnp.minimum(t, steps - 1))
+    deep = lambda t, index: (jnp.minimum(t, steps - 1), 0)
+    across = lambda t, index: (0, jnp.maximum(t - 1, 0))
+    below = lambda t, index: (jnp.maximum(t - 1, 0), 0)
+    mine = lambda t, index: (0, index[0])
     anywhere = pl.BlockSpec(memory_space=pl.ANY)
     sum_specs = [pl.BlockSpec((part, tile), across), pl.BlockSpec((tile, part), below)]
+    if own:
+        own_rows = own[0].shape[0]
+        more = [pl.BlockSpec((own_rows, part), mine)] * 2
+        more += [pl.BlockSpec((own_rows, tile), across)] * 2
+    else:
+        more = sum_specs
     index = lax.axis_index("seq").astype(jnp.int32).reshape(1)
-    at = 1 + 2 * count + 2
-    return pl.pallas_call(
-        partial(all_kernel, counts=counts, add=add),
+    return pl.pallas_call(
+        partial(all_kernel, counts=counts),
         grid_spec=pltpu.PrefetchScalarGridSpec(
             num_scalar_prefetch=1,
-            grid=(steps,),
+            grid=(steps + 1,),
             in_specs=[anywhere] * (2 * count)
-            + [pl.BlockSpec((width, tile), across), pl.BlockSpec((tile, width), below)]
-            + ((sum_specs if add else [anywhere] * 2) if sums else []),
+            + [pl.BlockSpec((width, tile), wide), pl.BlockSpec((tile, width), deep)]
+            + more,
             out_specs=sum_specs,
             scratch_shapes=[pltpu.VMEM((rows, width), bf16)] * 2
+            + [pltpu.VMEM((part, rows), bf16)]
+            + [pltpu.VMEM((rows, tile), f32)] * 2
             + [pltpu.SemaphoreType.DMA((2 * count,))],
         ),
-        out_shape=[
-            jax.ShapeDtypeStruct((part, hidden), f32),
-            jax.ShapeDtypeStruct((hidden, part), f32),
-        ],
-        input_output_aliases={at: 0, at + 1: 1} if sums else {},
-        compiler_params=params(10 + 20 * rows // 640),
+        out_shape=[pltpu.HBM((part, hidden), f32), pltpu.HBM((hidden, part), f32)],
+        compiler_params=params(8 + 15 * rows // 640),
         cost_estimate=cost(
-            4 * rows * hidden // places * (width + part),
-            4 * width * hidden // places + 4 * rows * width,
-            share=4,
+            4 * rows * hidden * (width + part),
+            4 * width * hidden + 4 * rows * width,
         ),
         name="feed_all",
-    )(index, *lifted, *grad, in_hbm(up), in_hbm(down), *sums)
+    )(
+        index,
+        *lifted,
+        *grad,
+        in_hbm(up),
+        in_hbm(down),
+        *(own or [in_hbm(array) for array in sums]),
+    )
 
 
 def project_kernel(index, *refs):
@@ -657,40 +728,49 @@
         ),
         out_shape=[jax.ShapeDtypeStruct((part, across), f32)] * 3
         + [jax.ShapeDtypeStruct((gain.shape[0], part), f32)],
-        compiler_params=params(20),
+        compiler_params=params(14),
         cost_estimate=cost(24 * rows * part * across, 12 * rows * across + 12 * part * across),
         name="project",
     )(index, *normed, *[low for pair in lows for low in pair], *weights, gain, *kinds)
 
 
-def output_kernel(index, attended_a, attended_b, mixed_a, mixed_b, out, *, groups):
-    total = 0.0
-    shards, half, part = mixed_a.shape
+def output_kernel(index, attended_a, attended_b, came_a, came_b, out, gain_grad, *, groups):
+    total, sums = 0.0, 0.0
+    shards, rows, part = came_a.shape
+    half = rows - 8
     each = half // groups
-    for attended, mixed in ((attended_a, mixed_a), (attended_b, mixed_b)):
-        rows = [
-            mixed[index[0] ^ d, pl.ds(group * each, each), :]
+    for attended, came in ((attended_a, came_a), (attended_b, came_b)):
+        mixed = [
+            came[index[0] ^ d, pl.ds(group * each, each), :]
             for group in range(groups)
             for d in range(shards)
         ]
-        total += dot(attended[...], jnp.concatenate(rows, axis=0), TN)
+        total += dot(attended[...], jnp.concatenate(mixed, axis=0), TN)
+        own_sums = 0.0
+        for k in range(shards):
+            own_sums += came[k, pl.ds(half, 8), :].astype(f32)
+        sums += own_sums
     out[...] = total
-
-
-def output_part(attended, mixed, groups):
+    gain_grad[...] = sums[0:3, :] + sums[3:6, :]
+
+
+def output_part(attended, came, groups):
     index = lax.axis_index("seq").astype(jnp.int32).reshape(1)
-    across, part = attended[0].shape[1], mixed[0].shape[2]
+    across, part = attended[0].shape[1], came[0].shape[2]
     return pl.pallas_call(
         partial(output_kernel, groups=groups),
         in_specs=[pl.BlockSpec(memory_space=pltpu.SMEM)]
         + [pl.BlockSpec(memory_space=pltpu.VMEM)] * 4,
-        out_shape=jax.ShapeDtypeStruct((across, part), f32),
-        compiler_params=params(10),
+        out_shape=[
+            jax.ShapeDtypeStruct((across, part), f32),
+            jax.ShapeDtypeStruct((3, part), f32),
+        ],
+        compiler_params=params(6),
         cost_estimate=cost(
             4 * attended[0].shape[0] * across * part, 4 * attended[0].shape[0] * (across + part)
         ),
         name="output_part",
-    )(index, *attended, *mixed)
+    )(index, *attended, *came)
 
 
 def mask_of(key_place, query_place, clip_length, clips):
@@ -727,8 +807,8 @@
             for mask, key in zip(allowed, (key_a, key_b))
         ]
         prob = [block.astype(bf16) for block in probabilities(scores, scale)]
-        result = dot(prob[0], value_a[:, at], TN) + dot(prob[1], value_b[:, at], TN)
-        out[:, at] = result.astype(bf16)
+        result = dot(value_a[:, at], prob[0], TN) + dot(value_b[:, at], prob[1], TN)
+        out[:, at] = result.T.astype(bf16)
 
 
 def attend(query, keys, values, places, query_place, clip_length, clips):
@@ -739,7 +819,7 @@
             forward_kernel, scale=1.0 / math.sqrt(HEAD_DIM), clip_length=clip_length, clips=clips
         ),
         out_shape=jax.ShapeDtypeStruct((rows, width), bf16),
-        compiler_params=params(16),
+        compiler_params=params(8),
         cost_estimate=cost(
             4 * rows * total * width, 4 * total * width, rows * total * (width // HEAD_DIM)
         ),
@@ -747,20 +827,106 @@
     )(query, *keys, *values, *places, query_place)
 
 
-def backward_kernel(*refs, count, groups, scale, clip_length, clips):
-    grads = refs[:count]
-    query_a, query_b, key_a, key_b, value_a, value_b, place_a, place_b, query_place = refs[
+def block_of(half):
+    return min(128, half)
+
+
+def reaches(half, groups):
+    blocks = half // block_of(half)
+    found, start = [], 0
+    for index in range(blocks):
+        seen, free = (index + 1, index) if groups > 1 else (blocks, 0)
+        found.append((seen, free, start))
+        start += seen
+    return found, start
+
+
+def take(first, second, low, high, at):
+    block = block_of(first.shape[0])
+    rows = [side[pl.ds(k * block, block), at] for k in range(low, high) for side in (first, second)]
+    return jnp.concatenate(rows, axis=0)
+
+
+def columns_of(head):
+    return pl.ds(pl.multiple_of(head * HEAD_DIM, HEAD_DIM), HEAD_DIM)
+
+
+def all_forward_kernel(*refs, groups, scale, clip_length, clips):
+    query_a, query_b, key_a, key_b, value_a, value_b, place_a, place_b, query_place = refs[:9]
+    attended_a, attended_b, stored = refs[9:]
+    half, width = key_a.shape
+    block = block_of(half)
+    pair = 2 * block
+    everything = slice(None)
+
+    def one_head(head, _):
+        cut = columns_of(head)
+        values_across = take(value_a, value_b, 0, half // block, cut).T
+        for index, (seen, free, start) in enumerate(reaches(half, groups)[0]):
+            mine = pl.ds(index * block, block)
+            query = take(query_a, query_b, index, index + 1, cut)
+            at_place = query_place[:, pl.ds(index * pair, pair)]
+            place = take(place_a, place_b, free, seen, everything)
+            mask = mask_of(place, at_place, clip_length, clips)
+            score = dot(take(key_a, key_b, free, seen, cut), query, NT)
+            scores = [jnp.where(mask, score, NEGATIVE)]
+            if free:
+                scores.insert(0, dot(take(key_a, key_b, 0, free, cut), query, NT))
+            result, at = 0.0, 0
+            for prob in probabilities(scores, scale):
+                kept = prob.astype(bf16)
+                rows = kept.shape[0]
+                stored[head, pl.ds(start * pair + at, rows), :] = kept
+                result += dot(values_across[:, at : at + rows], kept, NN)
+                at += rows
+            result = result.T.astype(bf16)
+            attended_a[mine, cut] = result[:block]
+            attended_b[mine, cut] = result[block:]
+        return 0
+
+    lax.fori_loop(0, width // HEAD_DIM, one_head, 0)
+
+
+def attend_all(queries, keys, values, places, query_place, groups, clip_length, clips):
+    half, width = keys[0].shape
+    heads = width // HEAD_DIM
+    pair = 2 * block_of(half)
+    deep = reaches(half, groups)[1] * pair
+    outs = pl.pallas_call(
+        partial(
+            all_forward_kernel,
+            groups=groups,
+            scale=1.0 / math.sqrt(HEAD_DIM),
+            clip_length=clip_length,
+            clips=clips,
+        ),
+        in_specs=[pl.BlockSpec(memory_space=pltpu.VMEM)] * 9,
+        out_specs=[pl.BlockSpec(memory_space=pltpu.VMEM)] * 3,
+        out_shape=[jax.ShapeDtypeStruct((half, width), bf16)] * 2
+        + [jax.ShapeDtypeStruct((heads, deep, pair), bf16)],
+        compiler_params=params(max(8, half * half // 2**15)),
+        cost_estimate=cost(16 * half * half * width, 16 * half * width, 4 * half * half * heads),
+        name="attend_all",
+    )(*queries, *keys, *values, *places, query_place)
+    return outs[:2], outs[2]
+
+
+def backward_kernel(*refs, count, groups, scale):
+    grad_pieces = refs[:count]
+    query_a, query_b, key_a, key_b, value_a, value_b, attended_a, attended_b, stored = refs[
         count : count + 9
     ]
-    outs = refs[count + 9 : count + 20]
-    attended, grad_query, grad_key, grad_value = outs[0:2], outs[2:4], outs[4:6], outs[6:8]
-    own_query, own_key, own_value = outs[8:11]
-    sums = refs[count + 20 :]
-    half = key_a.shape[0]
+    outs = refs[count + 9 : count + 18]
+    grad_query, grad_key, grad_value = outs[0:2], outs[2:4], outs[4:6]
+    own_query, own_key, own_value = outs[6:9]
+    (scores,) = refs[count + 18 :]
+    half, width = key_a.shape
     rows = half // count
     group_rows = rows // groups
-    block = min(128, half)
+    block = block_of(half)
     blocks = half // block
+    pair = 2 * block
+    reach = reaches(half, groups)[0]
 
     def sources(index):
         found = []
@@ -774,114 +940,82 @@
                 found.append((d, j * group_rows, group_rows))
         return found
 
-    def keep_own(target, values, index):
-        for side in range(2):
-            at = side * block
-            for d, start, size in sources(index):
-                if d == 0:
-                    target[pl.ds(side * rows + start, size), :] = values[at : at + size]
-                at += size
-
-    for ref in sums:
-        ref[...] = jnp.zeros_like(ref)
-    for index in range(blocks):
-        mine = pl.ds(index * block, block)
-        reach = (index + 1) * block if groups > 1 else half
-        free = index * block if groups > 1 else 0
-        query = jnp.concatenate([query_a[mine, :], query_b[mine, :]], axis=0)
-        grad = jnp.concatenate(
-            [
-                grads[d][pl.ds(side * rows + start, size), :]
-                for side in range(2)
-                for d, start, size in sources(index)
-            ],
-            axis=0,
-        )
-        at_place = query_place[:, pl.ds(index * 2 * block, 2 * block)]
-        spans = []
-        for side in range(2):
-            if free:
-                spans.append((side, 0, free, False))
-            spans.append((side, free, reach, True))
-        keys, values, places = (key_a, key_b), (value_a, value_b), (place_a, place_b)
-        scores = []
-        for side, low, high, masked in spans:
-            score = dot(keys[side][pl.ds(low, high - low), :], query, NT)
-            if masked:
-                place = places[side][pl.ds(low, high - low), :]
-                score = jnp.where(mask_of(place, at_place, clip_length, clips), score, NEGATIVE)
-            scores.append(score)
-        prob = probabilities(scores, scale)
-        lows = [part.astype(bf16) for part in prob]
-        grad_prob = [
-            dot(values[side][pl.ds(low, high - low), :], grad, NT) for side, low, high, _ in spans
-        ]
-        delta = sum((p * g).sum(axis=0, keepdims=True) for p, g in zip(prob, grad_prob))
-        grad_score = [(p * (g - delta)).astype(bf16) for p, g in zip(prob, grad_prob)]
-        result = sum(
-            dot(part, values[side][pl.ds(low, high - low), :], TN)
-            for part, (side, low, high, _) in zip(lows, spans)
-        ).astype(bf16)
-        back = (
-            sum(
-                dot(part, keys[side][pl.ds(low, high - low), :], TN)
-                for part, (side, low, high, _) in zip(grad_score, spans)
+    def one_head(head, _):
+        cut = columns_of(head)
+
+        def keep(targets, own, values, index):
+            for side in range(2):
+                at = side * block
+                targets[side][pl.ds(index * block, block), cut] = values[at : at + block]
+                for d, start, size in sources(index):
+                    if d == 0:
+                        own[pl.ds(side * rows + start, size), cut] = values[at : at + size]
+                    at += size
+
+        def take_grads(index):
+            return jnp.concatenate(
+                [
+                    grad_pieces[d][pl.ds(side * rows + start, size), cut]
+                    for side in range(2)
+                    for d, start, size in sources(index)
+                ],
+                axis=0,
             )
-            * scale
-        ).astype(bf16)
-        for side in range(2):
-            attended[side][mine, :] = result[side * block : (side + 1) * block]
-            grad_query[side][mine, :] = back[side * block : (side + 1) * block]
-        keep_own(own_query, back, index)
-        for (side, low, high, _), score, part in zip(spans, grad_score, lows):
-            at = pl.ds(low, high - low)
-            sums[side][at, :] += dot(score, query, NN)
-            sums[2 + side][at, :] += dot(part, grad, NN)
-    low_key = [(sums[side][...] * scale).astype(bf16) for side in range(2)]
-    low_value = [sums[2 + side][...].astype(bf16) for side in range(2)]
-    for side in range(2):
-        grad_key[side][...] = low_key[side]
-        grad_value[side][...] = low_value[side]
-    for index in range(blocks):
-        cut = slice(index * block, (index + 1) * block)
-        keep_own(own_key, jnp.concatenate([low[cut] for low in low_key], axis=0), index)
-        keep_own(own_value, jnp.concatenate([low[cut] for low in low_value], axis=0), index)
-
-
-def attend_back(grads, queries, keys, values, places, query_place, groups, clip_length, clips):
+
+        keys_across = take(key_a, key_b, 0, blocks, cut).T
+        ones = jnp.ones((8, HEAD_DIM), f32)
+        for index, (seen, _, start) in enumerate(reach):
+            result = take(attended_a, attended_b, index, index + 1, cut)
+            grad = take_grads(index)
+            delta = lax.dot_general(
+                ones,
+                grad.astype(f32) * result.astype(f32),
+                (NT, ((), ())),
+                precision=lax.Precision.HIGHEST,
+                preferred_element_type=f32,
+            )[0:1, :]
+            at = pl.ds(start * pair, seen * pair)
+            grad_prob = dot(take(value_a, value_b, 0, seen, cut), grad, NT)
+            score = (stored[head, at, :].astype(f32) * (grad_prob - delta)).astype(bf16)
+            scores[at, :] = score
+            back = dot(keys_across[:, : seen * pair], score, NN)
+            keep(grad_query, own_query, (back * scale).T.astype(bf16), index)
+        for index in range(blocks):
+            key_sum, value_sum = 0.0, 0.0
+            for other, (seen, _, start) in enumerate(reach):
+                if index < seen:
+                    at = pl.ds((start + index) * pair, pair)
+                    query = take(query_a, query_b, other, other + 1, cut)
+                    key_sum += dot(scores[at, :], query, NN)
+                    value_sum += dot(stored[head, at, :], take_grads(other), NN)
+            keep(grad_key, own_key, (key_sum * scale).astype(bf16), index)
+            keep(grad_value, own_value, value_sum.astype(bf16), index)
+        return 0
+
+    lax.fori_loop(0, width // HEAD_DIM, one_head, 0)
+
+
+def attend_back(grads, queries, keys, values, attended, stored, groups):
     half, width = keys[0].shape
     count = len(grads)
-    heads = width // HEAD_DIM
     rows = grads[0].shape[0]
-    by_head = lambda h: (0, h)
-    whole = lambda h: (0, 0)
-    tall = pl.BlockSpec((half, HEAD_DIM), by_head)
-    short = pl.BlockSpec((rows, HEAD_DIM), by_head)
     outs = pl.pallas_call(
         partial(
             backward_kernel,
             count=count,
             groups=groups,
             scale=1.0 / math.sqrt(HEAD_DIM),
-            clip_length=clip_length,
-            clips=clips,
         ),
-        grid=(heads,),
-        in_specs=[short] * count
-        + [tall] * 6
-        + [pl.BlockSpec((half, 1), whole)] * 2
-        + [pl.BlockSpec((1, 2 * half), whole)],
-        out_specs=[tall] * 8 + [short] * 3,
-        out_shape=[jax.ShapeDtypeStruct((half, width), bf16)] * 8
+        in_specs=[pl.BlockSpec(memory_space=pltpu.VMEM)] * (count + 9),
+        out_specs=[pl.BlockSpec(memory_space=pltpu.VMEM)] * 9,
+        out_shape=[jax.ShapeDtypeStruct((half, width), bf16)] * 6
         + [jax.ShapeDtypeStruct((rows, width), bf16)] * 3,
-        scratch_shapes=[pltpu.VMEM((half, HEAD_DIM), f32)] * 4,
-        compiler_params=params(32),
-        cost_estimate=cost(
-            12 * 4 * half * half * width, 32 * half * width, 4 * half * half * heads
-        ),
+        scratch_shapes=[pltpu.VMEM(stored.shape[1:], bf16)],
+        compiler_params=params(8 + 2 * stored.shape[1] * stored.shape[2] // 2**20),
+        cost_estimate=cost(8 * 4 * half * half * width, 32 * half * width + 2 * stored.size),
         name="attend_back",
-    )(*[in_hbm(grad) for grad in grads], *queries, *keys, *values, *places, query_place)
-    return outs[0:2], outs[2:4], outs[4:6], outs[6:8], outs[8:11]
+    )(*grads, *queries, *keys, *values, *attended, stored)
+    return outs[0:2], outs[2:4], outs[4:6], outs[6:9]
 
 
 def body(
@@ -920,13 +1054,6 @@
             other.transpose(1, 0, 2).reshape(half, width),
         )
 
-    def restore(mine):
-        other = swap(mine, "mlp", 1)
-        upper = jnp.where(core == 0, mine, other)
-        lower = jnp.where(core == 0, other, mine)
-        rows = jnp.stack([upper, lower]).reshape(2, shards, piece, width)
-        return rows.transpose(0, 2, 1, 3).reshape(length, width)
-
     inputs_half, inputs_other = halves(inputs)
     pieces = gather_early(inputs_half)
     arrived = pieces[inner_size() :: inner_size()]
@@ -942,106 +1069,94 @@
     grad_half, grad_other = halves(cotangent)
     grad_own = jnp.concatenate([grad_half, grad_other], axis=0)
     (query_own,) = project_rows(after(own_normed, arrived), query_weight)
-    own_activated_grad = grad_activated(after(grad_own, query_own), down_weight)
-    grad_far = gather_outer(after(grad_half, arrived))
-    pieces, grad_far = after((pieces, grad_far), own_activated_grad)
+    grad_far = gather_outer(after(grad_half, arrived, pieces[inner_size() + 1]))
+    pieces = after(pieces, query_own)
 
     normed = [norm_pieces(pieces, first_gain, kind_a, groups)]
+    normed[0], grad_far = after((normed[0], grad_far), normed[0])
     normed.append(swap(normed[0], "mlp", 1))
     keys, values = zip(*[project_rows(rows, key_weight, value_weight) for rows in normed])
     heads_own = attend(query_own, keys, values, places, own_place, clip_length, clips)
-    grad_far = join_x(jnp.concatenate(after(grad_far, normed[0]), axis=0), heads_own)
+    grad_inner = gather_inner(after(grad_half, normed[0]))
+    heads_own, grad_inner = after((heads_own, grad_inner), heads_own)
+    grad_far = join_x(jnp.concatenate(grad_far, axis=0), heads_own)
     mine, other = product_halves([heads_own], [output_weight], NN)
     other, grad_far = after((other, grad_far), other)
-    grad_inner = gather_inner(grad_half) + gather_inner(grad_far)
+    grad_inner += gather_inner(grad_far)
     low, other = pair_mlp(mine, other)
-    queries = [project_rows(rows, query_weight)[0] for rows in after(normed, low)]
-    other = after(other, queries)
+    own_activated_grad = grad_activated(after(grad_own, low), down_weight)
+    other = after(other, own_activated_grad)
     residual, lifted_half = lift(inputs_half, low, other, second_gain, half_kind)
 
     lifted_own = both(lifted_half)
-    activated_own, mine, other = feed_own(lifted_own, up_weight, own_activated_grad)
+    activated_own, hidden_own, mine, other = feed_own(lifted_own, up_weight, own_activated_grad)
     lifted_far = gather_outer(after(lifted_half, other))
     other, grad_inner = after((other, grad_inner), other)
     low, other = pair_mlp(mine, other)
     down_mine, down_other = down_own(after(activated_own, low), down_weight)
     other, lifted_far = after((other, lifted_far), down_other)
-    grad_residual, mixed_half, second_sums = middle(
-        residual, low, other, grad_half, second_gain, half_kind
+    grad_residual, mixed_half, mixed_columns = middle(
+        residual, low, other, grad_half, second_gain, half_kind, shards
     )
     heads_grad = product_back(both(mixed_half), output_weight)
 
-    places_up = 2
-    sums = ()
-
-    def feed(lifted, grads, place, add, *earlier):
-        return feed_all(
-            after(lifted, earlier), grads, up_weight, down_weight, shards, place, places_up, sums, add
-        )
-
     heads_first = gather_first(heads_grad)
-    lifted_far = join_x(jnp.concatenate(lifted_far, axis=0), heads_first)
+    queries = [project_rows(rows, query_weight)[0] for rows in after(normed, heads_grad)]
+    attended, stored = attend_all(
+        queries, keys, values, places, query_place, groups, clip_length, clips
+    )
+    lifted_far = jnp.concatenate(lifted_far, axis=0)
+    lifted_inner = gather_inner(after(lifted_half, heads_grad))
+    lifted_inner_far = gather_inner(lifted_far)
+    lifted_far = join_x(lifted_far, heads_first, attended)
     heads_grads = gather_pieces(*heads_first)
-    first_lifted = [lifted_own] + with_core([lifted_far])
-    first_grads = [grad_own] + with_core([grad_far])
-    sums = feed(first_lifted, first_grads, 0, False, heads_grads[inner_size() + 1])
-    sums = feed(first_lifted, first_grads, 1, False)
+    first_lifted, first_grads = with_core([lifted_far]), with_core([grad_far])
+    own = (lifted_own, grad_own, activated_own, hidden_own)
+    sums = feed_all(first_lifted, first_grads, up_weight, down_weight, shards, own=own)
     down_low, down_other = pair_mlp(down_mine, after(down_other, heads_grad))
-    heads_grads, down_low = after((heads_grads, down_low), sums)
-    lifted_inner = gather_inner(after(lifted_half, heads_grads))
-    lifted_inner += gather_inner(after(lifted_far, heads_grads))
-
-    attended, query_low, key_low, value_low, own_low = attend_back(
-        heads_grads,
-        queries,
-        keys,
-        values,
-        places,
-        query_place,
-        groups,
-        clip_length,
-        clips,
-    )
-    own_low, lifted_inner, down_other = after((own_low, lifted_inner, down_other), own_low)
-    rest_lifted, rest_grads = with_core(lifted_inner), with_core(grad_inner)
+    heads_grads, down_low, down_other, lifted_inner, lifted_inner_far = after(
+        (heads_grads, down_low, down_other, lifted_inner, lifted_inner_far), sums
+    )
+
+    query_low, key_low, value_low, own_low = attend_back(
+        heads_grads, queries, keys, values, attended, stored, groups
+    )
     attention_weights = (query_weight, key_weight, value_weight)
+    lifted_inner += [join_x(far, own_low) for far in lifted_inner_far]
+    own_low, lifted_inner = after((own_low, lifted_inner), own_low)
     low, other = pair_mlp(*product_halves(own_low, attention_weights, NT))
-    sums = feed(rest_lifted, rest_grads, 0, True, low)
-    other = after(other, sums)
-    input_grad_half = last(inputs_half, low, other, grad_residual, first_gain, half_kind)
-    input_grad = restore(input_grad_half)
-
-    mixed_part = lax.all_to_all(
-        after(jnp.concatenate([mixed_half, second_sums], axis=0), other).reshape(
-            half + 8, shards, part
-        ),
-        "seq",
-        split_axis=1,
-        concat_axis=0,
-        tiled=False,
-    )
-    down_total = down_low.astype(f32) + after(down_other, input_grad_half).astype(f32)
-    outputs = restore((residual + down_total).astype(bf16))
 
     query_grad, key_grad, value_grad, first_gain_grad = project(
         normed,
-        after((query_low, key_low, value_low), other),
+        after((query_low, key_low, value_low), low),
         attention_weights,
         first_gain,
         kinds,
         shards,
     )
-    bit = 1
+    mixed_part = lax.all_to_all(
+        after(mixed_columns, query_grad), "seq", split_axis=0, concat_axis=0, tiled=True
+    )
+    first_gain_grad = first_gain_grad + swap(first_gain_grad, "mlp", 1)
+    other, first_gain_grad = after((other, first_gain_grad), query_grad)
+    input_half = last(inputs_half, low, other, grad_residual, first_gain, half_kind, shards)
+    outputs_half = finish(residual, down_low, after(down_other, input_half), shards)
+    rest_lifted = with_core(after(lifted_inner, other))
+    rest_grads = with_core(after(grad_inner, other))
+    up_grad, down_grad = feed_all(
+        after(rest_lifted, outputs_half), rest_grads, up_weight, down_weight, shards, sums
+    )
+    bit = 2
     while bit < lax.axis_size("mlp"):
-        first_gain_grad = first_gain_grad + swap(first_gain_grad, "mlp", bit)
+        came = after(swap(first_gain_grad, "mlp", bit), up_grad)
+        first_gain_grad = first_gain_grad + came
         bit *= 2
-    up_grad, down_grad = feed(rest_lifted, rest_grads, 1, True, query_grad)
-
-    second_sums = jnp.sum(mixed_part[:, half : half + 6].astype(f32), axis=0)
-    second_sums = second_sums[:3] + second_sums[3:]
-    second_gain_grad = second_sums + swap(second_sums, "mlp", 1)
-    mixed_part = after(mixed_part[:, :half], up_grad)
-    output_grad = output_part(attended, (mixed_part, swap(mixed_part, "mlp", 1)), groups)
+    input_grad = place_halves(input_half)
+    outputs = place_halves(outputs_half)
+    mixed_part = after(mixed_part, up_grad)
+    output_grad, second_gain_grad = output_part(
+        attended, (mixed_part, swap(mixed_part, "mlp", 1)), groups
+    )
 
     return (
         outputs,

time: 233 us -> 199 us (0.85)
  Pallas kernels: 103 us -> 88.5 us
  other arithmetic: 10.2 us -> 1.74 us
  waiting for transfers between devices: 52.1 us -> 46.1 us
  local copies, waits for them, and re-layouts: 12.9 us -> 6.92 us
    pallas_call x1, Pallas kernels: 17.2 us -> 9.98 us  [attend_back(): pl.pallas_call(partial(backward_kernel, count=count, groups=groups, scale...]
    ppermute x52, waiting for transfers between devices: 52.1 us -> 46.1 us  [swap(): return lax.ppermute(value, axis, [(i, i ^ bit) for i in range(size)])]
    pallas_call x8 -> x10, Pallas kernels: 60.7 us -> 55 us  [the longest x2 33 us: feed_all(): pl.pallas_call(partial(all_kernel, counts=counts), grid_spec=pltpu.Prefet...]
    ppermute x52, starting transfers between devices: 47.2 us -> 50 us  [swap(): return lax.ppermute(value, axis, [(i, i ^ bit) for i in range(size)])]
    unnamed x125 -> x64, local copies, waits for them, and re-layouts: 4.61 us -> 4.98 us
  transfers between devices with their start and end apart: 53 -> 53, of which waited for: 20 -> 21; matrix products, arithmetic and copies ran while one was open for 6% -> 1% of each run, Pallas kernels for 40% -> 42%
where the time goes in v2:
time: 199 us; the launch traced here: 198 us
  Pallas kernels  88.5 us (44%)
  starting transfers between devices  53.6 us (27%)
  waiting for transfers between devices  46.1 us (23%)
  local copies, waits for them, and re-layouts  6.92 us (3%)
    ppermute x52, starting transfers between devices, swap(): return lax.ppermute(value, axis, [(i, i ^ bit) for i in range(size)])  50 us
    ppermute x52, waiting for transfers between devices, swap(): return lax.ppermute(value, axis, [(i, i ^ bit) for i in range(size)])  46.1 us
    pallas_call x2, Pallas kernels, feed_all(): pl.pallas_call(partial(all_kernel, counts=counts), grid_spec=pltpu.Prefet...  33 us
    pallas_call x1, Pallas kernels, attend_back(): pl.pallas_call(partial(backward_kernel, count=count, groups=groups, scale...  9.98 us
    pallas_call x1, Pallas kernels, attend_all(): pl.pallas_call(partial(all_forward_kernel, groups=groups, scale=1.0 / mat...  8.56 us
    pallas_call x5, Pallas kernels, project_rows(): pl.pallas_call(partial(rows_kernel, count=len(weights)), out_shape=[jax.S...  7.6 us
    pallas_call x1, Pallas kernels, feed_own(): pl.pallas_call(own_kernel, in_specs=[WHOLE] * 3, out_specs=[WHOLE] * 4, o...  5.45 us
    unnamed x64, local copies, waits for them, and re-layouts  4.98 us
  transfers between devices with their start and end apart: 53, of which 21 were waited for; matrix products, arithmetic and copies ran while one was open for 1% of the time, Pallas kernels for 42%

profile of v2, /device:TPU:0, one launch (start us, length us, event | category | flops | bytes accessed | tf_op | source)
XLA Modules:
  0.0 198.4 jit_solution(821239677489686050)
XLA Ops:
  2.2 3.1 %collective-permute-start = (bf16[32,2048]{1,0:T(8,128)(2,1)S(1)}, bf16[32,2048]{1,0:T(8,128)(2,1)S(1)}, u32[]{:S(2)}, u32[]{:S(2)}) collective-permute-start(bf16[32,2048]{1,0:T(8,128)(2,1)S(1)} %constant_dynamic-slice_fusion.4), channel_id=1, source_target_pairs={{0,8},{4,12},{8,0},{12,4},{16,24},{20,28},{24,16},{28,20},{1,9},{5... | collective-permute-start | bytes 393224 | tf_op jit(solution)/shard_map/ppermute | solution.py:40
  5.2 2.6 %collective-permute-start.2 = (bf16[32,2048]{1,0:T(8,128)(2,1)S(1)}, bf16[32,2048]{1,0:T(8,128)(2,1)S(1)}, u32[]{:S(2)}, u32[]{:S(2)}) collective-permute-start(bf16[32,2048]{1,0:T(8,128)(2,1)S(1)} %constant_dynamic-slice_fusion.4), channel_id=1, source_target_pairs={{0,16},{4,20},{8,24},{12,28},{16,0},{20,4},{24,8},{28,12},{1,17},{... | collective-permute-start | bytes 393224 | tf_op jit(solution)/shard_map/ppermute | solution.py:40
  7.8 2.4 %collective-permute-done = bf16[32,2048]{1,0:T(8,128)(2,1)S(1)} collective-permute-done((bf16[32,2048]{1,0:T(8,128)(2,1)S(1)}, bf16[32,2048]{1,0:T(8,128)(2,1)S(1)}, u32[]{:S(2)}, u32[]{:S(2)}) %collective-permute-start) | collective-permute-done | bytes 131104 | tf_op jit(solution)/shard_map/ppermute | solution.py:40
  10.3 1.7 collective-permute-start.1
  12.0 1.5 collective-permute-start.6
  14.1 2.4 %tables.1 = (s32[512,1]{1,0:T(8,128)}, s32[512,1]{1,0:T(8,128)}, s32[512,1]{1,0:T(8,128)}, s32[512,1]{1,0:T(8,128)}, s32[1,1024]{1,0:T(1,128)}, /*index=5*/s32[1,128]{1,0:T(1,128)}, s32[128,1]{1,0:T(8,128)}) custom-call(s32[2]{0:T(128)} %pad_add_fusion.index, s32[1,8]{1,0:T(1,128)} %frames.1, s32[1,8]{1,0:T(1,128)} %texts.1, s32[1,8]{1,0:T(1,128)} %actions.1), custom_call_target="tpu_custom_call" | custom-call | flops 10485 | bytes 10485 | tf_op jit(solution)/shard_map/tables/pallas_call | solution.py:205
  18.2 1.5 collective-permute-start.3
  20.2 1.6 collective-permute-start.7
  23.2 1.6 collective-permute-start.8
  24.8 1.5 collective-permute-start.9
  26.2 3.3 %collective-permute-done.7.refs_4_ = bf16[64,2048]{1,0:T(8,128)(2,1)S(1)} collective-permute-done((bf16[64,2048]{1,0:T(8,128)(2,1)S(1)}, bf16[64,2048]{1,0:T(8,128)(2,1)S(1)}, u32[]{:S(2)}, u32[]{:S(2)}) %collective-permute-start.7) | collective-permute-done | bytes 262176 | tf_op jit(solution)/shard_map/ppermute | solution.py:40
  29.5 1.5 collective-permute-start.10
  31.0 1.4 collective-permute-start.11
  32.5 1.5 collective-permute-start.12
  36.3 2.5 %norm_pieces.1 = bf16[8,8,8,2048]{3,2,1,0:T(8,128)(2,1)S(1)} custom-call(s32[1]{0:T(128)} %bitcast.11.refs_0_, bf16[64,2048]{1,0:T(8,128)(2,1)S(1)} %bitcast.46, bf16[64,2048]{1,0:T(8,128)(2,1)S(1)} %collective-permute-done.6.refs_2_, bf16[64,2048]{1,0:T(8,128)(2,1)S(1)} %pad_maximum_fusion.6.refs_3_, bf16[64,2048]{1,0:T(8,128)(2,1)S(1)} %collective-permute-done.7.refs_4_, ...), custom_call_target="tpu_custom_call" | custom-call | flops 104857 | bytes 41943 | tf_op jit(solution)/shard_map/norm_pieces/pallas_call | solution.py:359
  40.9 1.5 collective-permute-start.14
  42.5 2.3 %project_rows.6 = (bf16[512,512]{1,0:T(8,128)(2,1)S(1)}, bf16[512,512]{1,0:T(8,128)(2,1)S(1)}) custom-call(bf16[512,2048]{1,0:T(8,128)(2,1)S(1)} %bitcast.40, bf16[2048,512]{1,0:T(8,128)(2,1)S(1)} %copy-done.1, bf16[2048,512]{1,0:T(8,128)(2,1)S(1)} %copy-done.2), custom_call_target="tpu_custom_call" | custom-call | flops 21474836 | bytes 20971 | tf_op jit(solution)/shard_map/project_rows/pallas_call | solution.py:233
  44.9 2.3 %project_rows.7 = (bf16[512,512]{1,0:T(8,128)(2,1)S(1)}, bf16[512,512]{1,0:T(8,128)(2,1)S(1)}) custom-call(bf16[512,2048]{1,0:T(8,128)(2,1)S(1)} %collective-permute-done.13.refs_0_.refs_1_, bf16[2048,512]{1,0:T(8,128)(2,1)S(1)} %copy-done.1, bf16[2048,512]{1,0:T(8,128)(2,1)S(1)} %copy-done.2), custom_call_target="tpu_custom_call" | custom-call | flops 21474836 | bytes 20971 | tf_op jit(solution)/shard_map/project_rows/pallas_call | solution.py:233
  47.2 1.9 attend.1.refs_0_
  49.4 2.0 collective-permute-done.15
  52.0 1.6 collective-permute-start.19
  55.1 3.5 %grad_activated.1 = f32[128,2048]{1,0:T(8,128)S(1)} custom-call(bf16[128,2048]{1,0:T(8,128)(2,1)S(1)} %pad_maximum_fusion.3.grad.refs_7_, bf16[2048,2048]{1,0:T(8,128)(2,1)S(1)} %bitcast.36), custom_call_target="tpu_custom_call" | custom-call | flops 10737418 | bytes 83886 | tf_op jit(solution)/shard_map/grad_activated/pallas_call | solution.py:567
  58.6 3.5 %collective-permute-done.17.other = bf16[64,2048]{1,0:T(8,128)(2,1)S(1)} collective-permute-done((bf16[64,2048]{1,0:T(8,128)(2,1)S(1)}, bf16[64,2048]{1,0:T(8,128)(2,1)S(1)}, u32[]{:S(2)}, u32[]{:S(2)}) %collective-permute-start.17) | collective-permute-done | bytes 262176 | tf_op jit(solution)/shard_map/ppermute | solution.py:40
  62.6 1.5 collective-permute-done.18
  64.1 5.4 %feed_own.1 = (bf16[128,2048]{1,0:T(8,128)(2,1)S(1)}, bf16[128,2048]{1,0:T(8,128)(2,1)S(1)}, f32[64,2048]{1,0:T(8,128)S(1)}, bf16[64,2048]{1,0:T(8,128)(2,1)S(1)}) custom-call(bf16[128,2048]{1,0:T(8,128)(2,1)S(1)} %constant_dynamic-update-slice_fusion.lifted.refs_6_, bf16[2048,2048]{1,0:T(8,128)(2,1)S(1)} %bitcast.38, f32[128,2048]{1,0:T(8,128)S(1)} %grad_activated.1), custom_call_target="tpu_custom_call" | custom-call | flops 21474836 | bytes 83886 | tf_op jit(solution)/shard_map/feed_own/pallas_call | solution.py:541
  69.6 2.5 %collective-permute-done.19.refs_6_ = bf16[192,2048]{1,0:T(8,128)(2,1)} collective-permute-done((bf16[192,2048]{1,0:T(8,128)(2,1)S(1)}, bf16[192,2048]{1,0:T(8,128)(2,1)}, u32[]{:S(2)}, u32[]{:S(2)}) %collective-permute-start.19) | collective-permute-done | bytes 786464 | tf_op jit(solution)/shard_map/ppermute | solution.py:40
  72.1 1.5 collective-permute-done.20
  74.9 1.9 collective-permute-start.22
  78.1 1.4 collective-permute-start.24
  79.5 2.0 down_own.1
  82.0 7.7 %collective-permute-done.23 = bf16[32,2048]{1,0:T(8,128)(2,1)S(1)} collective-permute-done((bf16[32,2048]{1,0:T(8,128)(2,1)S(1)}, bf16[32,2048]{1,0:T(8,128)(2,1)S(1)}, u32[]{:S(2)}, u32[]{:S(2)}) %collective-permute-start.23) | collective-permute-done | bytes 131104 | tf_op jit(solution)/shard_map/ppermute | solution.py:40
  93.6 1.6 collective-permute-start.26
  95.2 2.0 %collective-permute-start.27 = (bf16[128,512]{1,0:T(8,128)(2,1)S(1)}, bf16[128,512]{1,0:T(8,128)(2,1)S(1)}, u32[]{:S(2)}, u32[]{:S(2)}) collective-permute-start(bf16[128,512]{1,0:T(8,128)(2,1)S(1)} %product_back.1.refs_0_), channel_id=1, source_target_pairs={{0,8},{4,12},{8,0},{12,4},{16,24},{20,28},{24,16},{28,20},{1,9},{5... | collective-permute-start | bytes 393224 | tf_op jit(solution)/shard_map/ppermute | solution.py:40
  98.4 1.5 collective-permute-start.31
  102.4 8.6 %attend_all.1 = (bf16[512,512]{1,0:T(8,128)(2,1)S(1)}, bf16[512,512]{1,0:T(8,128)(2,1)S(1)}, bf16[4,2560,256]{2,1,0:T(8,128)(2,1)S(1)}) custom-call(bf16[512,512]{1,0:T(8,128)(2,1)S(1)} %project_rows.8.refs_0_.refs_8_, bf16[512,512]{1,0:T(8,128)(2,1)S(1)} %project_rows.9.refs_1_.refs_9_, bf16[512,512]{1,0:T(8,128)(2,1)S(1)} %get-tuple-element.145.key_a.refs_2_.refs_10_, ...), custom_call_target="tpu_custom_call" | custom-call | flops 21474836 | bytes 41943 | tf_op jit(solution)/shard_map/attend_all/pallas_call | solution.py:895
  112.3 1.5 collective-permute-start.35
  113.9 1.4 collective-permute-start.34
  115.8 7.9 %collective-permute-done.36 = bf16[96,2048]{1,0:T(8,128)(2,1)S(1)} collective-permute-done((bf16[96,2048]{1,0:T(8,128)(2,1)S(1)}, bf16[96,2048]{1,0:T(8,128)(2,1)S(1)}, u32[]{:S(2)}, u32[]{:S(2)}) %collective-permute-start.36) | collective-permute-done | bytes 393248 | tf_op jit(solution)/shard_map/ppermute | solution.py:40
  124.2 1.5 collective-permute-start.32
  125.7 14.9 %feed_all.2 = (f32[256,2048]{1,0:T(8,128)}, f32[2048,256]{1,0:T(8,128)}) custom-call(s32[1]{0:T(128)} %bitcast.10.index, bf16[192,2048]{1,0:T(8,128)(2,1)S(1)} %constant_dynamic-update-slice_fusion.5.refs_0_, bf16[192,2048]{1,0:T(8,128)(2,1)S(1)} %collective-permute-done.38.refs_1_, bf16[192,2048]{1,0:T(8,128)(2,1)S(1)} %pad_maximum_fusion.refs_2_, ...), custom_call_target="tpu_custom_call" | custom-call | flops 72477576 | bytes 199229 | tf_op jit(solution)/shard_map/feed_all/pallas_call | solution.py:661
  140.7 1.4 collective-permute-start.40
  142.1 10.0 %attend_back.1 = (bf16[512,512]{1,0:T(8,128)(2,1)S(1)}, bf16[512,512]{1,0:T(8,128)(2,1)S(1)}, bf16[512,512]{1,0:T(8,128)(2,1)S(1)}, bf16[512,512]{1,0:T(8,128)(2...) custom-call(bf16[128,512]{1,0:T(8,128)(2,1)S(1)} %product_back.1.ref, ...), custom_call_target="tpu_custom_call" | custom-call | flops 42949672 | bytes 136314 | tf_op jit(solution)/shard_map/attend_back/pallas_call | solution.py:1002
  152.2 2.1 %product_halves.3 = (f32[64,2048]{1,0:T(8,128)S(1)}, bf16[64,2048]{1,0:T(8,128)(2,1)S(1)}) custom-call(bf16[128,512]{1,0:T(8,128)(2,1)S(1)} %get-tuple-element.208.refs_0_, bf16[128,512]{1,0:T(8,128)(2,1)S(1)} %get-tuple-element.209.refs_1_, bf16[128,512]{1,0:T(8,128)(2,1)S(1)} %get-tuple-element.210.refs_2_, bf16[2048,512]{1,0:T(8,128)(2,1)S(1)} %copy-done, ...), custom_call_target="tpu_custom_call" | custom-call | flops 8053063 | bytes 62914 | tf_op jit(solution)/shard_map/product_halves/pallas_call | solution.py:269
  154.4 1.5 collective-permute-done.41
  156.7 2.8 %project.1 = (f32[256,512]{1,0:T(8,128)}, f32[256,512]{1,0:T(8,128)}, f32[256,512]{1,0:T(8,128)}, f32[3,256]{1,0:T(4,128)S(1)}) custom-call(s32[1]{0:T(128)} %bitcast.10.index, bf16[512,2048]{1,0:T(8,128)(2,1)S(1)} %bitcast.42, bf16[512,2048]{1,0:T(8,128)(2,1)S(1)} %collective-permute-done.13.refs_0_.refs_1_, ...), custom_call_target="tpu_custom_call" | custom-call | flops 16106127 | bytes 47185 | tf_op jit(solution)/shard_map/project/pallas_call | solution.py:716
  160.6 3.7 %collective-permute-done.42.other = bf16[64,2048]{1,0:T(8,128)(2,1)S(1)} collective-permute-done((bf16[64,2048]{1,0:T(8,128)(2,1)S(1)}, bf16[64,2048]{1,0:T(8,128)(2,1)S(1)}, u32[]{:S(2)}, u32[]{:S(2)}) %collective-permute-start.42) | collective-permute-done | bytes 262176 | tf_op jit(solution)/shard_map/ppermute | solution.py:40
  165.6 3.7 %all-to-all-start = ((bf16[8,72,256]{2,1,0:T(8,128)(2,1)}), bf16[8,72,256]{2,1,0:T(8,128)(2,1)S(1)}, u32[]{:S(2)}, u32[]{:S(2)}) async-start(bf16[8,72,256]{2,1,0:T(8,128)(2,1)} %copy-done.12), calls=%async_computation | async-start | bytes 589824 | tf_op jit(solution)/shard_map/all_to_all | solution.py:1137
  174.1 18.1 %feed_all.3 = (f32[256,2048]{1,0:T(8,128)}, f32[2048,256]{1,0:T(8,128)}) custom-call(s32[1]{0:T(128)} %bitcast.10.index, bf16[64,2048]{1,0:T(8,128)(2,1)S(1)} %copy-done.16, bf16[64,2048]{1,0:T(8,128)(2,1)S(1)} %collective-permute-done.47.refs_1_, bf16[192,2048]{1,0:T(8,128)(2,1)S(1)} %pad_maximum_fusion.1.refs_2_, ...), custom_call_target="tpu_custom_call" | custom-call | flops 96636768 | bytes 209715 | tf_op jit(solution)/shard_map/feed_all/pallas_call | solution.py:661
  (178 shorter events, 40.0 us)
Async XLA Ops:
  2.2 8.1 %collective-permute-start = (bf16[32,2048]{1,0:T(8,128)(2,1)S(1)}, bf16[32,2048]{1,0:T(8,128)(2,1)S(1)}, u32[]{:S(2)}, u32[]{:S(2)}) collective-permute-start(bf16[32,2048]{1,0:T(8,128)(2,1)S(1)} %constant_dynamic-slice_fusion.4), channel_id=1, source_target_pairs={{0,8},{4,12},{8,0},{12,4},{16,24},{20,28},{24,16},{28,20},{1,9},{5... | collective-permute-start | bytes 393224 | tf_op jit(solution)/shard_map/ppermute | solution.py:40
  5.2 12.9 %collective-permute-start.2 = (bf16[32,2048]{1,0:T(8,128)(2,1)S(1)}, bf16[32,2048]{1,0:T(8,128)(2,1)S(1)}, u32[]{:S(2)}, u32[]{:S(2)}) collective-permute-start(bf16[32,2048]{1,0:T(8,128)(2,1)S(1)} %constant_dynamic-slice_fusion.4), channel_id=1, source_target_pairs={{0,16},{4,20},{8,24},{12,28},{16,0},{20,4},{24,8},{28,12},{1,17},{... | collective-permute-start | bytes 393224 | tf_op jit(solution)/shard_map/ppermute | solution.py:40
  7.8 11.8 %collective-permute-start.4 = (bf16[32,2048]{1,0:T(8,128)(2,1)S(1)}, bf16[32,2048]{1,0:T(8,128)(2,1)S(1)}, u32[]{:S(2)}, u32[]{:S(2)}) collective-permute-start(bf16[32,2048]{1,0:T(8,128)(2,1)S(1)} %constant_dynamic-slice_fusion.4), channel_id=1, source_target_pairs={{0,24},{4,28},{8,16},{12,20},{16,8},{20,12},{24,0},{28,4},{1,25},{... | collective-permute-start | bytes 393224 | tf_op jit(solution)/shard_map/ppermute | solution.py:40
  10.3 9.9 %collective-permute-start.1 = (bf16[32,2048]{1,0:T(8,128)(2,1)S(1)}, bf16[32,2048]{1,0:T(8,128)(2,1)S(1)}, u32[]{:S(2)}, u32[]{:S(2)}) collective-permute-start(bf16[32,2048]{1,0:T(8,128)(2,1)S(1)} %collective-permute-done), channel_id=1, source_target_pairs={{0,2},{1,3},{2,0},{3,1},{4,6},{5,7},{6,4},{7,5},{8,10},{9,11},{10,... | collective-permute-start | bytes 393224 | tf_op jit(solution)/shard_map/ppermute | solution.py:40
  12.0 20.5 %collective-permute-start.6 = (bf16[64,2048]{1,0:T(8,128)(2,1)S(1)}, bf16[64,2048]{1,0:T(8,128)(2,1)S(1)}, u32[]{:S(2)}, u32[]{:S(2)}) collective-permute-start(bf16[64,2048]{1,0:T(8,128)(2,1)S(1)} %bitcast.44), channel_id=1, source_target_pairs={{0,4},{4,0},{8,12},{12,8},{16,20},{20,16},{24,28},{28,24},{1,5},{5... | collective-permute-start | bytes 786440 | tf_op jit(solution)/shard_map/ppermute | solution.py:40
  18.2 5.0 %collective-permute-start.3 = (bf16[32,2048]{1,0:T(8,128)(2,1)S(1)}, bf16[32,2048]{1,0:T(8,128)(2,1)S(1)}, u32[]{:S(2)}, u32[]{:S(2)}) collective-permute-start(bf16[32,2048]{1,0:T(8,128)(2,1)S(1)} %collective-permute-done.2), channel_id=1, source_target_pairs={{0,2},{1,3},{2,0},{3,1},{4,6},{5,7},{6,4},{7,5},{8,10},{9,11},{10,... | collective-permute-start | bytes 393224 | tf_op jit(solution)/shard_map/ppermute | solution.py:40
  19.7 5.1 %collective-permute-start.5 = (bf16[32,2048]{1,0:T(8,128)(2,1)S(1)}, bf16[32,2048]{1,0:T(8,128)(2,1)S(1)}, u32[]{:S(2)}, u32[]{:S(2)}) collective-permute-start(bf16[32,2048]{1,0:T(8,128)(2,1)S(1)} %collective-permute-done.4), channel_id=1, source_target_pairs={{0,2},{1,3},{2,0},{3,1},{4,6},{5,7},{6,4},{7,5},{8,10},{9,11},{10,... | collective-permute-start | bytes 393224 | tf_op jit(solution)/shard_map/ppermute | solution.py:40
  20.2 9.3 %collective-permute-start.7 = (bf16[64,2048]{1,0:T(8,128)(2,1)S(1)}, bf16[64,2048]{1,0:T(8,128)(2,1)S(1)}, u32[]{:S(2)}, u32[]{:S(2)}) collective-permute-start(bf16[64,2048]{1,0:T(8,128)(2,1)S(1)} %pad_maximum_fusion.6.refs_3_), channel_id=1, source_target_pairs={{0,4},{4,0},{8,12},{12,8},{16,20},{20,16},{24,28},{28,24},{1,5},{5... | collective-permute-start | bytes 786440 | tf_op jit(solution)/shard_map/ppermute | solution.py:40
  23.2 11.9 %collective-permute-start.8 = (bf16[64,2048]{1,0:T(8,128)(2,1)S(1)}, bf16[64,2048]{1,0:T(8,128)(2,1)S(1)}, u32[]{:S(2)}, u32[]{:S(2)}) collective-permute-start(bf16[64,2048]{1,0:T(8,128)(2,1)S(1)} %pad_maximum_fusion.7.refs_5_), channel_id=1, source_target_pairs={{0,4},{4,0},{8,12},{12,8},{16,20},{20,16},{24,28},{28,24},{1,5},{5... | collective-permute-start | bytes 786440 | tf_op jit(solution)/shard_map/ppermute | solution.py:40
  24.8 11.5 %collective-permute-start.9 = (bf16[64,2048]{1,0:T(8,128)(2,1)S(1)}, bf16[64,2048]{1,0:T(8,128)(2,1)S(1)}, u32[]{:S(2)}, u32[]{:S(2)}) collective-permute-start(bf16[64,2048]{1,0:T(8,128)(2,1)S(1)} %pad_maximum_fusion.8.refs_7_), channel_id=1, source_target_pairs={{0,4},{4,0},{8,12},{12,8},{16,20},{20,16},{24,28},{28,24},{1,5},{5... | collective-permute-start | bytes 786440 | tf_op jit(solution)/shard_map/ppermute | solution.py:40
  29.5 9.3 %collective-permute-start.10 = (bf16[32,2048]{1,0:T(8,128)(2,1)S(1)}, bf16[32,2048]{1,0:T(8,128)(2,1)S(1)}, u32[]{:S(2)}, u32[]{:S(2)}) collective-permute-start(bf16[32,2048]{1,0:T(8,128)(2,1)S(1)} %constant_dynamic-slice_fusion.2), channel_id=1, source_target_pairs={{0,8},{4,12},{8,0},{12,4},{16,24},{20,28},{24,16},{28,20},{1,9},{5... | collective-permute-start | bytes 393224 | tf_op jit(solution)/shard_map/ppermute | solution.py:40
  31.0 8.7 %collective-permute-start.11 = (bf16[32,2048]{1,0:T(8,128)(2,1)S(1)}, bf16[32,2048]{1,0:T(8,128)(2,1)S(1)}, u32[]{:S(2)}, u32[]{:S(2)}) collective-permute-start(bf16[32,2048]{1,0:T(8,128)(2,1)S(1)} %constant_dynamic-slice_fusion.2), channel_id=1, source_target_pairs={{0,16},{4,20},{8,24},{12,28},{16,0},{20,4},{24,8},{28,12},{1,17},{... | collective-permute-start | bytes 393224 | tf_op jit(solution)/shard_map/ppermute | solution.py:40
  32.5 7.2 %collective-permute-start.12 = (bf16[32,2048]{1,0:T(8,128)(2,1)S(1)}, bf16[32,2048]{1,0:T(8,128)(2,1)S(1)}, u32[]{:S(2)}, u32[]{:S(2)}) collective-permute-start(bf16[32,2048]{1,0:T(8,128)(2,1)S(1)} %constant_dynamic-slice_fusion.2), channel_id=1, source_target_pairs={{0,24},{4,28},{8,16},{12,20},{16,8},{20,12},{24,0},{28,4},{1,25},{... | collective-permute-start | bytes 393224 | tf_op jit(solution)/shard_map/ppermute | solution.py:40
  39.7 5.1 %collective-permute-start.13 = (bf16[512,2048]{1,0:T(8,128)(2,1)S(1)}, bf16[512,2048]{1,0:T(8,128)(2,1)S(1)}, u32[]{:S(2)}, u32[]{:S(2)}) collective-permute-start(bf16[512,2048]{1,0:T(8,128)(2,1)S(1)} %bitcast.39), channel_id=1, source_target_pairs={{0,1},{1,0},{2,3},{3,2},{4,5},{5,4},{6,7},{7,6},{8,9},{9,8},{10,11... | collective-permute-start | bytes 6291464 | tf_op jit(solution)/shard_map/ppermute | solution.py:40
  39.8 11.6 %collective-permute-start.15 = (bf16[96,2048]{1,0:T(8,128)(2,1)S(1)}, bf16[96,2048]{1,0:T(8,128)(2,1)S(1)}, u32[]{:S(2)}, u32[]{:S(2)}) collective-permute-start(bf16[96,2048]{1,0:T(8,128)(2,1)S(1)} %pad_maximum_fusion.5), channel_id=1, source_target_pairs={{0,2},{1,3},{2,0},{3,1},{4,6},{5,7},{6,4},{7,5},{8,10},{9,11},{10,... | collective-permute-start | bytes 1179656 | tf_op jit(solution)/shard_map/ppermute | solution.py:40
  40.9 8.4 %collective-permute-start.14 = (bf16[64,2048]{1,0:T(8,128)(2,1)S(1)}, bf16[64,2048]{1,0:T(8,128)(2,1)S(1)}, u32[]{:S(2)}, u32[]{:S(2)}) collective-permute-start(bf16[64,2048]{1,0:T(8,128)(2,1)S(1)} %bitcast.50), channel_id=1, source_target_pairs={{0,4},{4,0},{8,12},{12,8},{16,20},{20,16},{24,28},{28,24},{1,5},{5... | collective-permute-start | bytes 786440 | tf_op jit(solution)/shard_map/ppermute | solution.py:40
  51.9 1.7 collective-permute-start.16
  52.0 20.1 %collective-permute-start.19 = (bf16[192,2048]{1,0:T(8,128)(2,1)S(1)}, bf16[192,2048]{1,0:T(8,128)(2,1)}, u32[]{:S(2)}, u32[]{:S(2)}) collective-permute-start(bf16[192,2048]{1,0:T(8,128)(2,1)S(1)} %pad_maximum_fusion.refs_2_), channel_id=1, source_target_pairs={{0,4},{4,0},{8,12},{12,8},{16,20},{20,16},{24,28},{28,24},{1,5},{5... | collective-permute-start | bytes 2359304 | tf_op jit(solution)/shard_map/ppermute | solution.py:40
  53.7 8.4 %collective-permute-start.17 = (bf16[64,2048]{1,0:T(8,128)(2,1)S(1)}, bf16[64,2048]{1,0:T(8,128)(2,1)S(1)}, u32[]{:S(2)}, u32[]{:S(2)}) collective-permute-start(bf16[64,2048]{1,0:T(8,128)(2,1)S(1)} %add_convert_fusion.3.low), channel_id=1, source_target_pairs={{0,2},{1,3},{2,0},{3,1},{4,6},{5,7},{6,4},{7,5},{8,10},{9,11},{10,... | collective-permute-start | bytes 786440 | tf_op jit(solution)/shard_map/ppermute | solution.py:40
  73.7 16.0 %collective-permute-start.21 = (bf16[64,2048]{1,0:T(8,128)(2,1)S(1)}, bf16[64,2048]{1,0:T(8,128)(2,1)S(1)}, u32[]{:S(2)}, u32[]{:S(2)}) collective-permute-start(bf16[64,2048]{1,0:T(8,128)(2,1)S(1)} %add_convert_fusion.2.low), channel_id=1, source_target_pairs={{0,2},{1,3},{2,0},{3,1},{4,6},{5,7},{6,4},{7,5},{8,10},{9,11},{10,... | collective-permute-start | bytes 786440 | tf_op jit(solution)/shard_map/ppermute | solution.py:40
  74.9 7.1 %collective-permute-start.22 = (bf16[32,2048]{1,0:T(8,128)(2,1)S(1)}, bf16[32,2048]{1,0:T(8,128)(2,1)S(1)}, u32[]{:S(2)}, u32[]{:S(2)}) collective-permute-start(bf16[32,2048]{1,0:T(8,128)(2,1)S(1)} %constant_dynamic-slice_fusion), channel_id=1, source_target_pairs={{0,8},{4,12},{8,0},{12,4},{16,24},{20,28},{24,16},{28,20},{1,9},{5... | collective-permute-start | bytes 393224 | tf_op jit(solution)/shard_map/ppermute | solution.py:40
  76.8 12.9 %collective-permute-start.23 = (bf16[32,2048]{1,0:T(8,128)(2,1)S(1)}, bf16[32,2048]{1,0:T(8,128)(2,1)S(1)}, u32[]{:S(2)}, u32[]{:S(2)}) collective-permute-start(bf16[32,2048]{1,0:T(8,128)(2,1)S(1)} %constant_dynamic-slice_fusion), channel_id=1, source_target_pairs={{0,16},{4,20},{8,24},{12,28},{16,0},{20,4},{24,8},{28,12},{1,17},{... | collective-permute-start | bytes 393224 | tf_op jit(solution)/shard_map/ppermute | solution.py:40
  78.1 11.6 %collective-permute-start.24 = (bf16[32,2048]{1,0:T(8,128)(2,1)S(1)}, bf16[32,2048]{1,0:T(8,128)(2,1)S(1)}, u32[]{:S(2)}, u32[]{:S(2)}) collective-permute-start(bf16[32,2048]{1,0:T(8,128)(2,1)S(1)} %constant_dynamic-slice_fusion), channel_id=1, source_target_pairs={{0,24},{4,28},{8,16},{12,20},{16,8},{20,12},{24,0},{28,4},{1,25},{... | collective-permute-start | bytes 393224 | tf_op jit(solution)/shard_map/ppermute | solution.py:40
  91.2 19.7 %collective-permute-start.37 = (bf16[96,2048]{1,0:T(8,128)(2,1)S(1)}, bf16[96,2048]{1,0:T(8,128)(2,1)S(1)}, u32[]{:S(2)}, u32[]{:S(2)}) collective-permute-start(bf16[96,2048]{1,0:T(8,128)(2,1)S(1)} %get-tuple-element.259), channel_id=1, source_target_pairs={{0,2},{1,3},{2,0},{3,1},{4,6},{5,7},{6,4},{7,5},{8,10},{9,11},{10,... | collective-permute-start | bytes 1179656 | tf_op jit(solution)/shard_map/ppermute | solution.py:40
  93.6 17.5 %collective-permute-start.26 = (bf16[128,512]{1,0:T(8,128)(2,1)S(1)}, bf16[128,512]{1,0:T(8,128)(2,1)S(1)}, u32[]{:S(2)}, u32[]{:S(2)}) collective-permute-start(bf16[128,512]{1,0:T(8,128)(2,1)S(1)} %product_back.1.refs_0_), channel_id=1, source_target_pairs={{0,4},{4,0},{8,12},{12,8},{16,20},{20,16},{24,28},{28,24},{1,5},{5... | collective-permute-start | bytes 393224 | tf_op jit(solution)/shard_map/ppermute | solution.py:40
  95.2 16.4 %collective-permute-start.27 = (bf16[128,512]{1,0:T(8,128)(2,1)S(1)}, bf16[128,512]{1,0:T(8,128)(2,1)S(1)}, u32[]{:S(2)}, u32[]{:S(2)}) collective-permute-start(bf16[128,512]{1,0:T(8,128)(2,1)S(1)} %product_back.1.refs_0_), channel_id=1, source_target_pairs={{0,8},{4,12},{8,0},{12,4},{16,24},{20,28},{24,16},{28,20},{1,9},{5... | collective-permute-start | bytes 393224 | tf_op jit(solution)/shard_map/ppermute | solution.py:40
  97.2 14.4 %collective-permute-start.29 = (bf16[128,512]{1,0:T(8,128)(2,1)S(1)}, bf16[128,512]{1,0:T(8,128)(2,1)S(1)}, u32[]{:S(2)}, u32[]{:S(2)}) collective-permute-start(bf16[128,512]{1,0:T(8,128)(2,1)S(1)} %product_back.1.refs_0_), channel_id=1, source_target_pairs={{0,16},{4,20},{8,24},{12,28},{16,0},{20,4},{24,8},{28,12},{1,17},{... | collective-permute-start | bytes 393224 | tf_op jit(solution)/shard_map/ppermute | solution.py:40
  98.4 13.1 %collective-permute-start.31 = (bf16[128,512]{1,0:T(8,128)(2,1)S(1)}, bf16[128,512]{1,0:T(8,128)(2,1)S(1)}, u32[]{:S(2)}, u32[]{:S(2)}) collective-permute-start(bf16[128,512]{1,0:T(8,128)(2,1)S(1)} %product_back.1.refs_0_), channel_id=1, source_target_pairs={{0,24},{4,28},{8,16},{12,20},{16,8},{20,12},{24,0},{28,4},{1,25},{... | collective-permute-start | bytes 393224 | tf_op jit(solution)/shard_map/ppermute | solution.py:40
  111.0 4.3 %collective-permute-start.39 = (bf16[192,2048]{1,0:T(8,128)(2,1)S(1)}, bf16[192,2048]{1,0:T(8,128)(2,1)S(1)}, u32[]{:S(2)}, u32[]{:S(2)}) collective-permute-start(bf16[192,2048]{1,0:T(8,128)(2,1)S(1)} %pad_maximum_fusion.refs_2_), channel_id=1, source_target_pairs={{0,1},{1,0},{2,3},{3,2},{4,5},{5,4},{6,7},{7,6},{8,9},{9,8},{10,11... | collective-permute-start | bytes 2359304 | tf_op jit(solution)/shard_map/ppermute | solution.py:40
  111.1 2.7 %collective-permute-start.33 = (bf16[64,2048]{1,0:T(8,128)(2,1)S(1)}, bf16[64,2048]{1,0:T(8,128)(2,1)S(1)}, u32[]{:S(2)}, u32[]{:S(2)}) collective-permute-start(bf16[64,2048]{1,0:T(8,128)(2,1)S(1)} %get-tuple-element.177), channel_id=1, source_target_pairs={{0,1},{1,0},{2,3},{3,2},{4,5},{5,4},{6,7},{7,6},{8,9},{9,8},{10,11... | collective-permute-start | bytes 786440 | tf_op jit(solution)/shard_map/ppermute | solution.py:40
  111.6 12.6 %collective-permute-start.38 = (bf16[192,2048]{1,0:T(8,128)(2,1)S(1)}, bf16[192,2048]{1,0:T(8,128)(2,1)S(1)}, u32[]{:S(2)}, u32[]{:S(2)}) collective-permute-start(bf16[192,2048]{1,0:T(8,128)(2,1)S(1)} %constant_dynamic-update-slice_fusion.5.refs_0_), channel_id=1, source_target_pairs={{0,1},{1,0},{2,3},{3,2},{4,5},{5,4},{6,7},{7,6},{8,9},{9,8},{10,11... | collective-permute-start | bytes 2359304 | tf_op jit(solution)/shard_map/ppermute | solution.py:40
  111.8 11.9 %collective-permute-start.36 = (bf16[96,2048]{1,0:T(8,128)(2,1)S(1)}, bf16[96,2048]{1,0:T(8,128)(2,1)S(1)}, u32[]{:S(2)}, u32[]{:S(2)}) collective-permute-start(bf16[96,2048]{1,0:T(8,128)(2,1)S(1)} %get-tuple-element.259), channel_id=1, source_target_pairs={{0,4},{4,0},{8,12},{12,8},{16,20},{20,16},{24,28},{28,24},{1,5},{5... | collective-permute-start | bytes 1179656 | tf_op jit(solution)/shard_map/ppermute | solution.py:40
  112.3 28.3 %collective-permute-start.35 = (bf16[64,2048]{1,0:T(8,128)(2,1)S(1)}, bf16[64,2048]{1,0:T(8,128)(2,1)S(1)}, u32[]{:S(2)}, u32[]{:S(2)}) collective-permute-start(bf16[64,2048]{1,0:T(8,128)(2,1)S(1)} %get-tuple-element.178), channel_id=1, source_target_pairs={{0,4},{4,0},{8,12},{12,8},{16,20},{20,16},{24,28},{28,24},{1,5},{5... | collective-permute-start | bytes 786440 | tf_op jit(solution)/shard_map/ppermute | solution.py:40
  113.9 26.8 %collective-permute-start.34 = (bf16[64,2048]{1,0:T(8,128)(2,1)S(1)}, bf16[64,2048]{1,0:T(8,128)(2,1)S(1)}, u32[]{:S(2)}, u32[]{:S(2)}) collective-permute-start(bf16[64,2048]{1,0:T(8,128)(2,1)S(1)} %add_convert_fusion.1.low), channel_id=1, source_target_pairs={{0,2},{1,3},{2,0},{3,1},{4,6},{5,7},{6,4},{7,5},{8,10},{9,11},{10,... | collective-permute-start | bytes 786440 | tf_op jit(solution)/shard_map/ppermute | solution.py:40
  115.3 25.3 %collective-permute-start.28 = (bf16[128,512]{1,0:T(8,128)(2,1)S(1)}, bf16[128,512]{1,0:T(8,128)(2,1)S(1)}, u32[]{:S(2)}, u32[]{:S(2)}) collective-permute-start(bf16[128,512]{1,0:T(8,128)(2,1)S(1)} %collective-permute-done.27.refs_2_), channel_id=1, source_target_pairs={{0,4},{4,0},{8,12},{12,8},{16,20},{20,16},{24,28},{28,24},{1,5},{5... | collective-permute-start | bytes 393224 | tf_op jit(solution)/shard_map/ppermute | solution.py:40
  123.7 16.9 %collective-permute-start.30 = (bf16[128,512]{1,0:T(8,128)(2,1)S(1)}, bf16[128,512]{1,0:T(8,128)(2,1)S(1)}, u32[]{:S(2)}, u32[]{:S(2)}) collective-permute-start(bf16[128,512]{1,0:T(8,128)(2,1)S(1)} %collective-permute-done.29.refs_4_), channel_id=1, source_target_pairs={{0,4},{4,0},{8,12},{12,8},{16,20},{20,16},{24,28},{28,24},{1,5},{5... | collective-permute-start | bytes 393224 | tf_op jit(solution)/shard_map/ppermute | solution.py:40
  124.2 16.4 %collective-permute-start.32 = (bf16[128,512]{1,0:T(8,128)(2,1)S(1)}, bf16[128,512]{1,0:T(8,128)(2,1)S(1)}, u32[]{:S(2)}, u32[]{:S(2)}) collective-permute-start(bf16[128,512]{1,0:T(8,128)(2,1)S(1)} %collective-permute-done.31.refs_6_), channel_id=1, source_target_pairs={{0,4},{4,0},{8,12},{12,8},{16,20},{20,16},{24,28},{28,24},{1,5},{5... | collective-permute-start | bytes 393224 | tf_op jit(solution)/shard_map/ppermute | solution.py:40
  140.7 11.4 %collective-permute-start.40 = (bf16[96,2048]{1,0:T(8,128)(2,1)S(1)}, bf16[96,2048]{1,0:T(8,128)(2,1)S(1)}, u32[]{:S(2)}, u32[]{:S(2)}) collective-permute-start(bf16[96,2048]{1,0:T(8,128)(2,1)S(1)} %collective-permute-done.36), channel_id=1, source_target_pairs={{0,2},{1,3},{2,0},{3,1},{4,6},{5,7},{6,4},{7,5},{8,10},{9,11},{10,... | collective-permute-start | bytes 1179656 | tf_op jit(solution)/shard_map/ppermute | solution.py:40
  156.0 8.4 %collective-permute-start.42 = (bf16[64,2048]{1,0:T(8,128)(2,1)S(1)}, bf16[64,2048]{1,0:T(8,128)(2,1)S(1)}, u32[]{:S(2)}, u32[]{:S(2)}) collective-permute-start(bf16[64,2048]{1,0:T(8,128)(2,1)S(1)} %add_convert_fusion.low), channel_id=1, source_target_pairs={{0,2},{1,3},{2,0},{3,1},{4,6},{5,7},{6,4},{7,5},{8,10},{9,11},{10,... | collective-permute-start | bytes 786440 | tf_op jit(solution)/shard_map/ppermute | solution.py:40
  165.1 8.6 %collective-permute-start.48 = (bf16[192,2048]{1,0:T(8,128)(2,1)S(1)}, bf16[192,2048]{1,0:T(8,128)(2,1)}, u32[]{:S(2)}, u32[]{:S(2)}) collective-permute-start(bf16[192,2048]{1,0:T(8,128)(2,1)S(1)} %pad_maximum_fusion.1.refs_2_), channel_id=1, source_target_pairs={{0,1},{1,0},{2,3},{3,2},{4,5},{5,4},{6,7},{7,6},{8,9},{9,8},{10,11... | collective-permute-start | bytes 2359304 | tf_op jit(solution)/shard_map/ppermute | solution.py:40
  165.1 9.0 %collective-permute-start.50 = (bf16[192,2048]{1,0:T(8,128)(2,1)}, bf16[192,2048]{1,0:T(8,128)(2,1)}, u32[]{:S(2)}, u32[]{:S(2)}) collective-permute-start(bf16[192,2048]{1,0:T(8,128)(2,1)} %collective-permute-done.19.refs_6_), channel_id=1, source_target_pairs={{0,1},{1,0},{2,3},{3,2},{4,5},{5,4},{6,7},{7,6},{8,9},{9,8},{10,11... | collective-permute-start | bytes 2359304 | tf_op jit(solution)/shard_map/ppermute | solution.py:40
  165.6 26.6 %all-to-all-start = ((bf16[8,72,256]{2,1,0:T(8,128)(2,1)}), bf16[8,72,256]{2,1,0:T(8,128)(2,1)S(1)}, u32[]{:S(2)}, u32[]{:S(2)}) async-start(bf16[8,72,256]{2,1,0:T(8,128)(2,1)} %copy-done.12), calls=%async_computation | async-start | bytes 589824 | tf_op jit(solution)/shard_map/all_to_all | solution.py:1137
  169.2 4.4 %collective-permute-start.47 = (bf16[64,2048]{1,0:T(8,128)(2,1)}, bf16[64,2048]{1,0:T(8,128)(2,1)S(1)}, u32[]{:S(2)}, u32[]{:S(2)}) collective-permute-start(bf16[64,2048]{1,0:T(8,128)(2,1)} %copy-done.15), channel_id=1, source_target_pairs={{0,1},{1,0},{2,3},{3,2},{4,5},{5,4},{6,7},{7,6},{8,9},{9,8},{10,11... | collective-permute-start | bytes 786440 | tf_op jit(solution)/shard_map/ppermute | solution.py:40
  169.2 4.8 %collective-permute-start.49 = (bf16[64,2048]{1,0:T(8,128)(2,1)}, bf16[64,2048]{1,0:T(8,128)(2,1)S(1)}, u32[]{:S(2)}, u32[]{:S(2)}) collective-permute-start(bf16[64,2048]{1,0:T(8,128)(2,1)} %copy-done.13), channel_id=1, source_target_pairs={{0,1},{1,0},{2,3},{3,2},{4,5},{5,4},{6,7},{7,6},{8,9},{9,8},{10,11... | collective-permute-start | bytes 786440 | tf_op jit(solution)/shard_map/ppermute | solution.py:40
  192.2 4.9 %collective-permute-start.51 = (bf16[8,72,256]{2,1,0:T(8,128)(2,1)S(1)}, bf16[8,72,256]{2,1,0:T(8,128)(2,1)S(1)}, u32[]{:S(2)}, u32[]{:S(2)}) collective-permute-start(bf16[8,72,256]{2,1,0:T(8,128)(2,1)S(1)} %all-to-all-done.came_a), channel_id=1, source_target_pairs={{0,1},{1,0},{2,3},{3,2},{4,5},{5,4},{6,7},{7,6},{8,9},{9,8},{10,11... | collective-permute-start | bytes 884744 | tf_op jit(solution)/shard_map/ppermute | solution.py:40
  192.4 1.9 collective-permute-start.45
  192.8 2.3 %collective-permute-start.44 = (bf16[64,2048]{1,0:T(8,128)(2,1)S(1)}, bf16[64,2048]{1,0:T(8,128)(2,1)S(1)}, u32[]{:S(2)}, u32[]{:S(2)}) collective-permute-start(bf16[64,2048]{1,0:T(8,128)(2,1)S(1)} %finish.1.mine), channel_id=1, source_target_pairs={{0,1},{1,0},{2,3},{3,2},{4,5},{5,4},{6,7},{7,6},{8,9},{9,8},{10,11... | collective-permute-start | bytes 786440 | tf_op jit(solution)/shard_map/ppermute | solution.py:40
  192.9 3.6 %collective-permute-start.46 = (f32[3,256]{1,0:T(4,128)S(1)}, f32[3,256]{1,0:T(4,128)S(1)}, u32[]{:S(2)}, u32[]{:S(2)}) collective-permute-start(f32[3,256]{1,0:T(4,128)S(1)} %add.49), channel_id=1, source_target_pairs={{0,2},{1,3},{2,0},{3,1},{4,6},{5,7},{6,4},{7,5},{8,10},{9,11},{10,... | collective-permute-start | bytes 9224 | tf_op jit(solution)/shard_map/ppermute | solution.py:40
  (35 other events, 212.6 us)

commit v3 on v2

--- a/solution.py
+++ b/solution.py
@@ -602,8 +602,12 @@
     first = pl.program_id(0) == 0
     last_step = pl.num_programs(0) - 1
 
+    tile = hidden_kept.shape[1]
+    at = jnp.minimum(pl.program_id(0), last_step - 1) if up.shape[1] > tile else 0
+    here = pl.ds(pl.multiple_of(at * tile, tile), tile)
+
     def products():
-        return dot(lifted[...], up[...], NN), dot(grad[...], down[...], NT)
+        return dot(lifted[...], up[:, here], NN), dot(grad[...], down[here, :], NT)
 
     def finish_tile(hidden_value, activated_grad):
         value, slope = gelu_parts(hidden_value)
@@ -664,7 +668,11 @@
             num_scalar_prefetch=1,
             grid=(steps + 1,),
             in_specs=[anywhere] * (2 * count)
-            + [pl.BlockSpec((width, tile), wide), pl.BlockSpec((tile, width), deep)]
+            + (
+                [WHOLE] * 2
+                if own
+                else [pl.BlockSpec((width, tile), wide), pl.BlockSpec((tile, width), deep)]
+            )
             + more,
             out_specs=sum_specs,
             scratch_shapes=[pltpu.VMEM((rows, width), bf16)] * 2
@@ -673,7 +681,7 @@
             + [pltpu.SemaphoreType.DMA((2 * count,))],
         ),
         out_shape=[pltpu.HBM((part, hidden), f32), pltpu.HBM((hidden, part), f32)],
-        compiler_params=params(8 + 15 * rows // 640),
+        compiler_params=params((6 if own else 8) + 8 * rows // 512),
         cost_estimate=cost(
             4 * rows * hidden * (width + part),
             4 * width * hidden + 4 * rows * width,
@@ -683,8 +691,7 @@
         index,
         *lifted,
         *grad,
-        in_hbm(up),
-        in_hbm(down),
+        *((up, down) if own else (in_hbm(up), in_hbm(down))),
         *(own or [in_hbm(array) for array in sums]),
     )
 
@@ -853,14 +860,25 @@
 
 def all_forward_kernel(*refs, groups, scale, clip_length, clips):
     query_a, query_b, key_a, key_b, value_a, value_b, place_a, place_b, query_place = refs[:9]
-    attended_a, attended_b, stored = refs[9:]
+    attended_a, attended_b, stored, kept_probs, sems = refs[9:]
     half, width = key_a.shape
+    heads = width // HEAD_DIM
     block = block_of(half)
     pair = 2 * block
     everything = slice(None)
 
+    def copy_of(head):
+        slot = head % 2
+        return pltpu.make_async_copy(kept_probs.at[slot], stored.at[head], sems.at[slot])
+
     def one_head(head, _):
         cut = columns_of(head)
+        slot = head % 2
+
+        @pl.when(head >= 2)
+        def _():
+            copy_of(head - 2).wait()
+
         values_across = take(value_a, value_b, 0, half // block, cut).T
         for index, (seen, free, start) in enumerate(reaches(half, groups)[0]):
             mine = pl.ds(index * block, block)
@@ -876,15 +894,18 @@
             for prob in probabilities(scores, scale):
                 kept = prob.astype(bf16)
                 rows = kept.shape[0]
-                stored[head, pl.ds(start * pair + at, rows), :] = kept
+                kept_probs[slot, pl.ds(start * pair + at, rows), :] = kept
                 result += dot(values_across[:, at : at + rows], kept, NN)
                 at += rows
             result = result.T.astype(bf16)
             attended_a[mine, cut] = result[:block]
             attended_b[mine, cut] = result[block:]
+        copy_of(head).start()
         return 0
 
-    lax.fori_loop(0, width // HEAD_DIM, one_head, 0)
+    lax.fori_loop(0, heads, one_head, 0)
+    for head in range(max(0, heads - 2), heads):
+        copy_of(head).wait()
 
 
 def attend_all(queries, keys, values, places, query_place, groups, clip_length, clips):
@@ -901,10 +922,15 @@
             clips=clips,
         ),
         in_specs=[pl.BlockSpec(memory_space=pltpu.VMEM)] * 9,
-        out_specs=[pl.BlockSpec(memory_space=pltpu.VMEM)] * 3,
+        out_specs=[pl.BlockSpec(memory_space=pltpu.VMEM)] * 2
+        + [pl.BlockSpec(memory_space=pl.ANY)],
         out_shape=[jax.ShapeDtypeStruct((half, width), bf16)] * 2
-        + [jax.ShapeDtypeStruct((heads, deep, pair), bf16)],
-        compiler_params=params(max(8, half * half // 2**15)),
+        + [pltpu.HBM((heads, deep, pair), bf16)],
+        scratch_shapes=[
+            pltpu.VMEM((2, deep, pair), bf16),
+            pltpu.SemaphoreType.DMA((2,)),
+        ],
+        compiler_params=params(max(10, half * half // 2**14)),
         cost_estimate=cost(16 * half * half * width, 16 * half * width, 4 * half * half * heads),
         name="attend_all",
     )(*queries, *keys, *values, *places, query_place)
@@ -1085,7 +1111,10 @@
     grad_inner += gather_inner(grad_far)
     low, other = pair_mlp(mine, other)
     own_activated_grad = grad_activated(after(grad_own, low), down_weight)
-    other = after(other, own_activated_grad)
+    queries = [
+        project_rows(rows, query_weight)[0] for rows in after(normed, own_activated_grad)
+    ]
+    other = after(other, queries)
     residual, lifted_half = lift(inputs_half, low, other, second_gain, half_kind)
 
     lifted_own = both(lifted_half)
@@ -1093,30 +1122,35 @@
     lifted_far = gather_outer(after(lifted_half, other))
     other, grad_inner = after((other, grad_inner), other)
     low, other = pair_mlp(mine, other)
-    down_mine, down_other = down_own(after(activated_own, low), down_weight)
-    other, lifted_far = after((other, lifted_far), down_other)
+    attended, stored = attend_all(
+        after(queries, low),
+        keys,
+        values,
+        places,
+        query_place,
+        groups,
+        clip_length,
+        clips,
+    )
+    other, lifted_far = after((other, lifted_far), attended)
     grad_residual, mixed_half, mixed_columns = middle(
         residual, low, other, grad_half, second_gain, half_kind, shards
     )
     heads_grad = product_back(both(mixed_half), output_weight)
 
     heads_first = gather_first(heads_grad)
-    queries = [project_rows(rows, query_weight)[0] for rows in after(normed, heads_grad)]
-    attended, stored = attend_all(
-        queries, keys, values, places, query_place, groups, clip_length, clips
-    )
     lifted_far = jnp.concatenate(lifted_far, axis=0)
-    lifted_inner = gather_inner(after(lifted_half, heads_grad))
     lifted_inner_far = gather_inner(lifted_far)
-    lifted_far = join_x(lifted_far, heads_first, attended)
+    down_mine, down_other = down_own(after(activated_own, heads_grad), down_weight)
+    lifted_far = join_x(lifted_far, heads_first[1], down_other, lifted_inner_far)
     heads_grads = gather_pieces(*heads_first)
     first_lifted, first_grads = with_core([lifted_far]), with_core([grad_far])
+    first_lifted = after(first_lifted, heads_grads[inner_size() + 1])
     own = (lifted_own, grad_own, activated_own, hidden_own)
     sums = feed_all(first_lifted, first_grads, up_weight, down_weight, shards, own=own)
-    down_low, down_other = pair_mlp(down_mine, after(down_other, heads_grad))
-    heads_grads, down_low, down_other, lifted_inner, lifted_inner_far = after(
-        (heads_grads, down_low, down_other, lifted_inner, lifted_inner_far), sums
-    )
+    down_low, down_other = pair_mlp(down_mine, down_other)
+    heads_grads, down_low, down_other = after((heads_grads, down_low, down_other), sums)
+    lifted_inner = gather_inner(after(lifted_half, down_other))
 
     query_low, key_low, value_low, own_low = attend_back(
         heads_grads, queries, keys, values, attended, stored, groups

time: 199 us -> 190 us (0.955)
  waiting for transfers between devices: 46.1 us -> 37 us
    ppermute x52, waiting for transfers between devices: 46.1 us -> 37 us  [swap(): return lax.ppermute(value, axis, [(i, i ^ bit) for i in range(size)])]
    pallas_call x2, Pallas kernels: 33 us -> 30.6 us  [feed_all(): pl.pallas_call(partial(all_kernel, counts=counts), grid_spec=pltpu.Prefet...]
    unnamed x64 -> x67, local copies, waits for them, and re-layouts: 4.98 us -> 4.88 us
  transfers between devices with their start and end apart: 53 -> 53, of which waited for: 21 -> 22; matrix products, arithmetic and copies ran while one was open for 1% -> 1% of each run, Pallas kernels for 42% -> 44%
where the time goes in v3:
time: 190 us; the launch traced here: 189 us
  Pallas kernels  87 us (46%)
  starting transfers between devices  54.9 us (29%)
  waiting for transfers between devices  37 us (19%)
  local copies, waits for them, and re-layouts  6.85 us (4%)
    ppermute x52, starting transfers between devices, swap(): return lax.ppermute(value, axis, [(i, i ^ bit) for i in range(size)])  49.5 us
    ppermute x52, waiting for transfers between devices, swap(): return lax.ppermute(value, axis, [(i, i ^ bit) for i in range(size)])  37 us
    pallas_call x2, Pallas kernels, feed_all(): pl.pallas_call(partial(all_kernel, counts=counts), grid_spec=pltpu.Prefet...  30.6 us
    pallas_call x1, Pallas kernels, attend_back(): pl.pallas_call(partial(backward_kernel, count=count, groups=groups, scale...  10.2 us
    pallas_call x1, Pallas kernels, attend_all(): pl.pallas_call(partial(all_forward_kernel, groups=groups, scale=1.0 / mat...  9.33 us
    pallas_call x5, Pallas kernels, project_rows(): pl.pallas_call(partial(rows_kernel, count=len(weights)), out_shape=[jax.S...  7.61 us
    pallas_call x1, Pallas kernels, feed_own(): pl.pallas_call(own_kernel, in_specs=[WHOLE] * 3, out_specs=[WHOLE] * 4, o...  5.44 us
    all_to_all x1, starting transfers between devices, body(): lax.all_to_all(after(mixed_columns, query_grad), 'seq', split_axis=0, con...  5.41 us
  transfers between devices with their start and end apart: 53, of which 22 were waited for; matrix products, arithmetic and copies ran while one was open for 1% of the time, Pallas kernels for 44%

profile of v3, /device:TPU:0, one launch (start us, length us, event | category | flops | bytes accessed | tf_op | source)
XLA Modules:
  0.0 189.0 jit_solution(3821811032578688679)
XLA Ops:
  2.2 3.1 %collective-permute-start = (bf16[32,2048]{1,0:T(8,128)(2,1)S(1)}, bf16[32,2048]{1,0:T(8,128)(2,1)S(1)}, u32[]{:S(2)}, u32[]{:S(2)}) collective-permute-start(bf16[32,2048]{1,0:T(8,128)(2,1)S(1)} %constant_dynamic-slice_fusion.4), channel_id=1, source_target_pairs={{0,8},{4,12},{8,0},{12,4},{16,24},{20,28},{24,16},{28,20},{1,9},{5... | collective-permute-start | bytes 393224 | tf_op jit(solution)/shard_map/ppermute | solution.py:40
  5.2 2.6 %collective-permute-start.2 = (bf16[32,2048]{1,0:T(8,128)(2,1)S(1)}, bf16[32,2048]{1,0:T(8,128)(2,1)S(1)}, u32[]{:S(2)}, u32[]{:S(2)}) collective-permute-start(bf16[32,2048]{1,0:T(8,128)(2,1)S(1)} %constant_dynamic-slice_fusion.4), channel_id=1, source_target_pairs={{0,16},{4,20},{8,24},{12,28},{16,0},{20,4},{24,8},{28,12},{1,17},{... | collective-permute-start | bytes 393224 | tf_op jit(solution)/shard_map/ppermute | solution.py:40
  7.8 2.4 %collective-permute-done = bf16[32,2048]{1,0:T(8,128)(2,1)S(1)} collective-permute-done((bf16[32,2048]{1,0:T(8,128)(2,1)S(1)}, bf16[32,2048]{1,0:T(8,128)(2,1)S(1)}, u32[]{:S(2)}, u32[]{:S(2)}) %collective-permute-start) | collective-permute-done | bytes 131104 | tf_op jit(solution)/shard_map/ppermute | solution.py:40
  10.3 1.7 collective-permute-start.1
  12.0 1.5 collective-permute-start.6
  14.1 2.4 %tables.1 = (s32[512,1]{1,0:T(8,128)}, s32[512,1]{1,0:T(8,128)}, s32[512,1]{1,0:T(8,128)}, s32[512,1]{1,0:T(8,128)}, s32[1,1024]{1,0:T(1,128)}, /*index=5*/s32[1,128]{1,0:T(1,128)}, s32[128,1]{1,0:T(8,128)}) custom-call(s32[2]{0:T(128)} %pad_add_fusion.index, s32[1,8]{1,0:T(1,128)} %frames.1, s32[1,8]{1,0:T(1,128)} %texts.1, s32[1,8]{1,0:T(1,128)} %actions.1), custom_call_target="tpu_custom_call" | custom-call | flops 10485 | bytes 10485 | tf_op jit(solution)/shard_map/tables/pallas_call | solution.py:205
  16.8 1.4 collective-permute-done.2
  18.2 1.5 collective-permute-start.3
  20.2 1.6 collective-permute-start.7
  23.2 1.6 collective-permute-start.8
  24.8 1.5 collective-permute-start.9
  26.2 3.3 %collective-permute-done.7.refs_4_ = bf16[64,2048]{1,0:T(8,128)(2,1)S(1)} collective-permute-done((bf16[64,2048]{1,0:T(8,128)(2,1)S(1)}, bf16[64,2048]{1,0:T(8,128)(2,1)S(1)}, u32[]{:S(2)}, u32[]{:S(2)}) %collective-permute-start.7) | collective-permute-done | bytes 262176 | tf_op jit(solution)/shard_map/ppermute | solution.py:40
  29.5 1.5 collective-permute-start.10
  31.0 1.4 collective-permute-start.11
  32.5 1.5 collective-permute-start.12
  36.3 2.5 %norm_pieces.1 = bf16[8,8,8,2048]{3,2,1,0:T(8,128)(2,1)S(1)} custom-call(s32[1]{0:T(128)} %bitcast.11.refs_0_, bf16[64,2048]{1,0:T(8,128)(2,1)S(1)} %bitcast.46, bf16[64,2048]{1,0:T(8,128)(2,1)S(1)} %collective-permute-done.6.refs_2_, bf16[64,2048]{1,0:T(8,128)(2,1)S(1)} %pad_maximum_fusion.6.refs_3_, bf16[64,2048]{1,0:T(8,128)(2,1)S(1)} %collective-permute-done.7.refs_4_, ...), custom_call_target="tpu_custom_call" | custom-call | flops 104857 | bytes 41943 | tf_op jit(solution)/shard_map/norm_pieces/pallas_call | solution.py:359
  40.9 1.5 collective-permute-start.14
  42.5 2.3 %project_rows.6 = (bf16[512,512]{1,0:T(8,128)(2,1)S(1)}, bf16[512,512]{1,0:T(8,128)(2,1)S(1)}) custom-call(bf16[512,2048]{1,0:T(8,128)(2,1)S(1)} %bitcast.40, bf16[2048,512]{1,0:T(8,128)(2,1)S(1)} %copy-done.1, bf16[2048,512]{1,0:T(8,128)(2,1)S(1)} %copy-done.2), custom_call_target="tpu_custom_call" | custom-call | flops 21474836 | bytes 20971 | tf_op jit(solution)/shard_map/project_rows/pallas_call | solution.py:233
  44.9 2.3 %project_rows.7 = (bf16[512,512]{1,0:T(8,128)(2,1)S(1)}, bf16[512,512]{1,0:T(8,128)(2,1)S(1)}) custom-call(bf16[512,2048]{1,0:T(8,128)(2,1)S(1)} %collective-permute-done.13.refs_0_.refs_1_, bf16[2048,512]{1,0:T(8,128)(2,1)S(1)} %copy-done.1, bf16[2048,512]{1,0:T(8,128)(2,1)S(1)} %copy-done.2), custom_call_target="tpu_custom_call" | custom-call | flops 21474836 | bytes 20971 | tf_op jit(solution)/shard_map/project_rows/pallas_call | solution.py:233
  47.2 1.9 %attend.1.refs_0_ = bf16[128,512]{1,0:T(8,128)(2,1)S(1)} custom-call(bf16[128,512]{1,0:T(8,128)(2,1)S(1)} %project_rows.5.query, bf16[512,512]{1,0:T(8,128)(2,1)S(1)} %get-tuple-element.146.key_a.refs_2_.refs_10_, bf16[512,512]{1,0:T(8,128)(2,1)S(1)} %get-tuple-element.147.key_b.refs_3_.refs_11_, ...), custom_call_target="tpu_custom_call" | custom-call | flops 2684354 | bytes 20971 | tf_op jit(solution)/shard_map/attend/pallas_call | solution.py:824
  49.4 2.0 %collective-permute-done.15 = bf16[96,2048]{1,0:T(8,128)(2,1)S(1)} collective-permute-done((bf16[96,2048]{1,0:T(8,128)(2,1)S(1)}, bf16[96,2048]{1,0:T(8,128)(2,1)S(1)}, u32[]{:S(2)}, u32[]{:S(2)}) %collective-permute-start.15) | collective-permute-done | bytes 393248 | tf_op jit(solution)/shard_map/ppermute | solution.py:40
  52.0 1.6 collective-permute-start.19
  55.0 3.5 %grad_activated.1 = f32[128,2048]{1,0:T(8,128)S(1)} custom-call(bf16[128,2048]{1,0:T(8,128)(2,1)S(1)} %pad_maximum_fusion.3.grad.refs_7_, bf16[2048,2048]{1,0:T(8,128)(2,1)S(1)} %bitcast.36), custom_call_target="tpu_custom_call" | custom-call | flops 10737418 | bytes 83886 | tf_op jit(solution)/shard_map/grad_activated/pallas_call | solution.py:567
  62.5 1.5 collective-permute-done.18
  64.1 5.4 %feed_own.1 = (bf16[128,2048]{1,0:T(8,128)(2,1)S(1)}, bf16[128,2048]{1,0:T(8,128)(2,1)S(1)}, f32[64,2048]{1,0:T(8,128)S(1)}, bf16[64,2048]{1,0:T(8,128)(2,1)S(1)}) custom-call(bf16[128,2048]{1,0:T(8,128)(2,1)S(1)} %constant_dynamic-update-slice_fusion.lifted.refs_6_, bf16[2048,2048]{1,0:T(8,128)(2,1)S(1)} %bitcast.38, f32[128,2048]{1,0:T(8,128)S(1)} %grad_activated.1), custom_call_target="tpu_custom_call" | custom-call | flops 21474836 | bytes 83886 | tf_op jit(solution)/shard_map/feed_own/pallas_call | solution.py:541
  69.5 2.5 %collective-permute-done.19.refs_6_ = bf16[192,2048]{1,0:T(8,128)(2,1)} collective-permute-done((bf16[192,2048]{1,0:T(8,128)(2,1)S(1)}, bf16[192,2048]{1,0:T(8,128)(2,1)}, u32[]{:S(2)}, u32[]{:S(2)}) %collective-permute-start.19) | collective-permute-done | bytes 786464 | tf_op jit(solution)/shard_map/ppermute | solution.py:40
  72.0 1.5 collective-permute-done.20
  74.8 1.9 %collective-permute-start.22 = (bf16[32,2048]{1,0:T(8,128)(2,1)S(1)}, bf16[32,2048]{1,0:T(8,128)(2,1)S(1)}, u32[]{:S(2)}, u32[]{:S(2)}) collective-permute-start(bf16[32,2048]{1,0:T(8,128)(2,1)S(1)} %constant_dynamic-slice_fusion), channel_id=1, source_target_pairs={{0,8},{4,12},{8,0},{12,4},{16,24},{20,28},{24,16},{28,20},{1,9},{5... | collective-permute-start | bytes 393224 | tf_op jit(solution)/shard_map/ppermute | solution.py:40
  78.1 1.4 collective-permute-start.24
  79.5 9.3 %attend_all.1 = (bf16[512,512]{1,0:T(8,128)(2,1)S(1)}, bf16[512,512]{1,0:T(8,128)(2,1)S(1)}, bf16[4,2560,256]{2,1,0:T(8,128)(2,1)}) custom-call(bf16[512,512]{1,0:T(8,128)(2,1)S(1)} %project_rows.8.refs_0_.refs_8_, bf16[512,512]{1,0:T(8,128)(2,1)S(1)} %project_rows.9.refs_1_.refs_9_, bf16[512,512]{1,0:T(8,128)(2,1)S(1)} %get-tuple-element.146.key_a.refs_2_.refs_10_, ...), custom_call_target="tpu_custom_call" | custom-call | flops 21474836 | bytes 41943 | tf_op jit(solution)/shard_map/attend_all/pallas_call | solution.py:916
  92.2 1.5 collective-permute-start.36
  94.6 2.3 %collective-permute-start.27 = (bf16[128,512]{1,0:T(8,128)(2,1)S(1)}, bf16[128,512]{1,0:T(8,128)(2,1)S(1)}, u32[]{:S(2)}, u32[]{:S(2)}) collective-permute-start(bf16[128,512]{1,0:T(8,128)(2,1)S(1)} %product_back.1.refs_0_), channel_id=1, source_target_pairs={{0,8},{4,12},{8,0},{12,4},{16,24},{20,28},{24,16},{28,20},{1,9},{5... | collective-permute-start | bytes 393224 | tf_op jit(solution)/shard_map/ppermute | solution.py:40
  97.0 1.5 collective-permute-start.29
  98.4 1.4 collective-permute-start.31
  99.8 2.0 %down_own.1 = (f32[64,2048]{1,0:T(8,128)S(1)}, bf16[64,2048]{1,0:T(8,128)(2,1)S(1)}) custom-call(bf16[128,2048]{1,0:T(8,128)(2,1)S(1)} %get-tuple-element.182.rows.refs_8_, bf16[2048,2048]{1,0:T(8,128)(2,1)S(1)} %bitcast.36), custom_call_target="tpu_custom_call" | custom-call | flops 10737418 | bytes 83886 | tf_op jit(solution)/shard_map/down_own/pallas_call | solution.py:294
  102.8 6.7 %collective-permute-done.29.refs_4_ = bf16[128,512]{1,0:T(8,128)(2,1)S(1)} collective-permute-done((bf16[128,512]{1,0:T(8,128)(2,1)S(1)}, bf16[128,512]{1,0:T(8,128)(2,1)S(1)}, u32[]{:S(2)}, u32[]{:S(2)}) %collective-permute-start.29) | collective-permute-done | bytes 131104 | tf_op jit(solution)/shard_map/ppermute | solution.py:40
  112.4 1.5 collective-permute-start.26
  113.9 2.1 %collective-permute-done.28.refs_3_ = bf16[128,512]{1,0:T(8,128)(2,1)S(1)} collective-permute-done((bf16[128,512]{1,0:T(8,128)(2,1)S(1)}, bf16[128,512]{1,0:T(8,128)(2,1)S(1)}, u32[]{:S(2)}, u32[]{:S(2)}) %collective-permute-start.28) | collective-permute-done | bytes 131104 | tf_op jit(solution)/shard_map/ppermute | solution.py:40
  116.1 2.0 %collective-permute-start.32 = (bf16[128,512]{1,0:T(8,128)(2,1)S(1)}, bf16[128,512]{1,0:T(8,128)(2,1)S(1)}, u32[]{:S(2)}, u32[]{:S(2)}) collective-permute-start(bf16[128,512]{1,0:T(8,128)(2,1)S(1)} %collective-permute-done.31.refs_6_), channel_id=1, source_target_pairs={{0,4},{4,0},{8,12},{12,8},{16,20},{20,16},{24,28},{28,24},{1,5},{5... | collective-permute-start | bytes 393224 | tf_op jit(solution)/shard_map/ppermute | solution.py:40
  118.1 12.4 %feed_all.2 = (f32[256,2048]{1,0:T(8,128)}, f32[2048,256]{1,0:T(8,128)}) custom-call(s32[1]{0:T(128)} %bitcast.10.index, bf16[192,2048]{1,0:T(8,128)(2,1)S(1)} %constant_dynamic-update-slice_fusion.5.refs_0_, bf16[192,2048]{1,0:T(8,128)(2,1)S(1)} %collective-permute-done.37.refs_1_, bf16[192,2048]{1,0:T(8,128)(2,1)S(1)} %pad_maximum_fusion.refs_2_, ...), custom_call_target="tpu_custom_call" | custom-call | flops 72477576 | bytes 199229 | tf_op jit(solution)/shard_map/feed_all/pallas_call | solution.py:665
  130.7 10.2 %attend_back.1 = (bf16[512,512]{1,0:T(8,128)(2,1)S(1)}, bf16[512,512]{1,0:T(8,128)(2,1)S(1)}, bf16[512,512]{1,0:T(8,128)(2,1)S(1)}, bf16[512,512]{1,0:T(8,128)(2...) custom-call(bf16[128,512]{1,0:T(8,128)(2,1)S(1)} %product_back.1.ref, ...), custom_call_target="tpu_custom_call" | custom-call | flops 42949672 | bytes 136314 | tf_op jit(solution)/shard_map/attend_back/pallas_call | solution.py:1028
  140.9 2.1 %product_halves.3 = (f32[64,2048]{1,0:T(8,128)S(1)}, bf16[64,2048]{1,0:T(8,128)(2,1)S(1)}) custom-call(bf16[128,512]{1,0:T(8,128)(2,1)S(1)} %get-tuple-element.210.refs_0_, bf16[128,512]{1,0:T(8,128)(2,1)S(1)} %get-tuple-element.211.refs_1_, bf16[128,512]{1,0:T(8,128)(2,1)S(1)} %get-tuple-element.212.refs_2_, bf16[2048,512]{1,0:T(8,128)(2,1)S(1)} %copy-done, ...), custom_call_target="tpu_custom_call" | custom-call | flops 8053063 | bytes 62914 | tf_op jit(solution)/shard_map/product_halves/pallas_call | solution.py:269
  143.1 1.5 collective-permute-done.41
  144.7 1.3 collective-permute-start.42
  146.1 2.8 %project.1 = (f32[256,512]{1,0:T(8,128)}, f32[256,512]{1,0:T(8,128)}, f32[256,512]{1,0:T(8,128)}, f32[3,256]{1,0:T(4,128)S(1)}) custom-call(s32[1]{0:T(128)} %bitcast.10.index, bf16[512,2048]{1,0:T(8,128)(2,1)S(1)} %bitcast.42, bf16[512,2048]{1,0:T(8,128)(2,1)S(1)} %collective-permute-done.13.refs_0_.refs_1_, ...), custom_call_target="tpu_custom_call" | custom-call | flops 16106127 | bytes 47185 | tf_op jit(solution)/shard_map/project/pallas_call | solution.py:723
  150.0 3.1 %collective-permute-done.42.other = bf16[64,2048]{1,0:T(8,128)(2,1)S(1)} collective-permute-done((bf16[64,2048]{1,0:T(8,128)(2,1)S(1)}, bf16[64,2048]{1,0:T(8,128)(2,1)S(1)}, u32[]{:S(2)}, u32[]{:S(2)}) %collective-permute-start.42) | collective-permute-done | bytes 262176 | tf_op jit(solution)/shard_map/ppermute | solution.py:40
  154.4 5.4 %all-to-all-start = ((bf16[8,72,256]{2,1,0:T(8,128)(2,1)}), bf16[8,72,256]{2,1,0:T(8,128)(2,1)S(1)}, u32[]{:S(2)}, u32[]{:S(2)}) async-start(bf16[8,72,256]{2,1,0:T(8,128)(2,1)} %copy-done.12), calls=%async_computation | async-start | bytes 589824 | tf_op jit(solution)/shard_map/all_to_all | solution.py:1171
  164.6 18.2 %feed_all.3 = (f32[256,2048]{1,0:T(8,128)}, f32[2048,256]{1,0:T(8,128)}) custom-call(s32[1]{0:T(128)} %bitcast.10.index, bf16[64,2048]{1,0:T(8,128)(2,1)S(1)} %copy-done.16, bf16[64,2048]{1,0:T(8,128)(2,1)S(1)} %collective-permute-done.47.refs_1_, bf16[192,2048]{1,0:T(8,128)(2,1)S(1)} %pad_maximum_fusion.1.refs_2_, ...), custom_call_target="tpu_custom_call" | custom-call | flops 96636768 | bytes 209715 | tf_op jit(solution)/shard_map/feed_all/pallas_call | solution.py:665
  (183 shorter events, 39.3 us)
Async XLA Ops:
  2.2 8.1 %collective-permute-start = (bf16[32,2048]{1,0:T(8,128)(2,1)S(1)}, bf16[32,2048]{1,0:T(8,128)(2,1)S(1)}, u32[]{:S(2)}, u32[]{:S(2)}) collective-permute-start(bf16[32,2048]{1,0:T(8,128)(2,1)S(1)} %constant_dynamic-slice_fusion.4), channel_id=1, source_target_pairs={{0,8},{4,12},{8,0},{12,4},{16,24},{20,28},{24,16},{28,20},{1,9},{5... | collective-permute-start | bytes 393224 | tf_op jit(solution)/shard_map/ppermute | solution.py:40
  5.2 12.9 %collective-permute-start.2 = (bf16[32,2048]{1,0:T(8,128)(2,1)S(1)}, bf16[32,2048]{1,0:T(8,128)(2,1)S(1)}, u32[]{:S(2)}, u32[]{:S(2)}) collective-permute-start(bf16[32,2048]{1,0:T(8,128)(2,1)S(1)} %constant_dynamic-slice_fusion.4), channel_id=1, source_target_pairs={{0,16},{4,20},{8,24},{12,28},{16,0},{20,4},{24,8},{28,12},{1,17},{... | collective-permute-start | bytes 393224 | tf_op jit(solution)/shard_map/ppermute | solution.py:40
  7.8 11.8 %collective-permute-start.4 = (bf16[32,2048]{1,0:T(8,128)(2,1)S(1)}, bf16[32,2048]{1,0:T(8,128)(2,1)S(1)}, u32[]{:S(2)}, u32[]{:S(2)}) collective-permute-start(bf16[32,2048]{1,0:T(8,128)(2,1)S(1)} %constant_dynamic-slice_fusion.4), channel_id=1, source_target_pairs={{0,24},{4,28},{8,16},{12,20},{16,8},{20,12},{24,0},{28,4},{1,25},{... | collective-permute-start | bytes 393224 | tf_op jit(solution)/shard_map/ppermute | solution.py:40
  10.3 9.9 %collective-permute-start.1 = (bf16[32,2048]{1,0:T(8,128)(2,1)S(1)}, bf16[32,2048]{1,0:T(8,128)(2,1)S(1)}, u32[]{:S(2)}, u32[]{:S(2)}) collective-permute-start(bf16[32,2048]{1,0:T(8,128)(2,1)S(1)} %collective-permute-done), channel_id=1, source_target_pairs={{0,2},{1,3},{2,0},{3,1},{4,6},{5,7},{6,4},{7,5},{8,10},{9,11},{10,... | collective-permute-start | bytes 393224 | tf_op jit(solution)/shard_map/ppermute | solution.py:40
  12.0 20.5 %collective-permute-start.6 = (bf16[64,2048]{1,0:T(8,128)(2,1)S(1)}, bf16[64,2048]{1,0:T(8,128)(2,1)S(1)}, u32[]{:S(2)}, u32[]{:S(2)}) collective-permute-start(bf16[64,2048]{1,0:T(8,128)(2,1)S(1)} %bitcast.44), channel_id=1, source_target_pairs={{0,4},{4,0},{8,12},{12,8},{16,20},{20,16},{24,28},{28,24},{1,5},{5... | collective-permute-start | bytes 786440 | tf_op jit(solution)/shard_map/ppermute | solution.py:40
  18.2 5.0 %collective-permute-start.3 = (bf16[32,2048]{1,0:T(8,128)(2,1)S(1)}, bf16[32,2048]{1,0:T(8,128)(2,1)S(1)}, u32[]{:S(2)}, u32[]{:S(2)}) collective-permute-start(bf16[32,2048]{1,0:T(8,128)(2,1)S(1)} %collective-permute-done.2), channel_id=1, source_target_pairs={{0,2},{1,3},{2,0},{3,1},{4,6},{5,7},{6,4},{7,5},{8,10},{9,11},{10,... | collective-permute-start | bytes 393224 | tf_op jit(solution)/shard_map/ppermute | solution.py:40
  19.7 5.1 %collective-permute-start.5 = (bf16[32,2048]{1,0:T(8,128)(2,1)S(1)}, bf16[32,2048]{1,0:T(8,128)(2,1)S(1)}, u32[]{:S(2)}, u32[]{:S(2)}) collective-permute-start(bf16[32,2048]{1,0:T(8,128)(2,1)S(1)} %collective-permute-done.4), channel_id=1, source_target_pairs={{0,2},{1,3},{2,0},{3,1},{4,6},{5,7},{6,4},{7,5},{8,10},{9,11},{10,... | collective-permute-start | bytes 393224 | tf_op jit(solution)/shard_map/ppermute | solution.py:40
  20.2 9.3 %collective-permute-start.7 = (bf16[64,2048]{1,0:T(8,128)(2,1)S(1)}, bf16[64,2048]{1,0:T(8,128)(2,1)S(1)}, u32[]{:S(2)}, u32[]{:S(2)}) collective-permute-start(bf16[64,2048]{1,0:T(8,128)(2,1)S(1)} %pad_maximum_fusion.6.refs_3_), channel_id=1, source_target_pairs={{0,4},{4,0},{8,12},{12,8},{16,20},{20,16},{24,28},{28,24},{1,5},{5... | collective-permute-start | bytes 786440 | tf_op jit(solution)/shard_map/ppermute | solution.py:40
  23.2 11.9 %collective-permute-start.8 = (bf16[64,2048]{1,0:T(8,128)(2,1)S(1)}, bf16[64,2048]{1,0:T(8,128)(2,1)S(1)}, u32[]{:S(2)}, u32[]{:S(2)}) collective-permute-start(bf16[64,2048]{1,0:T(8,128)(2,1)S(1)} %pad_maximum_fusion.7.refs_5_), channel_id=1, source_target_pairs={{0,4},{4,0},{8,12},{12,8},{16,20},{20,16},{24,28},{28,24},{1,5},{5... | collective-permute-start | bytes 786440 | tf_op jit(solution)/shard_map/ppermute | solution.py:40
  24.8 11.5 %collective-permute-start.9 = (bf16[64,2048]{1,0:T(8,128)(2,1)S(1)}, bf16[64,2048]{1,0:T(8,128)(2,1)S(1)}, u32[]{:S(2)}, u32[]{:S(2)}) collective-permute-start(bf16[64,2048]{1,0:T(8,128)(2,1)S(1)} %pad_maximum_fusion.8.refs_7_), channel_id=1, source_target_pairs={{0,4},{4,0},{8,12},{12,8},{16,20},{20,16},{24,28},{28,24},{1,5},{5... | collective-permute-start | bytes 786440 | tf_op jit(solution)/shard_map/ppermute | solution.py:40
  29.5 9.3 %collective-permute-start.10 = (bf16[32,2048]{1,0:T(8,128)(2,1)S(1)}, bf16[32,2048]{1,0:T(8,128)(2,1)S(1)}, u32[]{:S(2)}, u32[]{:S(2)}) collective-permute-start(bf16[32,2048]{1,0:T(8,128)(2,1)S(1)} %constant_dynamic-slice_fusion.2), channel_id=1, source_target_pairs={{0,8},{4,12},{8,0},{12,4},{16,24},{20,28},{24,16},{28,20},{1,9},{5... | collective-permute-start | bytes 393224 | tf_op jit(solution)/shard_map/ppermute | solution.py:40
  31.0 8.7 %collective-permute-start.11 = (bf16[32,2048]{1,0:T(8,128)(2,1)S(1)}, bf16[32,2048]{1,0:T(8,128)(2,1)S(1)}, u32[]{:S(2)}, u32[]{:S(2)}) collective-permute-start(bf16[32,2048]{1,0:T(8,128)(2,1)S(1)} %constant_dynamic-slice_fusion.2), channel_id=1, source_target_pairs={{0,16},{4,20},{8,24},{12,28},{16,0},{20,4},{24,8},{28,12},{1,17},{... | collective-permute-start | bytes 393224 | tf_op jit(solution)/shard_map/ppermute | solution.py:40
  32.5 7.2 %collective-permute-start.12 = (bf16[32,2048]{1,0:T(8,128)(2,1)S(1)}, bf16[32,2048]{1,0:T(8,128)(2,1)S(1)}, u32[]{:S(2)}, u32[]{:S(2)}) collective-permute-start(bf16[32,2048]{1,0:T(8,128)(2,1)S(1)} %constant_dynamic-slice_fusion.2), channel_id=1, source_target_pairs={{0,24},{4,28},{8,16},{12,20},{16,8},{20,12},{24,0},{28,4},{1,25},{... | collective-permute-start | bytes 393224 | tf_op jit(solution)/shard_map/ppermute | solution.py:40
  39.7 5.1 %collective-permute-start.13 = (bf16[512,2048]{1,0:T(8,128)(2,1)S(1)}, bf16[512,2048]{1,0:T(8,128)(2,1)S(1)}, u32[]{:S(2)}, u32[]{:S(2)}) collective-permute-start(bf16[512,2048]{1,0:T(8,128)(2,1)S(1)} %bitcast.39), channel_id=1, source_target_pairs={{0,1},{1,0},{2,3},{3,2},{4,5},{5,4},{6,7},{7,6},{8,9},{9,8},{10,11... | collective-permute-start | bytes 6291464 | tf_op jit(solution)/shard_map/ppermute | solution.py:40
  39.8 11.6 %collective-permute-start.15 = (bf16[96,2048]{1,0:T(8,128)(2,1)S(1)}, bf16[96,2048]{1,0:T(8,128)(2,1)S(1)}, u32[]{:S(2)}, u32[]{:S(2)}) collective-permute-start(bf16[96,2048]{1,0:T(8,128)(2,1)S(1)} %pad_maximum_fusion.5), channel_id=1, source_target_pairs={{0,2},{1,3},{2,0},{3,1},{4,6},{5,7},{6,4},{7,5},{8,10},{9,11},{10,... | collective-permute-start | bytes 1179656 | tf_op jit(solution)/shard_map/ppermute | solution.py:40
  40.9 8.4 %collective-permute-start.14 = (bf16[64,2048]{1,0:T(8,128)(2,1)S(1)}, bf16[64,2048]{1,0:T(8,128)(2,1)S(1)}, u32[]{:S(2)}, u32[]{:S(2)}) collective-permute-start(bf16[64,2048]{1,0:T(8,128)(2,1)S(1)} %bitcast.52), channel_id=1, source_target_pairs={{0,4},{4,0},{8,12},{12,8},{16,20},{20,16},{24,28},{28,24},{1,5},{5... | collective-permute-start | bytes 786440 | tf_op jit(solution)/shard_map/ppermute | solution.py:40
  52.0 20.1 %collective-permute-start.19 = (bf16[192,2048]{1,0:T(8,128)(2,1)S(1)}, bf16[192,2048]{1,0:T(8,128)(2,1)}, u32[]{:S(2)}, u32[]{:S(2)}) collective-permute-start(bf16[192,2048]{1,0:T(8,128)(2,1)S(1)} %pad_maximum_fusion.refs_2_), channel_id=1, source_target_pairs={{0,4},{4,0},{8,12},{12,8},{16,20},{20,16},{24,28},{28,24},{1,5},{5... | collective-permute-start | bytes 2359304 | tf_op jit(solution)/shard_map/ppermute | solution.py:40
  53.6 8.4 %collective-permute-start.17 = (bf16[64,2048]{1,0:T(8,128)(2,1)S(1)}, bf16[64,2048]{1,0:T(8,128)(2,1)S(1)}, u32[]{:S(2)}, u32[]{:S(2)}) collective-permute-start(bf16[64,2048]{1,0:T(8,128)(2,1)S(1)} %add_convert_fusion.3.low), channel_id=1, source_target_pairs={{0,2},{1,3},{2,0},{3,1},{4,6},{5,7},{6,4},{7,5},{8,10},{9,11},{10,... | collective-permute-start | bytes 786440 | tf_op jit(solution)/shard_map/ppermute | solution.py:40
  73.6 16.0 %collective-permute-start.21 = (bf16[64,2048]{1,0:T(8,128)(2,1)S(1)}, bf16[64,2048]{1,0:T(8,128)(2,1)S(1)}, u32[]{:S(2)}, u32[]{:S(2)}) collective-permute-start(bf16[64,2048]{1,0:T(8,128)(2,1)S(1)} %add_convert_fusion.2.low), channel_id=1, source_target_pairs={{0,2},{1,3},{2,0},{3,1},{4,6},{5,7},{6,4},{7,5},{8,10},{9,11},{10,... | collective-permute-start | bytes 786440 | tf_op jit(solution)/shard_map/ppermute | solution.py:40
  74.8 14.0 %collective-permute-start.22 = (bf16[32,2048]{1,0:T(8,128)(2,1)S(1)}, bf16[32,2048]{1,0:T(8,128)(2,1)S(1)}, u32[]{:S(2)}, u32[]{:S(2)}) collective-permute-start(bf16[32,2048]{1,0:T(8,128)(2,1)S(1)} %constant_dynamic-slice_fusion), channel_id=1, source_target_pairs={{0,8},{4,12},{8,0},{12,4},{16,24},{20,28},{24,16},{28,20},{1,9},{5... | collective-permute-start | bytes 393224 | tf_op jit(solution)/shard_map/ppermute | solution.py:40
  76.8 12.9 %collective-permute-start.23 = (bf16[32,2048]{1,0:T(8,128)(2,1)S(1)}, bf16[32,2048]{1,0:T(8,128)(2,1)S(1)}, u32[]{:S(2)}, u32[]{:S(2)}) collective-permute-start(bf16[32,2048]{1,0:T(8,128)(2,1)S(1)} %constant_dynamic-slice_fusion), channel_id=1, source_target_pairs={{0,16},{4,20},{8,24},{12,28},{16,0},{20,4},{24,8},{28,12},{1,17},{... | collective-permute-start | bytes 393224 | tf_op jit(solution)/shard_map/ppermute | solution.py:40
  78.1 11.6 %collective-permute-start.24 = (bf16[32,2048]{1,0:T(8,128)(2,1)S(1)}, bf16[32,2048]{1,0:T(8,128)(2,1)S(1)}, u32[]{:S(2)}, u32[]{:S(2)}) collective-permute-start(bf16[32,2048]{1,0:T(8,128)(2,1)S(1)} %constant_dynamic-slice_fusion), channel_id=1, source_target_pairs={{0,24},{4,28},{8,16},{12,20},{16,8},{20,12},{24,0},{28,4},{1,25},{... | collective-permute-start | bytes 393224 | tf_op jit(solution)/shard_map/ppermute | solution.py:40
  90.5 3.3 %collective-permute-start.25 = (bf16[64,2048]{1,0:T(8,128)(2,1)S(1)}, bf16[64,2048]{1,0:T(8,128)(2,1)S(1)}, u32[]{:S(2)}, u32[]{:S(2)}) collective-permute-start(bf16[64,2048]{1,0:T(8,128)(2,1)S(1)} %get-tuple-element.180), channel_id=1, source_target_pairs={{0,1},{1,0},{2,3},{3,2},{4,5},{5,4},{6,7},{7,6},{8,9},{9,8},{10,11... | collective-permute-start | bytes 786440 | tf_op jit(solution)/shard_map/ppermute | solution.py:40
  91.2 11.0 %collective-permute-start.35 = (bf16[96,2048]{1,0:T(8,128)(2,1)S(1)}, bf16[96,2048]{1,0:T(8,128)(2,1)S(1)}, u32[]{:S(2)}, u32[]{:S(2)}) collective-permute-start(bf16[96,2048]{1,0:T(8,128)(2,1)S(1)} %get-tuple-element.260), channel_id=1, source_target_pairs={{0,2},{1,3},{2,0},{3,1},{4,6},{5,7},{6,4},{7,5},{8,10},{9,11},{10,... | collective-permute-start | bytes 1179656 | tf_op jit(solution)/shard_map/ppermute | solution.py:40
  92.2 10.6 %collective-permute-start.36 = (bf16[96,2048]{1,0:T(8,128)(2,1)S(1)}, bf16[96,2048]{1,0:T(8,128)(2,1)S(1)}, u32[]{:S(2)}, u32[]{:S(2)}) collective-permute-start(bf16[96,2048]{1,0:T(8,128)(2,1)S(1)} %get-tuple-element.260), channel_id=1, source_target_pairs={{0,4},{4,0},{8,12},{12,8},{16,20},{20,16},{24,28},{28,24},{1,5},{5... | collective-permute-start | bytes 1179656 | tf_op jit(solution)/shard_map/ppermute | solution.py:40
  94.6 8.2 %collective-permute-start.27 = (bf16[128,512]{1,0:T(8,128)(2,1)S(1)}, bf16[128,512]{1,0:T(8,128)(2,1)S(1)}, u32[]{:S(2)}, u32[]{:S(2)}) collective-permute-start(bf16[128,512]{1,0:T(8,128)(2,1)S(1)} %product_back.1.refs_0_), channel_id=1, source_target_pairs={{0,8},{4,12},{8,0},{12,4},{16,24},{20,28},{24,16},{28,20},{1,9},{5... | collective-permute-start | bytes 393224 | tf_op jit(solution)/shard_map/ppermute | solution.py:40
  97.0 12.6 %collective-permute-start.29 = (bf16[128,512]{1,0:T(8,128)(2,1)S(1)}, bf16[128,512]{1,0:T(8,128)(2,1)S(1)}, u32[]{:S(2)}, u32[]{:S(2)}) collective-permute-start(bf16[128,512]{1,0:T(8,128)(2,1)S(1)} %product_back.1.refs_0_), channel_id=1, source_target_pairs={{0,16},{4,20},{8,24},{12,28},{16,0},{20,4},{24,8},{28,12},{1,17},{... | collective-permute-start | bytes 393224 | tf_op jit(solution)/shard_map/ppermute | solution.py:40
  98.4 11.1 %collective-permute-start.31 = (bf16[128,512]{1,0:T(8,128)(2,1)S(1)}, bf16[128,512]{1,0:T(8,128)(2,1)S(1)}, u32[]{:S(2)}, u32[]{:S(2)}) collective-permute-start(bf16[128,512]{1,0:T(8,128)(2,1)S(1)} %product_back.1.refs_0_), channel_id=1, source_target_pairs={{0,24},{4,28},{8,16},{12,20},{16,8},{20,12},{24,0},{28,4},{1,25},{... | collective-permute-start | bytes 393224 | tf_op jit(solution)/shard_map/ppermute | solution.py:40
  102.2 10.2 %collective-permute-start.38 = (bf16[192,2048]{1,0:T(8,128)(2,1)S(1)}, bf16[192,2048]{1,0:T(8,128)(2,1)S(1)}, u32[]{:S(2)}, u32[]{:S(2)}) collective-permute-start(bf16[192,2048]{1,0:T(8,128)(2,1)S(1)} %pad_maximum_fusion.refs_2_), channel_id=1, source_target_pairs={{0,1},{1,0},{2,3},{3,2},{4,5},{5,4},{6,7},{7,6},{8,9},{9,8},{10,11... | collective-permute-start | bytes 2359304 | tf_op jit(solution)/shard_map/ppermute | solution.py:40
  102.8 8.5 %collective-permute-start.33 = (bf16[64,2048]{1,0:T(8,128)(2,1)S(1)}, bf16[64,2048]{1,0:T(8,128)(2,1)S(1)}, u32[]{:S(2)}, u32[]{:S(2)}) collective-permute-start(bf16[64,2048]{1,0:T(8,128)(2,1)S(1)} %get-tuple-element.184), channel_id=1, source_target_pairs={{0,1},{1,0},{2,3},{3,2},{4,5},{5,4},{6,7},{7,6},{8,9},{9,8},{10,11... | collective-permute-start | bytes 786440 | tf_op jit(solution)/shard_map/ppermute | solution.py:40
  109.6 6.5 %collective-permute-start.37 = (bf16[192,2048]{1,0:T(8,128)(2,1)S(1)}, bf16[192,2048]{1,0:T(8,128)(2,1)S(1)}, u32[]{:S(2)}, u32[]{:S(2)}) collective-permute-start(bf16[192,2048]{1,0:T(8,128)(2,1)S(1)} %constant_dynamic-update-slice_fusion.5.refs_0_), channel_id=1, source_target_pairs={{0,1},{1,0},{2,3},{3,2},{4,5},{5,4},{6,7},{7,6},{8,9},{9,8},{10,11... | collective-permute-start | bytes 2359304 | tf_op jit(solution)/shard_map/ppermute | solution.py:40
  109.7 6.4 %collective-permute-start.28 = (bf16[128,512]{1,0:T(8,128)(2,1)S(1)}, bf16[128,512]{1,0:T(8,128)(2,1)S(1)}, u32[]{:S(2)}, u32[]{:S(2)}) collective-permute-start(bf16[128,512]{1,0:T(8,128)(2,1)S(1)} %collective-permute-done.27.refs_2_), channel_id=1, source_target_pairs={{0,4},{4,0},{8,12},{12,8},{16,20},{20,16},{24,28},{28,24},{1,5},{5... | collective-permute-start | bytes 393224 | tf_op jit(solution)/shard_map/ppermute | solution.py:40
  110.2 30.6 %collective-permute-start.40 = (bf16[96,2048]{1,0:T(8,128)(2,1)S(1)}, bf16[96,2048]{1,0:T(8,128)(2,1)S(1)}, u32[]{:S(2)}, u32[]{:S(2)}) collective-permute-start(bf16[96,2048]{1,0:T(8,128)(2,1)S(1)} %collective-permute-done.36), channel_id=1, source_target_pairs={{0,2},{1,3},{2,0},{3,1},{4,6},{5,7},{6,4},{7,5},{8,10},{9,11},{10,... | collective-permute-start | bytes 1179656 | tf_op jit(solution)/shard_map/ppermute | solution.py:40
  111.4 19.1 %collective-permute-start.34 = (bf16[64,2048]{1,0:T(8,128)(2,1)S(1)}, bf16[64,2048]{1,0:T(8,128)(2,1)S(1)}, u32[]{:S(2)}, u32[]{:S(2)}) collective-permute-start(bf16[64,2048]{1,0:T(8,128)(2,1)S(1)} %add_convert_fusion.1.low), channel_id=1, source_target_pairs={{0,2},{1,3},{2,0},{3,1},{4,6},{5,7},{6,4},{7,5},{8,10},{9,11},{10,... | collective-permute-start | bytes 786440 | tf_op jit(solution)/shard_map/ppermute | solution.py:40
  112.4 18.0 %collective-permute-start.26 = (bf16[128,512]{1,0:T(8,128)(2,1)S(1)}, bf16[128,512]{1,0:T(8,128)(2,1)S(1)}, u32[]{:S(2)}, u32[]{:S(2)}) collective-permute-start(bf16[128,512]{1,0:T(8,128)(2,1)S(1)} %product_back.1.refs_0_), channel_id=1, source_target_pairs={{0,4},{4,0},{8,12},{12,8},{16,20},{20,16},{24,28},{28,24},{1,5},{5... | collective-permute-start | bytes 393224 | tf_op jit(solution)/shard_map/ppermute | solution.py:40
  116.0 14.4 %collective-permute-start.30 = (bf16[128,512]{1,0:T(8,128)(2,1)S(1)}, bf16[128,512]{1,0:T(8,128)(2,1)S(1)}, u32[]{:S(2)}, u32[]{:S(2)}) collective-permute-start(bf16[128,512]{1,0:T(8,128)(2,1)S(1)} %collective-permute-done.29.refs_4_), channel_id=1, source_target_pairs={{0,4},{4,0},{8,12},{12,8},{16,20},{20,16},{24,28},{28,24},{1,5},{5... | collective-permute-start | bytes 393224 | tf_op jit(solution)/shard_map/ppermute | solution.py:40
  116.1 14.4 %collective-permute-start.32 = (bf16[128,512]{1,0:T(8,128)(2,1)S(1)}, bf16[128,512]{1,0:T(8,128)(2,1)S(1)}, u32[]{:S(2)}, u32[]{:S(2)}) collective-permute-start(bf16[128,512]{1,0:T(8,128)(2,1)S(1)} %collective-permute-done.31.refs_6_), channel_id=1, source_target_pairs={{0,4},{4,0},{8,12},{12,8},{16,20},{20,16},{24,28},{28,24},{1,5},{5... | collective-permute-start | bytes 393224 | tf_op jit(solution)/shard_map/ppermute | solution.py:40
  130.5 10.4 %collective-permute-start.39 = (bf16[64,2048]{1,0:T(8,128)(2,1)S(1)}, bf16[64,2048]{1,0:T(8,128)(2,1)S(1)}, u32[]{:S(2)}, u32[]{:S(2)}) collective-permute-start(bf16[64,2048]{1,0:T(8,128)(2,1)S(1)} %get-tuple-element.208), channel_id=1, source_target_pairs={{0,4},{4,0},{8,12},{12,8},{16,20},{20,16},{24,28},{28,24},{1,5},{5... | collective-permute-start | bytes 786440 | tf_op jit(solution)/shard_map/ppermute | solution.py:40
  144.7 8.4 %collective-permute-start.42 = (bf16[64,2048]{1,0:T(8,128)(2,1)S(1)}, bf16[64,2048]{1,0:T(8,128)(2,1)S(1)}, u32[]{:S(2)}, u32[]{:S(2)}) collective-permute-start(bf16[64,2048]{1,0:T(8,128)(2,1)S(1)} %add_convert_fusion.low), channel_id=1, source_target_pairs={{0,2},{1,3},{2,0},{3,1},{4,6},{5,7},{6,4},{7,5},{8,10},{9,11},{10,... | collective-permute-start | bytes 786440 | tf_op jit(solution)/shard_map/ppermute | solution.py:40
  153.8 10.3 %collective-permute-start.48 = (bf16[192,2048]{1,0:T(8,128)(2,1)S(1)}, bf16[192,2048]{1,0:T(8,128)(2,1)}, u32[]{:S(2)}, u32[]{:S(2)}) collective-permute-start(bf16[192,2048]{1,0:T(8,128)(2,1)S(1)} %pad_maximum_fusion.1.refs_2_), channel_id=1, source_target_pairs={{0,1},{1,0},{2,3},{3,2},{4,5},{5,4},{6,7},{7,6},{8,9},{9,8},{10,11... | collective-permute-start | bytes 2359304 | tf_op jit(solution)/shard_map/ppermute | solution.py:40
  153.8 10.8 %collective-permute-start.50 = (bf16[192,2048]{1,0:T(8,128)(2,1)}, bf16[192,2048]{1,0:T(8,128)(2,1)}, u32[]{:S(2)}, u32[]{:S(2)}) collective-permute-start(bf16[192,2048]{1,0:T(8,128)(2,1)} %collective-permute-done.19.refs_6_), channel_id=1, source_target_pairs={{0,1},{1,0},{2,3},{3,2},{4,5},{5,4},{6,7},{7,6},{8,9},{9,8},{10,11... | collective-permute-start | bytes 2359304 | tf_op jit(solution)/shard_map/ppermute | solution.py:40
  154.4 28.5 %all-to-all-start = ((bf16[8,72,256]{2,1,0:T(8,128)(2,1)}), bf16[8,72,256]{2,1,0:T(8,128)(2,1)S(1)}, u32[]{:S(2)}, u32[]{:S(2)}) async-start(bf16[8,72,256]{2,1,0:T(8,128)(2,1)} %copy-done.12), calls=%async_computation | async-start | bytes 589824 | tf_op jit(solution)/shard_map/all_to_all | solution.py:1171
  159.8 4.4 %collective-permute-start.47 = (bf16[64,2048]{1,0:T(8,128)(2,1)}, bf16[64,2048]{1,0:T(8,128)(2,1)S(1)}, u32[]{:S(2)}, u32[]{:S(2)}) collective-permute-start(bf16[64,2048]{1,0:T(8,128)(2,1)} %copy-done.15), channel_id=1, source_target_pairs={{0,1},{1,0},{2,3},{3,2},{4,5},{5,4},{6,7},{7,6},{8,9},{9,8},{10,11... | collective-permute-start | bytes 786440 | tf_op jit(solution)/shard_map/ppermute | solution.py:40
  159.8 4.8 %collective-permute-start.49 = (bf16[64,2048]{1,0:T(8,128)(2,1)}, bf16[64,2048]{1,0:T(8,128)(2,1)S(1)}, u32[]{:S(2)}, u32[]{:S(2)}) collective-permute-start(bf16[64,2048]{1,0:T(8,128)(2,1)} %copy-done.13), channel_id=1, source_target_pairs={{0,1},{1,0},{2,3},{3,2},{4,5},{5,4},{6,7},{7,6},{8,9},{9,8},{10,11... | collective-permute-start | bytes 786440 | tf_op jit(solution)/shard_map/ppermute | solution.py:40
  182.9 4.9 %collective-permute-start.51 = (bf16[8,72,256]{2,1,0:T(8,128)(2,1)S(1)}, bf16[8,72,256]{2,1,0:T(8,128)(2,1)S(1)}, u32[]{:S(2)}, u32[]{:S(2)}) collective-permute-start(bf16[8,72,256]{2,1,0:T(8,128)(2,1)S(1)} %all-to-all-done.came_a), channel_id=1, source_target_pairs={{0,1},{1,0},{2,3},{3,2},{4,5},{5,4},{6,7},{7,6},{8,9},{9,8},{10,11... | collective-permute-start | bytes 884744 | tf_op jit(solution)/shard_map/ppermute | solution.py:40
  183.0 1.9 collective-permute-start.45
  183.5 2.3 %collective-permute-start.44 = (bf16[64,2048]{1,0:T(8,128)(2,1)S(1)}, bf16[64,2048]{1,0:T(8,128)(2,1)S(1)}, u32[]{:S(2)}, u32[]{:S(2)}) collective-permute-start(bf16[64,2048]{1,0:T(8,128)(2,1)S(1)} %finish.1.mine), channel_id=1, source_target_pairs={{0,1},{1,0},{2,3},{3,2},{4,5},{5,4},{6,7},{7,6},{8,9},{9,8},{10,11... | collective-permute-start | bytes 786440 | tf_op jit(solution)/shard_map/ppermute | solution.py:40
  183.5 3.6 %collective-permute-start.46 = (f32[3,256]{1,0:T(4,128)S(1)}, f32[3,256]{1,0:T(4,128)S(1)}, u32[]{:S(2)}, u32[]{:S(2)}) collective-permute-start(f32[3,256]{1,0:T(4,128)S(1)} %add.49), channel_id=1, source_target_pairs={{0,2},{1,3},{2,0},{3,1},{4,6},{5,7},{6,4},{7,5},{8,10},{9,11},{10,... | collective-permute-start | bytes 9224 | tf_op jit(solution)/shard_map/ppermute | solution.py:40
  (37 other events, 237.0 us)

commit v4 on v3

--- a/solution.py
+++ b/solution.py
@@ -14,6 +14,7 @@
 f32 = jnp.float32
 NEGATIVE = -1e30
 
+WHOLE = pl.BlockSpec(memory_space=pltpu.VMEM)
 NN = ((1,), (0,))
 NT = ((1,), (1,))
 TN = ((0,), (0,))
@@ -233,7 +234,7 @@
     return pl.pallas_call(
         partial(rows_kernel, count=len(weights)),
         out_shape=[jax.ShapeDtypeStruct((rows.shape[0], across), bf16)] * len(weights),
-        compiler_params=params(10),
+        compiler_params=params(8),
         cost_estimate=cost(2 * rows.size * across * len(weights), 2 * rows.size),
         name="project_rows",
     )(rows, *weights)
@@ -269,7 +270,7 @@
     return pl.pallas_call(
         partial(halves_kernel, count=count, dims=dims),
         out_shape=[jax.ShapeDtypeStruct(shape, f32), jax.ShapeDtypeStruct(shape, bf16)],
-        compiler_params=params(10),
+        compiler_params=params(6),
         cost_estimate=cost(2 * count * rows[0].size * across, 2 * count * weights[0].size),
         name="product_halves",
     )(*rows, *weights)
@@ -392,6 +393,8 @@
 def lift(rows, low, other, gain, kind):
     return pl.pallas_call(
         lift_kernel,
+        in_specs=[WHOLE] * 5,
+        out_specs=[WHOLE] * 2,
         out_shape=[jax.ShapeDtypeStruct(rows.shape, f32), jax.ShapeDtypeStruct(rows.shape, bf16)],
         compiler_params=params(4),
         cost_estimate=cost(10 * rows.size, 12 * rows.size),
@@ -427,6 +430,8 @@
     rows, width = residual.shape
     return pl.pallas_call(
         middle_kernel,
+        in_specs=[WHOLE] * 6,
+        out_specs=[WHOLE] * 3,
         out_shape=[
             jax.ShapeDtypeStruct(residual.shape, f32),
             jax.ShapeDtypeStruct(residual.shape, bf16),
@@ -455,6 +460,8 @@
 def finish(residual, low, other, shards):
     return pl.pallas_call(
         partial(finish_kernel, shards=shards),
+        in_specs=[WHOLE] * 3,
+        out_specs=WHOLE,
         out_shape=jax.ShapeDtypeStruct(residual.shape, bf16),
         compiler_params=params(4),
         cost_estimate=cost(2 * residual.size, 10 * residual.size),
@@ -492,6 +499,8 @@
 def last(rows, low, other, grad_residual, gain, kind, shards):
     return pl.pallas_call(
         partial(last_kernel, shards=shards),
+        in_specs=[WHOLE] * 6,
+        out_specs=WHOLE,
         out_shape=jax.ShapeDtypeStruct(rows.shape, bf16),
         compiler_params=params(6),
         cost_estimate=cost(20 * rows.size, 12 * rows.size),
@@ -506,9 +515,6 @@
     upper = 0.5 * (1 + bent)
     slope = upper + (0.5 * value) * (1 - bent * bent) * (rate + (rate * 3 * 0.044715) * square)
     return value * upper, slope
-
-
-WHOLE = pl.BlockSpec(memory_space=pltpu.VMEM)
 
 
 def tiles_of(extent, tile, step):
@@ -615,14 +621,14 @@
         down_term = dot(value.astype(bf16), grad[:, mine], TN)
         up_term = dot(lifted_across[...], hidden_grad, NN)
         if len(before) == 2:
-            up_term += before[0][...]
-            down_term += before[1][...]
+            up_term += before[0][...].astype(f32)
+            down_term += before[1][...].astype(f32)
         else:
             lifted_own, grad_own, activated, hidden_own = before
             up_term += dot(lifted_own[...], hidden_own[...], TN)
             down_term += dot(activated[...], grad_own[...], TN)
-        up_grad[...] = up_term
-        down_grad[...] = down_term
+        up_grad[...] = up_term.astype(up_grad.dtype)
+        down_grad[...] = down_term.astype(down_grad.dtype)
 
     @pl.when(first)
     def _():
@@ -680,7 +686,10 @@
             + [pltpu.VMEM((rows, tile), f32)] * 2
             + [pltpu.SemaphoreType.DMA((2 * count,))],
         ),
-        out_shape=[pltpu.HBM((part, hidden), f32), pltpu.HBM((hidden, part), f32)],
+        out_shape=[
+            pltpu.HBM((part, hidden), bf16 if own else f32),
+            pltpu.HBM((hidden, part), bf16 if own else f32),
+        ],
         compiler_params=params((6 if own else 8) + 8 * rows // 512),
         cost_estimate=cost(
             4 * rows * hidden * (width + part),
@@ -735,7 +744,7 @@
         ),
         out_shape=[jax.ShapeDtypeStruct((part, across), f32)] * 3
         + [jax.ShapeDtypeStruct((gain.shape[0], part), f32)],
-        compiler_params=params(14),
+        compiler_params=params(8),
         cost_estimate=cost(24 * rows * part * across, 12 * rows * across + 12 * part * across),
         name="project",
     )(index, *normed, *[low for pair in lows for low in pair], *weights, gain, *kinds)
@@ -1168,13 +1177,13 @@
         kinds,
         shards,
     )
-    mixed_part = lax.all_to_all(
-        after(mixed_columns, query_grad), "seq", split_axis=0, concat_axis=0, tiled=True
-    )
     first_gain_grad = first_gain_grad + swap(first_gain_grad, "mlp", 1)
     other, first_gain_grad = after((other, first_gain_grad), query_grad)
     input_half = last(inputs_half, low, other, grad_residual, first_gain, half_kind, shards)
     outputs_half = finish(residual, down_low, after(down_other, input_half), shards)
+    mixed_part = lax.all_to_all(
+        after(mixed_columns, outputs_half), "seq", split_axis=0, concat_axis=0, tiled=True
+    )
     rest_lifted = with_core(after(lifted_inner, other))
     rest_grads = with_core(after(grad_inner, other))
     up_grad, down_grad = feed_all(

time: 190 us -> 187 us (0.984)
  local copies, waits for them, and re-layouts: 6.85 us -> 3.1 us
  waiting for transfers between devices: 37 us -> 39.1 us
    unnamed x67 -> x47, local copies, waits for them, and re-layouts: 4.88 us -> 1.13 us
    ppermute x52, waiting for transfers between devices: 37 us -> 39.1 us  [swap(): return lax.ppermute(value, axis, [(i, i ^ bit) for i in range(size)])]
  transfers between devices with their start and end apart: 53 -> 53, of which waited for: 22 -> 24; matrix products, arithmetic and copies ran while one was open for 1% -> 1% of each run, Pallas kernels for 44% -> 44%
where the time goes in v4:
time: 187 us
  Pallas kernels  86.4 us (46%)
  starting transfers between devices  55.1 us (29%)
  waiting for transfers between devices  39.1 us (21%)
  local copies, waits for them, and re-layouts  3.1 us (2%)
    ppermute x52, starting transfers between devices, swap(): return lax.ppermute(value, axis, [(i, i ^ bit) for i in range(size)])  49.1 us
    ppermute x52, waiting for transfers between devices, swap(): return lax.ppermute(value, axis, [(i, i ^ bit) for i in range(size)])  39.1 us
    pallas_call x2, Pallas kernels, feed_all(): pl.pallas_call(partial(all_kernel, counts=counts), grid_spec=pltpu.Prefet...  29.9 us
    pallas_call x1, Pallas kernels, attend_back(): pl.pallas_call(partial(backward_kernel, count=count, groups=groups, scale...  10.2 us
    pallas_call x1, Pallas kernels, attend_all(): pl.pallas_call(partial(all_forward_kernel, groups=groups, scale=1.0 / mat...  9.38 us
    pallas_call x5, Pallas kernels, project_rows(): pl.pallas_call(partial(rows_kernel, count=len(weights)), out_shape=[jax.S...  7.64 us
    all_to_all x1, starting transfers between devices, body(): lax.all_to_all(after(mixed_columns, outputs_half), 'seq', split_axis=0, c...  6.01 us
    pallas_call x1, Pallas kernels, feed_own(): pl.pallas_call(own_kernel, in_specs=[WHOLE] * 3, out_specs=[WHOLE] * 4, o...  5.46 us
  transfers between devices with their start and end apart: 53, of which 24 were waited for; matrix products, arithmetic and copies ran while one was open for 1% of the time, Pallas kernels for 44%

profile of v4, /device:TPU:0, one launch (start us, length us, event | category | flops | bytes accessed | tf_op | source)
XLA Modules:
  0.0 186.8 jit_solution(3657782518482548074)
XLA Ops:
  2.2 3.1 %collective-permute-start = (bf16[32,2048]{1,0:T(8,128)(2,1)S(1)}, bf16[32,2048]{1,0:T(8,128)(2,1)S(1)}, u32[]{:S(2)}, u32[]{:S(2)}) collective-permute-start(bf16[32,2048]{1,0:T(8,128)(2,1)S(1)} %constant_dynamic-slice_fusion.4), channel_id=1, source_target_pairs={{0,8},{4,12},{8,0},{12,4},{16,24},{20,28},{24,16},{28,20},{1,9},{5... | collective-permute-start | bytes 393224 | tf_op jit(solution)/shard_map/ppermute | solution.py:41
  5.2 2.6 %collective-permute-start.2 = (bf16[32,2048]{1,0:T(8,128)(2,1)S(1)}, bf16[32,2048]{1,0:T(8,128)(2,1)S(1)}, u32[]{:S(2)}, u32[]{:S(2)}) collective-permute-start(bf16[32,2048]{1,0:T(8,128)(2,1)S(1)} %constant_dynamic-slice_fusion.4), channel_id=1, source_target_pairs={{0,16},{4,20},{8,24},{12,28},{16,0},{20,4},{24,8},{28,12},{1,17},{... | collective-permute-start | bytes 393224 | tf_op jit(solution)/shard_map/ppermute | solution.py:41
  7.8 2.4 %collective-permute-done = bf16[32,2048]{1,0:T(8,128)(2,1)S(1)} collective-permute-done((bf16[32,2048]{1,0:T(8,128)(2,1)S(1)}, bf16[32,2048]{1,0:T(8,128)(2,1)S(1)}, u32[]{:S(2)}, u32[]{:S(2)}) %collective-permute-start) | collective-permute-done | bytes 131104 | tf_op jit(solution)/shard_map/ppermute | solution.py:41
  10.3 1.7 collective-permute-start.1
  12.0 1.5 collective-permute-start.6
  14.1 2.4 %tables.1 = (s32[512,1]{1,0:T(8,128)}, s32[512,1]{1,0:T(8,128)}, s32[512,1]{1,0:T(8,128)}, s32[512,1]{1,0:T(8,128)}, s32[1,1024]{1,0:T(1,128)}, /*index=5*/s32[1,128]{1,0:T(1,128)}, s32[128,1]{1,0:T(8,128)}) custom-call(s32[2]{0:T(128)} %pad_add_fusion.index, s32[1,8]{1,0:T(1,128)} %frames.1, s32[1,8]{1,0:T(1,128)} %texts.1, s32[1,8]{1,0:T(1,128)} %actions.1), custom_call_target="tpu_custom_call" | custom-call | flops 10485 | bytes 10485 | tf_op jit(solution)/shard_map/tables/pallas_call | solution.py:206
  16.8 1.4 collective-permute-done.2
  18.2 1.5 collective-permute-start.3
  20.2 1.6 collective-permute-start.7
  21.8 1.3 collective-permute-done.3
  23.2 1.6 collective-permute-start.8
  24.8 1.5 collective-permute-start.9
  26.2 3.3 %collective-permute-done.7.refs_4_ = bf16[64,2048]{1,0:T(8,128)(2,1)S(1)} collective-permute-done((bf16[64,2048]{1,0:T(8,128)(2,1)S(1)}, bf16[64,2048]{1,0:T(8,128)(2,1)S(1)}, u32[]{:S(2)}, u32[]{:S(2)}) %collective-permute-start.7) | collective-permute-done | bytes 262176 | tf_op jit(solution)/shard_map/ppermute | solution.py:41
  29.5 1.5 collective-permute-start.10
  31.0 1.4 collective-permute-start.11
  32.5 1.5 collective-permute-start.12
  36.3 2.5 %norm_pieces.1 = bf16[8,8,8,2048]{3,2,1,0:T(8,128)(2,1)S(1)} custom-call(s32[1]{0:T(128)} %bitcast.11.refs_0_, bf16[64,2048]{1,0:T(8,128)(2,1)S(1)} %bitcast.46, bf16[64,2048]{1,0:T(8,128)(2,1)S(1)} %collective-permute-done.6.refs_2_, bf16[64,2048]{1,0:T(8,128)(2,1)S(1)} %pad_maximum_fusion.6.refs_3_, bf16[64,2048]{1,0:T(8,128)(2,1)S(1)} %collective-permute-done.7.refs_4_, ...), custom_call_target="tpu_custom_call" | custom-call | flops 104857 | bytes 41943 | tf_op jit(solution)/shard_map/norm_pieces/pallas_call | solution.py:360
  40.9 1.5 collective-permute-start.14
  42.5 2.3 %project_rows.6 = (bf16[512,512]{1,0:T(8,128)(2,1)S(1)}, bf16[512,512]{1,0:T(8,128)(2,1)S(1)}) custom-call(bf16[512,2048]{1,0:T(8,128)(2,1)S(1)} %bitcast.40, bf16[2048,512]{1,0:T(8,128)(2,1)S(1)} %copy-done.1, bf16[2048,512]{1,0:T(8,128)(2,1)S(1)} %copy-done.2), custom_call_target="tpu_custom_call" | custom-call | flops 21474836 | bytes 20971 | tf_op jit(solution)/shard_map/project_rows/pallas_call | solution.py:234
  44.9 2.4 %project_rows.7 = (bf16[512,512]{1,0:T(8,128)(2,1)S(1)}, bf16[512,512]{1,0:T(8,128)(2,1)S(1)}) custom-call(bf16[512,2048]{1,0:T(8,128)(2,1)S(1)} %collective-permute-done.13.refs_0_.refs_1_, bf16[2048,512]{1,0:T(8,128)(2,1)S(1)} %copy-done.1, bf16[2048,512]{1,0:T(8,128)(2,1)S(1)} %copy-done.2), custom_call_target="tpu_custom_call" | custom-call | flops 21474836 | bytes 20971 | tf_op jit(solution)/shard_map/project_rows/pallas_call | solution.py:234
  47.3 1.9 %attend.1.refs_0_ = bf16[128,512]{1,0:T(8,128)(2,1)S(1)} custom-call(bf16[128,512]{1,0:T(8,128)(2,1)S(1)} %project_rows.5.query, bf16[512,512]{1,0:T(8,128)(2,1)S(1)} %get-tuple-element.146.key_a.refs_2_.refs_10_, bf16[512,512]{1,0:T(8,128)(2,1)S(1)} %get-tuple-element.147.key_b.refs_3_.refs_11_, ...), custom_call_target="tpu_custom_call" | custom-call | flops 2684354 | bytes 20971 | tf_op jit(solution)/shard_map/attend/pallas_call | solution.py:833
  49.5 1.9 collective-permute-done.15
  52.0 1.6 collective-permute-start.19
  55.0 3.5 %grad_activated.1 = f32[128,2048]{1,0:T(8,128)S(1)} custom-call(bf16[128,2048]{1,0:T(8,128)(2,1)S(1)} %pad_maximum_fusion.3.grad.refs_7_, bf16[2048,2048]{1,0:T(8,128)(2,1)S(1)} %bitcast.36), custom_call_target="tpu_custom_call" | custom-call | flops 10737418 | bytes 83886 | tf_op jit(solution)/shard_map/grad_activated/pallas_call | solution.py:573
  62.5 1.5 collective-permute-done.18
  64.1 5.5 %feed_own.1 = (bf16[128,2048]{1,0:T(8,128)(2,1)S(1)}, bf16[128,2048]{1,0:T(8,128)(2,1)S(1)}, f32[64,2048]{1,0:T(8,128)S(1)}, bf16[64,2048]{1,0:T(8,128)(2,1)S(1)}) custom-call(bf16[128,2048]{1,0:T(8,128)(2,1)S(1)} %constant_dynamic-update-slice_fusion.lifted.refs_6_, bf16[2048,2048]{1,0:T(8,128)(2,1)S(1)} %bitcast.38, f32[128,2048]{1,0:T(8,128)S(1)} %grad_activated.1), custom_call_target="tpu_custom_call" | custom-call | flops 21474836 | bytes 83886 | tf_op jit(solution)/shard_map/feed_own/pallas_call | solution.py:547
  69.5 2.4 %collective-permute-done.19.refs_6_ = bf16[192,2048]{1,0:T(8,128)(2,1)S(1)} collective-permute-done((bf16[192,2048]{1,0:T(8,128)(2,1)S(1)}, bf16[192,2048]{1,0:T(8,128)(2,1)S(1)}, u32[]{:S(2)}, u32[]{:S(2)}) %collective-permute-start.19) | collective-permute-done | bytes 786464 | tf_op jit(solution)/shard_map/ppermute | solution.py:41
  71.9 1.5 collective-permute-done.20
  74.7 1.9 %collective-permute-start.22 = (bf16[32,2048]{1,0:T(8,128)(2,1)S(1)}, bf16[32,2048]{1,0:T(8,128)(2,1)S(1)}, u32[]{:S(2)}, u32[]{:S(2)}) collective-permute-start(bf16[32,2048]{1,0:T(8,128)(2,1)S(1)} %constant_dynamic-slice_fusion), channel_id=1, source_target_pairs={{0,8},{4,12},{8,0},{12,4},{16,24},{20,28},{24,16},{28,20},{1,9},{5... | collective-permute-start | bytes 393224 | tf_op jit(solution)/shard_map/ppermute | solution.py:41
  77.9 1.4 collective-permute-start.24
  79.3 9.4 %attend_all.1 = (bf16[512,512]{1,0:T(8,128)(2,1)S(1)}, bf16[512,512]{1,0:T(8,128)(2,1)S(1)}, bf16[4,2560,256]{2,1,0:T(8,128)(2,1)}) custom-call(bf16[512,512]{1,0:T(8,128)(2,1)S(1)} %project_rows.8.refs_0_.refs_8_, bf16[512,512]{1,0:T(8,128)(2,1)S(1)} %project_rows.9.refs_1_.refs_9_, bf16[512,512]{1,0:T(8,128)(2,1)S(1)} %get-tuple-element.146.key_a.refs_2_.refs_10_, ...), custom_call_target="tpu_custom_call" | custom-call | flops 21474836 | bytes 41943 | tf_op jit(solution)/shard_map/attend_all/pallas_call | solution.py:925
  91.4 1.5 collective-permute-start.36
  93.8 2.4 %collective-permute-start.27 = (bf16[128,512]{1,0:T(8,128)(2,1)S(1)}, bf16[128,512]{1,0:T(8,128)(2,1)S(1)}, u32[]{:S(2)}, u32[]{:S(2)}) collective-permute-start(bf16[128,512]{1,0:T(8,128)(2,1)S(1)} %product_back.1.refs_0_), channel_id=1, source_target_pairs={{0,8},{4,12},{8,0},{12,4},{16,24},{20,28},{24,16},{28,20},{1,9},{5... | collective-permute-start | bytes 393224 | tf_op jit(solution)/shard_map/ppermute | solution.py:41
  96.2 1.5 collective-permute-start.29
  97.7 1.4 collective-permute-start.31
  99.1 2.0 %down_own.1 = (f32[64,2048]{1,0:T(8,128)S(1)}, bf16[64,2048]{1,0:T(8,128)(2,1)S(1)}) custom-call(bf16[128,2048]{1,0:T(8,128)(2,1)S(1)} %get-tuple-element.182.rows.refs_8_, bf16[2048,2048]{1,0:T(8,128)(2,1)S(1)} %bitcast.36), custom_call_target="tpu_custom_call" | custom-call | flops 10737418 | bytes 83886 | tf_op jit(solution)/shard_map/down_own/pallas_call | solution.py:295
  102.7 6.3 %collective-permute-done.29.refs_4_ = bf16[128,512]{1,0:T(8,128)(2,1)S(1)} collective-permute-done((bf16[128,512]{1,0:T(8,128)(2,1)S(1)}, bf16[128,512]{1,0:T(8,128)(2,1)S(1)}, u32[]{:S(2)}, u32[]{:S(2)}) %collective-permute-start.29) | collective-permute-done | bytes 131104 | tf_op jit(solution)/shard_map/ppermute | solution.py:41
  111.8 1.5 collective-permute-start.26
  113.3 2.1 %collective-permute-done.28.refs_3_ = bf16[128,512]{1,0:T(8,128)(2,1)S(1)} collective-permute-done((bf16[128,512]{1,0:T(8,128)(2,1)S(1)}, bf16[128,512]{1,0:T(8,128)(2,1)S(1)}, u32[]{:S(2)}, u32[]{:S(2)}) %collective-permute-start.28) | collective-permute-done | bytes 131104 | tf_op jit(solution)/shard_map/ppermute | solution.py:41
  115.5 2.0 %collective-permute-start.32 = (bf16[128,512]{1,0:T(8,128)(2,1)S(1)}, bf16[128,512]{1,0:T(8,128)(2,1)S(1)}, u32[]{:S(2)}, u32[]{:S(2)}) collective-permute-start(bf16[128,512]{1,0:T(8,128)(2,1)S(1)} %collective-permute-done.31.refs_6_), channel_id=1, source_target_pairs={{0,4},{4,0},{8,12},{12,8},{16,20},{20,16},{24,28},{28,24},{1,5},{5... | collective-permute-start | bytes 393224 | tf_op jit(solution)/shard_map/ppermute | solution.py:41
  117.5 12.2 %feed_all.2 = (bf16[256,2048]{1,0:T(8,128)(2,1)}, bf16[2048,256]{1,0:T(8,128)(2,1)}) custom-call(s32[1]{0:T(128)} %bitcast.10.index, bf16[192,2048]{1,0:T(8,128)(2,1)S(1)} %constant_dynamic-update-slice_fusion.5.refs_0_, bf16[192,2048]{1,0:T(8,128)(2,1)S(1)} %collective-permute-done.37.refs_1_, bf16[192,2048]{1,0:T(8,128)(2,1)S(1)} %pad_maximum_fusion.refs_2_, ...), custom_call_target="tpu_custom_call" | custom-call | flops 72477576 | bytes 199229 | tf_op jit(solution)/shard_map/feed_all/pallas_call | solution.py:671
  130.0 10.2 %attend_back.1 = (bf16[512,512]{1,0:T(8,128)(2,1)S(1)}, bf16[512,512]{1,0:T(8,128)(2,1)S(1)}, bf16[512,512]{1,0:T(8,128)(2,1)S(1)}, bf16[512,512]{1,0:T(8,128)(2...) custom-call(bf16[128,512]{1,0:T(8,128)(2,1)S(1)} %product_back.1.ref, ...), custom_call_target="tpu_custom_call" | custom-call | flops 42949672 | bytes 136314 | tf_op jit(solution)/shard_map/attend_back/pallas_call | solution.py:1037
  140.2 2.1 %product_halves.3 = (f32[64,2048]{1,0:T(8,128)S(1)}, bf16[64,2048]{1,0:T(8,128)(2,1)S(1)}) custom-call(bf16[128,512]{1,0:T(8,128)(2,1)S(1)} %get-tuple-element.210.refs_0_, bf16[128,512]{1,0:T(8,128)(2,1)S(1)} %get-tuple-element.211.refs_1_, bf16[128,512]{1,0:T(8,128)(2,1)S(1)} %get-tuple-element.212.refs_2_, bf16[2048,512]{1,0:T(8,128)(2,1)S(1)} %copy-done, ...), custom_call_target="tpu_custom_call" | custom-call | flops 8053063 | bytes 62914 | tf_op jit(solution)/shard_map/product_halves/pallas_call | solution.py:270
  142.4 1.5 collective-permute-done.41
  145.1 2.8 %project.1 = (f32[256,512]{1,0:T(8,128)}, f32[256,512]{1,0:T(8,128)}, f32[256,512]{1,0:T(8,128)}, f32[3,256]{1,0:T(4,128)S(1)}) custom-call(s32[1]{0:T(128)} %bitcast.10.index, bf16[512,2048]{1,0:T(8,128)(2,1)S(1)} %bitcast.42, bf16[512,2048]{1,0:T(8,128)(2,1)S(1)} %collective-permute-done.13.refs_0_.refs_1_, ...), custom_call_target="tpu_custom_call" | custom-call | flops 16106127 | bytes 47185 | tf_op jit(solution)/shard_map/project/pallas_call | solution.py:732
  149.0 3.4 %collective-permute-done.42.other = bf16[64,2048]{1,0:T(8,128)(2,1)S(1)} collective-permute-done((bf16[64,2048]{1,0:T(8,128)(2,1)S(1)}, bf16[64,2048]{1,0:T(8,128)(2,1)S(1)}, u32[]{:S(2)}, u32[]{:S(2)}) %collective-permute-start.42) | collective-permute-done | bytes 262176 | tf_op jit(solution)/shard_map/ppermute | solution.py:41
  153.9 6.0 %all-to-all-start = ((bf16[8,72,256]{2,1,0:T(8,128)(2,1)}), bf16[8,72,256]{2,1,0:T(8,128)(2,1)S(1)}, u32[]{:S(2)}, u32[]{:S(2)}) async-start(bf16[8,72,256]{2,1,0:T(8,128)(2,1)} %copy-done.8), calls=%async_computation | async-start | bytes 589824 | tf_op jit(solution)/shard_map/all_to_all | solution.py:1184
  162.9 17.6 %feed_all.3 = (f32[256,2048]{1,0:T(8,128)}, f32[2048,256]{1,0:T(8,128)}) custom-call(s32[1]{0:T(128)} %bitcast.10.index, bf16[64,2048]{1,0:T(8,128)(2,1)S(1)} %copy-done.10, bf16[64,2048]{1,0:T(8,128)(2,1)S(1)} %collective-permute-done.47.refs_1_, bf16[192,2048]{1,0:T(8,128)(2,1)S(1)} %pad_maximum_fusion.1.refs_2_, ...), custom_call_target="tpu_custom_call" | custom-call | flops 96636768 | bytes 209715 | tf_op jit(solution)/shard_map/feed_all/pallas_call | solution.py:671
  (163 shorter events, 37.5 us)
Async XLA Ops:
  2.2 8.1 %collective-permute-start = (bf16[32,2048]{1,0:T(8,128)(2,1)S(1)}, bf16[32,2048]{1,0:T(8,128)(2,1)S(1)}, u32[]{:S(2)}, u32[]{:S(2)}) collective-permute-start(bf16[32,2048]{1,0:T(8,128)(2,1)S(1)} %constant_dynamic-slice_fusion.4), channel_id=1, source_target_pairs={{0,8},{4,12},{8,0},{12,4},{16,24},{20,28},{24,16},{28,20},{1,9},{5... | collective-permute-start | bytes 393224 | tf_op jit(solution)/shard_map/ppermute | solution.py:41
  5.2 12.9 %collective-permute-start.2 = (bf16[32,2048]{1,0:T(8,128)(2,1)S(1)}, bf16[32,2048]{1,0:T(8,128)(2,1)S(1)}, u32[]{:S(2)}, u32[]{:S(2)}) collective-permute-start(bf16[32,2048]{1,0:T(8,128)(2,1)S(1)} %constant_dynamic-slice_fusion.4), channel_id=1, source_target_pairs={{0,16},{4,20},{8,24},{12,28},{16,0},{20,4},{24,8},{28,12},{1,17},{... | collective-permute-start | bytes 393224 | tf_op jit(solution)/shard_map/ppermute | solution.py:41
  7.8 11.8 %collective-permute-start.4 = (bf16[32,2048]{1,0:T(8,128)(2,1)S(1)}, bf16[32,2048]{1,0:T(8,128)(2,1)S(1)}, u32[]{:S(2)}, u32[]{:S(2)}) collective-permute-start(bf16[32,2048]{1,0:T(8,128)(2,1)S(1)} %constant_dynamic-slice_fusion.4), channel_id=1, source_target_pairs={{0,24},{4,28},{8,16},{12,20},{16,8},{20,12},{24,0},{28,4},{1,25},{... | collective-permute-start | bytes 393224 | tf_op jit(solution)/shard_map/ppermute | solution.py:41
  10.3 9.9 %collective-permute-start.1 = (bf16[32,2048]{1,0:T(8,128)(2,1)S(1)}, bf16[32,2048]{1,0:T(8,128)(2,1)S(1)}, u32[]{:S(2)}, u32[]{:S(2)}) collective-permute-start(bf16[32,2048]{1,0:T(8,128)(2,1)S(1)} %collective-permute-done), channel_id=1, source_target_pairs={{0,2},{1,3},{2,0},{3,1},{4,6},{5,7},{6,4},{7,5},{8,10},{9,11},{10,... | collective-permute-start | bytes 393224 | tf_op jit(solution)/shard_map/ppermute | solution.py:41
  12.0 20.5 %collective-permute-start.6 = (bf16[64,2048]{1,0:T(8,128)(2,1)S(1)}, bf16[64,2048]{1,0:T(8,128)(2,1)S(1)}, u32[]{:S(2)}, u32[]{:S(2)}) collective-permute-start(bf16[64,2048]{1,0:T(8,128)(2,1)S(1)} %bitcast.44), channel_id=1, source_target_pairs={{0,4},{4,0},{8,12},{12,8},{16,20},{20,16},{24,28},{28,24},{1,5},{5... | collective-permute-start | bytes 786440 | tf_op jit(solution)/shard_map/ppermute | solution.py:41
  18.2 5.0 %collective-permute-start.3 = (bf16[32,2048]{1,0:T(8,128)(2,1)S(1)}, bf16[32,2048]{1,0:T(8,128)(2,1)S(1)}, u32[]{:S(2)}, u32[]{:S(2)}) collective-permute-start(bf16[32,2048]{1,0:T(8,128)(2,1)S(1)} %collective-permute-done.2), channel_id=1, source_target_pairs={{0,2},{1,3},{2,0},{3,1},{4,6},{5,7},{6,4},{7,5},{8,10},{9,11},{10,... | collective-permute-start | bytes 393224 | tf_op jit(solution)/shard_map/ppermute | solution.py:41
  19.7 5.1 %collective-permute-start.5 = (bf16[32,2048]{1,0:T(8,128)(2,1)S(1)}, bf16[32,2048]{1,0:T(8,128)(2,1)S(1)}, u32[]{:S(2)}, u32[]{:S(2)}) collective-permute-start(bf16[32,2048]{1,0:T(8,128)(2,1)S(1)} %collective-permute-done.4), channel_id=1, source_target_pairs={{0,2},{1,3},{2,0},{3,1},{4,6},{5,7},{6,4},{7,5},{8,10},{9,11},{10,... | collective-permute-start | bytes 393224 | tf_op jit(solution)/shard_map/ppermute | solution.py:41
  20.2 9.3 %collective-permute-start.7 = (bf16[64,2048]{1,0:T(8,128)(2,1)S(1)}, bf16[64,2048]{1,0:T(8,128)(2,1)S(1)}, u32[]{:S(2)}, u32[]{:S(2)}) collective-permute-start(bf16[64,2048]{1,0:T(8,128)(2,1)S(1)} %pad_maximum_fusion.6.refs_3_), channel_id=1, source_target_pairs={{0,4},{4,0},{8,12},{12,8},{16,20},{20,16},{24,28},{28,24},{1,5},{5... | collective-permute-start | bytes 786440 | tf_op jit(solution)/shard_map/ppermute | solution.py:41
  23.2 11.9 %collective-permute-start.8 = (bf16[64,2048]{1,0:T(8,128)(2,1)S(1)}, bf16[64,2048]{1,0:T(8,128)(2,1)S(1)}, u32[]{:S(2)}, u32[]{:S(2)}) collective-permute-start(bf16[64,2048]{1,0:T(8,128)(2,1)S(1)} %pad_maximum_fusion.7.refs_5_), channel_id=1, source_target_pairs={{0,4},{4,0},{8,12},{12,8},{16,20},{20,16},{24,28},{28,24},{1,5},{5... | collective-permute-start | bytes 786440 | tf_op jit(solution)/shard_map/ppermute | solution.py:41
  24.8 11.5 %collective-permute-start.9 = (bf16[64,2048]{1,0:T(8,128)(2,1)S(1)}, bf16[64,2048]{1,0:T(8,128)(2,1)S(1)}, u32[]{:S(2)}, u32[]{:S(2)}) collective-permute-start(bf16[64,2048]{1,0:T(8,128)(2,1)S(1)} %pad_maximum_fusion.8.refs_7_), channel_id=1, source_target_pairs={{0,4},{4,0},{8,12},{12,8},{16,20},{20,16},{24,28},{28,24},{1,5},{5... | collective-permute-start | bytes 786440 | tf_op jit(solution)/shard_map/ppermute | solution.py:41
  29.5 9.3 %collective-permute-start.10 = (bf16[32,2048]{1,0:T(8,128)(2,1)S(1)}, bf16[32,2048]{1,0:T(8,128)(2,1)S(1)}, u32[]{:S(2)}, u32[]{:S(2)}) collective-permute-start(bf16[32,2048]{1,0:T(8,128)(2,1)S(1)} %constant_dynamic-slice_fusion.2), channel_id=1, source_target_pairs={{0,8},{4,12},{8,0},{12,4},{16,24},{20,28},{24,16},{28,20},{1,9},{5... | collective-permute-start | bytes 393224 | tf_op jit(solution)/shard_map/ppermute | solution.py:41
  31.0 8.7 %collective-permute-start.11 = (bf16[32,2048]{1,0:T(8,128)(2,1)S(1)}, bf16[32,2048]{1,0:T(8,128)(2,1)S(1)}, u32[]{:S(2)}, u32[]{:S(2)}) collective-permute-start(bf16[32,2048]{1,0:T(8,128)(2,1)S(1)} %constant_dynamic-slice_fusion.2), channel_id=1, source_target_pairs={{0,16},{4,20},{8,24},{12,28},{16,0},{20,4},{24,8},{28,12},{1,17},{... | collective-permute-start | bytes 393224 | tf_op jit(solution)/shard_map/ppermute | solution.py:41
  32.5 7.2 %collective-permute-start.12 = (bf16[32,2048]{1,0:T(8,128)(2,1)S(1)}, bf16[32,2048]{1,0:T(8,128)(2,1)S(1)}, u32[]{:S(2)}, u32[]{:S(2)}) collective-permute-start(bf16[32,2048]{1,0:T(8,128)(2,1)S(1)} %constant_dynamic-slice_fusion.2), channel_id=1, source_target_pairs={{0,24},{4,28},{8,16},{12,20},{16,8},{20,12},{24,0},{28,4},{1,25},{... | collective-permute-start | bytes 393224 | tf_op jit(solution)/shard_map/ppermute | solution.py:41
  39.7 5.1 %collective-permute-start.13 = (bf16[512,2048]{1,0:T(8,128)(2,1)S(1)}, bf16[512,2048]{1,0:T(8,128)(2,1)S(1)}, u32[]{:S(2)}, u32[]{:S(2)}) collective-permute-start(bf16[512,2048]{1,0:T(8,128)(2,1)S(1)} %bitcast.39), channel_id=1, source_target_pairs={{0,1},{1,0},{2,3},{3,2},{4,5},{5,4},{6,7},{7,6},{8,9},{9,8},{10,11... | collective-permute-start | bytes 6291464 | tf_op jit(solution)/shard_map/ppermute | solution.py:41
  39.8 11.6 %collective-permute-start.15 = (bf16[96,2048]{1,0:T(8,128)(2,1)S(1)}, bf16[96,2048]{1,0:T(8,128)(2,1)S(1)}, u32[]{:S(2)}, u32[]{:S(2)}) collective-permute-start(bf16[96,2048]{1,0:T(8,128)(2,1)S(1)} %pad_maximum_fusion.5), channel_id=1, source_target_pairs={{0,2},{1,3},{2,0},{3,1},{4,6},{5,7},{6,4},{7,5},{8,10},{9,11},{10,... | collective-permute-start | bytes 1179656 | tf_op jit(solution)/shard_map/ppermute | solution.py:41
  40.9 8.5 %collective-permute-start.14 = (bf16[64,2048]{1,0:T(8,128)(2,1)S(1)}, bf16[64,2048]{1,0:T(8,128)(2,1)}, u32[]{:S(2)}, u32[]{:S(2)}) collective-permute-start(bf16[64,2048]{1,0:T(8,128)(2,1)S(1)} %bitcast.52), channel_id=1, source_target_pairs={{0,4},{4,0},{8,12},{12,8},{16,20},{20,16},{24,28},{28,24},{1,5},{5... | collective-permute-start | bytes 786440 | tf_op jit(solution)/shard_map/ppermute | solution.py:41
  52.0 20.0 %collective-permute-start.19 = (bf16[192,2048]{1,0:T(8,128)(2,1)S(1)}, bf16[192,2048]{1,0:T(8,128)(2,1)S(1)}, u32[]{:S(2)}, u32[]{:S(2)}) collective-permute-start(bf16[192,2048]{1,0:T(8,128)(2,1)S(1)} %pad_maximum_fusion.refs_2_), channel_id=1, source_target_pairs={{0,4},{4,0},{8,12},{12,8},{16,20},{20,16},{24,28},{28,24},{1,5},{5... | collective-permute-start | bytes 2359304 | tf_op jit(solution)/shard_map/ppermute | solution.py:41
  53.6 8.4 %collective-permute-start.17 = (bf16[64,2048]{1,0:T(8,128)(2,1)S(1)}, bf16[64,2048]{1,0:T(8,128)(2,1)S(1)}, u32[]{:S(2)}, u32[]{:S(2)}) collective-permute-start(bf16[64,2048]{1,0:T(8,128)(2,1)S(1)} %add_convert_fusion.3.low), channel_id=1, source_target_pairs={{0,2},{1,3},{2,0},{3,1},{4,6},{5,7},{6,4},{7,5},{8,10},{9,11},{10,... | collective-permute-start | bytes 786440 | tf_op jit(solution)/shard_map/ppermute | solution.py:41
  73.5 16.1 %collective-permute-start.21 = (bf16[64,2048]{1,0:T(8,128)(2,1)S(1)}, bf16[64,2048]{1,0:T(8,128)(2,1)S(1)}, u32[]{:S(2)}, u32[]{:S(2)}) collective-permute-start(bf16[64,2048]{1,0:T(8,128)(2,1)S(1)} %add_convert_fusion.2.low), channel_id=1, source_target_pairs={{0,2},{1,3},{2,0},{3,1},{4,6},{5,7},{6,4},{7,5},{8,10},{9,11},{10,... | collective-permute-start | bytes 786440 | tf_op jit(solution)/shard_map/ppermute | solution.py:41
  74.7 14.0 %collective-permute-start.22 = (bf16[32,2048]{1,0:T(8,128)(2,1)S(1)}, bf16[32,2048]{1,0:T(8,128)(2,1)S(1)}, u32[]{:S(2)}, u32[]{:S(2)}) collective-permute-start(bf16[32,2048]{1,0:T(8,128)(2,1)S(1)} %constant_dynamic-slice_fusion), channel_id=1, source_target_pairs={{0,8},{4,12},{8,0},{12,4},{16,24},{20,28},{24,16},{28,20},{1,9},{5... | collective-permute-start | bytes 393224 | tf_op jit(solution)/shard_map/ppermute | solution.py:41
  76.6 12.9 %collective-permute-start.23 = (bf16[32,2048]{1,0:T(8,128)(2,1)S(1)}, bf16[32,2048]{1,0:T(8,128)(2,1)S(1)}, u32[]{:S(2)}, u32[]{:S(2)}) collective-permute-start(bf16[32,2048]{1,0:T(8,128)(2,1)S(1)} %constant_dynamic-slice_fusion), channel_id=1, source_target_pairs={{0,16},{4,20},{8,24},{12,28},{16,0},{20,4},{24,8},{28,12},{1,17},{... | collective-permute-start | bytes 393224 | tf_op jit(solution)/shard_map/ppermute | solution.py:41
  77.9 11.6 %collective-permute-start.24 = (bf16[32,2048]{1,0:T(8,128)(2,1)S(1)}, bf16[32,2048]{1,0:T(8,128)(2,1)S(1)}, u32[]{:S(2)}, u32[]{:S(2)}) collective-permute-start(bf16[32,2048]{1,0:T(8,128)(2,1)S(1)} %constant_dynamic-slice_fusion), channel_id=1, source_target_pairs={{0,24},{4,28},{8,16},{12,20},{16,8},{20,12},{24,0},{28,4},{1,25},{... | collective-permute-start | bytes 393224 | tf_op jit(solution)/shard_map/ppermute | solution.py:41
  90.3 2.6 %collective-permute-start.25 = (bf16[64,2048]{1,0:T(8,128)(2,1)S(1)}, bf16[64,2048]{1,0:T(8,128)(2,1)S(1)}, u32[]{:S(2)}, u32[]{:S(2)}) collective-permute-start(bf16[64,2048]{1,0:T(8,128)(2,1)S(1)} %get-tuple-element.180), channel_id=1, source_target_pairs={{0,1},{1,0},{2,3},{3,2},{4,5},{5,4},{6,7},{7,6},{8,9},{9,8},{10,11... | collective-permute-start | bytes 786440 | tf_op jit(solution)/shard_map/ppermute | solution.py:41
  90.5 11.6 %collective-permute-start.35 = (bf16[96,2048]{1,0:T(8,128)(2,1)S(1)}, bf16[96,2048]{1,0:T(8,128)(2,1)S(1)}, u32[]{:S(2)}, u32[]{:S(2)}) collective-permute-start(bf16[96,2048]{1,0:T(8,128)(2,1)S(1)} %get-tuple-element.260), channel_id=1, source_target_pairs={{0,2},{1,3},{2,0},{3,1},{4,6},{5,7},{6,4},{7,5},{8,10},{9,11},{10,... | collective-permute-start | bytes 1179656 | tf_op jit(solution)/shard_map/ppermute | solution.py:41
  91.4 11.2 %collective-permute-start.36 = (bf16[96,2048]{1,0:T(8,128)(2,1)S(1)}, bf16[96,2048]{1,0:T(8,128)(2,1)S(1)}, u32[]{:S(2)}, u32[]{:S(2)}) collective-permute-start(bf16[96,2048]{1,0:T(8,128)(2,1)S(1)} %get-tuple-element.260), channel_id=1, source_target_pairs={{0,4},{4,0},{8,12},{12,8},{16,20},{20,16},{24,28},{28,24},{1,5},{5... | collective-permute-start | bytes 1179656 | tf_op jit(solution)/shard_map/ppermute | solution.py:41
  93.8 8.8 %collective-permute-start.27 = (bf16[128,512]{1,0:T(8,128)(2,1)S(1)}, bf16[128,512]{1,0:T(8,128)(2,1)S(1)}, u32[]{:S(2)}, u32[]{:S(2)}) collective-permute-start(bf16[128,512]{1,0:T(8,128)(2,1)S(1)} %product_back.1.refs_0_), channel_id=1, source_target_pairs={{0,8},{4,12},{8,0},{12,4},{16,24},{20,28},{24,16},{28,20},{1,9},{5... | collective-permute-start | bytes 393224 | tf_op jit(solution)/shard_map/ppermute | solution.py:41
  96.2 12.8 %collective-permute-start.29 = (bf16[128,512]{1,0:T(8,128)(2,1)S(1)}, bf16[128,512]{1,0:T(8,128)(2,1)S(1)}, u32[]{:S(2)}, u32[]{:S(2)}) collective-permute-start(bf16[128,512]{1,0:T(8,128)(2,1)S(1)} %product_back.1.refs_0_), channel_id=1, source_target_pairs={{0,16},{4,20},{8,24},{12,28},{16,0},{20,4},{24,8},{28,12},{1,17},{... | collective-permute-start | bytes 393224 | tf_op jit(solution)/shard_map/ppermute | solution.py:41
  97.7 11.3 %collective-permute-start.31 = (bf16[128,512]{1,0:T(8,128)(2,1)S(1)}, bf16[128,512]{1,0:T(8,128)(2,1)S(1)}, u32[]{:S(2)}, u32[]{:S(2)}) collective-permute-start(bf16[128,512]{1,0:T(8,128)(2,1)S(1)} %product_back.1.refs_0_), channel_id=1, source_target_pairs={{0,24},{4,28},{8,16},{12,20},{16,8},{20,12},{24,0},{28,4},{1,25},{... | collective-permute-start | bytes 393224 | tf_op jit(solution)/shard_map/ppermute | solution.py:41
  102.0 9.8 %collective-permute-start.38 = (bf16[192,2048]{1,0:T(8,128)(2,1)S(1)}, bf16[192,2048]{1,0:T(8,128)(2,1)S(1)}, u32[]{:S(2)}, u32[]{:S(2)}) collective-permute-start(bf16[192,2048]{1,0:T(8,128)(2,1)S(1)} %pad_maximum_fusion.refs_2_), channel_id=1, source_target_pairs={{0,1},{1,0},{2,3},{3,2},{4,5},{5,4},{6,7},{7,6},{8,9},{9,8},{10,11... | collective-permute-start | bytes 2359304 | tf_op jit(solution)/shard_map/ppermute | solution.py:41
  102.7 8.0 %collective-permute-start.33 = (bf16[64,2048]{1,0:T(8,128)(2,1)S(1)}, bf16[64,2048]{1,0:T(8,128)(2,1)S(1)}, u32[]{:S(2)}, u32[]{:S(2)}) collective-permute-start(bf16[64,2048]{1,0:T(8,128)(2,1)S(1)} %get-tuple-element.184), channel_id=1, source_target_pairs={{0,1},{1,0},{2,3},{3,2},{4,5},{5,4},{6,7},{7,6},{8,9},{9,8},{10,11... | collective-permute-start | bytes 786440 | tf_op jit(solution)/shard_map/ppermute | solution.py:41
  109.0 6.5 %collective-permute-start.37 = (bf16[192,2048]{1,0:T(8,128)(2,1)S(1)}, bf16[192,2048]{1,0:T(8,128)(2,1)S(1)}, u32[]{:S(2)}, u32[]{:S(2)}) collective-permute-start(bf16[192,2048]{1,0:T(8,128)(2,1)S(1)} %constant_dynamic-update-slice_fusion.5.refs_0_), channel_id=1, source_target_pairs={{0,1},{1,0},{2,3},{3,2},{4,5},{5,4},{6,7},{7,6},{8,9},{9,8},{10,11... | collective-permute-start | bytes 2359304 | tf_op jit(solution)/shard_map/ppermute | solution.py:41
  109.1 6.4 %collective-permute-start.28 = (bf16[128,512]{1,0:T(8,128)(2,1)S(1)}, bf16[128,512]{1,0:T(8,128)(2,1)S(1)}, u32[]{:S(2)}, u32[]{:S(2)}) collective-permute-start(bf16[128,512]{1,0:T(8,128)(2,1)S(1)} %collective-permute-done.27.refs_2_), channel_id=1, source_target_pairs={{0,4},{4,0},{8,12},{12,8},{16,20},{20,16},{24,28},{28,24},{1,5},{5... | collective-permute-start | bytes 393224 | tf_op jit(solution)/shard_map/ppermute | solution.py:41
  109.7 30.5 %collective-permute-start.40 = (bf16[96,2048]{1,0:T(8,128)(2,1)S(1)}, bf16[96,2048]{1,0:T(8,128)(2,1)S(1)}, u32[]{:S(2)}, u32[]{:S(2)}) collective-permute-start(bf16[96,2048]{1,0:T(8,128)(2,1)S(1)} %collective-permute-done.36), channel_id=1, source_target_pairs={{0,2},{1,3},{2,0},{3,1},{4,6},{5,7},{6,4},{7,5},{8,10},{9,11},{10,... | collective-permute-start | bytes 1179656 | tf_op jit(solution)/shard_map/ppermute | solution.py:41
  110.7 19.1 %collective-permute-start.34 = (bf16[64,2048]{1,0:T(8,128)(2,1)S(1)}, bf16[64,2048]{1,0:T(8,128)(2,1)S(1)}, u32[]{:S(2)}, u32[]{:S(2)}) collective-permute-start(bf16[64,2048]{1,0:T(8,128)(2,1)S(1)} %add_convert_fusion.1.low), channel_id=1, source_target_pairs={{0,2},{1,3},{2,0},{3,1},{4,6},{5,7},{6,4},{7,5},{8,10},{9,11},{10,... | collective-permute-start | bytes 786440 | tf_op jit(solution)/shard_map/ppermute | solution.py:41
  111.8 17.9 %collective-permute-start.26 = (bf16[128,512]{1,0:T(8,128)(2,1)S(1)}, bf16[128,512]{1,0:T(8,128)(2,1)S(1)}, u32[]{:S(2)}, u32[]{:S(2)}) collective-permute-start(bf16[128,512]{1,0:T(8,128)(2,1)S(1)} %product_back.1.refs_0_), channel_id=1, source_target_pairs={{0,4},{4,0},{8,12},{12,8},{16,20},{20,16},{24,28},{28,24},{1,5},{5... | collective-permute-start | bytes 393224 | tf_op jit(solution)/shard_map/ppermute | solution.py:41
  115.5 14.3 %collective-permute-start.30 = (bf16[128,512]{1,0:T(8,128)(2,1)S(1)}, bf16[128,512]{1,0:T(8,128)(2,1)S(1)}, u32[]{:S(2)}, u32[]{:S(2)}) collective-permute-start(bf16[128,512]{1,0:T(8,128)(2,1)S(1)} %collective-permute-done.29.refs_4_), channel_id=1, source_target_pairs={{0,4},{4,0},{8,12},{12,8},{16,20},{20,16},{24,28},{28,24},{1,5},{5... | collective-permute-start | bytes 393224 | tf_op jit(solution)/shard_map/ppermute | solution.py:41
  115.5 14.3 %collective-permute-start.32 = (bf16[128,512]{1,0:T(8,128)(2,1)S(1)}, bf16[128,512]{1,0:T(8,128)(2,1)S(1)}, u32[]{:S(2)}, u32[]{:S(2)}) collective-permute-start(bf16[128,512]{1,0:T(8,128)(2,1)S(1)} %collective-permute-done.31.refs_6_), channel_id=1, source_target_pairs={{0,4},{4,0},{8,12},{12,8},{16,20},{20,16},{24,28},{28,24},{1,5},{5... | collective-permute-start | bytes 393224 | tf_op jit(solution)/shard_map/ppermute | solution.py:41
  129.8 10.4 %collective-permute-start.39 = (bf16[64,2048]{1,0:T(8,128)(2,1)S(1)}, bf16[64,2048]{1,0:T(8,128)(2,1)S(1)}, u32[]{:S(2)}, u32[]{:S(2)}) collective-permute-start(bf16[64,2048]{1,0:T(8,128)(2,1)S(1)} %get-tuple-element.208), channel_id=1, source_target_pairs={{0,4},{4,0},{8,12},{12,8},{16,20},{20,16},{24,28},{28,24},{1,5},{5... | collective-permute-start | bytes 786440 | tf_op jit(solution)/shard_map/ppermute | solution.py:41
  144.0 8.4 %collective-permute-start.42 = (bf16[64,2048]{1,0:T(8,128)(2,1)S(1)}, bf16[64,2048]{1,0:T(8,128)(2,1)S(1)}, u32[]{:S(2)}, u32[]{:S(2)}) collective-permute-start(bf16[64,2048]{1,0:T(8,128)(2,1)S(1)} %add_convert_fusion.low), channel_id=1, source_target_pairs={{0,2},{1,3},{2,0},{3,1},{4,6},{5,7},{6,4},{7,5},{8,10},{9,11},{10,... | collective-permute-start | bytes 786440 | tf_op jit(solution)/shard_map/ppermute | solution.py:41
  152.4 9.2 %collective-permute-start.48 = (bf16[192,2048]{1,0:T(8,128)(2,1)S(1)}, bf16[192,2048]{1,0:T(8,128)(2,1)}, u32[]{:S(2)}, u32[]{:S(2)}) collective-permute-start(bf16[192,2048]{1,0:T(8,128)(2,1)S(1)} %pad_maximum_fusion.1.refs_2_), channel_id=1, source_target_pairs={{0,1},{1,0},{2,3},{3,2},{4,5},{5,4},{6,7},{7,6},{8,9},{9,8},{10,11... | collective-permute-start | bytes 2359304 | tf_op jit(solution)/shard_map/ppermute | solution.py:41
  152.4 9.6 %collective-permute-start.50 = (bf16[192,2048]{1,0:T(8,128)(2,1)S(1)}, bf16[192,2048]{1,0:T(8,128)(2,1)}, u32[]{:S(2)}, u32[]{:S(2)}) collective-permute-start(bf16[192,2048]{1,0:T(8,128)(2,1)S(1)} %collective-permute-done.19.refs_6_), channel_id=1, source_target_pairs={{0,1},{1,0},{2,3},{3,2},{4,5},{5,4},{6,7},{7,6},{8,9},{9,8},{10,11... | collective-permute-start | bytes 2359304 | tf_op jit(solution)/shard_map/ppermute | solution.py:41
  153.9 26.7 %all-to-all-start = ((bf16[8,72,256]{2,1,0:T(8,128)(2,1)}), bf16[8,72,256]{2,1,0:T(8,128)(2,1)S(1)}, u32[]{:S(2)}, u32[]{:S(2)}) async-start(bf16[8,72,256]{2,1,0:T(8,128)(2,1)} %copy-done.8), calls=%async_computation | async-start | bytes 589824 | tf_op jit(solution)/shard_map/all_to_all | solution.py:1184
  159.9 1.7 collective-permute-start.47
  159.9 2.1 %collective-permute-start.49 = (bf16[64,2048]{1,0:T(8,128)(2,1)}, bf16[64,2048]{1,0:T(8,128)(2,1)S(1)}, u32[]{:S(2)}, u32[]{:S(2)}) collective-permute-start(bf16[64,2048]{1,0:T(8,128)(2,1)} %collective-permute-done.14.refs_4_), channel_id=1, source_target_pairs={{0,1},{1,0},{2,3},{3,2},{4,5},{5,4},{6,7},{7,6},{8,9},{9,8},{10,11... | collective-permute-start | bytes 786440 | tf_op jit(solution)/shard_map/ppermute | solution.py:41
  180.6 4.9 %collective-permute-start.51 = (bf16[8,72,256]{2,1,0:T(8,128)(2,1)S(1)}, bf16[8,72,256]{2,1,0:T(8,128)(2,1)S(1)}, u32[]{:S(2)}, u32[]{:S(2)}) collective-permute-start(bf16[8,72,256]{2,1,0:T(8,128)(2,1)S(1)} %all-to-all-done.came_a), channel_id=1, source_target_pairs={{0,1},{1,0},{2,3},{3,2},{4,5},{5,4},{6,7},{7,6},{8,9},{9,8},{10,11... | collective-permute-start | bytes 884744 | tf_op jit(solution)/shard_map/ppermute | solution.py:41
  180.8 1.8 collective-permute-start.45
  181.2 2.3 %collective-permute-start.44 = (bf16[64,2048]{1,0:T(8,128)(2,1)S(1)}, bf16[64,2048]{1,0:T(8,128)(2,1)S(1)}, u32[]{:S(2)}, u32[]{:S(2)}) collective-permute-start(bf16[64,2048]{1,0:T(8,128)(2,1)S(1)} %finish.1.mine), channel_id=1, source_target_pairs={{0,1},{1,0},{2,3},{3,2},{4,5},{5,4},{6,7},{7,6},{8,9},{9,8},{10,11... | collective-permute-start | bytes 786440 | tf_op jit(solution)/shard_map/ppermute | solution.py:41
  181.3 3.6 %collective-permute-start.46 = (f32[3,256]{1,0:T(4,128)S(1)}, f32[3,256]{1,0:T(4,128)S(1)}, u32[]{:S(2)}, u32[]{:S(2)}) collective-permute-start(f32[3,256]{1,0:T(4,128)S(1)} %add.49), channel_id=1, source_target_pairs={{0,2},{1,3},{2,0},{3,1},{4,6},{5,7},{6,4},{7,5},{8,10},{9,11},{10,... | collective-permute-start | bytes 9224 | tf_op jit(solution)/shard_map/ppermute | solution.py:41
  (27 other events, 197.9 us)

commit v5 on v4

--- a/solution.py
+++ b/solution.py
@@ -469,24 +469,25 @@
     )(residual, low, other)
 
 
-def place_kernel(index, mine, other, out):
-    half = mine.shape[0]
-    out[pl.ds(pl.multiple_of(index[0] * half, half), half), :] = mine[...]
-    out[pl.ds(pl.multiple_of((1 - index[0]) * half, half), half), :] = other[...]
-
-
-def place_halves(mine):
-    half, width = mine.shape
+def place_kernel(index, *refs):
+    count = len(refs) // 3
+    for mine, other, out in zip(refs[:count], refs[count : 2 * count], refs[2 * count :]):
+        half = mine.shape[0]
+        out[pl.ds(pl.multiple_of(index[0] * half, half), half), :] = mine[...]
+        out[pl.ds(pl.multiple_of((1 - index[0]) * half, half), half), :] = other[...]
+
+
+def place_halves(arrays, others):
+    half, width = arrays[0].shape
     index = (lax.axis_index("mlp") % 2).astype(jnp.int32).reshape(1)
     return pl.pallas_call(
         place_kernel,
-        in_specs=[pl.BlockSpec(memory_space=pltpu.SMEM)]
-        + [pl.BlockSpec(memory_space=pltpu.VMEM)] * 2,
-        out_shape=jax.ShapeDtypeStruct((2 * half, width), bf16),
-        compiler_params=params(4),
-        cost_estimate=cost(mine.size, 8 * mine.size),
+        in_specs=[pl.BlockSpec(memory_space=pltpu.SMEM)] + [WHOLE] * (2 * len(arrays)),
+        out_shape=[jax.ShapeDtypeStruct((2 * half, width), bf16)] * len(arrays),
+        compiler_params=params(6),
+        cost_estimate=cost(half * width, 16 * half * width),
         name="place_halves",
-    )(index, mine, swap(mine, "mlp", 1))
+    )(index, *arrays, *others)
 
 
 def last_kernel(rows, low, other, grad_residual, gain, kind, out, *, shards):
@@ -581,29 +582,20 @@
     )(grad, down)
 
 
-def all_kernel(index, *refs, counts):
-    count = len(counts)
+def all_kernel(index, *refs, count):
     lifted_parts, grad_parts = refs[:count], refs[count : 2 * count]
     up, down = refs[2 * count : 2 * count + 2]
-    before = refs[2 * count + 2 : -8]
-    up_grad, down_grad, lifted, grad, lifted_across, hidden_kept, grad_kept, sems = refs[-8:]
+    before = refs[2 * count + 2 : -5]
+    up_grad, down_grad, lifted_across, hidden_kept, grad_kept = refs[-5:]
     part = up_grad.shape[0]
     mine = pl.ds(pl.multiple_of(index[0] * part, part), part)
 
+    def rows_of(parts, at):
+        return jnp.concatenate([ref[:, at] for ref in parts], axis=0)
+
     @pl.when(pl.program_id(0) == 0)
     def _():
-        copies = []
-        for k, (source, target) in enumerate(((lifted_parts, lifted), (grad_parts, grad))):
-            start = 0
-            for j, rows in enumerate(counts):
-                here = target.at[pl.ds(start, rows)]
-                copies.append(pltpu.make_async_copy(source[j], here, sems.at[k * count + j]))
-                start += rows
-        for copy in copies:
-            copy.start()
-        for copy in copies:
-            copy.wait()
-        lifted_across[...] = lifted[:, mine].T
+        lifted_across[...] = rows_of(lifted_parts, mine).T
 
     first = pl.program_id(0) == 0
     last_step = pl.num_programs(0) - 1
@@ -613,12 +605,16 @@
     here = pl.ds(pl.multiple_of(at * tile, tile), tile)
 
     def products():
-        return dot(lifted[...], up[:, here], NN), dot(grad[...], down[here, :], NT)
+        everything = slice(None)
+        return (
+            dot(rows_of(lifted_parts, everything), up[:, here], NN),
+            dot(rows_of(grad_parts, everything), down[here, :], NT),
+        )
 
     def finish_tile(hidden_value, activated_grad):
         value, slope = gelu_parts(hidden_value)
         hidden_grad = (activated_grad * slope).astype(bf16)
-        down_term = dot(value.astype(bf16), grad[:, mine], TN)
+        down_term = dot(value.astype(bf16), rows_of(grad_parts, mine), TN)
         up_term = dot(lifted_across[...], hidden_grad, NN)
         if len(before) == 2:
             up_term += before[0][...].astype(f32)
@@ -659,7 +655,6 @@
     across = lambda t, index: (0, jnp.maximum(t - 1, 0))
     below = lambda t, index: (jnp.maximum(t - 1, 0), 0)
     mine = lambda t, index: (0, index[0])
-    anywhere = pl.BlockSpec(memory_space=pl.ANY)
     sum_specs = [pl.BlockSpec((part, tile), across), pl.BlockSpec((tile, part), below)]
     if own:
         own_rows = own[0].shape[0]
@@ -669,11 +664,11 @@
         more = sum_specs
     index = lax.axis_index("seq").astype(jnp.int32).reshape(1)
     return pl.pallas_call(
-        partial(all_kernel, counts=counts),
+        partial(all_kernel, count=count),
         grid_spec=pltpu.PrefetchScalarGridSpec(
             num_scalar_prefetch=1,
             grid=(steps + 1,),
-            in_specs=[anywhere] * (2 * count)
+            in_specs=[WHOLE] * (2 * count)
             + (
                 [WHOLE] * 2
                 if own
@@ -681,10 +676,8 @@
             )
             + more,
             out_specs=sum_specs,
-            scratch_shapes=[pltpu.VMEM((rows, width), bf16)] * 2
-            + [pltpu.VMEM((part, rows), bf16)]
-            + [pltpu.VMEM((rows, tile), f32)] * 2
-            + [pltpu.SemaphoreType.DMA((2 * count,))],
+            scratch_shapes=[pltpu.VMEM((part, rows), bf16)]
+            + [pltpu.VMEM((rows, tile), f32)] * 2,
         ),
         out_shape=[
             pltpu.HBM((part, hidden), bf16 if own else f32),
@@ -946,6 +939,9 @@
     return outs[:2], outs[2]
 
 
+STEP = 2
+
+
 def backward_kernel(*refs, count, groups, scale):
     grad_pieces = refs[:count]
     query_a, query_b, key_a, key_b, value_a, value_b, attended_a, attended_b, stored = refs[
@@ -998,22 +994,23 @@
             )
 
         keys_across = take(key_a, key_b, 0, blocks, cut).T
-        ones = jnp.ones((8, HEAD_DIM), f32)
+        ones = jnp.ones((8, HEAD_DIM), bf16)
         for index, (seen, _, start) in enumerate(reach):
             result = take(attended_a, attended_b, index, index + 1, cut)
             grad = take_grads(index)
-            delta = lax.dot_general(
-                ones,
-                grad.astype(f32) * result.astype(f32),
-                (NT, ((), ())),
-                precision=lax.Precision.HIGHEST,
-                preferred_element_type=f32,
-            )[0:1, :]
-            at = pl.ds(start * pair, seen * pair)
-            grad_prob = dot(take(value_a, value_b, 0, seen, cut), grad, NT)
-            score = (stored[head, at, :].astype(f32) * (grad_prob - delta)).astype(bf16)
-            scores[at, :] = score
-            back = dot(keys_across[:, : seen * pair], score, NN)
+            product = grad.astype(f32) * result.astype(f32)
+            high = product.astype(bf16)
+            low = (product - high.astype(f32)).astype(bf16)
+            delta = (dot(ones, high, NT) + dot(ones, low, NT))[0:1, :]
+            back = 0.0
+            for low_block in range(0, seen, STEP):
+                high_block = min(low_block + STEP, seen)
+                at = pl.ds((start + low_block) * pair, (high_block - low_block) * pair)
+                values = take(value_a, value_b, low_block, high_block, cut)
+                score = stored[head, at, :].astype(f32) * (dot(values, grad, NT) - delta)
+                score = score.astype(bf16)
+                scores[at, :] = score
+                back += dot(keys_across[:, low_block * pair : high_block * pair], score, NN)
             keep(grad_query, own_query, (back * scale).T.astype(bf16), index)
         for index in range(blocks):
             key_sum, value_sum = 0.0, 0.0
@@ -1194,8 +1191,8 @@
         came = after(swap(first_gain_grad, "mlp", bit), up_grad)
         first_gain_grad = first_gain_grad + came
         bit *= 2
-    input_grad = place_halves(input_half)
-    outputs = place_halves(outputs_half)
+    placed = (input_half, outputs_half)
+    input_grad, outputs = place_halves(placed, [swap(array, "mlp", 1) for array in placed])
     mixed_part = after(mixed_part, up_grad)
     output_grad, second_gain_grad = output_part(
         attended, (mixed_part, swap(mixed_part, "mlp", 1)), groups

time: 187 us -> 185 us (0.989)
  Pallas kernels: 86.4 us -> 83.4 us
  transfers between devices with their start and end apart: 53 -> 53, of which waited for: 24 -> 25; matrix products, arithmetic and copies ran while one was open for 1% -> 1% of each run, Pallas kernels for 44% -> 43%
where the time goes in v5:
time: 185 us; the launch traced here: 184 us
  Pallas kernels  83.4 us (45%)
  starting transfers between devices  55.1 us (30%)
  waiting for transfers between devices  39.7 us (21%)
  local copies, waits for them, and re-layouts  3.1 us (2%)
    ppermute x52, starting transfers between devices, swap(): return lax.ppermute(value, axis, [(i, i ^ bit) for i in range(size)])  49.1 us
    ppermute x52, waiting for transfers between devices, swap(): return lax.ppermute(value, axis, [(i, i ^ bit) for i in range(size)])  39.7 us
    pallas_call x2, Pallas kernels, feed_all(): pl.pallas_call(partial(all_kernel, count=count), grid_spec=pltpu.Prefetch...  29.1 us
    pallas_call x1, Pallas kernels, attend_all(): pl.pallas_call(partial(all_forward_kernel, groups=groups, scale=1.0 / mat...  9.36 us
    pallas_call x1, Pallas kernels, attend_back(): pl.pallas_call(partial(backward_kernel, count=count, groups=groups, scale...  8.58 us
    pallas_call x5, Pallas kernels, project_rows(): pl.pallas_call(partial(rows_kernel, count=len(weights)), out_shape=[jax.S...  7.64 us
    all_to_all x1, starting transfers between devices, body(): lax.all_to_all(after(mixed_columns, outputs_half), 'seq', split_axis=0, c...  6.02 us
    pallas_call x1, Pallas kernels, feed_own(): pl.pallas_call(own_kernel, in_specs=[WHOLE] * 3, out_specs=[WHOLE] * 4, o...  5.46 us
  transfers between devices with their start and end apart: 53, of which 25 were waited for; matrix products, arithmetic and copies ran while one was open for 1% of the time, Pallas kernels for 43%

profile of v5, /device:TPU:0, one launch (start us, length us, event | category | flops | bytes accessed | tf_op | source)
XLA Modules:
  0.0 184.4 jit_solution(15989549636139951192)
XLA Ops:
  2.2 3.1 %collective-permute-start = (bf16[32,2048]{1,0:T(8,128)(2,1)S(1)}, bf16[32,2048]{1,0:T(8,128)(2,1)S(1)}, u32[]{:S(2)}, u32[]{:S(2)}) collective-permute-start(bf16[32,2048]{1,0:T(8,128)(2,1)S(1)} %constant_dynamic-slice_fusion.4), channel_id=1, source_target_pairs={{0,8},{4,12},{8,0},{12,4},{16,24},{20,28},{24,16},{28,20},{1,9},{5... | collective-permute-start | bytes 393224 | tf_op jit(solution)/shard_map/ppermute | solution.py:41
  5.2 2.6 %collective-permute-start.2 = (bf16[32,2048]{1,0:T(8,128)(2,1)S(1)}, bf16[32,2048]{1,0:T(8,128)(2,1)S(1)}, u32[]{:S(2)}, u32[]{:S(2)}) collective-permute-start(bf16[32,2048]{1,0:T(8,128)(2,1)S(1)} %constant_dynamic-slice_fusion.4), channel_id=1, source_target_pairs={{0,16},{4,20},{8,24},{12,28},{16,0},{20,4},{24,8},{28,12},{1,17},{... | collective-permute-start | bytes 393224 | tf_op jit(solution)/shard_map/ppermute | solution.py:41
  7.8 2.4 %collective-permute-done = bf16[32,2048]{1,0:T(8,128)(2,1)S(1)} collective-permute-done((bf16[32,2048]{1,0:T(8,128)(2,1)S(1)}, bf16[32,2048]{1,0:T(8,128)(2,1)S(1)}, u32[]{:S(2)}, u32[]{:S(2)}) %collective-permute-start) | collective-permute-done | bytes 131104 | tf_op jit(solution)/shard_map/ppermute | solution.py:41
  10.3 1.7 collective-permute-start.1
  12.0 1.5 collective-permute-start.6
  14.1 2.4 %tables.1 = (s32[512,1]{1,0:T(8,128)}, s32[512,1]{1,0:T(8,128)}, s32[512,1]{1,0:T(8,128)}, s32[512,1]{1,0:T(8,128)}, s32[1,1024]{1,0:T(1,128)}, /*index=5*/s32[1,128]{1,0:T(1,128)}, s32[128,1]{1,0:T(8,128)}) custom-call(s32[2]{0:T(128)} %pad_add_fusion.index, s32[1,8]{1,0:T(1,128)} %frames.1, s32[1,8]{1,0:T(1,128)} %texts.1, s32[1,8]{1,0:T(1,128)} %actions.1), custom_call_target="tpu_custom_call" | custom-call | flops 10485 | bytes 10485 | tf_op jit(solution)/shard_map/tables/pallas_call | solution.py:206
  16.8 1.4 collective-permute-done.2
  18.2 1.5 collective-permute-start.3
  20.2 1.6 collective-permute-start.7
  21.8 1.3 collective-permute-done.3
  23.2 1.6 collective-permute-start.8
  24.8 1.5 collective-permute-start.9
  26.2 3.3 %collective-permute-done.7.refs_4_ = bf16[64,2048]{1,0:T(8,128)(2,1)S(1)} collective-permute-done((bf16[64,2048]{1,0:T(8,128)(2,1)S(1)}, bf16[64,2048]{1,0:T(8,128)(2,1)S(1)}, u32[]{:S(2)}, u32[]{:S(2)}) %collective-permute-start.7) | collective-permute-done | bytes 262176 | tf_op jit(solution)/shard_map/ppermute | solution.py:41
  29.5 1.5 collective-permute-start.10
  31.0 1.4 collective-permute-start.11
  32.5 1.5 collective-permute-start.12
  36.3 2.5 %norm_pieces.1 = bf16[8,8,8,2048]{3,2,1,0:T(8,128)(2,1)S(1)} custom-call(s32[1]{0:T(128)} %bitcast.11.refs_0_, bf16[64,2048]{1,0:T(8,128)(2,1)S(1)} %bitcast.46, bf16[64,2048]{1,0:T(8,128)(2,1)S(1)} %collective-permute-done.6.refs_2_, bf16[64,2048]{1,0:T(8,128)(2,1)S(1)} %pad_maximum_fusion.6.refs_3_, bf16[64,2048]{1,0:T(8,128)(2,1)S(1)} %collective-permute-done.7.refs_4_, ...), custom_call_target="tpu_custom_call" | custom-call | flops 104857 | bytes 41943 | tf_op jit(solution)/shard_map/norm_pieces/pallas_call | solution.py:360
  40.9 1.5 collective-permute-start.14
  42.5 2.3 %project_rows.6 = (bf16[512,512]{1,0:T(8,128)(2,1)S(1)}, bf16[512,512]{1,0:T(8,128)(2,1)S(1)}) custom-call(bf16[512,2048]{1,0:T(8,128)(2,1)S(1)} %bitcast.40, bf16[2048,512]{1,0:T(8,128)(2,1)S(1)} %copy-done.1, bf16[2048,512]{1,0:T(8,128)(2,1)S(1)} %copy-done.2), custom_call_target="tpu_custom_call" | custom-call | flops 21474836 | bytes 20971 | tf_op jit(solution)/shard_map/project_rows/pallas_call | solution.py:234
  44.9 2.4 %project_rows.7 = (bf16[512,512]{1,0:T(8,128)(2,1)S(1)}, bf16[512,512]{1,0:T(8,128)(2,1)S(1)}) custom-call(bf16[512,2048]{1,0:T(8,128)(2,1)S(1)} %collective-permute-done.13.refs_0_.refs_1_, bf16[2048,512]{1,0:T(8,128)(2,1)S(1)} %copy-done.1, bf16[2048,512]{1,0:T(8,128)(2,1)S(1)} %copy-done.2), custom_call_target="tpu_custom_call" | custom-call | flops 21474836 | bytes 20971 | tf_op jit(solution)/shard_map/project_rows/pallas_call | solution.py:234
  47.3 1.9 %attend.1.refs_0_ = bf16[128,512]{1,0:T(8,128)(2,1)S(1)} custom-call(bf16[128,512]{1,0:T(8,128)(2,1)S(1)} %project_rows.5.query, bf16[512,512]{1,0:T(8,128)(2,1)S(1)} %get-tuple-element.148.key_a.refs_2_.refs_10_, bf16[512,512]{1,0:T(8,128)(2,1)S(1)} %get-tuple-element.149.key_b.refs_3_.refs_11_, ...), custom_call_target="tpu_custom_call" | custom-call | flops 2684354 | bytes 20971 | tf_op jit(solution)/shard_map/attend/pallas_call | solution.py:826
  49.5 1.9 %collective-permute-done.15 = bf16[96,2048]{1,0:T(8,128)(2,1)S(1)} collective-permute-done((bf16[96,2048]{1,0:T(8,128)(2,1)S(1)}, bf16[96,2048]{1,0:T(8,128)(2,1)S(1)}, u32[]{:S(2)}, u32[]{:S(2)}) %collective-permute-start.15) | collective-permute-done | bytes 393248 | tf_op jit(solution)/shard_map/ppermute | solution.py:41
  52.0 1.6 collective-permute-start.19
  55.0 3.5 %grad_activated.1 = f32[128,2048]{1,0:T(8,128)S(1)} custom-call(bf16[128,2048]{1,0:T(8,128)(2,1)S(1)} %pad_maximum_fusion.3.grad.refs_7_, bf16[2048,2048]{1,0:T(8,128)(2,1)S(1)} %bitcast.36), custom_call_target="tpu_custom_call" | custom-call | flops 10737418 | bytes 83886 | tf_op jit(solution)/shard_map/grad_activated/pallas_call | solution.py:574
  62.5 1.5 collective-permute-done.18
  64.1 5.5 %feed_own.1 = (bf16[128,2048]{1,0:T(8,128)(2,1)S(1)}, bf16[128,2048]{1,0:T(8,128)(2,1)S(1)}, f32[64,2048]{1,0:T(8,128)S(1)}, bf16[64,2048]{1,0:T(8,128)(2,1)S(1)}) custom-call(bf16[128,2048]{1,0:T(8,128)(2,1)S(1)} %constant_dynamic-update-slice_fusion.lifted.refs_6_, bf16[2048,2048]{1,0:T(8,128)(2,1)S(1)} %bitcast.38, f32[128,2048]{1,0:T(8,128)S(1)} %grad_activated.1), custom_call_target="tpu_custom_call" | custom-call | flops 21474836 | bytes 83886 | tf_op jit(solution)/shard_map/feed_own/pallas_call | solution.py:548
  69.5 2.4 %collective-permute-done.19.refs_6_ = bf16[192,2048]{1,0:T(8,128)(2,1)S(1)} collective-permute-done((bf16[192,2048]{1,0:T(8,128)(2,1)S(1)}, bf16[192,2048]{1,0:T(8,128)(2,1)S(1)}, u32[]{:S(2)}, u32[]{:S(2)}) %collective-permute-start.19) | collective-permute-done | bytes 786464 | tf_op jit(solution)/shard_map/ppermute | solution.py:41
  71.9 1.5 collective-permute-done.20
  74.7 1.9 %collective-permute-start.22 = (bf16[32,2048]{1,0:T(8,128)(2,1)S(1)}, bf16[32,2048]{1,0:T(8,128)(2,1)S(1)}, u32[]{:S(2)}, u32[]{:S(2)}) collective-permute-start(bf16[32,2048]{1,0:T(8,128)(2,1)S(1)} %constant_dynamic-slice_fusion), channel_id=1, source_target_pairs={{0,8},{4,12},{8,0},{12,4},{16,24},{20,28},{24,16},{28,20},{1,9},{5... | collective-permute-start | bytes 393224 | tf_op jit(solution)/shard_map/ppermute | solution.py:41
  77.9 1.4 collective-permute-start.24
  79.3 9.4 %attend_all.1 = (bf16[512,512]{1,0:T(8,128)(2,1)S(1)}, bf16[512,512]{1,0:T(8,128)(2,1)S(1)}, bf16[4,2560,256]{2,1,0:T(8,128)(2,1)}) custom-call(bf16[512,512]{1,0:T(8,128)(2,1)S(1)} %project_rows.8.refs_0_.refs_8_, bf16[512,512]{1,0:T(8,128)(2,1)S(1)} %project_rows.9.refs_1_.refs_9_, bf16[512,512]{1,0:T(8,128)(2,1)S(1)} %get-tuple-element.148.key_a.refs_2_.refs_10_, ...), custom_call_target="tpu_custom_call" | custom-call | flops 21474836 | bytes 41943 | tf_op jit(solution)/shard_map/attend_all/pallas_call | solution.py:918
  91.4 1.5 collective-permute-start.36
  93.8 2.4 %collective-permute-start.27 = (bf16[128,512]{1,0:T(8,128)(2,1)S(1)}, bf16[128,512]{1,0:T(8,128)(2,1)S(1)}, u32[]{:S(2)}, u32[]{:S(2)}) collective-permute-start(bf16[128,512]{1,0:T(8,128)(2,1)S(1)} %product_back.1.refs_0_), channel_id=1, source_target_pairs={{0,8},{4,12},{8,0},{12,4},{16,24},{20,28},{24,16},{28,20},{1,9},{5... | collective-permute-start | bytes 393224 | tf_op jit(solution)/shard_map/ppermute | solution.py:41
  96.2 1.5 collective-permute-start.29
  97.7 1.4 collective-permute-start.31
  99.1 2.0 %down_own.1 = (f32[64,2048]{1,0:T(8,128)S(1)}, bf16[64,2048]{1,0:T(8,128)(2,1)S(1)}) custom-call(bf16[128,2048]{1,0:T(8,128)(2,1)S(1)} %get-tuple-element.184.rows.refs_8_, bf16[2048,2048]{1,0:T(8,128)(2,1)S(1)} %bitcast.36), custom_call_target="tpu_custom_call" | custom-call | flops 10737418 | bytes 83886 | tf_op jit(solution)/shard_map/down_own/pallas_call | solution.py:295
  102.7 6.3 %collective-permute-done.29.refs_4_ = bf16[128,512]{1,0:T(8,128)(2,1)S(1)} collective-permute-done((bf16[128,512]{1,0:T(8,128)(2,1)S(1)}, bf16[128,512]{1,0:T(8,128)(2,1)S(1)}, u32[]{:S(2)}, u32[]{:S(2)}) %collective-permute-start.29) | collective-permute-done | bytes 131104 | tf_op jit(solution)/shard_map/ppermute | solution.py:41
  111.8 1.5 collective-permute-start.26
  113.3 2.1 %collective-permute-done.28.refs_3_ = bf16[128,512]{1,0:T(8,128)(2,1)S(1)} collective-permute-done((bf16[128,512]{1,0:T(8,128)(2,1)S(1)}, bf16[128,512]{1,0:T(8,128)(2,1)S(1)}, u32[]{:S(2)}, u32[]{:S(2)}) %collective-permute-start.28) | collective-permute-done | bytes 131104 | tf_op jit(solution)/shard_map/ppermute | solution.py:41
  115.5 2.0 %collective-permute-start.32 = (bf16[128,512]{1,0:T(8,128)(2,1)S(1)}, bf16[128,512]{1,0:T(8,128)(2,1)S(1)}, u32[]{:S(2)}, u32[]{:S(2)}) collective-permute-start(bf16[128,512]{1,0:T(8,128)(2,1)S(1)} %collective-permute-done.31.refs_6_), channel_id=1, source_target_pairs={{0,4},{4,0},{8,12},{12,8},{16,20},{20,16},{24,28},{28,24},{1,5},{5... | collective-permute-start | bytes 393224 | tf_op jit(solution)/shard_map/ppermute | solution.py:41
  117.5 12.2 %feed_all.2 = (bf16[256,2048]{1,0:T(8,128)(2,1)}, bf16[2048,256]{1,0:T(8,128)(2,1)}) custom-call(s32[1]{0:T(128)} %bitcast.10.index, bf16[192,2048]{1,0:T(8,128)(2,1)S(1)} %constant_dynamic-update-slice_fusion.5.refs_0_, bf16[192,2048]{1,0:T(8,128)(2,1)S(1)} %collective-permute-done.37.refs_1_, bf16[192,2048]{1,0:T(8,128)(2,1)S(1)} %pad_maximum_fusion.refs_2_, ...), custom_call_target="tpu_custom_call" | custom-call | flops 72477576 | bytes 199229 | tf_op jit(solution)/shard_map/feed_all/pallas_call | solution.py:666
  129.9 8.6 %attend_back.1 = (bf16[512,512]{1,0:T(8,128)(2,1)S(1)}, bf16[512,512]{1,0:T(8,128)(2,1)S(1)}, bf16[512,512]{1,0:T(8,128)(2,1)S(1)}, bf16[512,512]{1,0:T(8,128)(2...) custom-call(bf16[128,512]{1,0:T(8,128)(2,1)S(1)} %product_back.1.ref, ...), custom_call_target="tpu_custom_call" | custom-call | flops 42949672 | bytes 136314 | tf_op jit(solution)/shard_map/attend_back/pallas_call | solution.py:1034
  138.6 2.1 %product_halves.3 = (f32[64,2048]{1,0:T(8,128)S(1)}, bf16[64,2048]{1,0:T(8,128)(2,1)S(1)}) custom-call(bf16[128,512]{1,0:T(8,128)(2,1)S(1)} %get-tuple-element.211.refs_0_, bf16[128,512]{1,0:T(8,128)(2,1)S(1)} %get-tuple-element.212.refs_1_, bf16[128,512]{1,0:T(8,128)(2,1)S(1)} %get-tuple-element.213.refs_2_, bf16[2048,512]{1,0:T(8,128)(2,1)S(1)} %copy-done, ...), custom_call_target="tpu_custom_call" | custom-call | flops 8053063 | bytes 62914 | tf_op jit(solution)/shard_map/product_halves/pallas_call | solution.py:270
  140.8 1.5 collective-permute-done.41
  143.4 2.8 %project.1 = (f32[256,512]{1,0:T(8,128)}, f32[256,512]{1,0:T(8,128)}, f32[256,512]{1,0:T(8,128)}, f32[3,256]{1,0:T(4,128)S(1)}) custom-call(s32[1]{0:T(128)} %bitcast.10.index, bf16[512,2048]{1,0:T(8,128)(2,1)S(1)} %bitcast.42, bf16[512,2048]{1,0:T(8,128)(2,1)S(1)} %collective-permute-done.13.refs_0_.refs_1_, ...), custom_call_target="tpu_custom_call" | custom-call | flops 16106127 | bytes 47185 | tf_op jit(solution)/shard_map/project/pallas_call | solution.py:725
  147.4 3.4 %collective-permute-done.42.other = bf16[64,2048]{1,0:T(8,128)(2,1)S(1)} collective-permute-done((bf16[64,2048]{1,0:T(8,128)(2,1)S(1)}, bf16[64,2048]{1,0:T(8,128)(2,1)S(1)}, u32[]{:S(2)}, u32[]{:S(2)}) %collective-permute-start.42) | collective-permute-done | bytes 262176 | tf_op jit(solution)/shard_map/ppermute | solution.py:41
  152.2 6.0 %all-to-all-start = ((bf16[8,72,256]{2,1,0:T(8,128)(2,1)}), bf16[8,72,256]{2,1,0:T(8,128)(2,1)S(1)}, u32[]{:S(2)}, u32[]{:S(2)}) async-start(bf16[8,72,256]{2,1,0:T(8,128)(2,1)} %copy-done.8), calls=%async_computation | async-start | bytes 589824 | tf_op jit(solution)/shard_map/all_to_all | solution.py:1181
  161.3 16.9 %feed_all.3 = (f32[256,2048]{1,0:T(8,128)}, f32[2048,256]{1,0:T(8,128)}) custom-call(s32[1]{0:T(128)} %bitcast.10.index, bf16[64,2048]{1,0:T(8,128)(2,1)S(1)} %copy-done.10, bf16[64,2048]{1,0:T(8,128)(2,1)S(1)} %collective-permute-done.47.refs_1_, bf16[192,2048]{1,0:T(8,128)(2,1)S(1)} %pad_maximum_fusion.1.refs_2_, ...), custom_call_target="tpu_custom_call" | custom-call | flops 96636768 | bytes 209715 | tf_op jit(solution)/shard_map/feed_all/pallas_call | solution.py:666
  (162 shorter events, 37.5 us)
Async XLA Ops:
  2.2 8.1 %collective-permute-start = (bf16[32,2048]{1,0:T(8,128)(2,1)S(1)}, bf16[32,2048]{1,0:T(8,128)(2,1)S(1)}, u32[]{:S(2)}, u32[]{:S(2)}) collective-permute-start(bf16[32,2048]{1,0:T(8,128)(2,1)S(1)} %constant_dynamic-slice_fusion.4), channel_id=1, source_target_pairs={{0,8},{4,12},{8,0},{12,4},{16,24},{20,28},{24,16},{28,20},{1,9},{5... | collective-permute-start | bytes 393224 | tf_op jit(solution)/shard_map/ppermute | solution.py:41
  5.2 12.9 %collective-permute-start.2 = (bf16[32,2048]{1,0:T(8,128)(2,1)S(1)}, bf16[32,2048]{1,0:T(8,128)(2,1)S(1)}, u32[]{:S(2)}, u32[]{:S(2)}) collective-permute-start(bf16[32,2048]{1,0:T(8,128)(2,1)S(1)} %constant_dynamic-slice_fusion.4), channel_id=1, source_target_pairs={{0,16},{4,20},{8,24},{12,28},{16,0},{20,4},{24,8},{28,12},{1,17},{... | collective-permute-start | bytes 393224 | tf_op jit(solution)/shard_map/ppermute | solution.py:41
  7.8 11.8 %collective-permute-start.4 = (bf16[32,2048]{1,0:T(8,128)(2,1)S(1)}, bf16[32,2048]{1,0:T(8,128)(2,1)S(1)}, u32[]{:S(2)}, u32[]{:S(2)}) collective-permute-start(bf16[32,2048]{1,0:T(8,128)(2,1)S(1)} %constant_dynamic-slice_fusion.4), channel_id=1, source_target_pairs={{0,24},{4,28},{8,16},{12,20},{16,8},{20,12},{24,0},{28,4},{1,25},{... | collective-permute-start | bytes 393224 | tf_op jit(solution)/shard_map/ppermute | solution.py:41
  10.3 9.9 %collective-permute-start.1 = (bf16[32,2048]{1,0:T(8,128)(2,1)S(1)}, bf16[32,2048]{1,0:T(8,128)(2,1)S(1)}, u32[]{:S(2)}, u32[]{:S(2)}) collective-permute-start(bf16[32,2048]{1,0:T(8,128)(2,1)S(1)} %collective-permute-done), channel_id=1, source_target_pairs={{0,2},{1,3},{2,0},{3,1},{4,6},{5,7},{6,4},{7,5},{8,10},{9,11},{10,... | collective-permute-start | bytes 393224 | tf_op jit(solution)/shard_map/ppermute | solution.py:41
  12.0 20.5 %collective-permute-start.6 = (bf16[64,2048]{1,0:T(8,128)(2,1)S(1)}, bf16[64,2048]{1,0:T(8,128)(2,1)S(1)}, u32[]{:S(2)}, u32[]{:S(2)}) collective-permute-start(bf16[64,2048]{1,0:T(8,128)(2,1)S(1)} %bitcast.44), channel_id=1, source_target_pairs={{0,4},{4,0},{8,12},{12,8},{16,20},{20,16},{24,28},{28,24},{1,5},{5... | collective-permute-start | bytes 786440 | tf_op jit(solution)/shard_map/ppermute | solution.py:41
  18.2 5.0 %collective-permute-start.3 = (bf16[32,2048]{1,0:T(8,128)(2,1)S(1)}, bf16[32,2048]{1,0:T(8,128)(2,1)S(1)}, u32[]{:S(2)}, u32[]{:S(2)}) collective-permute-start(bf16[32,2048]{1,0:T(8,128)(2,1)S(1)} %collective-permute-done.2), channel_id=1, source_target_pairs={{0,2},{1,3},{2,0},{3,1},{4,6},{5,7},{6,4},{7,5},{8,10},{9,11},{10,... | collective-permute-start | bytes 393224 | tf_op jit(solution)/shard_map/ppermute | solution.py:41
  19.7 5.1 %collective-permute-start.5 = (bf16[32,2048]{1,0:T(8,128)(2,1)S(1)}, bf16[32,2048]{1,0:T(8,128)(2,1)S(1)}, u32[]{:S(2)}, u32[]{:S(2)}) collective-permute-start(bf16[32,2048]{1,0:T(8,128)(2,1)S(1)} %collective-permute-done.4), channel_id=1, source_target_pairs={{0,2},{1,3},{2,0},{3,1},{4,6},{5,7},{6,4},{7,5},{8,10},{9,11},{10,... | collective-permute-start | bytes 393224 | tf_op jit(solution)/shard_map/ppermute | solution.py:41
  20.2 9.3 %collective-permute-start.7 = (bf16[64,2048]{1,0:T(8,128)(2,1)S(1)}, bf16[64,2048]{1,0:T(8,128)(2,1)S(1)}, u32[]{:S(2)}, u32[]{:S(2)}) collective-permute-start(bf16[64,2048]{1,0:T(8,128)(2,1)S(1)} %pad_maximum_fusion.6.refs_3_), channel_id=1, source_target_pairs={{0,4},{4,0},{8,12},{12,8},{16,20},{20,16},{24,28},{28,24},{1,5},{5... | collective-permute-start | bytes 786440 | tf_op jit(solution)/shard_map/ppermute | solution.py:41
  23.2 11.9 %collective-permute-start.8 = (bf16[64,2048]{1,0:T(8,128)(2,1)S(1)}, bf16[64,2048]{1,0:T(8,128)(2,1)S(1)}, u32[]{:S(2)}, u32[]{:S(2)}) collective-permute-start(bf16[64,2048]{1,0:T(8,128)(2,1)S(1)} %pad_maximum_fusion.7.refs_5_), channel_id=1, source_target_pairs={{0,4},{4,0},{8,12},{12,8},{16,20},{20,16},{24,28},{28,24},{1,5},{5... | collective-permute-start | bytes 786440 | tf_op jit(solution)/shard_map/ppermute | solution.py:41
  24.8 11.5 %collective-permute-start.9 = (bf16[64,2048]{1,0:T(8,128)(2,1)S(1)}, bf16[64,2048]{1,0:T(8,128)(2,1)S(1)}, u32[]{:S(2)}, u32[]{:S(2)}) collective-permute-start(bf16[64,2048]{1,0:T(8,128)(2,1)S(1)} %pad_maximum_fusion.8.refs_7_), channel_id=1, source_target_pairs={{0,4},{4,0},{8,12},{12,8},{16,20},{20,16},{24,28},{28,24},{1,5},{5... | collective-permute-start | bytes 786440 | tf_op jit(solution)/shard_map/ppermute | solution.py:41
  29.5 9.3 %collective-permute-start.10 = (bf16[32,2048]{1,0:T(8,128)(2,1)S(1)}, bf16[32,2048]{1,0:T(8,128)(2,1)S(1)}, u32[]{:S(2)}, u32[]{:S(2)}) collective-permute-start(bf16[32,2048]{1,0:T(8,128)(2,1)S(1)} %constant_dynamic-slice_fusion.2), channel_id=1, source_target_pairs={{0,8},{4,12},{8,0},{12,4},{16,24},{20,28},{24,16},{28,20},{1,9},{5... | collective-permute-start | bytes 393224 | tf_op jit(solution)/shard_map/ppermute | solution.py:41
  31.0 8.7 %collective-permute-start.11 = (bf16[32,2048]{1,0:T(8,128)(2,1)S(1)}, bf16[32,2048]{1,0:T(8,128)(2,1)S(1)}, u32[]{:S(2)}, u32[]{:S(2)}) collective-permute-start(bf16[32,2048]{1,0:T(8,128)(2,1)S(1)} %constant_dynamic-slice_fusion.2), channel_id=1, source_target_pairs={{0,16},{4,20},{8,24},{12,28},{16,0},{20,4},{24,8},{28,12},{1,17},{... | collective-permute-start | bytes 393224 | tf_op jit(solution)/shard_map/ppermute | solution.py:41
  32.5 7.2 %collective-permute-start.12 = (bf16[32,2048]{1,0:T(8,128)(2,1)S(1)}, bf16[32,2048]{1,0:T(8,128)(2,1)S(1)}, u32[]{:S(2)}, u32[]{:S(2)}) collective-permute-start(bf16[32,2048]{1,0:T(8,128)(2,1)S(1)} %constant_dynamic-slice_fusion.2), channel_id=1, source_target_pairs={{0,24},{4,28},{8,16},{12,20},{16,8},{20,12},{24,0},{28,4},{1,25},{... | collective-permute-start | bytes 393224 | tf_op jit(solution)/shard_map/ppermute | solution.py:41
  39.7 5.1 %collective-permute-start.13 = (bf16[512,2048]{1,0:T(8,128)(2,1)S(1)}, bf16[512,2048]{1,0:T(8,128)(2,1)S(1)}, u32[]{:S(2)}, u32[]{:S(2)}) collective-permute-start(bf16[512,2048]{1,0:T(8,128)(2,1)S(1)} %bitcast.39), channel_id=1, source_target_pairs={{0,1},{1,0},{2,3},{3,2},{4,5},{5,4},{6,7},{7,6},{8,9},{9,8},{10,11... | collective-permute-start | bytes 6291464 | tf_op jit(solution)/shard_map/ppermute | solution.py:41
  39.8 11.6 %collective-permute-start.15 = (bf16[96,2048]{1,0:T(8,128)(2,1)S(1)}, bf16[96,2048]{1,0:T(8,128)(2,1)S(1)}, u32[]{:S(2)}, u32[]{:S(2)}) collective-permute-start(bf16[96,2048]{1,0:T(8,128)(2,1)S(1)} %pad_maximum_fusion.5), channel_id=1, source_target_pairs={{0,2},{1,3},{2,0},{3,1},{4,6},{5,7},{6,4},{7,5},{8,10},{9,11},{10,... | collective-permute-start | bytes 1179656 | tf_op jit(solution)/shard_map/ppermute | solution.py:41
  40.9 8.5 %collective-permute-start.14 = (bf16[64,2048]{1,0:T(8,128)(2,1)S(1)}, bf16[64,2048]{1,0:T(8,128)(2,1)}, u32[]{:S(2)}, u32[]{:S(2)}) collective-permute-start(bf16[64,2048]{1,0:T(8,128)(2,1)S(1)} %bitcast.52), channel_id=1, source_target_pairs={{0,4},{4,0},{8,12},{12,8},{16,20},{20,16},{24,28},{28,24},{1,5},{5... | collective-permute-start | bytes 786440 | tf_op jit(solution)/shard_map/ppermute | solution.py:41
  52.0 20.0 %collective-permute-start.19 = (bf16[192,2048]{1,0:T(8,128)(2,1)S(1)}, bf16[192,2048]{1,0:T(8,128)(2,1)S(1)}, u32[]{:S(2)}, u32[]{:S(2)}) collective-permute-start(bf16[192,2048]{1,0:T(8,128)(2,1)S(1)} %pad_maximum_fusion.refs_2_), channel_id=1, source_target_pairs={{0,4},{4,0},{8,12},{12,8},{16,20},{20,16},{24,28},{28,24},{1,5},{5... | collective-permute-start | bytes 2359304 | tf_op jit(solution)/shard_map/ppermute | solution.py:41
  53.6 8.4 %collective-permute-start.17 = (bf16[64,2048]{1,0:T(8,128)(2,1)S(1)}, bf16[64,2048]{1,0:T(8,128)(2,1)S(1)}, u32[]{:S(2)}, u32[]{:S(2)}) collective-permute-start(bf16[64,2048]{1,0:T(8,128)(2,1)S(1)} %add_convert_fusion.3.low), channel_id=1, source_target_pairs={{0,2},{1,3},{2,0},{3,1},{4,6},{5,7},{6,4},{7,5},{8,10},{9,11},{10,... | collective-permute-start | bytes 786440 | tf_op jit(solution)/shard_map/ppermute | solution.py:41
  73.5 16.1 %collective-permute-start.21 = (bf16[64,2048]{1,0:T(8,128)(2,1)S(1)}, bf16[64,2048]{1,0:T(8,128)(2,1)S(1)}, u32[]{:S(2)}, u32[]{:S(2)}) collective-permute-start(bf16[64,2048]{1,0:T(8,128)(2,1)S(1)} %add_convert_fusion.2.low), channel_id=1, source_target_pairs={{0,2},{1,3},{2,0},{3,1},{4,6},{5,7},{6,4},{7,5},{8,10},{9,11},{10,... | collective-permute-start | bytes 786440 | tf_op jit(solution)/shard_map/ppermute | solution.py:41
  74.7 14.0 %collective-permute-start.22 = (bf16[32,2048]{1,0:T(8,128)(2,1)S(1)}, bf16[32,2048]{1,0:T(8,128)(2,1)S(1)}, u32[]{:S(2)}, u32[]{:S(2)}) collective-permute-start(bf16[32,2048]{1,0:T(8,128)(2,1)S(1)} %constant_dynamic-slice_fusion), channel_id=1, source_target_pairs={{0,8},{4,12},{8,0},{12,4},{16,24},{20,28},{24,16},{28,20},{1,9},{5... | collective-permute-start | bytes 393224 | tf_op jit(solution)/shard_map/ppermute | solution.py:41
  76.6 12.9 %collective-permute-start.23 = (bf16[32,2048]{1,0:T(8,128)(2,1)S(1)}, bf16[32,2048]{1,0:T(8,128)(2,1)S(1)}, u32[]{:S(2)}, u32[]{:S(2)}) collective-permute-start(bf16[32,2048]{1,0:T(8,128)(2,1)S(1)} %constant_dynamic-slice_fusion), channel_id=1, source_target_pairs={{0,16},{4,20},{8,24},{12,28},{16,0},{20,4},{24,8},{28,12},{1,17},{... | collective-permute-start | bytes 393224 | tf_op jit(solution)/shard_map/ppermute | solution.py:41
  77.9 11.6 %collective-permute-start.24 = (bf16[32,2048]{1,0:T(8,128)(2,1)S(1)}, bf16[32,2048]{1,0:T(8,128)(2,1)S(1)}, u32[]{:S(2)}, u32[]{:S(2)}) collective-permute-start(bf16[32,2048]{1,0:T(8,128)(2,1)S(1)} %constant_dynamic-slice_fusion), channel_id=1, source_target_pairs={{0,24},{4,28},{8,16},{12,20},{16,8},{20,12},{24,0},{28,4},{1,25},{... | collective-permute-start | bytes 393224 | tf_op jit(solution)/shard_map/ppermute | solution.py:41
  90.3 2.6 %collective-permute-start.25 = (bf16[64,2048]{1,0:T(8,128)(2,1)S(1)}, bf16[64,2048]{1,0:T(8,128)(2,1)S(1)}, u32[]{:S(2)}, u32[]{:S(2)}) collective-permute-start(bf16[64,2048]{1,0:T(8,128)(2,1)S(1)} %get-tuple-element.182), channel_id=1, source_target_pairs={{0,1},{1,0},{2,3},{3,2},{4,5},{5,4},{6,7},{7,6},{8,9},{9,8},{10,11... | collective-permute-start | bytes 786440 | tf_op jit(solution)/shard_map/ppermute | solution.py:41
  90.5 11.6 %collective-permute-start.35 = (bf16[96,2048]{1,0:T(8,128)(2,1)S(1)}, bf16[96,2048]{1,0:T(8,128)(2,1)S(1)}, u32[]{:S(2)}, u32[]{:S(2)}) collective-permute-start(bf16[96,2048]{1,0:T(8,128)(2,1)S(1)} %get-tuple-element.264), channel_id=1, source_target_pairs={{0,2},{1,3},{2,0},{3,1},{4,6},{5,7},{6,4},{7,5},{8,10},{9,11},{10,... | collective-permute-start | bytes 1179656 | tf_op jit(solution)/shard_map/ppermute | solution.py:41
  91.4 11.2 %collective-permute-start.36 = (bf16[96,2048]{1,0:T(8,128)(2,1)S(1)}, bf16[96,2048]{1,0:T(8,128)(2,1)S(1)}, u32[]{:S(2)}, u32[]{:S(2)}) collective-permute-start(bf16[96,2048]{1,0:T(8,128)(2,1)S(1)} %get-tuple-element.264), channel_id=1, source_target_pairs={{0,4},{4,0},{8,12},{12,8},{16,20},{20,16},{24,28},{28,24},{1,5},{5... | collective-permute-start | bytes 1179656 | tf_op jit(solution)/shard_map/ppermute | solution.py:41
  93.8 8.8 %collective-permute-start.27 = (bf16[128,512]{1,0:T(8,128)(2,1)S(1)}, bf16[128,512]{1,0:T(8,128)(2,1)S(1)}, u32[]{:S(2)}, u32[]{:S(2)}) collective-permute-start(bf16[128,512]{1,0:T(8,128)(2,1)S(1)} %product_back.1.refs_0_), channel_id=1, source_target_pairs={{0,8},{4,12},{8,0},{12,4},{16,24},{20,28},{24,16},{28,20},{1,9},{5... | collective-permute-start | bytes 393224 | tf_op jit(solution)/shard_map/ppermute | solution.py:41
  96.2 12.8 %collective-permute-start.29 = (bf16[128,512]{1,0:T(8,128)(2,1)S(1)}, bf16[128,512]{1,0:T(8,128)(2,1)S(1)}, u32[]{:S(2)}, u32[]{:S(2)}) collective-permute-start(bf16[128,512]{1,0:T(8,128)(2,1)S(1)} %product_back.1.refs_0_), channel_id=1, source_target_pairs={{0,16},{4,20},{8,24},{12,28},{16,0},{20,4},{24,8},{28,12},{1,17},{... | collective-permute-start | bytes 393224 | tf_op jit(solution)/shard_map/ppermute | solution.py:41
  97.7 11.3 %collective-permute-start.31 = (bf16[128,512]{1,0:T(8,128)(2,1)S(1)}, bf16[128,512]{1,0:T(8,128)(2,1)S(1)}, u32[]{:S(2)}, u32[]{:S(2)}) collective-permute-start(bf16[128,512]{1,0:T(8,128)(2,1)S(1)} %product_back.1.refs_0_), channel_id=1, source_target_pairs={{0,24},{4,28},{8,16},{12,20},{16,8},{20,12},{24,0},{28,4},{1,25},{... | collective-permute-start | bytes 393224 | tf_op jit(solution)/shard_map/ppermute | solution.py:41
  102.0 9.8 %collective-permute-start.38 = (bf16[192,2048]{1,0:T(8,128)(2,1)S(1)}, bf16[192,2048]{1,0:T(8,128)(2,1)S(1)}, u32[]{:S(2)}, u32[]{:S(2)}) collective-permute-start(bf16[192,2048]{1,0:T(8,128)(2,1)S(1)} %pad_maximum_fusion.refs_2_), channel_id=1, source_target_pairs={{0,1},{1,0},{2,3},{3,2},{4,5},{5,4},{6,7},{7,6},{8,9},{9,8},{10,11... | collective-permute-start | bytes 2359304 | tf_op jit(solution)/shard_map/ppermute | solution.py:41
  102.7 8.0 %collective-permute-start.33 = (bf16[64,2048]{1,0:T(8,128)(2,1)S(1)}, bf16[64,2048]{1,0:T(8,128)(2,1)S(1)}, u32[]{:S(2)}, u32[]{:S(2)}) collective-permute-start(bf16[64,2048]{1,0:T(8,128)(2,1)S(1)} %get-tuple-element.186), channel_id=1, source_target_pairs={{0,1},{1,0},{2,3},{3,2},{4,5},{5,4},{6,7},{7,6},{8,9},{9,8},{10,11... | collective-permute-start | bytes 786440 | tf_op jit(solution)/shard_map/ppermute | solution.py:41
  109.0 6.5 %collective-permute-start.37 = (bf16[192,2048]{1,0:T(8,128)(2,1)S(1)}, bf16[192,2048]{1,0:T(8,128)(2,1)S(1)}, u32[]{:S(2)}, u32[]{:S(2)}) collective-permute-start(bf16[192,2048]{1,0:T(8,128)(2,1)S(1)} %constant_dynamic-update-slice_fusion.5.refs_0_), channel_id=1, source_target_pairs={{0,1},{1,0},{2,3},{3,2},{4,5},{5,4},{6,7},{7,6},{8,9},{9,8},{10,11... | collective-permute-start | bytes 2359304 | tf_op jit(solution)/shard_map/ppermute | solution.py:41
  109.1 6.4 %collective-permute-start.28 = (bf16[128,512]{1,0:T(8,128)(2,1)S(1)}, bf16[128,512]{1,0:T(8,128)(2,1)S(1)}, u32[]{:S(2)}, u32[]{:S(2)}) collective-permute-start(bf16[128,512]{1,0:T(8,128)(2,1)S(1)} %collective-permute-done.27.refs_2_), channel_id=1, source_target_pairs={{0,4},{4,0},{8,12},{12,8},{16,20},{20,16},{24,28},{28,24},{1,5},{5... | collective-permute-start | bytes 393224 | tf_op jit(solution)/shard_map/ppermute | solution.py:41
  109.7 28.8 %collective-permute-start.40 = (bf16[96,2048]{1,0:T(8,128)(2,1)S(1)}, bf16[96,2048]{1,0:T(8,128)(2,1)S(1)}, u32[]{:S(2)}, u32[]{:S(2)}) collective-permute-start(bf16[96,2048]{1,0:T(8,128)(2,1)S(1)} %collective-permute-done.36), channel_id=1, source_target_pairs={{0,2},{1,3},{2,0},{3,1},{4,6},{5,7},{6,4},{7,5},{8,10},{9,11},{10,... | collective-permute-start | bytes 1179656 | tf_op jit(solution)/shard_map/ppermute | solution.py:41
  110.7 19.0 %collective-permute-start.34 = (bf16[64,2048]{1,0:T(8,128)(2,1)S(1)}, bf16[64,2048]{1,0:T(8,128)(2,1)S(1)}, u32[]{:S(2)}, u32[]{:S(2)}) collective-permute-start(bf16[64,2048]{1,0:T(8,128)(2,1)S(1)} %add_convert_fusion.1.low), channel_id=1, source_target_pairs={{0,2},{1,3},{2,0},{3,1},{4,6},{5,7},{6,4},{7,5},{8,10},{9,11},{10,... | collective-permute-start | bytes 786440 | tf_op jit(solution)/shard_map/ppermute | solution.py:41
  111.8 17.9 %collective-permute-start.26 = (bf16[128,512]{1,0:T(8,128)(2,1)S(1)}, bf16[128,512]{1,0:T(8,128)(2,1)S(1)}, u32[]{:S(2)}, u32[]{:S(2)}) collective-permute-start(bf16[128,512]{1,0:T(8,128)(2,1)S(1)} %product_back.1.refs_0_), channel_id=1, source_target_pairs={{0,4},{4,0},{8,12},{12,8},{16,20},{20,16},{24,28},{28,24},{1,5},{5... | collective-permute-start | bytes 393224 | tf_op jit(solution)/shard_map/ppermute | solution.py:41
  115.5 14.3 %collective-permute-start.30 = (bf16[128,512]{1,0:T(8,128)(2,1)S(1)}, bf16[128,512]{1,0:T(8,128)(2,1)S(1)}, u32[]{:S(2)}, u32[]{:S(2)}) collective-permute-start(bf16[128,512]{1,0:T(8,128)(2,1)S(1)} %collective-permute-done.29.refs_4_), channel_id=1, source_target_pairs={{0,4},{4,0},{8,12},{12,8},{16,20},{20,16},{24,28},{28,24},{1,5},{5... | collective-permute-start | bytes 393224 | tf_op jit(solution)/shard_map/ppermute | solution.py:41
  115.5 14.2 %collective-permute-start.32 = (bf16[128,512]{1,0:T(8,128)(2,1)S(1)}, bf16[128,512]{1,0:T(8,128)(2,1)S(1)}, u32[]{:S(2)}, u32[]{:S(2)}) collective-permute-start(bf16[128,512]{1,0:T(8,128)(2,1)S(1)} %collective-permute-done.31.refs_6_), channel_id=1, source_target_pairs={{0,4},{4,0},{8,12},{12,8},{16,20},{20,16},{24,28},{28,24},{1,5},{5... | collective-permute-start | bytes 393224 | tf_op jit(solution)/shard_map/ppermute | solution.py:41
  129.7 8.8 %collective-permute-start.39 = (bf16[64,2048]{1,0:T(8,128)(2,1)S(1)}, bf16[64,2048]{1,0:T(8,128)(2,1)S(1)}, u32[]{:S(2)}, u32[]{:S(2)}) collective-permute-start(bf16[64,2048]{1,0:T(8,128)(2,1)S(1)} %get-tuple-element.209), channel_id=1, source_target_pairs={{0,4},{4,0},{8,12},{12,8},{16,20},{20,16},{24,28},{28,24},{1,5},{5... | collective-permute-start | bytes 786440 | tf_op jit(solution)/shard_map/ppermute | solution.py:41
  142.4 8.4 %collective-permute-start.42 = (bf16[64,2048]{1,0:T(8,128)(2,1)S(1)}, bf16[64,2048]{1,0:T(8,128)(2,1)S(1)}, u32[]{:S(2)}, u32[]{:S(2)}) collective-permute-start(bf16[64,2048]{1,0:T(8,128)(2,1)S(1)} %add_convert_fusion.low), channel_id=1, source_target_pairs={{0,2},{1,3},{2,0},{3,1},{4,6},{5,7},{6,4},{7,5},{8,10},{9,11},{10,... | collective-permute-start | bytes 786440 | tf_op jit(solution)/shard_map/ppermute | solution.py:41
  150.8 9.2 %collective-permute-start.48 = (bf16[192,2048]{1,0:T(8,128)(2,1)S(1)}, bf16[192,2048]{1,0:T(8,128)(2,1)}, u32[]{:S(2)}, u32[]{:S(2)}) collective-permute-start(bf16[192,2048]{1,0:T(8,128)(2,1)S(1)} %pad_maximum_fusion.1.refs_2_), channel_id=1, source_target_pairs={{0,1},{1,0},{2,3},{3,2},{4,5},{5,4},{6,7},{7,6},{8,9},{9,8},{10,11... | collective-permute-start | bytes 2359304 | tf_op jit(solution)/shard_map/ppermute | solution.py:41
  150.8 9.6 %collective-permute-start.50 = (bf16[192,2048]{1,0:T(8,128)(2,1)S(1)}, bf16[192,2048]{1,0:T(8,128)(2,1)}, u32[]{:S(2)}, u32[]{:S(2)}) collective-permute-start(bf16[192,2048]{1,0:T(8,128)(2,1)S(1)} %collective-permute-done.19.refs_6_), channel_id=1, source_target_pairs={{0,1},{1,0},{2,3},{3,2},{4,5},{5,4},{6,7},{7,6},{8,9},{9,8},{10,11... | collective-permute-start | bytes 2359304 | tf_op jit(solution)/shard_map/ppermute | solution.py:41
  152.2 26.0 %all-to-all-start = ((bf16[8,72,256]{2,1,0:T(8,128)(2,1)}), bf16[8,72,256]{2,1,0:T(8,128)(2,1)S(1)}, u32[]{:S(2)}, u32[]{:S(2)}) async-start(bf16[8,72,256]{2,1,0:T(8,128)(2,1)} %copy-done.8), calls=%async_computation | async-start | bytes 589824 | tf_op jit(solution)/shard_map/all_to_all | solution.py:1181
  158.2 1.7 collective-permute-start.47
  158.2 2.1 %collective-permute-start.49 = (bf16[64,2048]{1,0:T(8,128)(2,1)}, bf16[64,2048]{1,0:T(8,128)(2,1)S(1)}, u32[]{:S(2)}, u32[]{:S(2)}) collective-permute-start(bf16[64,2048]{1,0:T(8,128)(2,1)} %collective-permute-done.14.refs_4_), channel_id=1, source_target_pairs={{0,1},{1,0},{2,3},{3,2},{4,5},{5,4},{6,7},{7,6},{8,9},{9,8},{10,11... | collective-permute-start | bytes 786440 | tf_op jit(solution)/shard_map/ppermute | solution.py:41
  178.2 4.9 %collective-permute-start.51 = (bf16[8,72,256]{2,1,0:T(8,128)(2,1)S(1)}, bf16[8,72,256]{2,1,0:T(8,128)(2,1)S(1)}, u32[]{:S(2)}, u32[]{:S(2)}) collective-permute-start(bf16[8,72,256]{2,1,0:T(8,128)(2,1)S(1)} %all-to-all-done.came_a), channel_id=1, source_target_pairs={{0,1},{1,0},{2,3},{3,2},{4,5},{5,4},{6,7},{7,6},{8,9},{9,8},{10,11... | collective-permute-start | bytes 884744 | tf_op jit(solution)/shard_map/ppermute | solution.py:41
  178.4 1.8 collective-permute-start.45
  178.8 1.8 collective-permute-start.44
  178.9 3.6 %collective-permute-start.46 = (f32[3,256]{1,0:T(4,128)S(1)}, f32[3,256]{1,0:T(4,128)S(1)}, u32[]{:S(2)}, u32[]{:S(2)}) collective-permute-start(f32[3,256]{1,0:T(4,128)S(1)} %add.48), channel_id=1, source_target_pairs={{0,2},{1,3},{2,0},{3,1},{4,6},{5,7},{6,4},{7,5},{8,10},{9,11},{10,... | collective-permute-start | bytes 9224 | tf_op jit(solution)/shard_map/ppermute | solution.py:41
  (27 other events, 197.8 us)

commit v6 on v5

--- a/solution.py
+++ b/solution.py
@@ -410,7 +410,7 @@
     return jnp.concatenate(high + low + [zero, zero], axis=0)
 
 
-def middle_kernel(residual, low, other, grad, gain, kind, grad_residual, mixed, parts):
+def middle_kernel(index, residual, low, other, grad, gain, kind, grad_residual, mixed, parts):
     lifted_grad = low[...].astype(f32) + other[...].astype(f32)
     normal, inverse = normalize(residual[...])
     column = kind[...]
@@ -422,15 +422,17 @@
     sums = kind_sums(lifted_grad * normal, column)
     shards, rows, part = parts.shape
     for k in range(shards):
-        parts[k, pl.ds(0, rows - 8), :] = rounded_value[:, k * part : (k + 1) * part]
-        parts[k, pl.ds(rows - 8, 8), :] = sums[:, k * part : (k + 1) * part]
+        at = index[0] ^ k
+        parts[at, pl.ds(0, rows - 8), :] = rounded_value[:, k * part : (k + 1) * part]
+        parts[at, pl.ds(rows - 8, 8), :] = sums[:, k * part : (k + 1) * part]
 
 
 def middle(residual, low, other, grad, gain, kind, shards):
     rows, width = residual.shape
+    index = lax.axis_index("seq").astype(jnp.int32).reshape(1)
     return pl.pallas_call(
         middle_kernel,
-        in_specs=[WHOLE] * 6,
+        in_specs=[pl.BlockSpec(memory_space=pltpu.SMEM)] + [WHOLE] * 6,
         out_specs=[WHOLE] * 3,
         out_shape=[
             jax.ShapeDtypeStruct(residual.shape, f32),
@@ -440,7 +442,7 @@
         compiler_params=params(6),
         cost_estimate=cost(20 * residual.size, 16 * residual.size),
         name="middle",
-    )(residual, low, other, grad, gain, kind)
+    )(index, residual, low, other, grad, gain, kind)
 
 
 def reordered(values, shards):
@@ -650,8 +652,6 @@
     hidden = up.shape[1]
     tile = math.gcd(hidden, 256)
     steps = hidden // tile
-    wide = lambda t, index: (0, jnp.minimum(t, steps - 1))
-    deep = lambda t, index: (jnp.minimum(t, steps - 1), 0)
     across = lambda t, index: (0, jnp.maximum(t - 1, 0))
     below = lambda t, index: (jnp.maximum(t - 1, 0), 0)
     mine = lambda t, index: (0, index[0])
@@ -669,11 +669,7 @@
             num_scalar_prefetch=1,
             grid=(steps + 1,),
             in_specs=[WHOLE] * (2 * count)
-            + (
-                [WHOLE] * 2
-                if own
-                else [pl.BlockSpec((width, tile), wide), pl.BlockSpec((tile, width), deep)]
-            )
+            + [WHOLE] * 2
             + more,
             out_specs=sum_specs,
             scratch_shapes=[pltpu.VMEM((part, rows), bf16)]
@@ -693,7 +689,8 @@
         index,
         *lifted,
         *grad,
-        *((up, down) if own else (in_hbm(up), in_hbm(down))),
+        up,
+        down,
         *(own or [in_hbm(array) for array in sums]),
     )
 
@@ -743,14 +740,14 @@
     )(index, *normed, *[low for pair in lows for low in pair], *weights, gain, *kinds)
 
 
-def output_kernel(index, attended_a, attended_b, came_a, came_b, out, gain_grad, *, groups):
+def output_kernel(attended_a, attended_b, came_a, came_b, out, gain_grad, *, groups):
     total, sums = 0.0, 0.0
     shards, rows, part = came_a.shape
     half = rows - 8
     each = half // groups
     for attended, came in ((attended_a, came_a), (attended_b, came_b)):
         mixed = [
-            came[index[0] ^ d, pl.ds(group * each, each), :]
+            came[d, pl.ds(group * each, each), :]
             for group in range(groups)
             for d in range(shards)
         ]
@@ -764,12 +761,10 @@
 
 
 def output_part(attended, came, groups):
-    index = lax.axis_index("seq").astype(jnp.int32).reshape(1)
     across, part = attended[0].shape[1], came[0].shape[2]
     return pl.pallas_call(
         partial(output_kernel, groups=groups),
-        in_specs=[pl.BlockSpec(memory_space=pltpu.SMEM)]
-        + [pl.BlockSpec(memory_space=pltpu.VMEM)] * 4,
+        in_specs=[WHOLE] * 4,
         out_shape=[
             jax.ShapeDtypeStruct((across, part), f32),
             jax.ShapeDtypeStruct((3, part), f32),
@@ -779,7 +774,7 @@
             4 * attended[0].shape[0] * across * part, 4 * attended[0].shape[0] * (across + part)
         ),
         name="output_part",
-    )(index, *attended, *came)
+    )(*attended, *came)
 
 
 def mask_of(key_place, query_place, clip_length, clips):
@@ -1156,14 +1151,18 @@
     sums = feed_all(first_lifted, first_grads, up_weight, down_weight, shards, own=own)
     down_low, down_other = pair_mlp(down_mine, down_other)
     heads_grads, down_low, down_other = after((heads_grads, down_low, down_other), sums)
+    inner = inner_size()
+    columns_far = {
+        outer: swap(after(mixed_columns[outer : outer + inner], sums), "seq", outer)
+        for outer in range(inner, shards, inner)
+    }
     lifted_inner = gather_inner(after(lifted_half, down_other))
-
     query_low, key_low, value_low, own_low = attend_back(
         heads_grads, queries, keys, values, attended, stored, groups
     )
     attention_weights = (query_weight, key_weight, value_weight)
     lifted_inner += [join_x(far, own_low) for far in lifted_inner_far]
-    own_low, lifted_inner = after((own_low, lifted_inner), own_low)
+    own_low, lifted_inner, columns_far = after((own_low, lifted_inner, columns_far), own_low)
     low, other = pair_mlp(*product_halves(own_low, attention_weights, NT))
 
     query_grad, key_grad, value_grad, first_gain_grad = project(
@@ -1174,13 +1173,17 @@
         kinds,
         shards,
     )
+    columns_far = after(columns_far, low)
+    columns_far[0] = mixed_columns[:inner]
+    columns = {}
+    for outer, came in columns_far.items():
+        columns[outer] = came[0]
+        for bit in range(1, inner):
+            columns[outer | bit] = swap(came[bit], "seq", bit)
     first_gain_grad = first_gain_grad + swap(first_gain_grad, "mlp", 1)
-    other, first_gain_grad = after((other, first_gain_grad), query_grad)
+    other, first_gain_grad, columns = after((other, first_gain_grad, columns), query_grad)
     input_half = last(inputs_half, low, other, grad_residual, first_gain, half_kind, shards)
     outputs_half = finish(residual, down_low, after(down_other, input_half), shards)
-    mixed_part = lax.all_to_all(
-        after(mixed_columns, outputs_half), "seq", split_axis=0, concat_axis=0, tiled=True
-    )
     rest_lifted = with_core(after(lifted_inner, other))
     rest_grads = with_core(after(grad_inner, other))
     up_grad, down_grad = feed_all(
@@ -1193,7 +1196,7 @@
         bit *= 2
     placed = (input_half, outputs_half)
     input_grad, outputs = place_halves(placed, [swap(array, "mlp", 1) for array in placed])
-    mixed_part = after(mixed_part, up_grad)
+    mixed_part = jnp.stack([after(columns[d], up_grad) for d in range(shards)])
     output_grad, second_gain_grad = output_part(
         attended, (mixed_part, swap(mixed_part, "mlp", 1)), groups
     )

time: 185 us -> 184 us (level)
  starting transfers between devices: 55.1 us -> 59.5 us
  waiting for transfers between devices: 39.7 us -> 37.4 us
  Pallas kernels: 83.4 us -> 81.4 us
    ppermute x52 -> x59, starting transfers between devices: 49.1 us -> 59.5 us  [swap(): return lax.ppermute(value, axis, [(i, i ^ bit) for i in range(size)])]
    all_to_all x1 -> x0, starting transfers between devices: 6.02 us -> none  [body(): lax.all_to_all(after(mixed_columns, outputs_half), 'seq', split_axis=0, c...]
    ppermute x52 -> x59, waiting for transfers between devices: 39.7 us -> 37.4 us  [swap(): return lax.ppermute(value, axis, [(i, i ^ bit) for i in range(size)])]
    pallas_call x2, Pallas kernels: 29.1 us -> 27.2 us  [feed_all(): pl.pallas_call(partial(all_kernel, count=count), grid_spec=pltpu.Prefetch...]
  transfers between devices with their start and end apart: 53 -> 59, of which waited for: 25 -> 24; matrix products, arithmetic and copies ran while one was open for 1% -> 1% of each run, Pallas kernels for 43% -> 34%
where the time goes in v6:
time: 184 us
  Pallas kernels  81.4 us (44%)
  starting transfers between devices  59.5 us (32%)
  waiting for transfers between devices  37.4 us (20%)
  local copies, waits for them, and re-layouts  2.21 us (1%)
    ppermute x59, starting transfers between devices, swap(): return lax.ppermute(value, axis, [(i, i ^ bit) for i in range(size)])  59.5 us
    ppermute x59, waiting for transfers between devices, swap(): return lax.ppermute(value, axis, [(i, i ^ bit) for i in range(size)])  37.4 us
    pallas_call x2, Pallas kernels, feed_all(): pl.pallas_call(partial(all_kernel, count=count), grid_spec=pltpu.Prefetch...  27.2 us
    pallas_call x1, Pallas kernels, attend_all(): pl.pallas_call(partial(all_forward_kernel, groups=groups, scale=1.0 / mat...  9.35 us
    pallas_call x1, Pallas kernels, attend_back(): pl.pallas_call(partial(backward_kernel, count=count, groups=groups, scale...  8.36 us
    pallas_call x5, Pallas kernels, project_rows(): pl.pallas_call(partial(rows_kernel, count=len(weights)), out_shape=[jax.S...  7.65 us
    pallas_call x1, Pallas kernels, feed_own(): pl.pallas_call(own_kernel, in_specs=[WHOLE] * 3, out_specs=[WHOLE] * 4, o...  5.47 us
  transfers between devices with their start and end apart: 59, of which 24 were waited for; matrix products, arithmetic and copies ran while one was open for 1% of the time, Pallas kernels for 34%

profile of v6, /device:TPU:0, one launch (start us, length us, event | category | flops | bytes accessed | tf_op | source)
XLA Modules:
  0.0 183.7 jit_solution(7411342751790611909)
XLA Ops:
  2.2 3.1 %collective-permute-start = (bf16[32,2048]{1,0:T(8,128)(2,1)S(1)}, bf16[32,2048]{1,0:T(8,128)(2,1)S(1)}, u32[]{:S(2)}, u32[]{:S(2)}) collective-permute-start(bf16[32,2048]{1,0:T(8,128)(2,1)S(1)} %constant_dynamic-slice_fusion.4), channel_id=1, source_target_pairs={{0,8},{4,12},{8,0},{12,4},{16,24},{20,28},{24,16},{28,20},{1,9},{5... | collective-permute-start | bytes 393224 | tf_op jit(solution)/shard_map/ppermute | solution.py:41
  5.2 2.6 %collective-permute-start.2 = (bf16[32,2048]{1,0:T(8,128)(2,1)S(1)}, bf16[32,2048]{1,0:T(8,128)(2,1)S(1)}, u32[]{:S(2)}, u32[]{:S(2)}) collective-permute-start(bf16[32,2048]{1,0:T(8,128)(2,1)S(1)} %constant_dynamic-slice_fusion.4), channel_id=1, source_target_pairs={{0,16},{4,20},{8,24},{12,28},{16,0},{20,4},{24,8},{28,12},{1,17},{... | collective-permute-start | bytes 393224 | tf_op jit(solution)/shard_map/ppermute | solution.py:41
  7.8 2.4 %collective-permute-done = bf16[32,2048]{1,0:T(8,128)(2,1)S(1)} collective-permute-done((bf16[32,2048]{1,0:T(8,128)(2,1)S(1)}, bf16[32,2048]{1,0:T(8,128)(2,1)S(1)}, u32[]{:S(2)}, u32[]{:S(2)}) %collective-permute-start) | collective-permute-done | bytes 131104 | tf_op jit(solution)/shard_map/ppermute | solution.py:41
  10.3 1.7 collective-permute-start.1
  12.0 1.5 collective-permute-start.6
  14.1 2.4 %tables.1 = (s32[512,1]{1,0:T(8,128)}, s32[512,1]{1,0:T(8,128)}, s32[512,1]{1,0:T(8,128)}, s32[512,1]{1,0:T(8,128)}, s32[1,1024]{1,0:T(1,128)}, /*index=5*/s32[1,128]{1,0:T(1,128)}, s32[128,1]{1,0:T(8,128)}) custom-call(s32[2]{0:T(128)} %pad_add_fusion.index, s32[1,8]{1,0:T(1,128)} %frames.1, s32[1,8]{1,0:T(1,128)} %texts.1, s32[1,8]{1,0:T(1,128)} %actions.1), custom_call_target="tpu_custom_call" | custom-call | flops 10485 | bytes 10485 | tf_op jit(solution)/shard_map/tables/pallas_call | solution.py:206
  18.2 1.5 collective-permute-start.3
  20.2 1.6 collective-permute-start.7
  23.2 1.6 collective-permute-start.8
  24.8 1.5 collective-permute-start.9
  26.2 3.3 %collective-permute-done.7.refs_4_ = bf16[64,2048]{1,0:T(8,128)(2,1)S(1)} collective-permute-done((bf16[64,2048]{1,0:T(8,128)(2,1)S(1)}, bf16[64,2048]{1,0:T(8,128)(2,1)S(1)}, u32[]{:S(2)}, u32[]{:S(2)}) %collective-permute-start.7) | collective-permute-done | bytes 262176 | tf_op jit(solution)/shard_map/ppermute | solution.py:41
  29.5 1.5 collective-permute-start.10
  31.0 1.4 collective-permute-start.11
  32.5 1.5 collective-permute-start.12
  36.3 2.5 %norm_pieces.1 = bf16[8,8,8,2048]{3,2,1,0:T(8,128)(2,1)S(1)} custom-call(s32[1]{0:T(128)} %bitcast.11.refs_0_, bf16[64,2048]{1,0:T(8,128)(2,1)S(1)} %bitcast.78, bf16[64,2048]{1,0:T(8,128)(2,1)S(1)} %collective-permute-done.6.refs_2_, bf16[64,2048]{1,0:T(8,128)(2,1)S(1)} %pad_maximum_fusion.6.refs_3_, bf16[64,2048]{1,0:T(8,128)(2,1)S(1)} %collective-permute-done.7.refs_4_, ...), custom_call_target="tpu_custom_call" | custom-call | flops 104857 | bytes 41943 | tf_op jit(solution)/shard_map/norm_pieces/pallas_call | solution.py:360
  40.9 1.5 collective-permute-start.14
  42.5 2.3 %project_rows.6 = (bf16[512,512]{1,0:T(8,128)(2,1)S(1)}, bf16[512,512]{1,0:T(8,128)(2,1)S(1)}) custom-call(bf16[512,2048]{1,0:T(8,128)(2,1)S(1)} %bitcast.72, bf16[2048,512]{1,0:T(8,128)(2,1)S(1)} %copy-done.1, bf16[2048,512]{1,0:T(8,128)(2,1)S(1)} %copy-done.2), custom_call_target="tpu_custom_call" | custom-call | flops 21474836 | bytes 20971 | tf_op jit(solution)/shard_map/project_rows/pallas_call | solution.py:234
  44.9 2.4 %project_rows.7 = (bf16[512,512]{1,0:T(8,128)(2,1)S(1)}, bf16[512,512]{1,0:T(8,128)(2,1)S(1)}) custom-call(bf16[512,2048]{1,0:T(8,128)(2,1)S(1)} %collective-permute-done.13.refs_0_.refs_1_, bf16[2048,512]{1,0:T(8,128)(2,1)S(1)} %copy-done.1, bf16[2048,512]{1,0:T(8,128)(2,1)S(1)} %copy-done.2), custom_call_target="tpu_custom_call" | custom-call | flops 21474836 | bytes 20971 | tf_op jit(solution)/shard_map/project_rows/pallas_call | solution.py:234
  47.3 1.9 %attend.1.refs_0_ = bf16[128,512]{1,0:T(8,128)(2,1)S(1)} custom-call(bf16[128,512]{1,0:T(8,128)(2,1)S(1)} %project_rows.5.query, bf16[512,512]{1,0:T(8,128)(2,1)S(1)} %get-tuple-element.171.key_a.refs_2_.refs_10_, bf16[512,512]{1,0:T(8,128)(2,1)S(1)} %get-tuple-element.172.key_b.refs_3_.refs_11_, ...), custom_call_target="tpu_custom_call" | custom-call | flops 2684354 | bytes 20971 | tf_op jit(solution)/shard_map/attend/pallas_call | solution.py:821
  49.4 2.0 %collective-permute-done.15 = bf16[96,2048]{1,0:T(8,128)(2,1)S(1)} collective-permute-done((bf16[96,2048]{1,0:T(8,128)(2,1)S(1)}, bf16[96,2048]{1,0:T(8,128)(2,1)S(1)}, u32[]{:S(2)}, u32[]{:S(2)}) %collective-permute-start.15) | collective-permute-done | bytes 393248 | tf_op jit(solution)/shard_map/ppermute | solution.py:41
  52.0 1.6 collective-permute-start.19
  55.1 3.5 %grad_activated.1 = f32[128,2048]{1,0:T(8,128)S(1)} custom-call(bf16[128,2048]{1,0:T(8,128)(2,1)S(1)} %pad_maximum_fusion.3.grad.refs_7_, bf16[2048,2048]{1,0:T(8,128)(2,1)S(1)} %bitcast.68), custom_call_target="tpu_custom_call" | custom-call | flops 10737418 | bytes 83886 | tf_op jit(solution)/shard_map/grad_activated/pallas_call | solution.py:576
  62.5 1.5 collective-permute-done.18
  64.1 5.5 %feed_own.1 = (bf16[128,2048]{1,0:T(8,128)(2,1)S(1)}, bf16[128,2048]{1,0:T(8,128)(2,1)S(1)}, f32[64,2048]{1,0:T(8,128)S(1)}, bf16[64,2048]{1,0:T(8,128)(2,1)S(1)}) custom-call(bf16[128,2048]{1,0:T(8,128)(2,1)S(1)} %constant_dynamic-update-slice_fusion.lifted.refs_6_, bf16[2048,2048]{1,0:T(8,128)(2,1)S(1)} %bitcast.70, f32[128,2048]{1,0:T(8,128)S(1)} %grad_activated.1), custom_call_target="tpu_custom_call" | custom-call | flops 21474836 | bytes 83886 | tf_op jit(solution)/shard_map/feed_own/pallas_call | solution.py:550
  69.6 2.4 %collective-permute-done.19.refs_6_ = bf16[192,2048]{1,0:T(8,128)(2,1)S(1)} collective-permute-done((bf16[192,2048]{1,0:T(8,128)(2,1)S(1)}, bf16[192,2048]{1,0:T(8,128)(2,1)S(1)}, u32[]{:S(2)}, u32[]{:S(2)}) %collective-permute-start.19) | collective-permute-done | bytes 786464 | tf_op jit(solution)/shard_map/ppermute | solution.py:41
  71.9 1.5 collective-permute-done.20
  74.7 1.9 %collective-permute-start.22 = (bf16[32,2048]{1,0:T(8,128)(2,1)S(1)}, bf16[32,2048]{1,0:T(8,128)(2,1)S(1)}, u32[]{:S(2)}, u32[]{:S(2)}) collective-permute-start(bf16[32,2048]{1,0:T(8,128)(2,1)S(1)} %constant_dynamic-slice_fusion), channel_id=1, source_target_pairs={{0,8},{4,12},{8,0},{12,4},{16,24},{20,28},{24,16},{28,20},{1,9},{5... | collective-permute-start | bytes 393224 | tf_op jit(solution)/shard_map/ppermute | solution.py:41
  77.9 1.4 collective-permute-start.24
  79.3 9.3 %attend_all.1 = (bf16[512,512]{1,0:T(8,128)(2,1)S(1)}, bf16[512,512]{1,0:T(8,128)(2,1)S(1)}, bf16[4,2560,256]{2,1,0:T(8,128)(2,1)}) custom-call(bf16[512,512]{1,0:T(8,128)(2,1)S(1)} %project_rows.8.refs_0_.refs_8_, bf16[512,512]{1,0:T(8,128)(2,1)S(1)} %project_rows.9.refs_1_.refs_9_, bf16[512,512]{1,0:T(8,128)(2,1)S(1)} %get-tuple-element.171.key_a.refs_2_.refs_10_, ...), custom_call_target="tpu_custom_call" | custom-call | flops 21474836 | bytes 41943 | tf_op jit(solution)/shard_map/attend_all/pallas_call | solution.py:913
  91.4 1.5 collective-permute-start.36
  93.9 2.4 %collective-permute-start.27 = (bf16[128,512]{1,0:T(8,128)(2,1)S(1)}, bf16[128,512]{1,0:T(8,128)(2,1)S(1)}, u32[]{:S(2)}, u32[]{:S(2)}) collective-permute-start(bf16[128,512]{1,0:T(8,128)(2,1)S(1)} %product_back.1.refs_0_), channel_id=1, source_target_pairs={{0,8},{4,12},{8,0},{12,4},{16,24},{20,28},{24,16},{28,20},{1,9},{5... | collective-permute-start | bytes 393224 | tf_op jit(solution)/shard_map/ppermute | solution.py:41
  96.2 1.5 collective-permute-start.29
  99.1 2.0 %down_own.1 = (f32[64,2048]{1,0:T(8,128)S(1)}, bf16[64,2048]{1,0:T(8,128)(2,1)S(1)}) custom-call(bf16[128,2048]{1,0:T(8,128)(2,1)S(1)} %get-tuple-element.207.rows.refs_8_, bf16[2048,2048]{1,0:T(8,128)(2,1)S(1)} %bitcast.68), custom_call_target="tpu_custom_call" | custom-call | flops 10737418 | bytes 83886 | tf_op jit(solution)/shard_map/down_own/pallas_call | solution.py:295
  102.7 6.3 %collective-permute-done.29.refs_4_ = bf16[128,512]{1,0:T(8,128)(2,1)S(1)} collective-permute-done((bf16[128,512]{1,0:T(8,128)(2,1)S(1)}, bf16[128,512]{1,0:T(8,128)(2,1)S(1)}, u32[]{:S(2)}, u32[]{:S(2)}) %collective-permute-start.29) | collective-permute-done | bytes 131104 | tf_op jit(solution)/shard_map/ppermute | solution.py:41
  111.9 1.5 collective-permute-start.26
  113.4 2.1 %collective-permute-done.28.refs_3_ = bf16[128,512]{1,0:T(8,128)(2,1)S(1)} collective-permute-done((bf16[128,512]{1,0:T(8,128)(2,1)S(1)}, bf16[128,512]{1,0:T(8,128)(2,1)S(1)}, u32[]{:S(2)}, u32[]{:S(2)}) %collective-permute-start.28) | collective-permute-done | bytes 131104 | tf_op jit(solution)/shard_map/ppermute | solution.py:41
  115.5 2.0 %collective-permute-start.32 = (bf16[128,512]{1,0:T(8,128)(2,1)S(1)}, bf16[128,512]{1,0:T(8,128)(2,1)S(1)}, u32[]{:S(2)}, u32[]{:S(2)}) collective-permute-start(bf16[128,512]{1,0:T(8,128)(2,1)S(1)} %collective-permute-done.31.refs_6_), channel_id=1, source_target_pairs={{0,4},{4,0},{8,12},{12,8},{16,20},{20,16},{24,28},{28,24},{1,5},{5... | collective-permute-start | bytes 393224 | tf_op jit(solution)/shard_map/ppermute | solution.py:41
  117.5 12.3 %feed_all.2 = (bf16[256,2048]{1,0:T(8,128)(2,1)}, bf16[2048,256]{1,0:T(8,128)(2,1)}) custom-call(s32[1]{0:T(128)} %bitcast.5.index, bf16[192,2048]{1,0:T(8,128)(2,1)S(1)} %constant_dynamic-update-slice_fusion.5.refs_0_, bf16[192,2048]{1,0:T(8,128)(2,1)S(1)} %collective-permute-done.37.refs_1_, bf16[192,2048]{1,0:T(8,128)(2,1)S(1)} %pad_maximum_fusion.refs_2_, ...), custom_call_target="tpu_custom_call" | custom-call | flops 72477576 | bytes 199229 | tf_op jit(solution)/shard_map/feed_all/pallas_call | solution.py:666
  130.0 2.4 %collective-permute-start.43 = (bf16[2,72,256]{2,1,0:T(8,128)(2,1)S(1)}, bf16[2,72,256]{2,1,0:T(8,128)(2,1)S(1)}, u32[]{:S(2)}, u32[]{:S(2)}) collective-permute-start(bf16[2,72,256]{2,1,0:T(8,128)(2,1)S(1)} %get-tuple-element.237), channel_id=1, source_target_pairs={{0,24},{4,28},{8,16},{12,20},{16,8},{20,12},{24,0},{28,4},{1,25},{... | collective-permute-start | bytes 221192 | tf_op jit(solution)/shard_map/ppermute | solution.py:41
  134.4 8.4 %attend_back.1 = (bf16[512,512]{1,0:T(8,128)(2,1)S(1)}, bf16[512,512]{1,0:T(8,128)(2,1)S(1)}, bf16[512,512]{1,0:T(8,128)(2,1)S(1)}, bf16[512,512]{1,0:T(8,128)(2...) custom-call(bf16[128,512]{1,0:T(8,128)(2,1)S(1)} %product_back.1.ref, ...), custom_call_target="tpu_custom_call" | custom-call | flops 42949672 | bytes 136314 | tf_op jit(solution)/shard_map/attend_back/pallas_call | solution.py:1029
  142.9 2.1 %product_halves.3 = (f32[64,2048]{1,0:T(8,128)S(1)}, bf16[64,2048]{1,0:T(8,128)(2,1)S(1)}) custom-call(bf16[128,512]{1,0:T(8,128)(2,1)S(1)} %get-tuple-element.238.refs_0_, bf16[128,512]{1,0:T(8,128)(2,1)S(1)} %get-tuple-element.239.refs_1_, bf16[128,512]{1,0:T(8,128)(2,1)S(1)} %get-tuple-element.240.refs_2_, bf16[2048,512]{1,0:T(8,128)(2,1)S(1)} %copy-done, ...), custom_call_target="tpu_custom_call" | custom-call | flops 8053063 | bytes 62914 | tf_op jit(solution)/shard_map/product_halves/pallas_call | solution.py:270
  145.1 2.0 %collective-permute-start.47 = (bf16[72,256]{1,0:T(8,128)(2,1)S(1)}, bf16[72,256]{1,0:T(8,128)(2,1)S(1)}, u32[]{:S(2)}, u32[]{:S(2)}) collective-permute-start(bf16[72,256]{1,0:T(8,128)(2,1)S(1)} %get-tuple-element.310), channel_id=1, source_target_pairs={{0,4},{4,0},{8,12},{12,8},{16,20},{20,16},{24,28},{28,24},{1,5},{5... | collective-permute-start | bytes 110600 | tf_op jit(solution)/shard_map/ppermute | solution.py:41
  148.3 1.4 collective-permute-start.48
  150.3 2.8 %project.1 = (f32[256,512]{1,0:T(8,128)}, f32[256,512]{1,0:T(8,128)}, f32[256,512]{1,0:T(8,128)}, f32[3,256]{1,0:T(4,128)S(1)}) custom-call(s32[1]{0:T(128)} %bitcast.5.index, bf16[512,2048]{1,0:T(8,128)(2,1)S(1)} %bitcast.74, bf16[512,2048]{1,0:T(8,128)(2,1)S(1)} %collective-permute-done.13.refs_0_.refs_1_, ...), custom_call_target="tpu_custom_call" | custom-call | flops 16106127 | bytes 47185 | tf_op jit(solution)/shard_map/project/pallas_call | solution.py:722
  154.2 1.5 collective-permute-start.50
  155.7 2.5 %collective-permute-done.50 = bf16[72,256]{1,0:T(8,128)(2,1)S(1)} collective-permute-done((bf16[72,256]{1,0:T(8,128)(2,1)S(1)}, bf16[72,256]{1,0:T(8,128)(2,1)S(1)}, u32[]{:S(2)}, u32[]{:S(2)}) %collective-permute-start.50) | collective-permute-done | bytes 36896 | tf_op jit(solution)/shard_map/ppermute | solution.py:41
  160.2 1.8 collective-permute-done.54.refs_1_
  162.4 15.0 %feed_all.3 = (f32[256,2048]{1,0:T(8,128)}, f32[2048,256]{1,0:T(8,128)}) custom-call(s32[1]{0:T(128)} %bitcast.5.index, bf16[64,2048]{1,0:T(8,128)(2,1)S(1)} %collective-permute-done.39.refs_0_, bf16[64,2048]{1,0:T(8,128)(2,1)S(1)} %collective-permute-done.54.refs_1_, bf16[192,2048]{1,0:T(8,128)(2,1)S(1)} %pad_maximum_fusion.1.refs_2_, ...), custom_call_target="tpu_custom_call" | custom-call | flops 96636768 | bytes 209715 | tf_op jit(solution)/shard_map/feed_all/pallas_call | solution.py:666
  (181 shorter events, 42.0 us)
Async XLA Ops:
  2.2 8.1 %collective-permute-start = (bf16[32,2048]{1,0:T(8,128)(2,1)S(1)}, bf16[32,2048]{1,0:T(8,128)(2,1)S(1)}, u32[]{:S(2)}, u32[]{:S(2)}) collective-permute-start(bf16[32,2048]{1,0:T(8,128)(2,1)S(1)} %constant_dynamic-slice_fusion.4), channel_id=1, source_target_pairs={{0,8},{4,12},{8,0},{12,4},{16,24},{20,28},{24,16},{28,20},{1,9},{5... | collective-permute-start | bytes 393224 | tf_op jit(solution)/shard_map/ppermute | solution.py:41
  5.2 12.9 %collective-permute-start.2 = (bf16[32,2048]{1,0:T(8,128)(2,1)S(1)}, bf16[32,2048]{1,0:T(8,128)(2,1)S(1)}, u32[]{:S(2)}, u32[]{:S(2)}) collective-permute-start(bf16[32,2048]{1,0:T(8,128)(2,1)S(1)} %constant_dynamic-slice_fusion.4), channel_id=1, source_target_pairs={{0,16},{4,20},{8,24},{12,28},{16,0},{20,4},{24,8},{28,12},{1,17},{... | collective-permute-start | bytes 393224 | tf_op jit(solution)/shard_map/ppermute | solution.py:41
  7.8 11.8 %collective-permute-start.4 = (bf16[32,2048]{1,0:T(8,128)(2,1)S(1)}, bf16[32,2048]{1,0:T(8,128)(2,1)S(1)}, u32[]{:S(2)}, u32[]{:S(2)}) collective-permute-start(bf16[32,2048]{1,0:T(8,128)(2,1)S(1)} %constant_dynamic-slice_fusion.4), channel_id=1, source_target_pairs={{0,24},{4,28},{8,16},{12,20},{16,8},{20,12},{24,0},{28,4},{1,25},{... | collective-permute-start | bytes 393224 | tf_op jit(solution)/shard_map/ppermute | solution.py:41
  10.3 9.9 %collective-permute-start.1 = (bf16[32,2048]{1,0:T(8,128)(2,1)S(1)}, bf16[32,2048]{1,0:T(8,128)(2,1)S(1)}, u32[]{:S(2)}, u32[]{:S(2)}) collective-permute-start(bf16[32,2048]{1,0:T(8,128)(2,1)S(1)} %collective-permute-done), channel_id=1, source_target_pairs={{0,2},{1,3},{2,0},{3,1},{4,6},{5,7},{6,4},{7,5},{8,10},{9,11},{10,... | collective-permute-start | bytes 393224 | tf_op jit(solution)/shard_map/ppermute | solution.py:41
  12.0 20.5 %collective-permute-start.6 = (bf16[64,2048]{1,0:T(8,128)(2,1)S(1)}, bf16[64,2048]{1,0:T(8,128)(2,1)S(1)}, u32[]{:S(2)}, u32[]{:S(2)}) collective-permute-start(bf16[64,2048]{1,0:T(8,128)(2,1)S(1)} %bitcast.76), channel_id=1, source_target_pairs={{0,4},{4,0},{8,12},{12,8},{16,20},{20,16},{24,28},{28,24},{1,5},{5... | collective-permute-start | bytes 786440 | tf_op jit(solution)/shard_map/ppermute | solution.py:41
  18.2 5.0 %collective-permute-start.3 = (bf16[32,2048]{1,0:T(8,128)(2,1)S(1)}, bf16[32,2048]{1,0:T(8,128)(2,1)S(1)}, u32[]{:S(2)}, u32[]{:S(2)}) collective-permute-start(bf16[32,2048]{1,0:T(8,128)(2,1)S(1)} %collective-permute-done.2), channel_id=1, source_target_pairs={{0,2},{1,3},{2,0},{3,1},{4,6},{5,7},{6,4},{7,5},{8,10},{9,11},{10,... | collective-permute-start | bytes 393224 | tf_op jit(solution)/shard_map/ppermute | solution.py:41
  19.7 5.1 %collective-permute-start.5 = (bf16[32,2048]{1,0:T(8,128)(2,1)S(1)}, bf16[32,2048]{1,0:T(8,128)(2,1)S(1)}, u32[]{:S(2)}, u32[]{:S(2)}) collective-permute-start(bf16[32,2048]{1,0:T(8,128)(2,1)S(1)} %collective-permute-done.4), channel_id=1, source_target_pairs={{0,2},{1,3},{2,0},{3,1},{4,6},{5,7},{6,4},{7,5},{8,10},{9,11},{10,... | collective-permute-start | bytes 393224 | tf_op jit(solution)/shard_map/ppermute | solution.py:41
  20.2 9.3 %collective-permute-start.7 = (bf16[64,2048]{1,0:T(8,128)(2,1)S(1)}, bf16[64,2048]{1,0:T(8,128)(2,1)S(1)}, u32[]{:S(2)}, u32[]{:S(2)}) collective-permute-start(bf16[64,2048]{1,0:T(8,128)(2,1)S(1)} %pad_maximum_fusion.6.refs_3_), channel_id=1, source_target_pairs={{0,4},{4,0},{8,12},{12,8},{16,20},{20,16},{24,28},{28,24},{1,5},{5... | collective-permute-start | bytes 786440 | tf_op jit(solution)/shard_map/ppermute | solution.py:41
  23.2 11.9 %collective-permute-start.8 = (bf16[64,2048]{1,0:T(8,128)(2,1)S(1)}, bf16[64,2048]{1,0:T(8,128)(2,1)S(1)}, u32[]{:S(2)}, u32[]{:S(2)}) collective-permute-start(bf16[64,2048]{1,0:T(8,128)(2,1)S(1)} %pad_maximum_fusion.7.refs_5_), channel_id=1, source_target_pairs={{0,4},{4,0},{8,12},{12,8},{16,20},{20,16},{24,28},{28,24},{1,5},{5... | collective-permute-start | bytes 786440 | tf_op jit(solution)/shard_map/ppermute | solution.py:41
  24.8 11.5 %collective-permute-start.9 = (bf16[64,2048]{1,0:T(8,128)(2,1)S(1)}, bf16[64,2048]{1,0:T(8,128)(2,1)S(1)}, u32[]{:S(2)}, u32[]{:S(2)}) collective-permute-start(bf16[64,2048]{1,0:T(8,128)(2,1)S(1)} %pad_maximum_fusion.8.refs_7_), channel_id=1, source_target_pairs={{0,4},{4,0},{8,12},{12,8},{16,20},{20,16},{24,28},{28,24},{1,5},{5... | collective-permute-start | bytes 786440 | tf_op jit(solution)/shard_map/ppermute | solution.py:41
  29.5 9.3 %collective-permute-start.10 = (bf16[32,2048]{1,0:T(8,128)(2,1)S(1)}, bf16[32,2048]{1,0:T(8,128)(2,1)S(1)}, u32[]{:S(2)}, u32[]{:S(2)}) collective-permute-start(bf16[32,2048]{1,0:T(8,128)(2,1)S(1)} %constant_dynamic-slice_fusion.2), channel_id=1, source_target_pairs={{0,8},{4,12},{8,0},{12,4},{16,24},{20,28},{24,16},{28,20},{1,9},{5... | collective-permute-start | bytes 393224 | tf_op jit(solution)/shard_map/ppermute | solution.py:41
  31.0 8.7 %collective-permute-start.11 = (bf16[32,2048]{1,0:T(8,128)(2,1)S(1)}, bf16[32,2048]{1,0:T(8,128)(2,1)S(1)}, u32[]{:S(2)}, u32[]{:S(2)}) collective-permute-start(bf16[32,2048]{1,0:T(8,128)(2,1)S(1)} %constant_dynamic-slice_fusion.2), channel_id=1, source_target_pairs={{0,16},{4,20},{8,24},{12,28},{16,0},{20,4},{24,8},{28,12},{1,17},{... | collective-permute-start | bytes 393224 | tf_op jit(solution)/shard_map/ppermute | solution.py:41
  32.5 7.2 %collective-permute-start.12 = (bf16[32,2048]{1,0:T(8,128)(2,1)S(1)}, bf16[32,2048]{1,0:T(8,128)(2,1)S(1)}, u32[]{:S(2)}, u32[]{:S(2)}) collective-permute-start(bf16[32,2048]{1,0:T(8,128)(2,1)S(1)} %constant_dynamic-slice_fusion.2), channel_id=1, source_target_pairs={{0,24},{4,28},{8,16},{12,20},{16,8},{20,12},{24,0},{28,4},{1,25},{... | collective-permute-start | bytes 393224 | tf_op jit(solution)/shard_map/ppermute | solution.py:41
  39.7 5.1 %collective-permute-start.13 = (bf16[512,2048]{1,0:T(8,128)(2,1)S(1)}, bf16[512,2048]{1,0:T(8,128)(2,1)S(1)}, u32[]{:S(2)}, u32[]{:S(2)}) collective-permute-start(bf16[512,2048]{1,0:T(8,128)(2,1)S(1)} %bitcast.71), channel_id=1, source_target_pairs={{0,1},{1,0},{2,3},{3,2},{4,5},{5,4},{6,7},{7,6},{8,9},{9,8},{10,11... | collective-permute-start | bytes 6291464 | tf_op jit(solution)/shard_map/ppermute | solution.py:41
  39.8 11.6 %collective-permute-start.15 = (bf16[96,2048]{1,0:T(8,128)(2,1)S(1)}, bf16[96,2048]{1,0:T(8,128)(2,1)S(1)}, u32[]{:S(2)}, u32[]{:S(2)}) collective-permute-start(bf16[96,2048]{1,0:T(8,128)(2,1)S(1)} %pad_maximum_fusion.5), channel_id=1, source_target_pairs={{0,2},{1,3},{2,0},{3,1},{4,6},{5,7},{6,4},{7,5},{8,10},{9,11},{10,... | collective-permute-start | bytes 1179656 | tf_op jit(solution)/shard_map/ppermute | solution.py:41
  40.9 8.4 %collective-permute-start.14 = (bf16[64,2048]{1,0:T(8,128)(2,1)S(1)}, bf16[64,2048]{1,0:T(8,128)(2,1)S(1)}, u32[]{:S(2)}, u32[]{:S(2)}) collective-permute-start(bf16[64,2048]{1,0:T(8,128)(2,1)S(1)} %bitcast.84), channel_id=1, source_target_pairs={{0,4},{4,0},{8,12},{12,8},{16,20},{20,16},{24,28},{28,24},{1,5},{5... | collective-permute-start | bytes 786440 | tf_op jit(solution)/shard_map/ppermute | solution.py:41
  52.0 20.0 %collective-permute-start.19 = (bf16[192,2048]{1,0:T(8,128)(2,1)S(1)}, bf16[192,2048]{1,0:T(8,128)(2,1)S(1)}, u32[]{:S(2)}, u32[]{:S(2)}) collective-permute-start(bf16[192,2048]{1,0:T(8,128)(2,1)S(1)} %pad_maximum_fusion.refs_2_), channel_id=1, source_target_pairs={{0,4},{4,0},{8,12},{12,8},{16,20},{20,16},{24,28},{28,24},{1,5},{5... | collective-permute-start | bytes 2359304 | tf_op jit(solution)/shard_map/ppermute | solution.py:41
  53.6 8.4 %collective-permute-start.17 = (bf16[64,2048]{1,0:T(8,128)(2,1)S(1)}, bf16[64,2048]{1,0:T(8,128)(2,1)S(1)}, u32[]{:S(2)}, u32[]{:S(2)}) collective-permute-start(bf16[64,2048]{1,0:T(8,128)(2,1)S(1)} %add_convert_fusion.3.low), channel_id=1, source_target_pairs={{0,2},{1,3},{2,0},{3,1},{4,6},{5,7},{6,4},{7,5},{8,10},{9,11},{10,... | collective-permute-start | bytes 786440 | tf_op jit(solution)/shard_map/ppermute | solution.py:41
  73.5 16.1 %collective-permute-start.21 = (bf16[64,2048]{1,0:T(8,128)(2,1)S(1)}, bf16[64,2048]{1,0:T(8,128)(2,1)S(1)}, u32[]{:S(2)}, u32[]{:S(2)}) collective-permute-start(bf16[64,2048]{1,0:T(8,128)(2,1)S(1)} %add_convert_fusion.2.low), channel_id=1, source_target_pairs={{0,2},{1,3},{2,0},{3,1},{4,6},{5,7},{6,4},{7,5},{8,10},{9,11},{10,... | collective-permute-start | bytes 786440 | tf_op jit(solution)/shard_map/ppermute | solution.py:41
  74.7 14.0 %collective-permute-start.22 = (bf16[32,2048]{1,0:T(8,128)(2,1)S(1)}, bf16[32,2048]{1,0:T(8,128)(2,1)S(1)}, u32[]{:S(2)}, u32[]{:S(2)}) collective-permute-start(bf16[32,2048]{1,0:T(8,128)(2,1)S(1)} %constant_dynamic-slice_fusion), channel_id=1, source_target_pairs={{0,8},{4,12},{8,0},{12,4},{16,24},{20,28},{24,16},{28,20},{1,9},{5... | collective-permute-start | bytes 393224 | tf_op jit(solution)/shard_map/ppermute | solution.py:41
  76.7 12.9 %collective-permute-start.23 = (bf16[32,2048]{1,0:T(8,128)(2,1)S(1)}, bf16[32,2048]{1,0:T(8,128)(2,1)S(1)}, u32[]{:S(2)}, u32[]{:S(2)}) collective-permute-start(bf16[32,2048]{1,0:T(8,128)(2,1)S(1)} %constant_dynamic-slice_fusion), channel_id=1, source_target_pairs={{0,16},{4,20},{8,24},{12,28},{16,0},{20,4},{24,8},{28,12},{1,17},{... | collective-permute-start | bytes 393224 | tf_op jit(solution)/shard_map/ppermute | solution.py:41
  77.9 11.6 %collective-permute-start.24 = (bf16[32,2048]{1,0:T(8,128)(2,1)S(1)}, bf16[32,2048]{1,0:T(8,128)(2,1)S(1)}, u32[]{:S(2)}, u32[]{:S(2)}) collective-permute-start(bf16[32,2048]{1,0:T(8,128)(2,1)S(1)} %constant_dynamic-slice_fusion), channel_id=1, source_target_pairs={{0,24},{4,28},{8,16},{12,20},{16,8},{20,12},{24,0},{28,4},{1,25},{... | collective-permute-start | bytes 393224 | tf_op jit(solution)/shard_map/ppermute | solution.py:41
  90.5 11.6 %collective-permute-start.35 = (bf16[96,2048]{1,0:T(8,128)(2,1)S(1)}, bf16[96,2048]{1,0:T(8,128)(2,1)S(1)}, u32[]{:S(2)}, u32[]{:S(2)}) collective-permute-start(bf16[96,2048]{1,0:T(8,128)(2,1)S(1)} %get-tuple-element.315), channel_id=1, source_target_pairs={{0,2},{1,3},{2,0},{3,1},{4,6},{5,7},{6,4},{7,5},{8,10},{9,11},{10,... | collective-permute-start | bytes 1179656 | tf_op jit(solution)/shard_map/ppermute | solution.py:41
  91.4 11.2 %collective-permute-start.36 = (bf16[96,2048]{1,0:T(8,128)(2,1)S(1)}, bf16[96,2048]{1,0:T(8,128)(2,1)S(1)}, u32[]{:S(2)}, u32[]{:S(2)}) collective-permute-start(bf16[96,2048]{1,0:T(8,128)(2,1)S(1)} %get-tuple-element.315), channel_id=1, source_target_pairs={{0,4},{4,0},{8,12},{12,8},{16,20},{20,16},{24,28},{28,24},{1,5},{5... | collective-permute-start | bytes 1179656 | tf_op jit(solution)/shard_map/ppermute | solution.py:41
  93.9 8.8 %collective-permute-start.27 = (bf16[128,512]{1,0:T(8,128)(2,1)S(1)}, bf16[128,512]{1,0:T(8,128)(2,1)S(1)}, u32[]{:S(2)}, u32[]{:S(2)}) collective-permute-start(bf16[128,512]{1,0:T(8,128)(2,1)S(1)} %product_back.1.refs_0_), channel_id=1, source_target_pairs={{0,8},{4,12},{8,0},{12,4},{16,24},{20,28},{24,16},{28,20},{1,9},{5... | collective-permute-start | bytes 393224 | tf_op jit(solution)/shard_map/ppermute | solution.py:41
  96.2 12.8 %collective-permute-start.29 = (bf16[128,512]{1,0:T(8,128)(2,1)S(1)}, bf16[128,512]{1,0:T(8,128)(2,1)S(1)}, u32[]{:S(2)}, u32[]{:S(2)}) collective-permute-start(bf16[128,512]{1,0:T(8,128)(2,1)S(1)} %product_back.1.refs_0_), channel_id=1, source_target_pairs={{0,16},{4,20},{8,24},{12,28},{16,0},{20,4},{24,8},{28,12},{1,17},{... | collective-permute-start | bytes 393224 | tf_op jit(solution)/shard_map/ppermute | solution.py:41
  97.7 11.3 %collective-permute-start.31 = (bf16[128,512]{1,0:T(8,128)(2,1)S(1)}, bf16[128,512]{1,0:T(8,128)(2,1)S(1)}, u32[]{:S(2)}, u32[]{:S(2)}) collective-permute-start(bf16[128,512]{1,0:T(8,128)(2,1)S(1)} %product_back.1.refs_0_), channel_id=1, source_target_pairs={{0,24},{4,28},{8,16},{12,20},{16,8},{20,12},{24,0},{28,4},{1,25},{... | collective-permute-start | bytes 393224 | tf_op jit(solution)/shard_map/ppermute | solution.py:41
  102.0 9.8 %collective-permute-start.38 = (bf16[192,2048]{1,0:T(8,128)(2,1)S(1)}, bf16[192,2048]{1,0:T(8,128)(2,1)S(1)}, u32[]{:S(2)}, u32[]{:S(2)}) collective-permute-start(bf16[192,2048]{1,0:T(8,128)(2,1)S(1)} %pad_maximum_fusion.refs_2_), channel_id=1, source_target_pairs={{0,1},{1,0},{2,3},{3,2},{4,5},{5,4},{6,7},{7,6},{8,9},{9,8},{10,11... | collective-permute-start | bytes 2359304 | tf_op jit(solution)/shard_map/ppermute | solution.py:41
  102.7 7.0 %collective-permute-start.33 = (bf16[64,2048]{1,0:T(8,128)(2,1)S(1)}, bf16[64,2048]{1,0:T(8,128)(2,1)S(1)}, u32[]{:S(2)}, u32[]{:S(2)}) collective-permute-start(bf16[64,2048]{1,0:T(8,128)(2,1)S(1)} %get-tuple-element.209), channel_id=1, source_target_pairs={{0,1},{1,0},{2,3},{3,2},{4,5},{5,4},{6,7},{7,6},{8,9},{9,8},{10,11... | collective-permute-start | bytes 786440 | tf_op jit(solution)/shard_map/ppermute | solution.py:41
  109.0 6.5 %collective-permute-start.37 = (bf16[192,2048]{1,0:T(8,128)(2,1)S(1)}, bf16[192,2048]{1,0:T(8,128)(2,1)S(1)}, u32[]{:S(2)}, u32[]{:S(2)}) collective-permute-start(bf16[192,2048]{1,0:T(8,128)(2,1)S(1)} %constant_dynamic-update-slice_fusion.5.refs_0_), channel_id=1, source_target_pairs={{0,1},{1,0},{2,3},{3,2},{4,5},{5,4},{6,7},{7,6},{8,9},{9,8},{10,11... | collective-permute-start | bytes 2359304 | tf_op jit(solution)/shard_map/ppermute | solution.py:41
  109.1 6.4 %collective-permute-start.28 = (bf16[128,512]{1,0:T(8,128)(2,1)S(1)}, bf16[128,512]{1,0:T(8,128)(2,1)S(1)}, u32[]{:S(2)}, u32[]{:S(2)}) collective-permute-start(bf16[128,512]{1,0:T(8,128)(2,1)S(1)} %collective-permute-done.27.refs_2_), channel_id=1, source_target_pairs={{0,4},{4,0},{8,12},{12,8},{16,20},{20,16},{24,28},{28,24},{1,5},{5... | collective-permute-start | bytes 393224 | tf_op jit(solution)/shard_map/ppermute | solution.py:41
  109.8 20.0 %collective-permute-start.34 = (bf16[64,2048]{1,0:T(8,128)(2,1)S(1)}, bf16[64,2048]{1,0:T(8,128)(2,1)S(1)}, u32[]{:S(2)}, u32[]{:S(2)}) collective-permute-start(bf16[64,2048]{1,0:T(8,128)(2,1)S(1)} %add_convert_fusion.1.low), channel_id=1, source_target_pairs={{0,2},{1,3},{2,0},{3,1},{4,6},{5,7},{6,4},{7,5},{8,10},{9,11},{10,... | collective-permute-start | bytes 786440 | tf_op jit(solution)/shard_map/ppermute | solution.py:41
  110.8 32.0 %collective-permute-start.40 = (bf16[96,2048]{1,0:T(8,128)(2,1)S(1)}, bf16[96,2048]{1,0:T(8,128)(2,1)S(1)}, u32[]{:S(2)}, u32[]{:S(2)}) collective-permute-start(bf16[96,2048]{1,0:T(8,128)(2,1)S(1)} %collective-permute-done.36), channel_id=1, source_target_pairs={{0,2},{1,3},{2,0},{3,1},{4,6},{5,7},{6,4},{7,5},{8,10},{9,11},{10,... | collective-permute-start | bytes 1179656 | tf_op jit(solution)/shard_map/ppermute | solution.py:41
  111.9 17.9 %collective-permute-start.26 = (bf16[128,512]{1,0:T(8,128)(2,1)S(1)}, bf16[128,512]{1,0:T(8,128)(2,1)S(1)}, u32[]{:S(2)}, u32[]{:S(2)}) collective-permute-start(bf16[128,512]{1,0:T(8,128)(2,1)S(1)} %product_back.1.refs_0_), channel_id=1, source_target_pairs={{0,4},{4,0},{8,12},{12,8},{16,20},{20,16},{24,28},{28,24},{1,5},{5... | collective-permute-start | bytes 393224 | tf_op jit(solution)/shard_map/ppermute | solution.py:41
  115.5 14.3 %collective-permute-start.30 = (bf16[128,512]{1,0:T(8,128)(2,1)S(1)}, bf16[128,512]{1,0:T(8,128)(2,1)S(1)}, u32[]{:S(2)}, u32[]{:S(2)}) collective-permute-start(bf16[128,512]{1,0:T(8,128)(2,1)S(1)} %collective-permute-done.29.refs_4_), channel_id=1, source_target_pairs={{0,4},{4,0},{8,12},{12,8},{16,20},{20,16},{24,28},{28,24},{1,5},{5... | collective-permute-start | bytes 393224 | tf_op jit(solution)/shard_map/ppermute | solution.py:41
  115.5 14.2 %collective-permute-start.32 = (bf16[128,512]{1,0:T(8,128)(2,1)S(1)}, bf16[128,512]{1,0:T(8,128)(2,1)S(1)}, u32[]{:S(2)}, u32[]{:S(2)}) collective-permute-start(bf16[128,512]{1,0:T(8,128)(2,1)S(1)} %collective-permute-done.31.refs_6_), channel_id=1, source_target_pairs={{0,4},{4,0},{8,12},{12,8},{16,20},{20,16},{24,28},{28,24},{1,5},{5... | collective-permute-start | bytes 393224 | tf_op jit(solution)/shard_map/ppermute | solution.py:41
  129.8 13.1 %collective-permute-start.39 = (bf16[64,2048]{1,0:T(8,128)(2,1)S(1)}, bf16[64,2048]{1,0:T(8,128)(2,1)S(1)}, u32[]{:S(2)}, u32[]{:S(2)}) collective-permute-start(bf16[64,2048]{1,0:T(8,128)(2,1)S(1)} %get-tuple-element.232), channel_id=1, source_target_pairs={{0,4},{4,0},{8,12},{12,8},{16,20},{20,16},{24,28},{28,24},{1,5},{5... | collective-permute-start | bytes 786440 | tf_op jit(solution)/shard_map/ppermute | solution.py:41
  130.0 12.9 %collective-permute-start.43 = (bf16[2,72,256]{2,1,0:T(8,128)(2,1)S(1)}, bf16[2,72,256]{2,1,0:T(8,128)(2,1)S(1)}, u32[]{:S(2)}, u32[]{:S(2)}) collective-permute-start(bf16[2,72,256]{2,1,0:T(8,128)(2,1)S(1)} %get-tuple-element.237), channel_id=1, source_target_pairs={{0,24},{4,28},{8,16},{12,20},{16,8},{20,12},{24,0},{28,4},{1,25},{... | collective-permute-start | bytes 221192 | tf_op jit(solution)/shard_map/ppermute | solution.py:41
  132.4 10.5 %collective-permute-start.42 = (bf16[2,72,256]{2,1,0:T(8,128)(2,1)S(1)}, bf16[2,72,256]{2,1,0:T(8,128)(2,1)S(1)}, u32[]{:S(2)}, u32[]{:S(2)}) collective-permute-start(bf16[2,72,256]{2,1,0:T(8,128)(2,1)S(1)} %get-tuple-element.236), channel_id=1, source_target_pairs={{0,16},{4,20},{8,24},{12,28},{16,0},{20,4},{24,8},{28,12},{1,17},{... | collective-permute-start | bytes 221192 | tf_op jit(solution)/shard_map/ppermute | solution.py:41
  133.7 9.2 %collective-permute-start.41 = (bf16[2,72,256]{2,1,0:T(8,128)(2,1)S(1)}, bf16[2,72,256]{2,1,0:T(8,128)(2,1)S(1)}, u32[]{:S(2)}, u32[]{:S(2)}) collective-permute-start(bf16[2,72,256]{2,1,0:T(8,128)(2,1)S(1)} %get-tuple-element.235), channel_id=1, source_target_pairs={{0,8},{4,12},{8,0},{12,4},{16,24},{20,28},{24,16},{28,20},{1,9},{5... | collective-permute-start | bytes 221192 | tf_op jit(solution)/shard_map/ppermute | solution.py:41
  145.1 10.6 %collective-permute-start.47 = (bf16[72,256]{1,0:T(8,128)(2,1)S(1)}, bf16[72,256]{1,0:T(8,128)(2,1)S(1)}, u32[]{:S(2)}, u32[]{:S(2)}) collective-permute-start(bf16[72,256]{1,0:T(8,128)(2,1)S(1)} %get-tuple-element.310), channel_id=1, source_target_pairs={{0,4},{4,0},{8,12},{12,8},{16,20},{20,16},{24,28},{28,24},{1,5},{5... | collective-permute-start | bytes 110600 | tf_op jit(solution)/shard_map/ppermute | solution.py:41
  147.2 11.0 %collective-permute-start.45 = (bf16[64,2048]{1,0:T(8,128)(2,1)S(1)}, bf16[64,2048]{1,0:T(8,128)(2,1)S(1)}, u32[]{:S(2)}, u32[]{:S(2)}) collective-permute-start(bf16[64,2048]{1,0:T(8,128)(2,1)S(1)} %add_convert_fusion.low), channel_id=1, source_target_pairs={{0,2},{1,3},{2,0},{3,1},{4,6},{5,7},{6,4},{7,5},{8,10},{9,11},{10,... | collective-permute-start | bytes 786440 | tf_op jit(solution)/shard_map/ppermute | solution.py:41
  148.3 7.5 %collective-permute-start.48 = (bf16[72,256]{1,0:T(8,128)(2,1)S(1)}, bf16[72,256]{1,0:T(8,128)(2,1)S(1)}, u32[]{:S(2)}, u32[]{:S(2)}) collective-permute-start(bf16[72,256]{1,0:T(8,128)(2,1)S(1)} %get-tuple-element.325), channel_id=1, source_target_pairs={{0,4},{4,0},{8,12},{12,8},{16,20},{20,16},{24,28},{28,24},{1,5},{5... | collective-permute-start | bytes 110600 | tf_op jit(solution)/shard_map/ppermute | solution.py:41
  149.7 6.0 %collective-permute-start.49 = (bf16[72,256]{1,0:T(8,128)(2,1)S(1)}, bf16[72,256]{1,0:T(8,128)(2,1)S(1)}, u32[]{:S(2)}, u32[]{:S(2)}) collective-permute-start(bf16[72,256]{1,0:T(8,128)(2,1)S(1)} %get-tuple-element.323), channel_id=1, source_target_pairs={{0,4},{4,0},{8,12},{12,8},{16,20},{20,16},{24,28},{28,24},{1,5},{5... | collective-permute-start | bytes 110600 | tf_op jit(solution)/shard_map/ppermute | solution.py:41
  154.2 4.0 %collective-permute-start.50 = (bf16[72,256]{1,0:T(8,128)(2,1)S(1)}, bf16[72,256]{1,0:T(8,128)(2,1)S(1)}, u32[]{:S(2)}, u32[]{:S(2)}) collective-permute-start(bf16[72,256]{1,0:T(8,128)(2,1)S(1)} %get-tuple-element.321), channel_id=1, source_target_pairs={{0,4},{4,0},{8,12},{12,8},{16,20},{20,16},{24,28},{28,24},{1,5},{5... | collective-permute-start | bytes 110600 | tf_op jit(solution)/shard_map/ppermute | solution.py:41
  158.2 3.8 %collective-permute-start.55 = (bf16[192,2048]{1,0:T(8,128)(2,1)S(1)}, bf16[192,2048]{1,0:T(8,128)(2,1)S(1)}, u32[]{:S(2)}, u32[]{:S(2)}) collective-permute-start(bf16[192,2048]{1,0:T(8,128)(2,1)S(1)} %pad_maximum_fusion.1.refs_2_), channel_id=1, source_target_pairs={{0,1},{1,0},{2,3},{3,2},{4,5},{5,4},{6,7},{7,6},{8,9},{9,8},{10,11... | collective-permute-start | bytes 2359304 | tf_op jit(solution)/shard_map/ppermute | solution.py:41
  158.2 4.2 %collective-permute-start.57 = (bf16[192,2048]{1,0:T(8,128)(2,1)S(1)}, bf16[192,2048]{1,0:T(8,128)(2,1)S(1)}, u32[]{:S(2)}, u32[]{:S(2)}) collective-permute-start(bf16[192,2048]{1,0:T(8,128)(2,1)S(1)} %collective-permute-done.19.refs_6_), channel_id=1, source_target_pairs={{0,1},{1,0},{2,3},{3,2},{4,5},{5,4},{6,7},{7,6},{8,9},{9,8},{10,11... | collective-permute-start | bytes 2359304 | tf_op jit(solution)/shard_map/ppermute | solution.py:41
  177.5 4.9 %collective-permute-start.58 = (bf16[8,72,256]{2,1,0:T(8,128)(2,1)S(1)}, bf16[8,72,256]{2,1,0:T(8,128)(2,1)S(1)}, u32[]{:S(2)}, u32[]{:S(2)}) collective-permute-start(bf16[8,72,256]{2,1,0:T(8,128)(2,1)S(1)} %constant_dynamic-update-slice_fusion.9.came_a), channel_id=1, source_target_pairs={{0,1},{1,0},{2,3},{3,2},{4,5},{5,4},{6,7},{7,6},{8,9},{9,8},{10,11... | collective-permute-start | bytes 884744 | tf_op jit(solution)/shard_map/ppermute | solution.py:41
  (30 other events, 209.5 us)

commit v7 on v6

--- a/solution.py
+++ b/solution.py
@@ -1180,14 +1180,15 @@
         columns[outer] = came[0]
         for bit in range(1, inner):
             columns[outer | bit] = swap(came[bit], "seq", bit)
+    other, columns = after((other, columns), query_grad)
+    first_gain_grad = after(first_gain_grad, other)
     first_gain_grad = first_gain_grad + swap(first_gain_grad, "mlp", 1)
-    other, first_gain_grad, columns = after((other, first_gain_grad, columns), query_grad)
     input_half = last(inputs_half, low, other, grad_residual, first_gain, half_kind, shards)
     outputs_half = finish(residual, down_low, after(down_other, input_half), shards)
     rest_lifted = with_core(after(lifted_inner, other))
     rest_grads = with_core(after(grad_inner, other))
     up_grad, down_grad = feed_all(
-        after(rest_lifted, outputs_half), rest_grads, up_weight, down_weight, shards, sums
+        after(rest_lifted, outputs_half, first_gain_grad), rest_grads, up_weight, down_weight, shards, sums
     )
     bit = 2
     while bit < lax.axis_size("mlp"):

time: 184 us -> 181 us (0.984)
  waiting for transfers between devices: 37.4 us -> 34.9 us
    ppermute x59, waiting for transfers between devices: 37.4 us -> 34.9 us  [swap(): return lax.ppermute(value, axis, [(i, i ^ bit) for i in range(size)])]
  transfers between devices with their start and end apart: 59 -> 59, of which waited for: 24 -> 22; matrix products, arithmetic and copies ran while one was open for 1% -> 1% of each run, Pallas kernels for 34% -> 34%
where the time goes in v7:
time: 181 us
  Pallas kernels  81.4 us (45%)
  starting transfers between devices  59.4 us (33%)
  waiting for transfers between devices  34.9 us (19%)
  local copies, waits for them, and re-layouts  2.21 us (1%)
    ppermute x59, starting transfers between devices, swap(): return lax.ppermute(value, axis, [(i, i ^ bit) for i in range(size)])  59.4 us
    ppermute x59, waiting for transfers between devices, swap(): return lax.ppermute(value, axis, [(i, i ^ bit) for i in range(size)])  34.9 us
    pallas_call x2, Pallas kernels, feed_all(): pl.pallas_call(partial(all_kernel, count=count), grid_spec=pltpu.Prefetch...  27.3 us
    pallas_call x1, Pallas kernels, attend_all(): pl.pallas_call(partial(all_forward_kernel, groups=groups, scale=1.0 / mat...  9.35 us
    pallas_call x1, Pallas kernels, attend_back(): pl.pallas_call(partial(backward_kernel, count=count, groups=groups, scale...  8.36 us
    pallas_call x5, Pallas kernels, project_rows(): pl.pallas_call(partial(rows_kernel, count=len(weights)), out_shape=[jax.S...  7.65 us
    pallas_call x1, Pallas kernels, feed_own(): pl.pallas_call(own_kernel, in_specs=[WHOLE] * 3, out_specs=[WHOLE] * 4, o...  5.47 us
  transfers between devices with their start and end apart: 59, of which 22 were waited for; matrix products, arithmetic and copies ran while one was open for 1% of the time, Pallas kernels for 34%

profile of v7, /device:TPU:0, one launch (start us, length us, event | category | flops | bytes accessed | tf_op | source)
XLA Modules:
  0.0 181.2 jit_solution(1499504144718770639)
XLA Ops:
  2.2 3.1 %collective-permute-start = (bf16[32,2048]{1,0:T(8,128)(2,1)S(1)}, bf16[32,2048]{1,0:T(8,128)(2,1)S(1)}, u32[]{:S(2)}, u32[]{:S(2)}) collective-permute-start(bf16[32,2048]{1,0:T(8,128)(2,1)S(1)} %constant_dynamic-slice_fusion.4), channel_id=1, source_target_pairs={{0,8},{4,12},{8,0},{12,4},{16,24},{20,28},{24,16},{28,20},{1,9},{5... | collective-permute-start | bytes 393224 | tf_op jit(solution)/shard_map/ppermute | solution.py:41
  5.2 2.6 %collective-permute-start.2 = (bf16[32,2048]{1,0:T(8,128)(2,1)S(1)}, bf16[32,2048]{1,0:T(8,128)(2,1)S(1)}, u32[]{:S(2)}, u32[]{:S(2)}) collective-permute-start(bf16[32,2048]{1,0:T(8,128)(2,1)S(1)} %constant_dynamic-slice_fusion.4), channel_id=1, source_target_pairs={{0,16},{4,20},{8,24},{12,28},{16,0},{20,4},{24,8},{28,12},{1,17},{... | collective-permute-start | bytes 393224 | tf_op jit(solution)/shard_map/ppermute | solution.py:41
  7.8 2.4 %collective-permute-done = bf16[32,2048]{1,0:T(8,128)(2,1)S(1)} collective-permute-done((bf16[32,2048]{1,0:T(8,128)(2,1)S(1)}, bf16[32,2048]{1,0:T(8,128)(2,1)S(1)}, u32[]{:S(2)}, u32[]{:S(2)}) %collective-permute-start) | collective-permute-done | bytes 131104 | tf_op jit(solution)/shard_map/ppermute | solution.py:41
  10.3 1.7 collective-permute-start.1
  12.0 1.5 collective-permute-start.6
  14.1 2.4 %tables.1 = (s32[512,1]{1,0:T(8,128)}, s32[512,1]{1,0:T(8,128)}, s32[512,1]{1,0:T(8,128)}, s32[512,1]{1,0:T(8,128)}, s32[1,1024]{1,0:T(1,128)}, /*index=5*/s32[1,128]{1,0:T(1,128)}, s32[128,1]{1,0:T(8,128)}) custom-call(s32[2]{0:T(128)} %pad_add_fusion.index, s32[1,8]{1,0:T(1,128)} %frames.1, s32[1,8]{1,0:T(1,128)} %texts.1, s32[1,8]{1,0:T(1,128)} %actions.1), custom_call_target="tpu_custom_call" | custom-call | flops 10485 | bytes 10485 | tf_op jit(solution)/shard_map/tables/pallas_call | solution.py:206
  18.2 1.5 collective-permute-start.3
  20.2 1.6 collective-permute-start.7
  23.2 1.6 collective-permute-start.8
  24.8 1.5 collective-permute-start.9
  26.2 3.3 %collective-permute-done.7.refs_4_ = bf16[64,2048]{1,0:T(8,128)(2,1)S(1)} collective-permute-done((bf16[64,2048]{1,0:T(8,128)(2,1)S(1)}, bf16[64,2048]{1,0:T(8,128)(2,1)S(1)}, u32[]{:S(2)}, u32[]{:S(2)}) %collective-permute-start.7) | collective-permute-done | bytes 262176 | tf_op jit(solution)/shard_map/ppermute | solution.py:41
  29.5 1.5 collective-permute-start.10
  31.0 1.4 collective-permute-start.11
  32.5 1.5 collective-permute-start.12
  36.3 2.5 %norm_pieces.1 = bf16[8,8,8,2048]{3,2,1,0:T(8,128)(2,1)S(1)} custom-call(s32[1]{0:T(128)} %bitcast.11.refs_0_, bf16[64,2048]{1,0:T(8,128)(2,1)S(1)} %bitcast.78, bf16[64,2048]{1,0:T(8,128)(2,1)S(1)} %collective-permute-done.6.refs_2_, bf16[64,2048]{1,0:T(8,128)(2,1)S(1)} %pad_maximum_fusion.6.refs_3_, bf16[64,2048]{1,0:T(8,128)(2,1)S(1)} %collective-permute-done.7.refs_4_, ...), custom_call_target="tpu_custom_call" | custom-call | flops 104857 | bytes 41943 | tf_op jit(solution)/shard_map/norm_pieces/pallas_call | solution.py:360
  40.9 1.5 collective-permute-start.14
  42.5 2.3 %project_rows.6 = (bf16[512,512]{1,0:T(8,128)(2,1)S(1)}, bf16[512,512]{1,0:T(8,128)(2,1)S(1)}) custom-call(bf16[512,2048]{1,0:T(8,128)(2,1)S(1)} %bitcast.72, bf16[2048,512]{1,0:T(8,128)(2,1)S(1)} %copy-done.1, bf16[2048,512]{1,0:T(8,128)(2,1)S(1)} %copy-done.2), custom_call_target="tpu_custom_call" | custom-call | flops 21474836 | bytes 20971 | tf_op jit(solution)/shard_map/project_rows/pallas_call | solution.py:234
  44.9 2.4 %project_rows.7 = (bf16[512,512]{1,0:T(8,128)(2,1)S(1)}, bf16[512,512]{1,0:T(8,128)(2,1)S(1)}) custom-call(bf16[512,2048]{1,0:T(8,128)(2,1)S(1)} %collective-permute-done.13.refs_0_.refs_1_, bf16[2048,512]{1,0:T(8,128)(2,1)S(1)} %copy-done.1, bf16[2048,512]{1,0:T(8,128)(2,1)S(1)} %copy-done.2), custom_call_target="tpu_custom_call" | custom-call | flops 21474836 | bytes 20971 | tf_op jit(solution)/shard_map/project_rows/pallas_call | solution.py:234
  47.3 1.9 %attend.1.refs_0_ = bf16[128,512]{1,0:T(8,128)(2,1)S(1)} custom-call(bf16[128,512]{1,0:T(8,128)(2,1)S(1)} %project_rows.5.query, bf16[512,512]{1,0:T(8,128)(2,1)S(1)} %get-tuple-element.171.key_a.refs_2_.refs_10_, bf16[512,512]{1,0:T(8,128)(2,1)S(1)} %get-tuple-element.172.key_b.refs_3_.refs_11_, ...), custom_call_target="tpu_custom_call" | custom-call | flops 2684354 | bytes 20971 | tf_op jit(solution)/shard_map/attend/pallas_call | solution.py:821
  49.4 2.0 %collective-permute-done.15 = bf16[96,2048]{1,0:T(8,128)(2,1)S(1)} collective-permute-done((bf16[96,2048]{1,0:T(8,128)(2,1)S(1)}, bf16[96,2048]{1,0:T(8,128)(2,1)S(1)}, u32[]{:S(2)}, u32[]{:S(2)}) %collective-permute-start.15) | collective-permute-done | bytes 393248 | tf_op jit(solution)/shard_map/ppermute | solution.py:41
  52.0 1.6 collective-permute-start.19
  55.1 3.5 %grad_activated.1 = f32[128,2048]{1,0:T(8,128)S(1)} custom-call(bf16[128,2048]{1,0:T(8,128)(2,1)S(1)} %pad_maximum_fusion.3.grad.refs_7_, bf16[2048,2048]{1,0:T(8,128)(2,1)S(1)} %bitcast.68), custom_call_target="tpu_custom_call" | custom-call | flops 10737418 | bytes 83886 | tf_op jit(solution)/shard_map/grad_activated/pallas_call | solution.py:576
  62.5 1.5 collective-permute-done.18
  64.1 5.5 %feed_own.1 = (bf16[128,2048]{1,0:T(8,128)(2,1)S(1)}, bf16[128,2048]{1,0:T(8,128)(2,1)S(1)}, f32[64,2048]{1,0:T(8,128)S(1)}, bf16[64,2048]{1,0:T(8,128)(2,1)S(1)}) custom-call(bf16[128,2048]{1,0:T(8,128)(2,1)S(1)} %constant_dynamic-update-slice_fusion.lifted.refs_6_, bf16[2048,2048]{1,0:T(8,128)(2,1)S(1)} %bitcast.70, f32[128,2048]{1,0:T(8,128)S(1)} %grad_activated.1), custom_call_target="tpu_custom_call" | custom-call | flops 21474836 | bytes 83886 | tf_op jit(solution)/shard_map/feed_own/pallas_call | solution.py:550
  69.6 2.4 %collective-permute-done.19.refs_6_ = bf16[192,2048]{1,0:T(8,128)(2,1)S(1)} collective-permute-done((bf16[192,2048]{1,0:T(8,128)(2,1)S(1)}, bf16[192,2048]{1,0:T(8,128)(2,1)S(1)}, u32[]{:S(2)}, u32[]{:S(2)}) %collective-permute-start.19) | collective-permute-done | bytes 786464 | tf_op jit(solution)/shard_map/ppermute | solution.py:41
  71.9 1.5 collective-permute-done.20
  74.7 1.9 %collective-permute-start.22 = (bf16[32,2048]{1,0:T(8,128)(2,1)S(1)}, bf16[32,2048]{1,0:T(8,128)(2,1)S(1)}, u32[]{:S(2)}, u32[]{:S(2)}) collective-permute-start(bf16[32,2048]{1,0:T(8,128)(2,1)S(1)} %constant_dynamic-slice_fusion), channel_id=1, source_target_pairs={{0,8},{4,12},{8,0},{12,4},{16,24},{20,28},{24,16},{28,20},{1,9},{5... | collective-permute-start | bytes 393224 | tf_op jit(solution)/shard_map/ppermute | solution.py:41
  77.9 1.4 collective-permute-start.24
  79.3 9.3 %attend_all.1 = (bf16[512,512]{1,0:T(8,128)(2,1)S(1)}, bf16[512,512]{1,0:T(8,128)(2,1)S(1)}, bf16[4,2560,256]{2,1,0:T(8,128)(2,1)}) custom-call(bf16[512,512]{1,0:T(8,128)(2,1)S(1)} %project_rows.8.refs_0_.refs_8_, bf16[512,512]{1,0:T(8,128)(2,1)S(1)} %project_rows.9.refs_1_.refs_9_, bf16[512,512]{1,0:T(8,128)(2,1)S(1)} %get-tuple-element.171.key_a.refs_2_.refs_10_, ...), custom_call_target="tpu_custom_call" | custom-call | flops 21474836 | bytes 41943 | tf_op jit(solution)/shard_map/attend_all/pallas_call | solution.py:913
  91.4 1.5 collective-permute-start.36
  93.9 2.4 %collective-permute-start.27 = (bf16[128,512]{1,0:T(8,128)(2,1)S(1)}, bf16[128,512]{1,0:T(8,128)(2,1)S(1)}, u32[]{:S(2)}, u32[]{:S(2)}) collective-permute-start(bf16[128,512]{1,0:T(8,128)(2,1)S(1)} %product_back.1.refs_0_), channel_id=1, source_target_pairs={{0,8},{4,12},{8,0},{12,4},{16,24},{20,28},{24,16},{28,20},{1,9},{5... | collective-permute-start | bytes 393224 | tf_op jit(solution)/shard_map/ppermute | solution.py:41
  96.2 1.5 collective-permute-start.29
  97.7 1.4 collective-permute-start.31
  99.1 2.0 %down_own.1 = (f32[64,2048]{1,0:T(8,128)S(1)}, bf16[64,2048]{1,0:T(8,128)(2,1)S(1)}) custom-call(bf16[128,2048]{1,0:T(8,128)(2,1)S(1)} %get-tuple-element.207.rows.refs_8_, bf16[2048,2048]{1,0:T(8,128)(2,1)S(1)} %bitcast.68), custom_call_target="tpu_custom_call" | custom-call | flops 10737418 | bytes 83886 | tf_op jit(solution)/shard_map/down_own/pallas_call | solution.py:295
  102.7 6.3 %collective-permute-done.29.refs_4_ = bf16[128,512]{1,0:T(8,128)(2,1)S(1)} collective-permute-done((bf16[128,512]{1,0:T(8,128)(2,1)S(1)}, bf16[128,512]{1,0:T(8,128)(2,1)S(1)}, u32[]{:S(2)}, u32[]{:S(2)}) %collective-permute-start.29) | collective-permute-done | bytes 131104 | tf_op jit(solution)/shard_map/ppermute | solution.py:41
  111.9 1.5 collective-permute-start.26
  113.4 2.1 %collective-permute-done.28.refs_3_ = bf16[128,512]{1,0:T(8,128)(2,1)S(1)} collective-permute-done((bf16[128,512]{1,0:T(8,128)(2,1)S(1)}, bf16[128,512]{1,0:T(8,128)(2,1)S(1)}, u32[]{:S(2)}, u32[]{:S(2)}) %collective-permute-start.28) | collective-permute-done | bytes 131104 | tf_op jit(solution)/shard_map/ppermute | solution.py:41
  115.5 2.0 %collective-permute-start.32 = (bf16[128,512]{1,0:T(8,128)(2,1)S(1)}, bf16[128,512]{1,0:T(8,128)(2,1)S(1)}, u32[]{:S(2)}, u32[]{:S(2)}) collective-permute-start(bf16[128,512]{1,0:T(8,128)(2,1)S(1)} %collective-permute-done.31.refs_6_), channel_id=1, source_target_pairs={{0,4},{4,0},{8,12},{12,8},{16,20},{20,16},{24,28},{28,24},{1,5},{5... | collective-permute-start | bytes 393224 | tf_op jit(solution)/shard_map/ppermute | solution.py:41
  117.5 12.3 %feed_all.2 = (bf16[256,2048]{1,0:T(8,128)(2,1)}, bf16[2048,256]{1,0:T(8,128)(2,1)}) custom-call(s32[1]{0:T(128)} %bitcast.5.index, bf16[192,2048]{1,0:T(8,128)(2,1)S(1)} %constant_dynamic-update-slice_fusion.5.refs_0_, bf16[192,2048]{1,0:T(8,128)(2,1)S(1)} %collective-permute-done.37.refs_1_, bf16[192,2048]{1,0:T(8,128)(2,1)S(1)} %pad_maximum_fusion.refs_2_, ...), custom_call_target="tpu_custom_call" | custom-call | flops 72477576 | bytes 199229 | tf_op jit(solution)/shard_map/feed_all/pallas_call | solution.py:666
  130.0 2.4 %collective-permute-start.43 = (bf16[2,72,256]{2,1,0:T(8,128)(2,1)S(1)}, bf16[2,72,256]{2,1,0:T(8,128)(2,1)S(1)}, u32[]{:S(2)}, u32[]{:S(2)}) collective-permute-start(bf16[2,72,256]{2,1,0:T(8,128)(2,1)S(1)} %get-tuple-element.237), channel_id=1, source_target_pairs={{0,24},{4,28},{8,16},{12,20},{16,8},{20,12},{24,0},{28,4},{1,25},{... | collective-permute-start | bytes 221192 | tf_op jit(solution)/shard_map/ppermute | solution.py:41
  134.4 8.4 %attend_back.1 = (bf16[512,512]{1,0:T(8,128)(2,1)S(1)}, bf16[512,512]{1,0:T(8,128)(2,1)S(1)}, bf16[512,512]{1,0:T(8,128)(2,1)S(1)}, bf16[512,512]{1,0:T(8,128)(2...) custom-call(bf16[128,512]{1,0:T(8,128)(2,1)S(1)} %product_back.1.ref, ...), custom_call_target="tpu_custom_call" | custom-call | flops 42949672 | bytes 136314 | tf_op jit(solution)/shard_map/attend_back/pallas_call | solution.py:1029
  142.9 2.1 %product_halves.3 = (f32[64,2048]{1,0:T(8,128)S(1)}, bf16[64,2048]{1,0:T(8,128)(2,1)S(1)}) custom-call(bf16[128,512]{1,0:T(8,128)(2,1)S(1)} %get-tuple-element.238.refs_0_, bf16[128,512]{1,0:T(8,128)(2,1)S(1)} %get-tuple-element.239.refs_1_, bf16[128,512]{1,0:T(8,128)(2,1)S(1)} %get-tuple-element.240.refs_2_, bf16[2048,512]{1,0:T(8,128)(2,1)S(1)} %copy-done, ...), custom_call_target="tpu_custom_call" | custom-call | flops 8053063 | bytes 62914 | tf_op jit(solution)/shard_map/product_halves/pallas_call | solution.py:270
  145.1 2.0 %collective-permute-start.46 = (bf16[72,256]{1,0:T(8,128)(2,1)S(1)}, bf16[72,256]{1,0:T(8,128)(2,1)S(1)}, u32[]{:S(2)}, u32[]{:S(2)}) collective-permute-start(bf16[72,256]{1,0:T(8,128)(2,1)S(1)} %get-tuple-element.310), channel_id=1, source_target_pairs={{0,4},{4,0},{8,12},{12,8},{16,20},{20,16},{24,28},{28,24},{1,5},{5... | collective-permute-start | bytes 110600 | tf_op jit(solution)/shard_map/ppermute | solution.py:41
  148.3 1.4 collective-permute-start.47
  150.3 1.4 collective-permute-start.49
  151.7 2.8 %project.1 = (f32[256,512]{1,0:T(8,128)}, f32[256,512]{1,0:T(8,128)}, f32[256,512]{1,0:T(8,128)}, f32[3,256]{1,0:T(4,128)S(1)}) custom-call(s32[1]{0:T(128)} %bitcast.5.index, bf16[512,2048]{1,0:T(8,128)(2,1)S(1)} %bitcast.74, bf16[512,2048]{1,0:T(8,128)(2,1)S(1)} %collective-permute-done.13.refs_0_.refs_1_, ...), custom_call_target="tpu_custom_call" | custom-call | flops 16106127 | bytes 47185 | tf_op jit(solution)/shard_map/project/pallas_call | solution.py:722
  157.6 2.2 %collective-permute-done.52 = f32[3,256]{1,0:T(4,128)S(1)} collective-permute-done((f32[3,256]{1,0:T(4,128)S(1)}, f32[3,256]{1,0:T(4,128)S(1)}, u32[]{:S(2)}, u32[]{:S(2)}) %collective-permute-start.52) | collective-permute-done | bytes 3104 | tf_op jit(solution)/shard_map/ppermute | solution.py:41
  159.8 15.0 %feed_all.3 = (f32[256,2048]{1,0:T(8,128)}, f32[2048,256]{1,0:T(8,128)}) custom-call(s32[1]{0:T(128)} %bitcast.5.index, bf16[64,2048]{1,0:T(8,128)(2,1)S(1)} %collective-permute-done.39.refs_0_, bf16[64,2048]{1,0:T(8,128)(2,1)S(1)} %collective-permute-done.54.refs_1_, bf16[192,2048]{1,0:T(8,128)(2,1)S(1)} %pad_maximum_fusion.1.refs_2_, ...), custom_call_target="tpu_custom_call" | custom-call | flops 96636768 | bytes 209715 | tf_op jit(solution)/shard_map/feed_all/pallas_call | solution.py:666
  (181 shorter events, 40.2 us)
Async XLA Ops:
  2.2 8.1 %collective-permute-start = (bf16[32,2048]{1,0:T(8,128)(2,1)S(1)}, bf16[32,2048]{1,0:T(8,128)(2,1)S(1)}, u32[]{:S(2)}, u32[]{:S(2)}) collective-permute-start(bf16[32,2048]{1,0:T(8,128)(2,1)S(1)} %constant_dynamic-slice_fusion.4), channel_id=1, source_target_pairs={{0,8},{4,12},{8,0},{12,4},{16,24},{20,28},{24,16},{28,20},{1,9},{5... | collective-permute-start | bytes 393224 | tf_op jit(solution)/shard_map/ppermute | solution.py:41
  5.2 12.9 %collective-permute-start.2 = (bf16[32,2048]{1,0:T(8,128)(2,1)S(1)}, bf16[32,2048]{1,0:T(8,128)(2,1)S(1)}, u32[]{:S(2)}, u32[]{:S(2)}) collective-permute-start(bf16[32,2048]{1,0:T(8,128)(2,1)S(1)} %constant_dynamic-slice_fusion.4), channel_id=1, source_target_pairs={{0,16},{4,20},{8,24},{12,28},{16,0},{20,4},{24,8},{28,12},{1,17},{... | collective-permute-start | bytes 393224 | tf_op jit(solution)/shard_map/ppermute | solution.py:41
  7.8 11.8 %collective-permute-start.4 = (bf16[32,2048]{1,0:T(8,128)(2,1)S(1)}, bf16[32,2048]{1,0:T(8,128)(2,1)S(1)}, u32[]{:S(2)}, u32[]{:S(2)}) collective-permute-start(bf16[32,2048]{1,0:T(8,128)(2,1)S(1)} %constant_dynamic-slice_fusion.4), channel_id=1, source_target_pairs={{0,24},{4,28},{8,16},{12,20},{16,8},{20,12},{24,0},{28,4},{1,25},{... | collective-permute-start | bytes 393224 | tf_op jit(solution)/shard_map/ppermute | solution.py:41
  10.3 9.9 %collective-permute-start.1 = (bf16[32,2048]{1,0:T(8,128)(2,1)S(1)}, bf16[32,2048]{1,0:T(8,128)(2,1)S(1)}, u32[]{:S(2)}, u32[]{:S(2)}) collective-permute-start(bf16[32,2048]{1,0:T(8,128)(2,1)S(1)} %collective-permute-done), channel_id=1, source_target_pairs={{0,2},{1,3},{2,0},{3,1},{4,6},{5,7},{6,4},{7,5},{8,10},{9,11},{10,... | collective-permute-start | bytes 393224 | tf_op jit(solution)/shard_map/ppermute | solution.py:41
  12.0 20.5 %collective-permute-start.6 = (bf16[64,2048]{1,0:T(8,128)(2,1)S(1)}, bf16[64,2048]{1,0:T(8,128)(2,1)S(1)}, u32[]{:S(2)}, u32[]{:S(2)}) collective-permute-start(bf16[64,2048]{1,0:T(8,128)(2,1)S(1)} %bitcast.76), channel_id=1, source_target_pairs={{0,4},{4,0},{8,12},{12,8},{16,20},{20,16},{24,28},{28,24},{1,5},{5... | collective-permute-start | bytes 786440 | tf_op jit(solution)/shard_map/ppermute | solution.py:41
  18.2 5.0 %collective-permute-start.3 = (bf16[32,2048]{1,0:T(8,128)(2,1)S(1)}, bf16[32,2048]{1,0:T(8,128)(2,1)S(1)}, u32[]{:S(2)}, u32[]{:S(2)}) collective-permute-start(bf16[32,2048]{1,0:T(8,128)(2,1)S(1)} %collective-permute-done.2), channel_id=1, source_target_pairs={{0,2},{1,3},{2,0},{3,1},{4,6},{5,7},{6,4},{7,5},{8,10},{9,11},{10,... | collective-permute-start | bytes 393224 | tf_op jit(solution)/shard_map/ppermute | solution.py:41
  19.7 5.1 %collective-permute-start.5 = (bf16[32,2048]{1,0:T(8,128)(2,1)S(1)}, bf16[32,2048]{1,0:T(8,128)(2,1)S(1)}, u32[]{:S(2)}, u32[]{:S(2)}) collective-permute-start(bf16[32,2048]{1,0:T(8,128)(2,1)S(1)} %collective-permute-done.4), channel_id=1, source_target_pairs={{0,2},{1,3},{2,0},{3,1},{4,6},{5,7},{6,4},{7,5},{8,10},{9,11},{10,... | collective-permute-start | bytes 393224 | tf_op jit(solution)/shard_map/ppermute | solution.py:41
  20.2 9.3 %collective-permute-start.7 = (bf16[64,2048]{1,0:T(8,128)(2,1)S(1)}, bf16[64,2048]{1,0:T(8,128)(2,1)S(1)}, u32[]{:S(2)}, u32[]{:S(2)}) collective-permute-start(bf16[64,2048]{1,0:T(8,128)(2,1)S(1)} %pad_maximum_fusion.6.refs_3_), channel_id=1, source_target_pairs={{0,4},{4,0},{8,12},{12,8},{16,20},{20,16},{24,28},{28,24},{1,5},{5... | collective-permute-start | bytes 786440 | tf_op jit(solution)/shard_map/ppermute | solution.py:41
  23.2 11.9 %collective-permute-start.8 = (bf16[64,2048]{1,0:T(8,128)(2,1)S(1)}, bf16[64,2048]{1,0:T(8,128)(2,1)S(1)}, u32[]{:S(2)}, u32[]{:S(2)}) collective-permute-start(bf16[64,2048]{1,0:T(8,128)(2,1)S(1)} %pad_maximum_fusion.7.refs_5_), channel_id=1, source_target_pairs={{0,4},{4,0},{8,12},{12,8},{16,20},{20,16},{24,28},{28,24},{1,5},{5... | collective-permute-start | bytes 786440 | tf_op jit(solution)/shard_map/ppermute | solution.py:41
  24.8 11.5 %collective-permute-start.9 = (bf16[64,2048]{1,0:T(8,128)(2,1)S(1)}, bf16[64,2048]{1,0:T(8,128)(2,1)S(1)}, u32[]{:S(2)}, u32[]{:S(2)}) collective-permute-start(bf16[64,2048]{1,0:T(8,128)(2,1)S(1)} %pad_maximum_fusion.8.refs_7_), channel_id=1, source_target_pairs={{0,4},{4,0},{8,12},{12,8},{16,20},{20,16},{24,28},{28,24},{1,5},{5... | collective-permute-start | bytes 786440 | tf_op jit(solution)/shard_map/ppermute | solution.py:41
  29.5 9.3 %collective-permute-start.10 = (bf16[32,2048]{1,0:T(8,128)(2,1)S(1)}, bf16[32,2048]{1,0:T(8,128)(2,1)S(1)}, u32[]{:S(2)}, u32[]{:S(2)}) collective-permute-start(bf16[32,2048]{1,0:T(8,128)(2,1)S(1)} %constant_dynamic-slice_fusion.2), channel_id=1, source_target_pairs={{0,8},{4,12},{8,0},{12,4},{16,24},{20,28},{24,16},{28,20},{1,9},{5... | collective-permute-start | bytes 393224 | tf_op jit(solution)/shard_map/ppermute | solution.py:41
  31.0 8.7 %collective-permute-start.11 = (bf16[32,2048]{1,0:T(8,128)(2,1)S(1)}, bf16[32,2048]{1,0:T(8,128)(2,1)S(1)}, u32[]{:S(2)}, u32[]{:S(2)}) collective-permute-start(bf16[32,2048]{1,0:T(8,128)(2,1)S(1)} %constant_dynamic-slice_fusion.2), channel_id=1, source_target_pairs={{0,16},{4,20},{8,24},{12,28},{16,0},{20,4},{24,8},{28,12},{1,17},{... | collective-permute-start | bytes 393224 | tf_op jit(solution)/shard_map/ppermute | solution.py:41
  32.5 7.2 %collective-permute-start.12 = (bf16[32,2048]{1,0:T(8,128)(2,1)S(1)}, bf16[32,2048]{1,0:T(8,128)(2,1)S(1)}, u32[]{:S(2)}, u32[]{:S(2)}) collective-permute-start(bf16[32,2048]{1,0:T(8,128)(2,1)S(1)} %constant_dynamic-slice_fusion.2), channel_id=1, source_target_pairs={{0,24},{4,28},{8,16},{12,20},{16,8},{20,12},{24,0},{28,4},{1,25},{... | collective-permute-start | bytes 393224 | tf_op jit(solution)/shard_map/ppermute | solution.py:41
  39.7 5.1 %collective-permute-start.13 = (bf16[512,2048]{1,0:T(8,128)(2,1)S(1)}, bf16[512,2048]{1,0:T(8,128)(2,1)S(1)}, u32[]{:S(2)}, u32[]{:S(2)}) collective-permute-start(bf16[512,2048]{1,0:T(8,128)(2,1)S(1)} %bitcast.71), channel_id=1, source_target_pairs={{0,1},{1,0},{2,3},{3,2},{4,5},{5,4},{6,7},{7,6},{8,9},{9,8},{10,11... | collective-permute-start | bytes 6291464 | tf_op jit(solution)/shard_map/ppermute | solution.py:41
  39.8 11.6 %collective-permute-start.15 = (bf16[96,2048]{1,0:T(8,128)(2,1)S(1)}, bf16[96,2048]{1,0:T(8,128)(2,1)S(1)}, u32[]{:S(2)}, u32[]{:S(2)}) collective-permute-start(bf16[96,2048]{1,0:T(8,128)(2,1)S(1)} %pad_maximum_fusion.5), channel_id=1, source_target_pairs={{0,2},{1,3},{2,0},{3,1},{4,6},{5,7},{6,4},{7,5},{8,10},{9,11},{10,... | collective-permute-start | bytes 1179656 | tf_op jit(solution)/shard_map/ppermute | solution.py:41
  40.9 8.4 %collective-permute-start.14 = (bf16[64,2048]{1,0:T(8,128)(2,1)S(1)}, bf16[64,2048]{1,0:T(8,128)(2,1)S(1)}, u32[]{:S(2)}, u32[]{:S(2)}) collective-permute-start(bf16[64,2048]{1,0:T(8,128)(2,1)S(1)} %bitcast.84), channel_id=1, source_target_pairs={{0,4},{4,0},{8,12},{12,8},{16,20},{20,16},{24,28},{28,24},{1,5},{5... | collective-permute-start | bytes 786440 | tf_op jit(solution)/shard_map/ppermute | solution.py:41
  52.0 20.0 %collective-permute-start.19 = (bf16[192,2048]{1,0:T(8,128)(2,1)S(1)}, bf16[192,2048]{1,0:T(8,128)(2,1)S(1)}, u32[]{:S(2)}, u32[]{:S(2)}) collective-permute-start(bf16[192,2048]{1,0:T(8,128)(2,1)S(1)} %pad_maximum_fusion.refs_2_), channel_id=1, source_target_pairs={{0,4},{4,0},{8,12},{12,8},{16,20},{20,16},{24,28},{28,24},{1,5},{5... | collective-permute-start | bytes 2359304 | tf_op jit(solution)/shard_map/ppermute | solution.py:41
  53.6 8.4 %collective-permute-start.17 = (bf16[64,2048]{1,0:T(8,128)(2,1)S(1)}, bf16[64,2048]{1,0:T(8,128)(2,1)S(1)}, u32[]{:S(2)}, u32[]{:S(2)}) collective-permute-start(bf16[64,2048]{1,0:T(8,128)(2,1)S(1)} %add_convert_fusion.3.low), channel_id=1, source_target_pairs={{0,2},{1,3},{2,0},{3,1},{4,6},{5,7},{6,4},{7,5},{8,10},{9,11},{10,... | collective-permute-start | bytes 786440 | tf_op jit(solution)/shard_map/ppermute | solution.py:41
  73.5 16.1 %collective-permute-start.21 = (bf16[64,2048]{1,0:T(8,128)(2,1)S(1)}, bf16[64,2048]{1,0:T(8,128)(2,1)S(1)}, u32[]{:S(2)}, u32[]{:S(2)}) collective-permute-start(bf16[64,2048]{1,0:T(8,128)(2,1)S(1)} %add_convert_fusion.2.low), channel_id=1, source_target_pairs={{0,2},{1,3},{2,0},{3,1},{4,6},{5,7},{6,4},{7,5},{8,10},{9,11},{10,... | collective-permute-start | bytes 786440 | tf_op jit(solution)/shard_map/ppermute | solution.py:41
  74.7 14.0 %collective-permute-start.22 = (bf16[32,2048]{1,0:T(8,128)(2,1)S(1)}, bf16[32,2048]{1,0:T(8,128)(2,1)S(1)}, u32[]{:S(2)}, u32[]{:S(2)}) collective-permute-start(bf16[32,2048]{1,0:T(8,128)(2,1)S(1)} %constant_dynamic-slice_fusion), channel_id=1, source_target_pairs={{0,8},{4,12},{8,0},{12,4},{16,24},{20,28},{24,16},{28,20},{1,9},{5... | collective-permute-start | bytes 393224 | tf_op jit(solution)/shard_map/ppermute | solution.py:41
  76.7 12.9 %collective-permute-start.23 = (bf16[32,2048]{1,0:T(8,128)(2,1)S(1)}, bf16[32,2048]{1,0:T(8,128)(2,1)S(1)}, u32[]{:S(2)}, u32[]{:S(2)}) collective-permute-start(bf16[32,2048]{1,0:T(8,128)(2,1)S(1)} %constant_dynamic-slice_fusion), channel_id=1, source_target_pairs={{0,16},{4,20},{8,24},{12,28},{16,0},{20,4},{24,8},{28,12},{1,17},{... | collective-permute-start | bytes 393224 | tf_op jit(solution)/shard_map/ppermute | solution.py:41
  77.9 11.6 %collective-permute-start.24 = (bf16[32,2048]{1,0:T(8,128)(2,1)S(1)}, bf16[32,2048]{1,0:T(8,128)(2,1)S(1)}, u32[]{:S(2)}, u32[]{:S(2)}) collective-permute-start(bf16[32,2048]{1,0:T(8,128)(2,1)S(1)} %constant_dynamic-slice_fusion), channel_id=1, source_target_pairs={{0,24},{4,28},{8,16},{12,20},{16,8},{20,12},{24,0},{28,4},{1,25},{... | collective-permute-start | bytes 393224 | tf_op jit(solution)/shard_map/ppermute | solution.py:41
  90.5 11.6 %collective-permute-start.35 = (bf16[96,2048]{1,0:T(8,128)(2,1)S(1)}, bf16[96,2048]{1,0:T(8,128)(2,1)S(1)}, u32[]{:S(2)}, u32[]{:S(2)}) collective-permute-start(bf16[96,2048]{1,0:T(8,128)(2,1)S(1)} %get-tuple-element.315), channel_id=1, source_target_pairs={{0,2},{1,3},{2,0},{3,1},{4,6},{5,7},{6,4},{7,5},{8,10},{9,11},{10,... | collective-permute-start | bytes 1179656 | tf_op jit(solution)/shard_map/ppermute | solution.py:41
  91.4 11.2 %collective-permute-start.36 = (bf16[96,2048]{1,0:T(8,128)(2,1)S(1)}, bf16[96,2048]{1,0:T(8,128)(2,1)S(1)}, u32[]{:S(2)}, u32[]{:S(2)}) collective-permute-start(bf16[96,2048]{1,0:T(8,128)(2,1)S(1)} %get-tuple-element.315), channel_id=1, source_target_pairs={{0,4},{4,0},{8,12},{12,8},{16,20},{20,16},{24,28},{28,24},{1,5},{5... | collective-permute-start | bytes 1179656 | tf_op jit(solution)/shard_map/ppermute | solution.py:41
  93.9 8.8 %collective-permute-start.27 = (bf16[128,512]{1,0:T(8,128)(2,1)S(1)}, bf16[128,512]{1,0:T(8,128)(2,1)S(1)}, u32[]{:S(2)}, u32[]{:S(2)}) collective-permute-start(bf16[128,512]{1,0:T(8,128)(2,1)S(1)} %product_back.1.refs_0_), channel_id=1, source_target_pairs={{0,8},{4,12},{8,0},{12,4},{16,24},{20,28},{24,16},{28,20},{1,9},{5... | collective-permute-start | bytes 393224 | tf_op jit(solution)/shard_map/ppermute | solution.py:41
  96.2 12.8 %collective-permute-start.29 = (bf16[128,512]{1,0:T(8,128)(2,1)S(1)}, bf16[128,512]{1,0:T(8,128)(2,1)S(1)}, u32[]{:S(2)}, u32[]{:S(2)}) collective-permute-start(bf16[128,512]{1,0:T(8,128)(2,1)S(1)} %product_back.1.refs_0_), channel_id=1, source_target_pairs={{0,16},{4,20},{8,24},{12,28},{16,0},{20,4},{24,8},{28,12},{1,17},{... | collective-permute-start | bytes 393224 | tf_op jit(solution)/shard_map/ppermute | solution.py:41
  97.7 11.3 %collective-permute-start.31 = (bf16[128,512]{1,0:T(8,128)(2,1)S(1)}, bf16[128,512]{1,0:T(8,128)(2,1)S(1)}, u32[]{:S(2)}, u32[]{:S(2)}) collective-permute-start(bf16[128,512]{1,0:T(8,128)(2,1)S(1)} %product_back.1.refs_0_), channel_id=1, source_target_pairs={{0,24},{4,28},{8,16},{12,20},{16,8},{20,12},{24,0},{28,4},{1,25},{... | collective-permute-start | bytes 393224 | tf_op jit(solution)/shard_map/ppermute | solution.py:41
  102.0 9.8 %collective-permute-start.38 = (bf16[192,2048]{1,0:T(8,128)(2,1)S(1)}, bf16[192,2048]{1,0:T(8,128)(2,1)S(1)}, u32[]{:S(2)}, u32[]{:S(2)}) collective-permute-start(bf16[192,2048]{1,0:T(8,128)(2,1)S(1)} %pad_maximum_fusion.refs_2_), channel_id=1, source_target_pairs={{0,1},{1,0},{2,3},{3,2},{4,5},{5,4},{6,7},{7,6},{8,9},{9,8},{10,11... | collective-permute-start | bytes 2359304 | tf_op jit(solution)/shard_map/ppermute | solution.py:41
  102.7 7.0 %collective-permute-start.33 = (bf16[64,2048]{1,0:T(8,128)(2,1)S(1)}, bf16[64,2048]{1,0:T(8,128)(2,1)S(1)}, u32[]{:S(2)}, u32[]{:S(2)}) collective-permute-start(bf16[64,2048]{1,0:T(8,128)(2,1)S(1)} %get-tuple-element.209), channel_id=1, source_target_pairs={{0,1},{1,0},{2,3},{3,2},{4,5},{5,4},{6,7},{7,6},{8,9},{9,8},{10,11... | collective-permute-start | bytes 786440 | tf_op jit(solution)/shard_map/ppermute | solution.py:41
  109.0 6.5 %collective-permute-start.37 = (bf16[192,2048]{1,0:T(8,128)(2,1)S(1)}, bf16[192,2048]{1,0:T(8,128)(2,1)S(1)}, u32[]{:S(2)}, u32[]{:S(2)}) collective-permute-start(bf16[192,2048]{1,0:T(8,128)(2,1)S(1)} %constant_dynamic-update-slice_fusion.5.refs_0_), channel_id=1, source_target_pairs={{0,1},{1,0},{2,3},{3,2},{4,5},{5,4},{6,7},{7,6},{8,9},{9,8},{10,11... | collective-permute-start | bytes 2359304 | tf_op jit(solution)/shard_map/ppermute | solution.py:41
  109.1 6.4 %collective-permute-start.28 = (bf16[128,512]{1,0:T(8,128)(2,1)S(1)}, bf16[128,512]{1,0:T(8,128)(2,1)S(1)}, u32[]{:S(2)}, u32[]{:S(2)}) collective-permute-start(bf16[128,512]{1,0:T(8,128)(2,1)S(1)} %collective-permute-done.27.refs_2_), channel_id=1, source_target_pairs={{0,4},{4,0},{8,12},{12,8},{16,20},{20,16},{24,28},{28,24},{1,5},{5... | collective-permute-start | bytes 393224 | tf_op jit(solution)/shard_map/ppermute | solution.py:41
  109.8 20.0 %collective-permute-start.34 = (bf16[64,2048]{1,0:T(8,128)(2,1)S(1)}, bf16[64,2048]{1,0:T(8,128)(2,1)S(1)}, u32[]{:S(2)}, u32[]{:S(2)}) collective-permute-start(bf16[64,2048]{1,0:T(8,128)(2,1)S(1)} %add_convert_fusion.1.low), channel_id=1, source_target_pairs={{0,2},{1,3},{2,0},{3,1},{4,6},{5,7},{6,4},{7,5},{8,10},{9,11},{10,... | collective-permute-start | bytes 786440 | tf_op jit(solution)/shard_map/ppermute | solution.py:41
  110.8 32.0 %collective-permute-start.40 = (bf16[96,2048]{1,0:T(8,128)(2,1)S(1)}, bf16[96,2048]{1,0:T(8,128)(2,1)S(1)}, u32[]{:S(2)}, u32[]{:S(2)}) collective-permute-start(bf16[96,2048]{1,0:T(8,128)(2,1)S(1)} %collective-permute-done.36), channel_id=1, source_target_pairs={{0,2},{1,3},{2,0},{3,1},{4,6},{5,7},{6,4},{7,5},{8,10},{9,11},{10,... | collective-permute-start | bytes 1179656 | tf_op jit(solution)/shard_map/ppermute | solution.py:41
  111.9 17.9 %collective-permute-start.26 = (bf16[128,512]{1,0:T(8,128)(2,1)S(1)}, bf16[128,512]{1,0:T(8,128)(2,1)S(1)}, u32[]{:S(2)}, u32[]{:S(2)}) collective-permute-start(bf16[128,512]{1,0:T(8,128)(2,1)S(1)} %product_back.1.refs_0_), channel_id=1, source_target_pairs={{0,4},{4,0},{8,12},{12,8},{16,20},{20,16},{24,28},{28,24},{1,5},{5... | collective-permute-start | bytes 393224 | tf_op jit(solution)/shard_map/ppermute | solution.py:41
  115.5 14.3 %collective-permute-start.30 = (bf16[128,512]{1,0:T(8,128)(2,1)S(1)}, bf16[128,512]{1,0:T(8,128)(2,1)S(1)}, u32[]{:S(2)}, u32[]{:S(2)}) collective-permute-start(bf16[128,512]{1,0:T(8,128)(2,1)S(1)} %collective-permute-done.29.refs_4_), channel_id=1, source_target_pairs={{0,4},{4,0},{8,12},{12,8},{16,20},{20,16},{24,28},{28,24},{1,5},{5... | collective-permute-start | bytes 393224 | tf_op jit(solution)/shard_map/ppermute | solution.py:41
  115.5 14.2 %collective-permute-start.32 = (bf16[128,512]{1,0:T(8,128)(2,1)S(1)}, bf16[128,512]{1,0:T(8,128)(2,1)S(1)}, u32[]{:S(2)}, u32[]{:S(2)}) collective-permute-start(bf16[128,512]{1,0:T(8,128)(2,1)S(1)} %collective-permute-done.31.refs_6_), channel_id=1, source_target_pairs={{0,4},{4,0},{8,12},{12,8},{16,20},{20,16},{24,28},{28,24},{1,5},{5... | collective-permute-start | bytes 393224 | tf_op jit(solution)/shard_map/ppermute | solution.py:41
  129.8 13.1 %collective-permute-start.39 = (bf16[64,2048]{1,0:T(8,128)(2,1)S(1)}, bf16[64,2048]{1,0:T(8,128)(2,1)S(1)}, u32[]{:S(2)}, u32[]{:S(2)}) collective-permute-start(bf16[64,2048]{1,0:T(8,128)(2,1)S(1)} %get-tuple-element.232), channel_id=1, source_target_pairs={{0,4},{4,0},{8,12},{12,8},{16,20},{20,16},{24,28},{28,24},{1,5},{5... | collective-permute-start | bytes 786440 | tf_op jit(solution)/shard_map/ppermute | solution.py:41
  130.0 12.9 %collective-permute-start.43 = (bf16[2,72,256]{2,1,0:T(8,128)(2,1)S(1)}, bf16[2,72,256]{2,1,0:T(8,128)(2,1)S(1)}, u32[]{:S(2)}, u32[]{:S(2)}) collective-permute-start(bf16[2,72,256]{2,1,0:T(8,128)(2,1)S(1)} %get-tuple-element.237), channel_id=1, source_target_pairs={{0,24},{4,28},{8,16},{12,20},{16,8},{20,12},{24,0},{28,4},{1,25},{... | collective-permute-start | bytes 221192 | tf_op jit(solution)/shard_map/ppermute | solution.py:41
  132.4 10.5 %collective-permute-start.42 = (bf16[2,72,256]{2,1,0:T(8,128)(2,1)S(1)}, bf16[2,72,256]{2,1,0:T(8,128)(2,1)S(1)}, u32[]{:S(2)}, u32[]{:S(2)}) collective-permute-start(bf16[2,72,256]{2,1,0:T(8,128)(2,1)S(1)} %get-tuple-element.236), channel_id=1, source_target_pairs={{0,16},{4,20},{8,24},{12,28},{16,0},{20,4},{24,8},{28,12},{1,17},{... | collective-permute-start | bytes 221192 | tf_op jit(solution)/shard_map/ppermute | solution.py:41
  133.7 9.2 %collective-permute-start.41 = (bf16[2,72,256]{2,1,0:T(8,128)(2,1)S(1)}, bf16[2,72,256]{2,1,0:T(8,128)(2,1)S(1)}, u32[]{:S(2)}, u32[]{:S(2)}) collective-permute-start(bf16[2,72,256]{2,1,0:T(8,128)(2,1)S(1)} %get-tuple-element.235), channel_id=1, source_target_pairs={{0,8},{4,12},{8,0},{12,4},{16,24},{20,28},{24,16},{28,20},{1,9},{5... | collective-permute-start | bytes 221192 | tf_op jit(solution)/shard_map/ppermute | solution.py:41
  145.1 9.4 %collective-permute-start.46 = (bf16[72,256]{1,0:T(8,128)(2,1)S(1)}, bf16[72,256]{1,0:T(8,128)(2,1)S(1)}, u32[]{:S(2)}, u32[]{:S(2)}) collective-permute-start(bf16[72,256]{1,0:T(8,128)(2,1)S(1)} %get-tuple-element.310), channel_id=1, source_target_pairs={{0,4},{4,0},{8,12},{12,8},{16,20},{20,16},{24,28},{28,24},{1,5},{5... | collective-permute-start | bytes 110600 | tf_op jit(solution)/shard_map/ppermute | solution.py:41
  147.2 8.4 %collective-permute-start.45 = (bf16[64,2048]{1,0:T(8,128)(2,1)S(1)}, bf16[64,2048]{1,0:T(8,128)(2,1)S(1)}, u32[]{:S(2)}, u32[]{:S(2)}) collective-permute-start(bf16[64,2048]{1,0:T(8,128)(2,1)S(1)} %add_convert_fusion.low), channel_id=1, source_target_pairs={{0,2},{1,3},{2,0},{3,1},{4,6},{5,7},{6,4},{7,5},{8,10},{9,11},{10,... | collective-permute-start | bytes 786440 | tf_op jit(solution)/shard_map/ppermute | solution.py:41
  148.3 6.3 %collective-permute-start.47 = (bf16[72,256]{1,0:T(8,128)(2,1)S(1)}, bf16[72,256]{1,0:T(8,128)(2,1)S(1)}, u32[]{:S(2)}, u32[]{:S(2)}) collective-permute-start(bf16[72,256]{1,0:T(8,128)(2,1)S(1)} %get-tuple-element.325), channel_id=1, source_target_pairs={{0,4},{4,0},{8,12},{12,8},{16,20},{20,16},{24,28},{28,24},{1,5},{5... | collective-permute-start | bytes 110600 | tf_op jit(solution)/shard_map/ppermute | solution.py:41
  149.7 4.8 %collective-permute-start.48 = (bf16[72,256]{1,0:T(8,128)(2,1)S(1)}, bf16[72,256]{1,0:T(8,128)(2,1)S(1)}, u32[]{:S(2)}, u32[]{:S(2)}) collective-permute-start(bf16[72,256]{1,0:T(8,128)(2,1)S(1)} %get-tuple-element.323), channel_id=1, source_target_pairs={{0,4},{4,0},{8,12},{12,8},{16,20},{20,16},{24,28},{28,24},{1,5},{5... | collective-permute-start | bytes 110600 | tf_op jit(solution)/shard_map/ppermute | solution.py:41
  150.3 4.2 %collective-permute-start.49 = (bf16[72,256]{1,0:T(8,128)(2,1)S(1)}, bf16[72,256]{1,0:T(8,128)(2,1)S(1)}, u32[]{:S(2)}, u32[]{:S(2)}) collective-permute-start(bf16[72,256]{1,0:T(8,128)(2,1)S(1)} %get-tuple-element.321), channel_id=1, source_target_pairs={{0,4},{4,0},{8,12},{12,8},{16,20},{20,16},{24,28},{28,24},{1,5},{5... | collective-permute-start | bytes 110600 | tf_op jit(solution)/shard_map/ppermute | solution.py:41
  155.6 4.2 %collective-permute-start.55 = (bf16[192,2048]{1,0:T(8,128)(2,1)S(1)}, bf16[192,2048]{1,0:T(8,128)(2,1)S(1)}, u32[]{:S(2)}, u32[]{:S(2)}) collective-permute-start(bf16[192,2048]{1,0:T(8,128)(2,1)S(1)} %pad_maximum_fusion.1.refs_2_), channel_id=1, source_target_pairs={{0,1},{1,0},{2,3},{3,2},{4,5},{5,4},{6,7},{7,6},{8,9},{9,8},{10,11... | collective-permute-start | bytes 2359304 | tf_op jit(solution)/shard_map/ppermute | solution.py:41
  155.6 4.2 %collective-permute-start.57 = (bf16[192,2048]{1,0:T(8,128)(2,1)S(1)}, bf16[192,2048]{1,0:T(8,128)(2,1)S(1)}, u32[]{:S(2)}, u32[]{:S(2)}) collective-permute-start(bf16[192,2048]{1,0:T(8,128)(2,1)S(1)} %collective-permute-done.19.refs_6_), channel_id=1, source_target_pairs={{0,1},{1,0},{2,3},{3,2},{4,5},{5,4},{6,7},{7,6},{8,9},{9,8},{10,11... | collective-permute-start | bytes 2359304 | tf_op jit(solution)/shard_map/ppermute | solution.py:41
  174.9 4.9 %collective-permute-start.58 = (bf16[8,72,256]{2,1,0:T(8,128)(2,1)S(1)}, bf16[8,72,256]{2,1,0:T(8,128)(2,1)S(1)}, u32[]{:S(2)}, u32[]{:S(2)}) collective-permute-start(bf16[8,72,256]{2,1,0:T(8,128)(2,1)S(1)} %constant_dynamic-update-slice_fusion.9.came_a), channel_id=1, source_target_pairs={{0,1},{1,0},{2,3},{3,2},{4,5},{5,4},{6,7},{7,6},{8,9},{9,8},{10,11... | collective-permute-start | bytes 884744 | tf_op jit(solution)/shard_map/ppermute | solution.py:41
  (30 other events, 213.3 us)

commit v8 on v7

--- a/solution.py
+++ b/solution.py
@@ -1174,7 +1174,7 @@
         shards,
     )
     columns_far = after(columns_far, low)
-    columns_far[0] = mixed_columns[:inner]
+    columns_far[0] = after(mixed_columns[:inner], low)
     columns = {}
     for outer, came in columns_far.items():
         columns[outer] = came[0]

time: 181 us -> 181 us (level)
  transfers between devices with their start and end apart: 59 -> 59, of which waited for: 22 -> 23; matrix products, arithmetic and copies ran while one was open for 1% -> 1% of each run, Pallas kernels for 34% -> 34%
where the time goes in v8:
time: 181 us
  Pallas kernels  81.4 us (45%)
  starting transfers between devices  58.3 us (32%)
  waiting for transfers between devices  36.1 us (20%)
  local copies, waits for them, and re-layouts  2.22 us (1%)
    ppermute x59, starting transfers between devices, swap(): return lax.ppermute(value, axis, [(i, i ^ bit) for i in range(size)])  58.3 us
    ppermute x59, waiting for transfers between devices, swap(): return lax.ppermute(value, axis, [(i, i ^ bit) for i in range(size)])  36.1 us
    pallas_call x2, Pallas kernels, feed_all(): pl.pallas_call(partial(all_kernel, count=count), grid_spec=pltpu.Prefetch...  27.3 us
    pallas_call x1, Pallas kernels, attend_all(): pl.pallas_call(partial(all_forward_kernel, groups=groups, scale=1.0 / mat...  9.35 us
    pallas_call x1, Pallas kernels, attend_back(): pl.pallas_call(partial(backward_kernel, count=count, groups=groups, scale...  8.36 us
    pallas_call x5, Pallas kernels, project_rows(): pl.pallas_call(partial(rows_kernel, count=len(weights)), out_shape=[jax.S...  7.65 us
    pallas_call x1, Pallas kernels, feed_own(): pl.pallas_call(own_kernel, in_specs=[WHOLE] * 3, out_specs=[WHOLE] * 4, o...  5.47 us
  transfers between devices with their start and end apart: 59, of which 23 were waited for; matrix products, arithmetic and copies ran while one was open for 1% of the time, Pallas kernels for 34%

profile of v8, /device:TPU:0, one launch (start us, length us, event | category | flops | bytes accessed | tf_op | source)
XLA Modules:
  0.0 181.3 jit_solution(13896225820269139636)
XLA Ops:
  2.2 3.1 %collective-permute-start = (bf16[32,2048]{1,0:T(8,128)(2,1)S(1)}, bf16[32,2048]{1,0:T(8,128)(2,1)S(1)}, u32[]{:S(2)}, u32[]{:S(2)}) collective-permute-start(bf16[32,2048]{1,0:T(8,128)(2,1)S(1)} %constant_dynamic-slice_fusion.4), channel_id=1, source_target_pairs={{0,8},{4,12},{8,0},{12,4},{16,24},{20,28},{24,16},{28,20},{1,9},{5... | collective-permute-start | bytes 393224 | tf_op jit(solution)/shard_map/ppermute | solution.py:41
  5.2 2.6 %collective-permute-start.2 = (bf16[32,2048]{1,0:T(8,128)(2,1)S(1)}, bf16[32,2048]{1,0:T(8,128)(2,1)S(1)}, u32[]{:S(2)}, u32[]{:S(2)}) collective-permute-start(bf16[32,2048]{1,0:T(8,128)(2,1)S(1)} %constant_dynamic-slice_fusion.4), channel_id=1, source_target_pairs={{0,16},{4,20},{8,24},{12,28},{16,0},{20,4},{24,8},{28,12},{1,17},{... | collective-permute-start | bytes 393224 | tf_op jit(solution)/shard_map/ppermute | solution.py:41
  7.8 2.4 %collective-permute-done = bf16[32,2048]{1,0:T(8,128)(2,1)S(1)} collective-permute-done((bf16[32,2048]{1,0:T(8,128)(2,1)S(1)}, bf16[32,2048]{1,0:T(8,128)(2,1)S(1)}, u32[]{:S(2)}, u32[]{:S(2)}) %collective-permute-start) | collective-permute-done | bytes 131104 | tf_op jit(solution)/shard_map/ppermute | solution.py:41
  10.3 1.7 collective-permute-start.1
  12.0 1.5 collective-permute-start.6
  14.1 2.4 %tables.1 = (s32[512,1]{1,0:T(8,128)}, s32[512,1]{1,0:T(8,128)}, s32[512,1]{1,0:T(8,128)}, s32[512,1]{1,0:T(8,128)}, s32[1,1024]{1,0:T(1,128)}, /*index=5*/s32[1,128]{1,0:T(1,128)}, s32[128,1]{1,0:T(8,128)}) custom-call(s32[2]{0:T(128)} %pad_add_fusion.index, s32[1,8]{1,0:T(1,128)} %frames.1, s32[1,8]{1,0:T(1,128)} %texts.1, s32[1,8]{1,0:T(1,128)} %actions.1), custom_call_target="tpu_custom_call" | custom-call | flops 10485 | bytes 10485 | tf_op jit(solution)/shard_map/tables/pallas_call | solution.py:206
  18.2 1.5 collective-permute-start.3
  20.2 1.6 collective-permute-start.7
  23.2 1.6 collective-permute-start.8
  24.8 1.5 collective-permute-start.9
  26.2 3.3 %collective-permute-done.7.refs_4_ = bf16[64,2048]{1,0:T(8,128)(2,1)S(1)} collective-permute-done((bf16[64,2048]{1,0:T(8,128)(2,1)S(1)}, bf16[64,2048]{1,0:T(8,128)(2,1)S(1)}, u32[]{:S(2)}, u32[]{:S(2)}) %collective-permute-start.7) | collective-permute-done | bytes 262176 | tf_op jit(solution)/shard_map/ppermute | solution.py:41
  29.5 1.5 collective-permute-start.10
  31.0 1.4 collective-permute-start.11
  32.5 1.5 collective-permute-start.12
  36.3 2.5 %norm_pieces.1 = bf16[8,8,8,2048]{3,2,1,0:T(8,128)(2,1)S(1)} custom-call(s32[1]{0:T(128)} %bitcast.11.refs_0_, bf16[64,2048]{1,0:T(8,128)(2,1)S(1)} %bitcast.78, bf16[64,2048]{1,0:T(8,128)(2,1)S(1)} %collective-permute-done.6.refs_2_, bf16[64,2048]{1,0:T(8,128)(2,1)S(1)} %pad_maximum_fusion.6.refs_3_, bf16[64,2048]{1,0:T(8,128)(2,1)S(1)} %collective-permute-done.7.refs_4_, ...), custom_call_target="tpu_custom_call" | custom-call | flops 104857 | bytes 41943 | tf_op jit(solution)/shard_map/norm_pieces/pallas_call | solution.py:360
  40.9 1.5 collective-permute-start.14
  42.5 2.3 %project_rows.6 = (bf16[512,512]{1,0:T(8,128)(2,1)S(1)}, bf16[512,512]{1,0:T(8,128)(2,1)S(1)}) custom-call(bf16[512,2048]{1,0:T(8,128)(2,1)S(1)} %bitcast.72, bf16[2048,512]{1,0:T(8,128)(2,1)S(1)} %copy-done.1, bf16[2048,512]{1,0:T(8,128)(2,1)S(1)} %copy-done.2), custom_call_target="tpu_custom_call" | custom-call | flops 21474836 | bytes 20971 | tf_op jit(solution)/shard_map/project_rows/pallas_call | solution.py:234
  44.9 2.4 %project_rows.7 = (bf16[512,512]{1,0:T(8,128)(2,1)S(1)}, bf16[512,512]{1,0:T(8,128)(2,1)S(1)}) custom-call(bf16[512,2048]{1,0:T(8,128)(2,1)S(1)} %collective-permute-done.13.refs_0_.refs_1_, bf16[2048,512]{1,0:T(8,128)(2,1)S(1)} %copy-done.1, bf16[2048,512]{1,0:T(8,128)(2,1)S(1)} %copy-done.2), custom_call_target="tpu_custom_call" | custom-call | flops 21474836 | bytes 20971 | tf_op jit(solution)/shard_map/project_rows/pallas_call | solution.py:234
  47.3 1.9 %attend.1.refs_0_ = bf16[128,512]{1,0:T(8,128)(2,1)S(1)} custom-call(bf16[128,512]{1,0:T(8,128)(2,1)S(1)} %project_rows.5.query, bf16[512,512]{1,0:T(8,128)(2,1)S(1)} %get-tuple-element.172.key_a.refs_2_.refs_10_, bf16[512,512]{1,0:T(8,128)(2,1)S(1)} %get-tuple-element.173.key_b.refs_3_.refs_11_, ...), custom_call_target="tpu_custom_call" | custom-call | flops 2684354 | bytes 20971 | tf_op jit(solution)/shard_map/attend/pallas_call | solution.py:821
  49.4 2.0 %collective-permute-done.15 = bf16[96,2048]{1,0:T(8,128)(2,1)S(1)} collective-permute-done((bf16[96,2048]{1,0:T(8,128)(2,1)S(1)}, bf16[96,2048]{1,0:T(8,128)(2,1)S(1)}, u32[]{:S(2)}, u32[]{:S(2)}) %collective-permute-start.15) | collective-permute-done | bytes 393248 | tf_op jit(solution)/shard_map/ppermute | solution.py:41
  52.0 1.6 collective-permute-start.19
  55.1 3.5 %grad_activated.1 = f32[128,2048]{1,0:T(8,128)S(1)} custom-call(bf16[128,2048]{1,0:T(8,128)(2,1)S(1)} %pad_maximum_fusion.3.grad.refs_7_, bf16[2048,2048]{1,0:T(8,128)(2,1)S(1)} %bitcast.68), custom_call_target="tpu_custom_call" | custom-call | flops 10737418 | bytes 83886 | tf_op jit(solution)/shard_map/grad_activated/pallas_call | solution.py:576
  62.5 1.5 collective-permute-done.18
  64.1 5.5 %feed_own.1 = (bf16[128,2048]{1,0:T(8,128)(2,1)S(1)}, bf16[128,2048]{1,0:T(8,128)(2,1)S(1)}, f32[64,2048]{1,0:T(8,128)S(1)}, bf16[64,2048]{1,0:T(8,128)(2,1)S(1)}) custom-call(bf16[128,2048]{1,0:T(8,128)(2,1)S(1)} %constant_dynamic-update-slice_fusion.lifted.refs_6_, bf16[2048,2048]{1,0:T(8,128)(2,1)S(1)} %bitcast.70, f32[128,2048]{1,0:T(8,128)S(1)} %grad_activated.1), custom_call_target="tpu_custom_call" | custom-call | flops 21474836 | bytes 83886 | tf_op jit(solution)/shard_map/feed_own/pallas_call | solution.py:550
  69.6 2.4 %collective-permute-done.19.refs_6_ = bf16[192,2048]{1,0:T(8,128)(2,1)S(1)} collective-permute-done((bf16[192,2048]{1,0:T(8,128)(2,1)S(1)}, bf16[192,2048]{1,0:T(8,128)(2,1)S(1)}, u32[]{:S(2)}, u32[]{:S(2)}) %collective-permute-start.19) | collective-permute-done | bytes 786464 | tf_op jit(solution)/shard_map/ppermute | solution.py:41
  71.9 1.5 collective-permute-done.20
  74.7 1.9 %collective-permute-start.22 = (bf16[32,2048]{1,0:T(8,128)(2,1)S(1)}, bf16[32,2048]{1,0:T(8,128)(2,1)S(1)}, u32[]{:S(2)}, u32[]{:S(2)}) collective-permute-start(bf16[32,2048]{1,0:T(8,128)(2,1)S(1)} %constant_dynamic-slice_fusion), channel_id=1, source_target_pairs={{0,8},{4,12},{8,0},{12,4},{16,24},{20,28},{24,16},{28,20},{1,9},{5... | collective-permute-start | bytes 393224 | tf_op jit(solution)/shard_map/ppermute | solution.py:41
  77.9 1.4 collective-permute-start.24
  79.3 9.3 %attend_all.1 = (bf16[512,512]{1,0:T(8,128)(2,1)S(1)}, bf16[512,512]{1,0:T(8,128)(2,1)S(1)}, bf16[4,2560,256]{2,1,0:T(8,128)(2,1)}) custom-call(bf16[512,512]{1,0:T(8,128)(2,1)S(1)} %project_rows.8.refs_0_.refs_8_, bf16[512,512]{1,0:T(8,128)(2,1)S(1)} %project_rows.9.refs_1_.refs_9_, bf16[512,512]{1,0:T(8,128)(2,1)S(1)} %get-tuple-element.172.key_a.refs_2_.refs_10_, ...), custom_call_target="tpu_custom_call" | custom-call | flops 21474836 | bytes 41943 | tf_op jit(solution)/shard_map/attend_all/pallas_call | solution.py:913
  91.4 1.5 collective-permute-start.36
  93.9 2.4 %collective-permute-start.27 = (bf16[128,512]{1,0:T(8,128)(2,1)S(1)}, bf16[128,512]{1,0:T(8,128)(2,1)S(1)}, u32[]{:S(2)}, u32[]{:S(2)}) collective-permute-start(bf16[128,512]{1,0:T(8,128)(2,1)S(1)} %product_back.1.refs_0_), channel_id=1, source_target_pairs={{0,8},{4,12},{8,0},{12,4},{16,24},{20,28},{24,16},{28,20},{1,9},{5... | collective-permute-start | bytes 393224 | tf_op jit(solution)/shard_map/ppermute | solution.py:41
  96.2 1.5 collective-permute-start.29
  97.7 1.4 collective-permute-start.31
  99.1 2.0 %down_own.1 = (f32[64,2048]{1,0:T(8,128)S(1)}, bf16[64,2048]{1,0:T(8,128)(2,1)S(1)}) custom-call(bf16[128,2048]{1,0:T(8,128)(2,1)S(1)} %get-tuple-element.208.rows.refs_8_, bf16[2048,2048]{1,0:T(8,128)(2,1)S(1)} %bitcast.68), custom_call_target="tpu_custom_call" | custom-call | flops 10737418 | bytes 83886 | tf_op jit(solution)/shard_map/down_own/pallas_call | solution.py:295
  102.7 6.3 %collective-permute-done.29.refs_4_ = bf16[128,512]{1,0:T(8,128)(2,1)S(1)} collective-permute-done((bf16[128,512]{1,0:T(8,128)(2,1)S(1)}, bf16[128,512]{1,0:T(8,128)(2,1)S(1)}, u32[]{:S(2)}, u32[]{:S(2)}) %collective-permute-start.29) | collective-permute-done | bytes 131104 | tf_op jit(solution)/shard_map/ppermute | solution.py:41
  111.9 1.5 collective-permute-start.26
  113.4 2.1 %collective-permute-done.28.refs_3_ = bf16[128,512]{1,0:T(8,128)(2,1)S(1)} collective-permute-done((bf16[128,512]{1,0:T(8,128)(2,1)S(1)}, bf16[128,512]{1,0:T(8,128)(2,1)S(1)}, u32[]{:S(2)}, u32[]{:S(2)}) %collective-permute-start.28) | collective-permute-done | bytes 131104 | tf_op jit(solution)/shard_map/ppermute | solution.py:41
  115.5 2.0 %collective-permute-start.32 = (bf16[128,512]{1,0:T(8,128)(2,1)S(1)}, bf16[128,512]{1,0:T(8,128)(2,1)S(1)}, u32[]{:S(2)}, u32[]{:S(2)}) collective-permute-start(bf16[128,512]{1,0:T(8,128)(2,1)S(1)} %collective-permute-done.31.refs_6_), channel_id=1, source_target_pairs={{0,4},{4,0},{8,12},{12,8},{16,20},{20,16},{24,28},{28,24},{1,5},{5... | collective-permute-start | bytes 393224 | tf_op jit(solution)/shard_map/ppermute | solution.py:41
  117.5 12.3 %feed_all.2 = (bf16[256,2048]{1,0:T(8,128)(2,1)}, bf16[2048,256]{1,0:T(8,128)(2,1)}) custom-call(s32[1]{0:T(128)} %bitcast.5.index, bf16[192,2048]{1,0:T(8,128)(2,1)S(1)} %constant_dynamic-update-slice_fusion.5.refs_0_, bf16[192,2048]{1,0:T(8,128)(2,1)S(1)} %collective-permute-done.37.refs_1_, bf16[192,2048]{1,0:T(8,128)(2,1)S(1)} %pad_maximum_fusion.refs_2_, ...), custom_call_target="tpu_custom_call" | custom-call | flops 72477576 | bytes 199229 | tf_op jit(solution)/shard_map/feed_all/pallas_call | solution.py:666
  130.0 2.4 %collective-permute-start.43 = (bf16[2,72,256]{2,1,0:T(8,128)(2,1)S(1)}, bf16[2,72,256]{2,1,0:T(8,128)(2,1)S(1)}, u32[]{:S(2)}, u32[]{:S(2)}) collective-permute-start(bf16[2,72,256]{2,1,0:T(8,128)(2,1)S(1)} %get-tuple-element.238), channel_id=1, source_target_pairs={{0,24},{4,28},{8,16},{12,20},{16,8},{20,12},{24,0},{28,4},{1,25},{... | collective-permute-start | bytes 221192 | tf_op jit(solution)/shard_map/ppermute | solution.py:41
  134.4 8.4 %attend_back.1 = (bf16[512,512]{1,0:T(8,128)(2,1)S(1)}, bf16[512,512]{1,0:T(8,128)(2,1)S(1)}, bf16[512,512]{1,0:T(8,128)(2,1)S(1)}, bf16[512,512]{1,0:T(8,128)(2...) custom-call(bf16[128,512]{1,0:T(8,128)(2,1)S(1)} %product_back.1.ref, ...), custom_call_target="tpu_custom_call" | custom-call | flops 42949672 | bytes 136314 | tf_op jit(solution)/shard_map/attend_back/pallas_call | solution.py:1029
  142.9 2.1 %product_halves.3 = (f32[64,2048]{1,0:T(8,128)S(1)}, bf16[64,2048]{1,0:T(8,128)(2,1)S(1)}) custom-call(bf16[128,512]{1,0:T(8,128)(2,1)S(1)} %get-tuple-element.239.refs_0_, bf16[128,512]{1,0:T(8,128)(2,1)S(1)} %get-tuple-element.240.refs_1_, bf16[128,512]{1,0:T(8,128)(2,1)S(1)} %get-tuple-element.241.refs_2_, bf16[2048,512]{1,0:T(8,128)(2,1)S(1)} %copy-done, ...), custom_call_target="tpu_custom_call" | custom-call | flops 8053063 | bytes 62914 | tf_op jit(solution)/shard_map/product_halves/pallas_call | solution.py:270
  145.1 1.5 collective-permute-done.44
  148.1 1.7 collective-permute-start.47
  150.1 1.7 collective-permute-start.49
  152.1 2.8 %project.1 = (f32[256,512]{1,0:T(8,128)}, f32[256,512]{1,0:T(8,128)}, f32[256,512]{1,0:T(8,128)}, f32[3,256]{1,0:T(4,128)S(1)}) custom-call(s32[1]{0:T(128)} %bitcast.5.index, bf16[512,2048]{1,0:T(8,128)(2,1)S(1)} %bitcast.74, bf16[512,2048]{1,0:T(8,128)(2,1)S(1)} %collective-permute-done.13.refs_0_.refs_1_, ...), custom_call_target="tpu_custom_call" | custom-call | flops 16106127 | bytes 47185 | tf_op jit(solution)/shard_map/project/pallas_call | solution.py:722
  157.7 2.2 %collective-permute-done.52 = f32[3,256]{1,0:T(4,128)S(1)} collective-permute-done((f32[3,256]{1,0:T(4,128)S(1)}, f32[3,256]{1,0:T(4,128)S(1)}, u32[]{:S(2)}, u32[]{:S(2)}) %collective-permute-start.52) | collective-permute-done | bytes 3104 | tf_op jit(solution)/shard_map/ppermute | solution.py:41
  159.9 15.0 %feed_all.3 = (f32[256,2048]{1,0:T(8,128)}, f32[2048,256]{1,0:T(8,128)}) custom-call(s32[1]{0:T(128)} %bitcast.5.index, bf16[64,2048]{1,0:T(8,128)(2,1)S(1)} %collective-permute-done.39.refs_0_, bf16[64,2048]{1,0:T(8,128)(2,1)S(1)} %collective-permute-done.54.refs_1_, bf16[192,2048]{1,0:T(8,128)(2,1)S(1)} %pad_maximum_fusion.1.refs_2_, ...), custom_call_target="tpu_custom_call" | custom-call | flops 96636768 | bytes 209715 | tf_op jit(solution)/shard_map/feed_all/pallas_call | solution.py:666
  (181 shorter events, 40.3 us)
Async XLA Ops:
  2.2 8.1 %collective-permute-start = (bf16[32,2048]{1,0:T(8,128)(2,1)S(1)}, bf16[32,2048]{1,0:T(8,128)(2,1)S(1)}, u32[]{:S(2)}, u32[]{:S(2)}) collective-permute-start(bf16[32,2048]{1,0:T(8,128)(2,1)S(1)} %constant_dynamic-slice_fusion.4), channel_id=1, source_target_pairs={{0,8},{4,12},{8,0},{12,4},{16,24},{20,28},{24,16},{28,20},{1,9},{5... | collective-permute-start | bytes 393224 | tf_op jit(solution)/shard_map/ppermute | solution.py:41
  5.2 12.9 %collective-permute-start.2 = (bf16[32,2048]{1,0:T(8,128)(2,1)S(1)}, bf16[32,2048]{1,0:T(8,128)(2,1)S(1)}, u32[]{:S(2)}, u32[]{:S(2)}) collective-permute-start(bf16[32,2048]{1,0:T(8,128)(2,1)S(1)} %constant_dynamic-slice_fusion.4), channel_id=1, source_target_pairs={{0,16},{4,20},{8,24},{12,28},{16,0},{20,4},{24,8},{28,12},{1,17},{... | collective-permute-start | bytes 393224 | tf_op jit(solution)/shard_map/ppermute | solution.py:41
  7.8 11.8 %collective-permute-start.4 = (bf16[32,2048]{1,0:T(8,128)(2,1)S(1)}, bf16[32,2048]{1,0:T(8,128)(2,1)S(1)}, u32[]{:S(2)}, u32[]{:S(2)}) collective-permute-start(bf16[32,2048]{1,0:T(8,128)(2,1)S(1)} %constant_dynamic-slice_fusion.4), channel_id=1, source_target_pairs={{0,24},{4,28},{8,16},{12,20},{16,8},{20,12},{24,0},{28,4},{1,25},{... | collective-permute-start | bytes 393224 | tf_op jit(solution)/shard_map/ppermute | solution.py:41
  10.3 9.9 %collective-permute-start.1 = (bf16[32,2048]{1,0:T(8,128)(2,1)S(1)}, bf16[32,2048]{1,0:T(8,128)(2,1)S(1)}, u32[]{:S(2)}, u32[]{:S(2)}) collective-permute-start(bf16[32,2048]{1,0:T(8,128)(2,1)S(1)} %collective-permute-done), channel_id=1, source_target_pairs={{0,2},{1,3},{2,0},{3,1},{4,6},{5,7},{6,4},{7,5},{8,10},{9,11},{10,... | collective-permute-start | bytes 393224 | tf_op jit(solution)/shard_map/ppermute | solution.py:41
  12.0 20.5 %collective-permute-start.6 = (bf16[64,2048]{1,0:T(8,128)(2,1)S(1)}, bf16[64,2048]{1,0:T(8,128)(2,1)S(1)}, u32[]{:S(2)}, u32[]{:S(2)}) collective-permute-start(bf16[64,2048]{1,0:T(8,128)(2,1)S(1)} %bitcast.76), channel_id=1, source_target_pairs={{0,4},{4,0},{8,12},{12,8},{16,20},{20,16},{24,28},{28,24},{1,5},{5... | collective-permute-start | bytes 786440 | tf_op jit(solution)/shard_map/ppermute | solution.py:41
  18.2 5.0 %collective-permute-start.3 = (bf16[32,2048]{1,0:T(8,128)(2,1)S(1)}, bf16[32,2048]{1,0:T(8,128)(2,1)S(1)}, u32[]{:S(2)}, u32[]{:S(2)}) collective-permute-start(bf16[32,2048]{1,0:T(8,128)(2,1)S(1)} %collective-permute-done.2), channel_id=1, source_target_pairs={{0,2},{1,3},{2,0},{3,1},{4,6},{5,7},{6,4},{7,5},{8,10},{9,11},{10,... | collective-permute-start | bytes 393224 | tf_op jit(solution)/shard_map/ppermute | solution.py:41
  19.7 5.1 %collective-permute-start.5 = (bf16[32,2048]{1,0:T(8,128)(2,1)S(1)}, bf16[32,2048]{1,0:T(8,128)(2,1)S(1)}, u32[]{:S(2)}, u32[]{:S(2)}) collective-permute-start(bf16[32,2048]{1,0:T(8,128)(2,1)S(1)} %collective-permute-done.4), channel_id=1, source_target_pairs={{0,2},{1,3},{2,0},{3,1},{4,6},{5,7},{6,4},{7,5},{8,10},{9,11},{10,... | collective-permute-start | bytes 393224 | tf_op jit(solution)/shard_map/ppermute | solution.py:41
  20.2 9.3 %collective-permute-start.7 = (bf16[64,2048]{1,0:T(8,128)(2,1)S(1)}, bf16[64,2048]{1,0:T(8,128)(2,1)S(1)}, u32[]{:S(2)}, u32[]{:S(2)}) collective-permute-start(bf16[64,2048]{1,0:T(8,128)(2,1)S(1)} %pad_maximum_fusion.6.refs_3_), channel_id=1, source_target_pairs={{0,4},{4,0},{8,12},{12,8},{16,20},{20,16},{24,28},{28,24},{1,5},{5... | collective-permute-start | bytes 786440 | tf_op jit(solution)/shard_map/ppermute | solution.py:41
  23.2 11.9 %collective-permute-start.8 = (bf16[64,2048]{1,0:T(8,128)(2,1)S(1)}, bf16[64,2048]{1,0:T(8,128)(2,1)S(1)}, u32[]{:S(2)}, u32[]{:S(2)}) collective-permute-start(bf16[64,2048]{1,0:T(8,128)(2,1)S(1)} %pad_maximum_fusion.7.refs_5_), channel_id=1, source_target_pairs={{0,4},{4,0},{8,12},{12,8},{16,20},{20,16},{24,28},{28,24},{1,5},{5... | collective-permute-start | bytes 786440 | tf_op jit(solution)/shard_map/ppermute | solution.py:41
  24.8 11.5 %collective-permute-start.9 = (bf16[64,2048]{1,0:T(8,128)(2,1)S(1)}, bf16[64,2048]{1,0:T(8,128)(2,1)S(1)}, u32[]{:S(2)}, u32[]{:S(2)}) collective-permute-start(bf16[64,2048]{1,0:T(8,128)(2,1)S(1)} %pad_maximum_fusion.8.refs_7_), channel_id=1, source_target_pairs={{0,4},{4,0},{8,12},{12,8},{16,20},{20,16},{24,28},{28,24},{1,5},{5... | collective-permute-start | bytes 786440 | tf_op jit(solution)/shard_map/ppermute | solution.py:41
  29.5 9.3 %collective-permute-start.10 = (bf16[32,2048]{1,0:T(8,128)(2,1)S(1)}, bf16[32,2048]{1,0:T(8,128)(2,1)S(1)}, u32[]{:S(2)}, u32[]{:S(2)}) collective-permute-start(bf16[32,2048]{1,0:T(8,128)(2,1)S(1)} %constant_dynamic-slice_fusion.2), channel_id=1, source_target_pairs={{0,8},{4,12},{8,0},{12,4},{16,24},{20,28},{24,16},{28,20},{1,9},{5... | collective-permute-start | bytes 393224 | tf_op jit(solution)/shard_map/ppermute | solution.py:41
  31.0 8.7 %collective-permute-start.11 = (bf16[32,2048]{1,0:T(8,128)(2,1)S(1)}, bf16[32,2048]{1,0:T(8,128)(2,1)S(1)}, u32[]{:S(2)}, u32[]{:S(2)}) collective-permute-start(bf16[32,2048]{1,0:T(8,128)(2,1)S(1)} %constant_dynamic-slice_fusion.2), channel_id=1, source_target_pairs={{0,16},{4,20},{8,24},{12,28},{16,0},{20,4},{24,8},{28,12},{1,17},{... | collective-permute-start | bytes 393224 | tf_op jit(solution)/shard_map/ppermute | solution.py:41
  32.5 7.2 %collective-permute-start.12 = (bf16[32,2048]{1,0:T(8,128)(2,1)S(1)}, bf16[32,2048]{1,0:T(8,128)(2,1)S(1)}, u32[]{:S(2)}, u32[]{:S(2)}) collective-permute-start(bf16[32,2048]{1,0:T(8,128)(2,1)S(1)} %constant_dynamic-slice_fusion.2), channel_id=1, source_target_pairs={{0,24},{4,28},{8,16},{12,20},{16,8},{20,12},{24,0},{28,4},{1,25},{... | collective-permute-start | bytes 393224 | tf_op jit(solution)/shard_map/ppermute | solution.py:41
  39.7 5.1 %collective-permute-start.13 = (bf16[512,2048]{1,0:T(8,128)(2,1)S(1)}, bf16[512,2048]{1,0:T(8,128)(2,1)S(1)}, u32[]{:S(2)}, u32[]{:S(2)}) collective-permute-start(bf16[512,2048]{1,0:T(8,128)(2,1)S(1)} %bitcast.71), channel_id=1, source_target_pairs={{0,1},{1,0},{2,3},{3,2},{4,5},{5,4},{6,7},{7,6},{8,9},{9,8},{10,11... | collective-permute-start | bytes 6291464 | tf_op jit(solution)/shard_map/ppermute | solution.py:41
  39.8 11.6 %collective-permute-start.15 = (bf16[96,2048]{1,0:T(8,128)(2,1)S(1)}, bf16[96,2048]{1,0:T(8,128)(2,1)S(1)}, u32[]{:S(2)}, u32[]{:S(2)}) collective-permute-start(bf16[96,2048]{1,0:T(8,128)(2,1)S(1)} %pad_maximum_fusion.5), channel_id=1, source_target_pairs={{0,2},{1,3},{2,0},{3,1},{4,6},{5,7},{6,4},{7,5},{8,10},{9,11},{10,... | collective-permute-start | bytes 1179656 | tf_op jit(solution)/shard_map/ppermute | solution.py:41
  40.9 8.4 %collective-permute-start.14 = (bf16[64,2048]{1,0:T(8,128)(2,1)S(1)}, bf16[64,2048]{1,0:T(8,128)(2,1)S(1)}, u32[]{:S(2)}, u32[]{:S(2)}) collective-permute-start(bf16[64,2048]{1,0:T(8,128)(2,1)S(1)} %bitcast.84), channel_id=1, source_target_pairs={{0,4},{4,0},{8,12},{12,8},{16,20},{20,16},{24,28},{28,24},{1,5},{5... | collective-permute-start | bytes 786440 | tf_op jit(solution)/shard_map/ppermute | solution.py:41
  52.0 20.0 %collective-permute-start.19 = (bf16[192,2048]{1,0:T(8,128)(2,1)S(1)}, bf16[192,2048]{1,0:T(8,128)(2,1)S(1)}, u32[]{:S(2)}, u32[]{:S(2)}) collective-permute-start(bf16[192,2048]{1,0:T(8,128)(2,1)S(1)} %pad_maximum_fusion.refs_2_), channel_id=1, source_target_pairs={{0,4},{4,0},{8,12},{12,8},{16,20},{20,16},{24,28},{28,24},{1,5},{5... | collective-permute-start | bytes 2359304 | tf_op jit(solution)/shard_map/ppermute | solution.py:41
  53.6 8.4 %collective-permute-start.17 = (bf16[64,2048]{1,0:T(8,128)(2,1)S(1)}, bf16[64,2048]{1,0:T(8,128)(2,1)S(1)}, u32[]{:S(2)}, u32[]{:S(2)}) collective-permute-start(bf16[64,2048]{1,0:T(8,128)(2,1)S(1)} %add_convert_fusion.3.low), channel_id=1, source_target_pairs={{0,2},{1,3},{2,0},{3,1},{4,6},{5,7},{6,4},{7,5},{8,10},{9,11},{10,... | collective-permute-start | bytes 786440 | tf_op jit(solution)/shard_map/ppermute | solution.py:41
  73.5 16.1 %collective-permute-start.21 = (bf16[64,2048]{1,0:T(8,128)(2,1)S(1)}, bf16[64,2048]{1,0:T(8,128)(2,1)S(1)}, u32[]{:S(2)}, u32[]{:S(2)}) collective-permute-start(bf16[64,2048]{1,0:T(8,128)(2,1)S(1)} %add_convert_fusion.2.low), channel_id=1, source_target_pairs={{0,2},{1,3},{2,0},{3,1},{4,6},{5,7},{6,4},{7,5},{8,10},{9,11},{10,... | collective-permute-start | bytes 786440 | tf_op jit(solution)/shard_map/ppermute | solution.py:41
  74.7 14.0 %collective-permute-start.22 = (bf16[32,2048]{1,0:T(8,128)(2,1)S(1)}, bf16[32,2048]{1,0:T(8,128)(2,1)S(1)}, u32[]{:S(2)}, u32[]{:S(2)}) collective-permute-start(bf16[32,2048]{1,0:T(8,128)(2,1)S(1)} %constant_dynamic-slice_fusion), channel_id=1, source_target_pairs={{0,8},{4,12},{8,0},{12,4},{16,24},{20,28},{24,16},{28,20},{1,9},{5... | collective-permute-start | bytes 393224 | tf_op jit(solution)/shard_map/ppermute | solution.py:41
  76.7 12.9 %collective-permute-start.23 = (bf16[32,2048]{1,0:T(8,128)(2,1)S(1)}, bf16[32,2048]{1,0:T(8,128)(2,1)S(1)}, u32[]{:S(2)}, u32[]{:S(2)}) collective-permute-start(bf16[32,2048]{1,0:T(8,128)(2,1)S(1)} %constant_dynamic-slice_fusion), channel_id=1, source_target_pairs={{0,16},{4,20},{8,24},{12,28},{16,0},{20,4},{24,8},{28,12},{1,17},{... | collective-permute-start | bytes 393224 | tf_op jit(solution)/shard_map/ppermute | solution.py:41
  77.9 11.6 %collective-permute-start.24 = (bf16[32,2048]{1,0:T(8,128)(2,1)S(1)}, bf16[32,2048]{1,0:T(8,128)(2,1)S(1)}, u32[]{:S(2)}, u32[]{:S(2)}) collective-permute-start(bf16[32,2048]{1,0:T(8,128)(2,1)S(1)} %constant_dynamic-slice_fusion), channel_id=1, source_target_pairs={{0,24},{4,28},{8,16},{12,20},{16,8},{20,12},{24,0},{28,4},{1,25},{... | collective-permute-start | bytes 393224 | tf_op jit(solution)/shard_map/ppermute | solution.py:41
  90.5 11.6 %collective-permute-start.35 = (bf16[96,2048]{1,0:T(8,128)(2,1)S(1)}, bf16[96,2048]{1,0:T(8,128)(2,1)S(1)}, u32[]{:S(2)}, u32[]{:S(2)}) collective-permute-start(bf16[96,2048]{1,0:T(8,128)(2,1)S(1)} %get-tuple-element.316), channel_id=1, source_target_pairs={{0,2},{1,3},{2,0},{3,1},{4,6},{5,7},{6,4},{7,5},{8,10},{9,11},{10,... | collective-permute-start | bytes 1179656 | tf_op jit(solution)/shard_map/ppermute | solution.py:41
  91.4 11.2 %collective-permute-start.36 = (bf16[96,2048]{1,0:T(8,128)(2,1)S(1)}, bf16[96,2048]{1,0:T(8,128)(2,1)S(1)}, u32[]{:S(2)}, u32[]{:S(2)}) collective-permute-start(bf16[96,2048]{1,0:T(8,128)(2,1)S(1)} %get-tuple-element.316), channel_id=1, source_target_pairs={{0,4},{4,0},{8,12},{12,8},{16,20},{20,16},{24,28},{28,24},{1,5},{5... | collective-permute-start | bytes 1179656 | tf_op jit(solution)/shard_map/ppermute | solution.py:41
  93.9 8.8 %collective-permute-start.27 = (bf16[128,512]{1,0:T(8,128)(2,1)S(1)}, bf16[128,512]{1,0:T(8,128)(2,1)S(1)}, u32[]{:S(2)}, u32[]{:S(2)}) collective-permute-start(bf16[128,512]{1,0:T(8,128)(2,1)S(1)} %product_back.1.refs_0_), channel_id=1, source_target_pairs={{0,8},{4,12},{8,0},{12,4},{16,24},{20,28},{24,16},{28,20},{1,9},{5... | collective-permute-start | bytes 393224 | tf_op jit(solution)/shard_map/ppermute | solution.py:41
  96.2 12.8 %collective-permute-start.29 = (bf16[128,512]{1,0:T(8,128)(2,1)S(1)}, bf16[128,512]{1,0:T(8,128)(2,1)S(1)}, u32[]{:S(2)}, u32[]{:S(2)}) collective-permute-start(bf16[128,512]{1,0:T(8,128)(2,1)S(1)} %product_back.1.refs_0_), channel_id=1, source_target_pairs={{0,16},{4,20},{8,24},{12,28},{16,0},{20,4},{24,8},{28,12},{1,17},{... | collective-permute-start | bytes 393224 | tf_op jit(solution)/shard_map/ppermute | solution.py:41
  97.7 11.3 %collective-permute-start.31 = (bf16[128,512]{1,0:T(8,128)(2,1)S(1)}, bf16[128,512]{1,0:T(8,128)(2,1)S(1)}, u32[]{:S(2)}, u32[]{:S(2)}) collective-permute-start(bf16[128,512]{1,0:T(8,128)(2,1)S(1)} %product_back.1.refs_0_), channel_id=1, source_target_pairs={{0,24},{4,28},{8,16},{12,20},{16,8},{20,12},{24,0},{28,4},{1,25},{... | collective-permute-start | bytes 393224 | tf_op jit(solution)/shard_map/ppermute | solution.py:41
  102.1 9.8 %collective-permute-start.38 = (bf16[192,2048]{1,0:T(8,128)(2,1)S(1)}, bf16[192,2048]{1,0:T(8,128)(2,1)S(1)}, u32[]{:S(2)}, u32[]{:S(2)}) collective-permute-start(bf16[192,2048]{1,0:T(8,128)(2,1)S(1)} %pad_maximum_fusion.refs_2_), channel_id=1, source_target_pairs={{0,1},{1,0},{2,3},{3,2},{4,5},{5,4},{6,7},{7,6},{8,9},{9,8},{10,11... | collective-permute-start | bytes 2359304 | tf_op jit(solution)/shard_map/ppermute | solution.py:41
  102.7 7.0 %collective-permute-start.33 = (bf16[64,2048]{1,0:T(8,128)(2,1)S(1)}, bf16[64,2048]{1,0:T(8,128)(2,1)S(1)}, u32[]{:S(2)}, u32[]{:S(2)}) collective-permute-start(bf16[64,2048]{1,0:T(8,128)(2,1)S(1)} %get-tuple-element.210), channel_id=1, source_target_pairs={{0,1},{1,0},{2,3},{3,2},{4,5},{5,4},{6,7},{7,6},{8,9},{9,8},{10,11... | collective-permute-start | bytes 786440 | tf_op jit(solution)/shard_map/ppermute | solution.py:41
  109.1 6.5 %collective-permute-start.37 = (bf16[192,2048]{1,0:T(8,128)(2,1)S(1)}, bf16[192,2048]{1,0:T(8,128)(2,1)S(1)}, u32[]{:S(2)}, u32[]{:S(2)}) collective-permute-start(bf16[192,2048]{1,0:T(8,128)(2,1)S(1)} %constant_dynamic-update-slice_fusion.5.refs_0_), channel_id=1, source_target_pairs={{0,1},{1,0},{2,3},{3,2},{4,5},{5,4},{6,7},{7,6},{8,9},{9,8},{10,11... | collective-permute-start | bytes 2359304 | tf_op jit(solution)/shard_map/ppermute | solution.py:41
  109.1 6.4 %collective-permute-start.28 = (bf16[128,512]{1,0:T(8,128)(2,1)S(1)}, bf16[128,512]{1,0:T(8,128)(2,1)S(1)}, u32[]{:S(2)}, u32[]{:S(2)}) collective-permute-start(bf16[128,512]{1,0:T(8,128)(2,1)S(1)} %collective-permute-done.27.refs_2_), channel_id=1, source_target_pairs={{0,4},{4,0},{8,12},{12,8},{16,20},{20,16},{24,28},{28,24},{1,5},{5... | collective-permute-start | bytes 393224 | tf_op jit(solution)/shard_map/ppermute | solution.py:41
  109.8 20.0 %collective-permute-start.34 = (bf16[64,2048]{1,0:T(8,128)(2,1)S(1)}, bf16[64,2048]{1,0:T(8,128)(2,1)S(1)}, u32[]{:S(2)}, u32[]{:S(2)}) collective-permute-start(bf16[64,2048]{1,0:T(8,128)(2,1)S(1)} %add_convert_fusion.1.low), channel_id=1, source_target_pairs={{0,2},{1,3},{2,0},{3,1},{4,6},{5,7},{6,4},{7,5},{8,10},{9,11},{10,... | collective-permute-start | bytes 786440 | tf_op jit(solution)/shard_map/ppermute | solution.py:41
  110.8 32.0 %collective-permute-start.40 = (bf16[96,2048]{1,0:T(8,128)(2,1)S(1)}, bf16[96,2048]{1,0:T(8,128)(2,1)S(1)}, u32[]{:S(2)}, u32[]{:S(2)}) collective-permute-start(bf16[96,2048]{1,0:T(8,128)(2,1)S(1)} %collective-permute-done.36), channel_id=1, source_target_pairs={{0,2},{1,3},{2,0},{3,1},{4,6},{5,7},{6,4},{7,5},{8,10},{9,11},{10,... | collective-permute-start | bytes 1179656 | tf_op jit(solution)/shard_map/ppermute | solution.py:41
  111.9 17.9 %collective-permute-start.26 = (bf16[128,512]{1,0:T(8,128)(2,1)S(1)}, bf16[128,512]{1,0:T(8,128)(2,1)S(1)}, u32[]{:S(2)}, u32[]{:S(2)}) collective-permute-start(bf16[128,512]{1,0:T(8,128)(2,1)S(1)} %product_back.1.refs_0_), channel_id=1, source_target_pairs={{0,4},{4,0},{8,12},{12,8},{16,20},{20,16},{24,28},{28,24},{1,5},{5... | collective-permute-start | bytes 393224 | tf_op jit(solution)/shard_map/ppermute | solution.py:41
  115.5 14.3 %collective-permute-start.30 = (bf16[128,512]{1,0:T(8,128)(2,1)S(1)}, bf16[128,512]{1,0:T(8,128)(2,1)S(1)}, u32[]{:S(2)}, u32[]{:S(2)}) collective-permute-start(bf16[128,512]{1,0:T(8,128)(2,1)S(1)} %collective-permute-done.29.refs_4_), channel_id=1, source_target_pairs={{0,4},{4,0},{8,12},{12,8},{16,20},{20,16},{24,28},{28,24},{1,5},{5... | collective-permute-start | bytes 393224 | tf_op jit(solution)/shard_map/ppermute | solution.py:41
  115.5 14.2 %collective-permute-start.32 = (bf16[128,512]{1,0:T(8,128)(2,1)S(1)}, bf16[128,512]{1,0:T(8,128)(2,1)S(1)}, u32[]{:S(2)}, u32[]{:S(2)}) collective-permute-start(bf16[128,512]{1,0:T(8,128)(2,1)S(1)} %collective-permute-done.31.refs_6_), channel_id=1, source_target_pairs={{0,4},{4,0},{8,12},{12,8},{16,20},{20,16},{24,28},{28,24},{1,5},{5... | collective-permute-start | bytes 393224 | tf_op jit(solution)/shard_map/ppermute | solution.py:41
  129.8 13.1 %collective-permute-start.39 = (bf16[64,2048]{1,0:T(8,128)(2,1)S(1)}, bf16[64,2048]{1,0:T(8,128)(2,1)S(1)}, u32[]{:S(2)}, u32[]{:S(2)}) collective-permute-start(bf16[64,2048]{1,0:T(8,128)(2,1)S(1)} %get-tuple-element.233), channel_id=1, source_target_pairs={{0,4},{4,0},{8,12},{12,8},{16,20},{20,16},{24,28},{28,24},{1,5},{5... | collective-permute-start | bytes 786440 | tf_op jit(solution)/shard_map/ppermute | solution.py:41
  130.0 12.9 %collective-permute-start.43 = (bf16[2,72,256]{2,1,0:T(8,128)(2,1)S(1)}, bf16[2,72,256]{2,1,0:T(8,128)(2,1)S(1)}, u32[]{:S(2)}, u32[]{:S(2)}) collective-permute-start(bf16[2,72,256]{2,1,0:T(8,128)(2,1)S(1)} %get-tuple-element.238), channel_id=1, source_target_pairs={{0,24},{4,28},{8,16},{12,20},{16,8},{20,12},{24,0},{28,4},{1,25},{... | collective-permute-start | bytes 221192 | tf_op jit(solution)/shard_map/ppermute | solution.py:41
  132.4 10.5 %collective-permute-start.42 = (bf16[2,72,256]{2,1,0:T(8,128)(2,1)S(1)}, bf16[2,72,256]{2,1,0:T(8,128)(2,1)S(1)}, u32[]{:S(2)}, u32[]{:S(2)}) collective-permute-start(bf16[2,72,256]{2,1,0:T(8,128)(2,1)S(1)} %get-tuple-element.237), channel_id=1, source_target_pairs={{0,16},{4,20},{8,24},{12,28},{16,0},{20,4},{24,8},{28,12},{1,17},{... | collective-permute-start | bytes 221192 | tf_op jit(solution)/shard_map/ppermute | solution.py:41
  133.7 9.2 %collective-permute-start.41 = (bf16[2,72,256]{2,1,0:T(8,128)(2,1)S(1)}, bf16[2,72,256]{2,1,0:T(8,128)(2,1)S(1)}, u32[]{:S(2)}, u32[]{:S(2)}) collective-permute-start(bf16[2,72,256]{2,1,0:T(8,128)(2,1)S(1)} %get-tuple-element.236), channel_id=1, source_target_pairs={{0,8},{4,12},{8,0},{12,4},{16,24},{20,28},{24,16},{28,20},{1,9},{5... | collective-permute-start | bytes 221192 | tf_op jit(solution)/shard_map/ppermute | solution.py:41
  146.7 9.0 %collective-permute-start.45 = (bf16[64,2048]{1,0:T(8,128)(2,1)S(1)}, bf16[64,2048]{1,0:T(8,128)(2,1)S(1)}, u32[]{:S(2)}, u32[]{:S(2)}) collective-permute-start(bf16[64,2048]{1,0:T(8,128)(2,1)S(1)} %add_convert_fusion.low), channel_id=1, source_target_pairs={{0,2},{1,3},{2,0},{3,1},{4,6},{5,7},{6,4},{7,5},{8,10},{9,11},{10,... | collective-permute-start | bytes 786440 | tf_op jit(solution)/shard_map/ppermute | solution.py:41
  148.1 6.9 %collective-permute-start.47 = (bf16[72,256]{1,0:T(8,128)(2,1)S(1)}, bf16[72,256]{1,0:T(8,128)(2,1)S(1)}, u32[]{:S(2)}, u32[]{:S(2)}) collective-permute-start(bf16[72,256]{1,0:T(8,128)(2,1)S(1)} %get-tuple-element.326), channel_id=1, source_target_pairs={{0,4},{4,0},{8,12},{12,8},{16,20},{20,16},{24,28},{28,24},{1,5},{5... | collective-permute-start | bytes 110600 | tf_op jit(solution)/shard_map/ppermute | solution.py:41
  149.7 5.2 %collective-permute-start.48 = (bf16[72,256]{1,0:T(8,128)(2,1)S(1)}, bf16[72,256]{1,0:T(8,128)(2,1)S(1)}, u32[]{:S(2)}, u32[]{:S(2)}) collective-permute-start(bf16[72,256]{1,0:T(8,128)(2,1)S(1)} %get-tuple-element.324), channel_id=1, source_target_pairs={{0,4},{4,0},{8,12},{12,8},{16,20},{20,16},{24,28},{28,24},{1,5},{5... | collective-permute-start | bytes 110600 | tf_op jit(solution)/shard_map/ppermute | solution.py:41
  150.1 4.8 %collective-permute-start.49 = (bf16[72,256]{1,0:T(8,128)(2,1)S(1)}, bf16[72,256]{1,0:T(8,128)(2,1)S(1)}, u32[]{:S(2)}, u32[]{:S(2)}) collective-permute-start(bf16[72,256]{1,0:T(8,128)(2,1)S(1)} %get-tuple-element.322), channel_id=1, source_target_pairs={{0,4},{4,0},{8,12},{12,8},{16,20},{20,16},{24,28},{28,24},{1,5},{5... | collective-permute-start | bytes 110600 | tf_op jit(solution)/shard_map/ppermute | solution.py:41
  151.8 4.0 %collective-permute-start.46 = (bf16[72,256]{1,0:T(8,128)(2,1)S(1)}, bf16[72,256]{1,0:T(8,128)(2,1)S(1)}, u32[]{:S(2)}, u32[]{:S(2)}) collective-permute-start(bf16[72,256]{1,0:T(8,128)(2,1)S(1)} %get-tuple-element.328), channel_id=1, source_target_pairs={{0,4},{4,0},{8,12},{12,8},{16,20},{20,16},{24,28},{28,24},{1,5},{5... | collective-permute-start | bytes 110600 | tf_op jit(solution)/shard_map/ppermute | solution.py:41
  155.7 4.2 %collective-permute-start.55 = (bf16[192,2048]{1,0:T(8,128)(2,1)S(1)}, bf16[192,2048]{1,0:T(8,128)(2,1)S(1)}, u32[]{:S(2)}, u32[]{:S(2)}) collective-permute-start(bf16[192,2048]{1,0:T(8,128)(2,1)S(1)} %pad_maximum_fusion.1.refs_2_), channel_id=1, source_target_pairs={{0,1},{1,0},{2,3},{3,2},{4,5},{5,4},{6,7},{7,6},{8,9},{9,8},{10,11... | collective-permute-start | bytes 2359304 | tf_op jit(solution)/shard_map/ppermute | solution.py:41
  155.7 4.2 %collective-permute-start.57 = (bf16[192,2048]{1,0:T(8,128)(2,1)S(1)}, bf16[192,2048]{1,0:T(8,128)(2,1)S(1)}, u32[]{:S(2)}, u32[]{:S(2)}) collective-permute-start(bf16[192,2048]{1,0:T(8,128)(2,1)S(1)} %collective-permute-done.19.refs_6_), channel_id=1, source_target_pairs={{0,1},{1,0},{2,3},{3,2},{4,5},{5,4},{6,7},{7,6},{8,9},{9,8},{10,11... | collective-permute-start | bytes 2359304 | tf_op jit(solution)/shard_map/ppermute | solution.py:41
  175.0 4.9 %collective-permute-start.58 = (bf16[8,72,256]{2,1,0:T(8,128)(2,1)S(1)}, bf16[8,72,256]{2,1,0:T(8,128)(2,1)S(1)}, u32[]{:S(2)}, u32[]{:S(2)}) collective-permute-start(bf16[8,72,256]{2,1,0:T(8,128)(2,1)S(1)} %constant_dynamic-update-slice_fusion.9.came_a), channel_id=1, source_target_pairs={{0,1},{1,0},{2,3},{3,2},{4,5},{5,4},{6,7},{7,6},{8,9},{9,8},{10,11... | collective-permute-start | bytes 884744 | tf_op jit(solution)/shard_map/ppermute | solution.py:41
  (30 other events, 213.2 us)

commit v9 on v8

--- a/solution.py
+++ b/solution.py
@@ -740,7 +740,9 @@
     )(index, *normed, *[low for pair in lows for low in pair], *weights, gain, *kinds)
 
 
-def output_kernel(attended_a, attended_b, came_a, came_b, out, gain_grad, *, groups):
+def output_kernel(
+    attended_a, attended_b, came_a, came_b, first_mine, first_came, out, gain_grad, first, *, groups
+):
     total, sums = 0.0, 0.0
     shards, rows, part = came_a.shape
     half = rows - 8
@@ -758,23 +760,24 @@
         sums += own_sums
     out[...] = total
     gain_grad[...] = sums[0:3, :] + sums[3:6, :]
-
-
-def output_part(attended, came, groups):
+    first[...] = first_mine[...] + first_came[...]
+
+
+def output_part(attended, came, first, groups):
     across, part = attended[0].shape[1], came[0].shape[2]
     return pl.pallas_call(
         partial(output_kernel, groups=groups),
-        in_specs=[WHOLE] * 4,
+        in_specs=[WHOLE] * 6,
         out_shape=[
             jax.ShapeDtypeStruct((across, part), f32),
-            jax.ShapeDtypeStruct((3, part), f32),
-        ],
+        ]
+        + [jax.ShapeDtypeStruct((3, part), f32)] * 2,
         compiler_params=params(6),
         cost_estimate=cost(
             4 * attended[0].shape[0] * across * part, 4 * attended[0].shape[0] * (across + part)
         ),
         name="output_part",
-    )(*attended, *came)
+    )(*attended, *came, *first)
 
 
 def mask_of(key_place, query_place, clip_length, clips):
@@ -1190,16 +1193,21 @@
     up_grad, down_grad = feed_all(
         after(rest_lifted, outputs_half, first_gain_grad), rest_grads, up_weight, down_weight, shards, sums
     )
+    first_came = jnp.zeros_like(first_gain_grad)
     bit = 2
     while bit < lax.axis_size("mlp"):
-        came = after(swap(first_gain_grad, "mlp", bit), up_grad)
-        first_gain_grad = first_gain_grad + came
+        if bit > 2:
+            first_gain_grad = first_gain_grad + first_came
+        first_came = after(swap(first_gain_grad, "mlp", bit), up_grad)
         bit *= 2
     placed = (input_half, outputs_half)
     input_grad, outputs = place_halves(placed, [swap(array, "mlp", 1) for array in placed])
     mixed_part = jnp.stack([after(columns[d], up_grad) for d in range(shards)])
-    output_grad, second_gain_grad = output_part(
-        attended, (mixed_part, swap(mixed_part, "mlp", 1)), groups
+    output_grad, second_gain_grad, first_gain_grad = output_part(
+        attended,
+        (mixed_part, swap(mixed_part, "mlp", 1)),
+        (first_gain_grad, first_came),
+        groups,
     )
 
     return (

time: 181 us -> 181 us (level)
  no operation moved by 1% of the time
where the time goes in v9:
time: 181 us
  Pallas kernels  81.4 us (45%)
  starting transfers between devices  58.3 us (32%)
  waiting for transfers between devices  36.1 us (20%)
  local copies, waits for them, and re-layouts  2.22 us (1%)
    ppermute x59, starting transfers between devices, swap(): return lax.ppermute(value, axis, [(i, i ^ bit) for i in range(size)])  58.3 us
    ppermute x59, waiting for transfers between devices, swap(): return lax.ppermute(value, axis, [(i, i ^ bit) for i in range(size)])  36.1 us
    pallas_call x2, Pallas kernels, feed_all(): pl.pallas_call(partial(all_kernel, count=count), grid_spec=pltpu.Prefetch...  27.3 us
    pallas_call x1, Pallas kernels, attend_all(): pl.pallas_call(partial(all_forward_kernel, groups=groups, scale=1.0 / mat...  9.35 us
    pallas_call x1, Pallas kernels, attend_back(): pl.pallas_call(partial(backward_kernel, count=count, groups=groups, scale...  8.36 us
    pallas_call x5, Pallas kernels, project_rows(): pl.pallas_call(partial(rows_kernel, count=len(weights)), out_shape=[jax.S...  7.65 us
    pallas_call x1, Pallas kernels, feed_own(): pl.pallas_call(own_kernel, in_specs=[WHOLE] * 3, out_specs=[WHOLE] * 4, o...  5.47 us
  transfers between devices with their start and end apart: 59, of which 23 were waited for; matrix products, arithmetic and copies ran while one was open for 1% of the time, Pallas kernels for 34%

profile of v9, /device:TPU:0, one launch (start us, length us, event | category | flops | bytes accessed | tf_op | source)
XLA Modules:
  0.0 180.7 jit_solution(13998175660504633901)
XLA Ops:
  2.2 3.1 %collective-permute-start = (bf16[32,2048]{1,0:T(8,128)(2,1)S(1)}, bf16[32,2048]{1,0:T(8,128)(2,1)S(1)}, u32[]{:S(2)}, u32[]{:S(2)}) collective-permute-start(bf16[32,2048]{1,0:T(8,128)(2,1)S(1)} %constant_dynamic-slice_fusion.4), channel_id=1, source_target_pairs={{0,8},{4,12},{8,0},{12,4},{16,24},{20,28},{24,16},{28,20},{1,9},{5... | collective-permute-start | bytes 393224 | tf_op jit(solution)/shard_map/ppermute | solution.py:41
  5.2 2.6 %collective-permute-start.2 = (bf16[32,2048]{1,0:T(8,128)(2,1)S(1)}, bf16[32,2048]{1,0:T(8,128)(2,1)S(1)}, u32[]{:S(2)}, u32[]{:S(2)}) collective-permute-start(bf16[32,2048]{1,0:T(8,128)(2,1)S(1)} %constant_dynamic-slice_fusion.4), channel_id=1, source_target_pairs={{0,16},{4,20},{8,24},{12,28},{16,0},{20,4},{24,8},{28,12},{1,17},{... | collective-permute-start | bytes 393224 | tf_op jit(solution)/shard_map/ppermute | solution.py:41
  7.8 2.4 %collective-permute-done = bf16[32,2048]{1,0:T(8,128)(2,1)S(1)} collective-permute-done((bf16[32,2048]{1,0:T(8,128)(2,1)S(1)}, bf16[32,2048]{1,0:T(8,128)(2,1)S(1)}, u32[]{:S(2)}, u32[]{:S(2)}) %collective-permute-start) | collective-permute-done | bytes 131104 | tf_op jit(solution)/shard_map/ppermute | solution.py:41
  10.3 1.7 collective-permute-start.1
  12.0 1.5 collective-permute-start.6
  14.1 2.4 %tables.1 = (s32[512,1]{1,0:T(8,128)}, s32[512,1]{1,0:T(8,128)}, s32[512,1]{1,0:T(8,128)}, s32[512,1]{1,0:T(8,128)}, s32[1,1024]{1,0:T(1,128)}, /*index=5*/s32[1,128]{1,0:T(1,128)}, s32[128,1]{1,0:T(8,128)}) custom-call(s32[2]{0:T(128)} %pad_add_fusion.index, s32[1,8]{1,0:T(1,128)} %frames.1, s32[1,8]{1,0:T(1,128)} %texts.1, s32[1,8]{1,0:T(1,128)} %actions.1), custom_call_target="tpu_custom_call" | custom-call | flops 10485 | bytes 10485 | tf_op jit(solution)/shard_map/tables/pallas_call | solution.py:206
  18.2 1.5 collective-permute-start.3
  20.2 1.6 collective-permute-start.7
  23.2 1.6 collective-permute-start.8
  24.8 1.5 collective-permute-start.9
  26.2 3.3 %collective-permute-done.7.refs_4_ = bf16[64,2048]{1,0:T(8,128)(2,1)S(1)} collective-permute-done((bf16[64,2048]{1,0:T(8,128)(2,1)S(1)}, bf16[64,2048]{1,0:T(8,128)(2,1)S(1)}, u32[]{:S(2)}, u32[]{:S(2)}) %collective-permute-start.7) | collective-permute-done | bytes 262176 | tf_op jit(solution)/shard_map/ppermute | solution.py:41
  29.5 1.5 collective-permute-start.10
  31.0 1.4 collective-permute-start.11
  32.5 1.5 collective-permute-start.12
  36.3 2.5 %norm_pieces.1 = bf16[8,8,8,2048]{3,2,1,0:T(8,128)(2,1)S(1)} custom-call(s32[1]{0:T(128)} %bitcast.11.refs_0_, bf16[64,2048]{1,0:T(8,128)(2,1)S(1)} %bitcast.78, bf16[64,2048]{1,0:T(8,128)(2,1)S(1)} %collective-permute-done.6.refs_2_, bf16[64,2048]{1,0:T(8,128)(2,1)S(1)} %pad_maximum_fusion.6.refs_3_, bf16[64,2048]{1,0:T(8,128)(2,1)S(1)} %collective-permute-done.7.refs_4_, ...), custom_call_target="tpu_custom_call" | custom-call | flops 104857 | bytes 41943 | tf_op jit(solution)/shard_map/norm_pieces/pallas_call | solution.py:360
  40.9 1.5 collective-permute-start.14
  42.5 2.3 %project_rows.6 = (bf16[512,512]{1,0:T(8,128)(2,1)S(1)}, bf16[512,512]{1,0:T(8,128)(2,1)S(1)}) custom-call(bf16[512,2048]{1,0:T(8,128)(2,1)S(1)} %bitcast.72, bf16[2048,512]{1,0:T(8,128)(2,1)S(1)} %copy-done.1, bf16[2048,512]{1,0:T(8,128)(2,1)S(1)} %copy-done.2), custom_call_target="tpu_custom_call" | custom-call | flops 21474836 | bytes 20971 | tf_op jit(solution)/shard_map/project_rows/pallas_call | solution.py:234
  44.9 2.4 %project_rows.7 = (bf16[512,512]{1,0:T(8,128)(2,1)S(1)}, bf16[512,512]{1,0:T(8,128)(2,1)S(1)}) custom-call(bf16[512,2048]{1,0:T(8,128)(2,1)S(1)} %collective-permute-done.13.refs_0_.refs_1_, bf16[2048,512]{1,0:T(8,128)(2,1)S(1)} %copy-done.1, bf16[2048,512]{1,0:T(8,128)(2,1)S(1)} %copy-done.2), custom_call_target="tpu_custom_call" | custom-call | flops 21474836 | bytes 20971 | tf_op jit(solution)/shard_map/project_rows/pallas_call | solution.py:234
  47.3 1.9 %attend.1.refs_0_ = bf16[128,512]{1,0:T(8,128)(2,1)S(1)} custom-call(bf16[128,512]{1,0:T(8,128)(2,1)S(1)} %project_rows.5.query, bf16[512,512]{1,0:T(8,128)(2,1)S(1)} %get-tuple-element.173.key_a.refs_2_.refs_10_, bf16[512,512]{1,0:T(8,128)(2,1)S(1)} %get-tuple-element.174.key_b.refs_3_.refs_11_, ...), custom_call_target="tpu_custom_call" | custom-call | flops 2684354 | bytes 20971 | tf_op jit(solution)/shard_map/attend/pallas_call | solution.py:824
  49.4 2.0 %collective-permute-done.15 = bf16[96,2048]{1,0:T(8,128)(2,1)S(1)} collective-permute-done((bf16[96,2048]{1,0:T(8,128)(2,1)S(1)}, bf16[96,2048]{1,0:T(8,128)(2,1)S(1)}, u32[]{:S(2)}, u32[]{:S(2)}) %collective-permute-start.15) | collective-permute-done | bytes 393248 | tf_op jit(solution)/shard_map/ppermute | solution.py:41
  52.0 1.6 collective-permute-start.19
  55.1 3.5 %grad_activated.1 = f32[128,2048]{1,0:T(8,128)S(1)} custom-call(bf16[128,2048]{1,0:T(8,128)(2,1)S(1)} %pad_maximum_fusion.3.grad.refs_7_, bf16[2048,2048]{1,0:T(8,128)(2,1)S(1)} %bitcast.68), custom_call_target="tpu_custom_call" | custom-call | flops 10737418 | bytes 83886 | tf_op jit(solution)/shard_map/grad_activated/pallas_call | solution.py:576
  62.5 1.5 collective-permute-done.18
  64.1 5.5 %feed_own.1 = (bf16[128,2048]{1,0:T(8,128)(2,1)S(1)}, bf16[128,2048]{1,0:T(8,128)(2,1)S(1)}, f32[64,2048]{1,0:T(8,128)S(1)}, bf16[64,2048]{1,0:T(8,128)(2,1)S(1)}) custom-call(bf16[128,2048]{1,0:T(8,128)(2,1)S(1)} %constant_dynamic-update-slice_fusion.lifted.refs_6_, bf16[2048,2048]{1,0:T(8,128)(2,1)S(1)} %bitcast.70, f32[128,2048]{1,0:T(8,128)S(1)} %grad_activated.1), custom_call_target="tpu_custom_call" | custom-call | flops 21474836 | bytes 83886 | tf_op jit(solution)/shard_map/feed_own/pallas_call | solution.py:550
  69.6 2.4 %collective-permute-done.19.refs_6_ = bf16[192,2048]{1,0:T(8,128)(2,1)S(1)} collective-permute-done((bf16[192,2048]{1,0:T(8,128)(2,1)S(1)}, bf16[192,2048]{1,0:T(8,128)(2,1)S(1)}, u32[]{:S(2)}, u32[]{:S(2)}) %collective-permute-start.19) | collective-permute-done | bytes 786464 | tf_op jit(solution)/shard_map/ppermute | solution.py:41
  71.9 1.5 collective-permute-done.20
  74.7 1.9 %collective-permute-start.22 = (bf16[32,2048]{1,0:T(8,128)(2,1)S(1)}, bf16[32,2048]{1,0:T(8,128)(2,1)S(1)}, u32[]{:S(2)}, u32[]{:S(2)}) collective-permute-start(bf16[32,2048]{1,0:T(8,128)(2,1)S(1)} %constant_dynamic-slice_fusion), channel_id=1, source_target_pairs={{0,8},{4,12},{8,0},{12,4},{16,24},{20,28},{24,16},{28,20},{1,9},{5... | collective-permute-start | bytes 393224 | tf_op jit(solution)/shard_map/ppermute | solution.py:41
  77.9 1.4 collective-permute-start.24
  79.3 9.3 %attend_all.1 = (bf16[512,512]{1,0:T(8,128)(2,1)S(1)}, bf16[512,512]{1,0:T(8,128)(2,1)S(1)}, bf16[4,2560,256]{2,1,0:T(8,128)(2,1)}) custom-call(bf16[512,512]{1,0:T(8,128)(2,1)S(1)} %project_rows.8.refs_0_.refs_8_, bf16[512,512]{1,0:T(8,128)(2,1)S(1)} %project_rows.9.refs_1_.refs_9_, bf16[512,512]{1,0:T(8,128)(2,1)S(1)} %get-tuple-element.173.key_a.refs_2_.refs_10_, ...), custom_call_target="tpu_custom_call" | custom-call | flops 21474836 | bytes 41943 | tf_op jit(solution)/shard_map/attend_all/pallas_call | solution.py:916
  91.4 1.5 collective-permute-start.36
  93.9 2.4 %collective-permute-start.27 = (bf16[128,512]{1,0:T(8,128)(2,1)S(1)}, bf16[128,512]{1,0:T(8,128)(2,1)S(1)}, u32[]{:S(2)}, u32[]{:S(2)}) collective-permute-start(bf16[128,512]{1,0:T(8,128)(2,1)S(1)} %product_back.1.refs_0_), channel_id=1, source_target_pairs={{0,8},{4,12},{8,0},{12,4},{16,24},{20,28},{24,16},{28,20},{1,9},{5... | collective-permute-start | bytes 393224 | tf_op jit(solution)/shard_map/ppermute | solution.py:41
  96.2 1.5 collective-permute-start.29
  97.7 1.4 collective-permute-start.31
  99.1 2.0 %down_own.1 = (f32[64,2048]{1,0:T(8,128)S(1)}, bf16[64,2048]{1,0:T(8,128)(2,1)S(1)}) custom-call(bf16[128,2048]{1,0:T(8,128)(2,1)S(1)} %get-tuple-element.209.rows.refs_8_, bf16[2048,2048]{1,0:T(8,128)(2,1)S(1)} %bitcast.68), custom_call_target="tpu_custom_call" | custom-call | flops 10737418 | bytes 83886 | tf_op jit(solution)/shard_map/down_own/pallas_call | solution.py:295
  102.7 6.3 %collective-permute-done.29.refs_4_ = bf16[128,512]{1,0:T(8,128)(2,1)S(1)} collective-permute-done((bf16[128,512]{1,0:T(8,128)(2,1)S(1)}, bf16[128,512]{1,0:T(8,128)(2,1)S(1)}, u32[]{:S(2)}, u32[]{:S(2)}) %collective-permute-start.29) | collective-permute-done | bytes 131104 | tf_op jit(solution)/shard_map/ppermute | solution.py:41
  111.9 1.5 collective-permute-start.26
  113.4 2.1 %collective-permute-done.28.refs_3_ = bf16[128,512]{1,0:T(8,128)(2,1)S(1)} collective-permute-done((bf16[128,512]{1,0:T(8,128)(2,1)S(1)}, bf16[128,512]{1,0:T(8,128)(2,1)S(1)}, u32[]{:S(2)}, u32[]{:S(2)}) %collective-permute-start.28) | collective-permute-done | bytes 131104 | tf_op jit(solution)/shard_map/ppermute | solution.py:41
  115.5 2.0 %collective-permute-start.32 = (bf16[128,512]{1,0:T(8,128)(2,1)S(1)}, bf16[128,512]{1,0:T(8,128)(2,1)S(1)}, u32[]{:S(2)}, u32[]{:S(2)}) collective-permute-start(bf16[128,512]{1,0:T(8,128)(2,1)S(1)} %collective-permute-done.31.refs_6_), channel_id=1, source_target_pairs={{0,4},{4,0},{8,12},{12,8},{16,20},{20,16},{24,28},{28,24},{1,5},{5... | collective-permute-start | bytes 393224 | tf_op jit(solution)/shard_map/ppermute | solution.py:41
  117.5 12.3 %feed_all.2 = (bf16[256,2048]{1,0:T(8,128)(2,1)}, bf16[2048,256]{1,0:T(8,128)(2,1)}) custom-call(s32[1]{0:T(128)} %bitcast.5.index, bf16[192,2048]{1,0:T(8,128)(2,1)S(1)} %constant_dynamic-update-slice_fusion.5.refs_0_, bf16[192,2048]{1,0:T(8,128)(2,1)S(1)} %collective-permute-done.37.refs_1_, bf16[192,2048]{1,0:T(8,128)(2,1)S(1)} %pad_maximum_fusion.refs_2_, ...), custom_call_target="tpu_custom_call" | custom-call | flops 72477576 | bytes 199229 | tf_op jit(solution)/shard_map/feed_all/pallas_call | solution.py:666
  130.0 2.4 %collective-permute-start.43 = (bf16[2,72,256]{2,1,0:T(8,128)(2,1)S(1)}, bf16[2,72,256]{2,1,0:T(8,128)(2,1)S(1)}, u32[]{:S(2)}, u32[]{:S(2)}) collective-permute-start(bf16[2,72,256]{2,1,0:T(8,128)(2,1)S(1)} %get-tuple-element.239), channel_id=1, source_target_pairs={{0,24},{4,28},{8,16},{12,20},{16,8},{20,12},{24,0},{28,4},{1,25},{... | collective-permute-start | bytes 221192 | tf_op jit(solution)/shard_map/ppermute | solution.py:41
  134.4 8.4 %attend_back.1 = (bf16[512,512]{1,0:T(8,128)(2,1)S(1)}, bf16[512,512]{1,0:T(8,128)(2,1)S(1)}, bf16[512,512]{1,0:T(8,128)(2,1)S(1)}, bf16[512,512]{1,0:T(8,128)(2...) custom-call(bf16[128,512]{1,0:T(8,128)(2,1)S(1)} %product_back.1.ref, ...), custom_call_target="tpu_custom_call" | custom-call | flops 42949672 | bytes 136314 | tf_op jit(solution)/shard_map/attend_back/pallas_call | solution.py:1032
  142.9 2.1 %product_halves.3 = (f32[64,2048]{1,0:T(8,128)S(1)}, bf16[64,2048]{1,0:T(8,128)(2,1)S(1)}) custom-call(bf16[128,512]{1,0:T(8,128)(2,1)S(1)} %get-tuple-element.240.refs_0_, bf16[128,512]{1,0:T(8,128)(2,1)S(1)} %get-tuple-element.241.refs_1_, bf16[128,512]{1,0:T(8,128)(2,1)S(1)} %get-tuple-element.242.refs_2_, bf16[2048,512]{1,0:T(8,128)(2,1)S(1)} %copy-done, ...), custom_call_target="tpu_custom_call" | custom-call | flops 8053063 | bytes 62914 | tf_op jit(solution)/shard_map/product_halves/pallas_call | solution.py:270
  145.1 1.5 collective-permute-done.44
  148.1 1.7 collective-permute-start.47
  150.1 1.7 collective-permute-start.49
  152.1 2.8 %project.1 = (f32[256,512]{1,0:T(8,128)}, f32[256,512]{1,0:T(8,128)}, f32[256,512]{1,0:T(8,128)}, f32[3,256]{1,0:T(4,128)S(1)}) custom-call(s32[1]{0:T(128)} %bitcast.5.index, bf16[512,2048]{1,0:T(8,128)(2,1)S(1)} %bitcast.74, bf16[512,2048]{1,0:T(8,128)(2,1)S(1)} %collective-permute-done.13.refs_0_.refs_1_, ...), custom_call_target="tpu_custom_call" | custom-call | flops 16106127 | bytes 47185 | tf_op jit(solution)/shard_map/project/pallas_call | solution.py:722
  157.7 2.2 %collective-permute-done.54 = f32[3,256]{1,0:T(4,128)S(1)} collective-permute-done((f32[3,256]{1,0:T(4,128)S(1)}, f32[3,256]{1,0:T(4,128)S(1)}, u32[]{:S(2)}, u32[]{:S(2)}) %collective-permute-start.54) | collective-permute-done | bytes 3104 | tf_op jit(solution)/shard_map/ppermute | solution.py:41
  159.9 15.0 %feed_all.3 = (f32[256,2048]{1,0:T(8,128)}, f32[2048,256]{1,0:T(8,128)}) custom-call(s32[1]{0:T(128)} %bitcast.5.index, bf16[64,2048]{1,0:T(8,128)(2,1)S(1)} %collective-permute-done.39.refs_0_, bf16[64,2048]{1,0:T(8,128)(2,1)S(1)} %collective-permute-done.52.refs_1_, bf16[192,2048]{1,0:T(8,128)(2,1)S(1)} %pad_maximum_fusion.1.refs_2_, ...), custom_call_target="tpu_custom_call" | custom-call | flops 96636768 | bytes 209715 | tf_op jit(solution)/shard_map/feed_all/pallas_call | solution.py:666
  (180 shorter events, 39.7 us)
Async XLA Ops:
  2.2 8.1 %collective-permute-start = (bf16[32,2048]{1,0:T(8,128)(2,1)S(1)}, bf16[32,2048]{1,0:T(8,128)(2,1)S(1)}, u32[]{:S(2)}, u32[]{:S(2)}) collective-permute-start(bf16[32,2048]{1,0:T(8,128)(2,1)S(1)} %constant_dynamic-slice_fusion.4), channel_id=1, source_target_pairs={{0,8},{4,12},{8,0},{12,4},{16,24},{20,28},{24,16},{28,20},{1,9},{5... | collective-permute-start | bytes 393224 | tf_op jit(solution)/shard_map/ppermute | solution.py:41
  5.2 12.9 %collective-permute-start.2 = (bf16[32,2048]{1,0:T(8,128)(2,1)S(1)}, bf16[32,2048]{1,0:T(8,128)(2,1)S(1)}, u32[]{:S(2)}, u32[]{:S(2)}) collective-permute-start(bf16[32,2048]{1,0:T(8,128)(2,1)S(1)} %constant_dynamic-slice_fusion.4), channel_id=1, source_target_pairs={{0,16},{4,20},{8,24},{12,28},{16,0},{20,4},{24,8},{28,12},{1,17},{... | collective-permute-start | bytes 393224 | tf_op jit(solution)/shard_map/ppermute | solution.py:41
  7.8 11.8 %collective-permute-start.4 = (bf16[32,2048]{1,0:T(8,128)(2,1)S(1)}, bf16[32,2048]{1,0:T(8,128)(2,1)S(1)}, u32[]{:S(2)}, u32[]{:S(2)}) collective-permute-start(bf16[32,2048]{1,0:T(8,128)(2,1)S(1)} %constant_dynamic-slice_fusion.4), channel_id=1, source_target_pairs={{0,24},{4,28},{8,16},{12,20},{16,8},{20,12},{24,0},{28,4},{1,25},{... | collective-permute-start | bytes 393224 | tf_op jit(solution)/shard_map/ppermute | solution.py:41
  10.3 9.9 %collective-permute-start.1 = (bf16[32,2048]{1,0:T(8,128)(2,1)S(1)}, bf16[32,2048]{1,0:T(8,128)(2,1)S(1)}, u32[]{:S(2)}, u32[]{:S(2)}) collective-permute-start(bf16[32,2048]{1,0:T(8,128)(2,1)S(1)} %collective-permute-done), channel_id=1, source_target_pairs={{0,2},{1,3},{2,0},{3,1},{4,6},{5,7},{6,4},{7,5},{8,10},{9,11},{10,... | collective-permute-start | bytes 393224 | tf_op jit(solution)/shard_map/ppermute | solution.py:41
  12.0 20.5 %collective-permute-start.6 = (bf16[64,2048]{1,0:T(8,128)(2,1)S(1)}, bf16[64,2048]{1,0:T(8,128)(2,1)S(1)}, u32[]{:S(2)}, u32[]{:S(2)}) collective-permute-start(bf16[64,2048]{1,0:T(8,128)(2,1)S(1)} %bitcast.76), channel_id=1, source_target_pairs={{0,4},{4,0},{8,12},{12,8},{16,20},{20,16},{24,28},{28,24},{1,5},{5... | collective-permute-start | bytes 786440 | tf_op jit(solution)/shard_map/ppermute | solution.py:41
  18.2 5.0 %collective-permute-start.3 = (bf16[32,2048]{1,0:T(8,128)(2,1)S(1)}, bf16[32,2048]{1,0:T(8,128)(2,1)S(1)}, u32[]{:S(2)}, u32[]{:S(2)}) collective-permute-start(bf16[32,2048]{1,0:T(8,128)(2,1)S(1)} %collective-permute-done.2), channel_id=1, source_target_pairs={{0,2},{1,3},{2,0},{3,1},{4,6},{5,7},{6,4},{7,5},{8,10},{9,11},{10,... | collective-permute-start | bytes 393224 | tf_op jit(solution)/shard_map/ppermute | solution.py:41
  19.7 5.1 %collective-permute-start.5 = (bf16[32,2048]{1,0:T(8,128)(2,1)S(1)}, bf16[32,2048]{1,0:T(8,128)(2,1)S(1)}, u32[]{:S(2)}, u32[]{:S(2)}) collective-permute-start(bf16[32,2048]{1,0:T(8,128)(2,1)S(1)} %collective-permute-done.4), channel_id=1, source_target_pairs={{0,2},{1,3},{2,0},{3,1},{4,6},{5,7},{6,4},{7,5},{8,10},{9,11},{10,... | collective-permute-start | bytes 393224 | tf_op jit(solution)/shard_map/ppermute | solution.py:41
  20.2 9.3 %collective-permute-start.7 = (bf16[64,2048]{1,0:T(8,128)(2,1)S(1)}, bf16[64,2048]{1,0:T(8,128)(2,1)S(1)}, u32[]{:S(2)}, u32[]{:S(2)}) collective-permute-start(bf16[64,2048]{1,0:T(8,128)(2,1)S(1)} %pad_maximum_fusion.6.refs_3_), channel_id=1, source_target_pairs={{0,4},{4,0},{8,12},{12,8},{16,20},{20,16},{24,28},{28,24},{1,5},{5... | collective-permute-start | bytes 786440 | tf_op jit(solution)/shard_map/ppermute | solution.py:41
  23.2 11.9 %collective-permute-start.8 = (bf16[64,2048]{1,0:T(8,128)(2,1)S(1)}, bf16[64,2048]{1,0:T(8,128)(2,1)S(1)}, u32[]{:S(2)}, u32[]{:S(2)}) collective-permute-start(bf16[64,2048]{1,0:T(8,128)(2,1)S(1)} %pad_maximum_fusion.7.refs_5_), channel_id=1, source_target_pairs={{0,4},{4,0},{8,12},{12,8},{16,20},{20,16},{24,28},{28,24},{1,5},{5... | collective-permute-start | bytes 786440 | tf_op jit(solution)/shard_map/ppermute | solution.py:41
  24.8 11.5 %collective-permute-start.9 = (bf16[64,2048]{1,0:T(8,128)(2,1)S(1)}, bf16[64,2048]{1,0:T(8,128)(2,1)S(1)}, u32[]{:S(2)}, u32[]{:S(2)}) collective-permute-start(bf16[64,2048]{1,0:T(8,128)(2,1)S(1)} %pad_maximum_fusion.8.refs_7_), channel_id=1, source_target_pairs={{0,4},{4,0},{8,12},{12,8},{16,20},{20,16},{24,28},{28,24},{1,5},{5... | collective-permute-start | bytes 786440 | tf_op jit(solution)/shard_map/ppermute | solution.py:41
  29.5 9.3 %collective-permute-start.10 = (bf16[32,2048]{1,0:T(8,128)(2,1)S(1)}, bf16[32,2048]{1,0:T(8,128)(2,1)S(1)}, u32[]{:S(2)}, u32[]{:S(2)}) collective-permute-start(bf16[32,2048]{1,0:T(8,128)(2,1)S(1)} %constant_dynamic-slice_fusion.2), channel_id=1, source_target_pairs={{0,8},{4,12},{8,0},{12,4},{16,24},{20,28},{24,16},{28,20},{1,9},{5... | collective-permute-start | bytes 393224 | tf_op jit(solution)/shard_map/ppermute | solution.py:41
  31.0 8.7 %collective-permute-start.11 = (bf16[32,2048]{1,0:T(8,128)(2,1)S(1)}, bf16[32,2048]{1,0:T(8,128)(2,1)S(1)}, u32[]{:S(2)}, u32[]{:S(2)}) collective-permute-start(bf16[32,2048]{1,0:T(8,128)(2,1)S(1)} %constant_dynamic-slice_fusion.2), channel_id=1, source_target_pairs={{0,16},{4,20},{8,24},{12,28},{16,0},{20,4},{24,8},{28,12},{1,17},{... | collective-permute-start | bytes 393224 | tf_op jit(solution)/shard_map/ppermute | solution.py:41
  32.5 7.2 %collective-permute-start.12 = (bf16[32,2048]{1,0:T(8,128)(2,1)S(1)}, bf16[32,2048]{1,0:T(8,128)(2,1)S(1)}, u32[]{:S(2)}, u32[]{:S(2)}) collective-permute-start(bf16[32,2048]{1,0:T(8,128)(2,1)S(1)} %constant_dynamic-slice_fusion.2), channel_id=1, source_target_pairs={{0,24},{4,28},{8,16},{12,20},{16,8},{20,12},{24,0},{28,4},{1,25},{... | collective-permute-start | bytes 393224 | tf_op jit(solution)/shard_map/ppermute | solution.py:41
  39.7 5.1 %collective-permute-start.13 = (bf16[512,2048]{1,0:T(8,128)(2,1)S(1)}, bf16[512,2048]{1,0:T(8,128)(2,1)S(1)}, u32[]{:S(2)}, u32[]{:S(2)}) collective-permute-start(bf16[512,2048]{1,0:T(8,128)(2,1)S(1)} %bitcast.71), channel_id=1, source_target_pairs={{0,1},{1,0},{2,3},{3,2},{4,5},{5,4},{6,7},{7,6},{8,9},{9,8},{10,11... | collective-permute-start | bytes 6291464 | tf_op jit(solution)/shard_map/ppermute | solution.py:41
  39.8 11.6 %collective-permute-start.15 = (bf16[96,2048]{1,0:T(8,128)(2,1)S(1)}, bf16[96,2048]{1,0:T(8,128)(2,1)S(1)}, u32[]{:S(2)}, u32[]{:S(2)}) collective-permute-start(bf16[96,2048]{1,0:T(8,128)(2,1)S(1)} %pad_maximum_fusion.5), channel_id=1, source_target_pairs={{0,2},{1,3},{2,0},{3,1},{4,6},{5,7},{6,4},{7,5},{8,10},{9,11},{10,... | collective-permute-start | bytes 1179656 | tf_op jit(solution)/shard_map/ppermute | solution.py:41
  40.9 8.4 %collective-permute-start.14 = (bf16[64,2048]{1,0:T(8,128)(2,1)S(1)}, bf16[64,2048]{1,0:T(8,128)(2,1)S(1)}, u32[]{:S(2)}, u32[]{:S(2)}) collective-permute-start(bf16[64,2048]{1,0:T(8,128)(2,1)S(1)} %bitcast.84), channel_id=1, source_target_pairs={{0,4},{4,0},{8,12},{12,8},{16,20},{20,16},{24,28},{28,24},{1,5},{5... | collective-permute-start | bytes 786440 | tf_op jit(solution)/shard_map/ppermute | solution.py:41
  52.0 20.0 %collective-permute-start.19 = (bf16[192,2048]{1,0:T(8,128)(2,1)S(1)}, bf16[192,2048]{1,0:T(8,128)(2,1)S(1)}, u32[]{:S(2)}, u32[]{:S(2)}) collective-permute-start(bf16[192,2048]{1,0:T(8,128)(2,1)S(1)} %pad_maximum_fusion.refs_2_), channel_id=1, source_target_pairs={{0,4},{4,0},{8,12},{12,8},{16,20},{20,16},{24,28},{28,24},{1,5},{5... | collective-permute-start | bytes 2359304 | tf_op jit(solution)/shard_map/ppermute | solution.py:41
  53.6 8.4 %collective-permute-start.17 = (bf16[64,2048]{1,0:T(8,128)(2,1)S(1)}, bf16[64,2048]{1,0:T(8,128)(2,1)S(1)}, u32[]{:S(2)}, u32[]{:S(2)}) collective-permute-start(bf16[64,2048]{1,0:T(8,128)(2,1)S(1)} %add_convert_fusion.3.low), channel_id=1, source_target_pairs={{0,2},{1,3},{2,0},{3,1},{4,6},{5,7},{6,4},{7,5},{8,10},{9,11},{10,... | collective-permute-start | bytes 786440 | tf_op jit(solution)/shard_map/ppermute | solution.py:41
  73.5 16.1 %collective-permute-start.21 = (bf16[64,2048]{1,0:T(8,128)(2,1)S(1)}, bf16[64,2048]{1,0:T(8,128)(2,1)S(1)}, u32[]{:S(2)}, u32[]{:S(2)}) collective-permute-start(bf16[64,2048]{1,0:T(8,128)(2,1)S(1)} %add_convert_fusion.2.low), channel_id=1, source_target_pairs={{0,2},{1,3},{2,0},{3,1},{4,6},{5,7},{6,4},{7,5},{8,10},{9,11},{10,... | collective-permute-start | bytes 786440 | tf_op jit(solution)/shard_map/ppermute | solution.py:41
  74.7 14.0 %collective-permute-start.22 = (bf16[32,2048]{1,0:T(8,128)(2,1)S(1)}, bf16[32,2048]{1,0:T(8,128)(2,1)S(1)}, u32[]{:S(2)}, u32[]{:S(2)}) collective-permute-start(bf16[32,2048]{1,0:T(8,128)(2,1)S(1)} %constant_dynamic-slice_fusion), channel_id=1, source_target_pairs={{0,8},{4,12},{8,0},{12,4},{16,24},{20,28},{24,16},{28,20},{1,9},{5... | collective-permute-start | bytes 393224 | tf_op jit(solution)/shard_map/ppermute | solution.py:41
  76.7 12.9 %collective-permute-start.23 = (bf16[32,2048]{1,0:T(8,128)(2,1)S(1)}, bf16[32,2048]{1,0:T(8,128)(2,1)S(1)}, u32[]{:S(2)}, u32[]{:S(2)}) collective-permute-start(bf16[32,2048]{1,0:T(8,128)(2,1)S(1)} %constant_dynamic-slice_fusion), channel_id=1, source_target_pairs={{0,16},{4,20},{8,24},{12,28},{16,0},{20,4},{24,8},{28,12},{1,17},{... | collective-permute-start | bytes 393224 | tf_op jit(solution)/shard_map/ppermute | solution.py:41
  77.9 11.6 %collective-permute-start.24 = (bf16[32,2048]{1,0:T(8,128)(2,1)S(1)}, bf16[32,2048]{1,0:T(8,128)(2,1)S(1)}, u32[]{:S(2)}, u32[]{:S(2)}) collective-permute-start(bf16[32,2048]{1,0:T(8,128)(2,1)S(1)} %constant_dynamic-slice_fusion), channel_id=1, source_target_pairs={{0,24},{4,28},{8,16},{12,20},{16,8},{20,12},{24,0},{28,4},{1,25},{... | collective-permute-start | bytes 393224 | tf_op jit(solution)/shard_map/ppermute | solution.py:41
  90.5 11.6 %collective-permute-start.35 = (bf16[96,2048]{1,0:T(8,128)(2,1)S(1)}, bf16[96,2048]{1,0:T(8,128)(2,1)S(1)}, u32[]{:S(2)}, u32[]{:S(2)}) collective-permute-start(bf16[96,2048]{1,0:T(8,128)(2,1)S(1)} %get-tuple-element.318), channel_id=1, source_target_pairs={{0,2},{1,3},{2,0},{3,1},{4,6},{5,7},{6,4},{7,5},{8,10},{9,11},{10,... | collective-permute-start | bytes 1179656 | tf_op jit(solution)/shard_map/ppermute | solution.py:41
  91.4 11.2 %collective-permute-start.36 = (bf16[96,2048]{1,0:T(8,128)(2,1)S(1)}, bf16[96,2048]{1,0:T(8,128)(2,1)S(1)}, u32[]{:S(2)}, u32[]{:S(2)}) collective-permute-start(bf16[96,2048]{1,0:T(8,128)(2,1)S(1)} %get-tuple-element.318), channel_id=1, source_target_pairs={{0,4},{4,0},{8,12},{12,8},{16,20},{20,16},{24,28},{28,24},{1,5},{5... | collective-permute-start | bytes 1179656 | tf_op jit(solution)/shard_map/ppermute | solution.py:41
  93.9 8.8 %collective-permute-start.27 = (bf16[128,512]{1,0:T(8,128)(2,1)S(1)}, bf16[128,512]{1,0:T(8,128)(2,1)S(1)}, u32[]{:S(2)}, u32[]{:S(2)}) collective-permute-start(bf16[128,512]{1,0:T(8,128)(2,1)S(1)} %product_back.1.refs_0_), channel_id=1, source_target_pairs={{0,8},{4,12},{8,0},{12,4},{16,24},{20,28},{24,16},{28,20},{1,9},{5... | collective-permute-start | bytes 393224 | tf_op jit(solution)/shard_map/ppermute | solution.py:41
  96.2 12.8 %collective-permute-start.29 = (bf16[128,512]{1,0:T(8,128)(2,1)S(1)}, bf16[128,512]{1,0:T(8,128)(2,1)S(1)}, u32[]{:S(2)}, u32[]{:S(2)}) collective-permute-start(bf16[128,512]{1,0:T(8,128)(2,1)S(1)} %product_back.1.refs_0_), channel_id=1, source_target_pairs={{0,16},{4,20},{8,24},{12,28},{16,0},{20,4},{24,8},{28,12},{1,17},{... | collective-permute-start | bytes 393224 | tf_op jit(solution)/shard_map/ppermute | solution.py:41
  97.7 11.3 %collective-permute-start.31 = (bf16[128,512]{1,0:T(8,128)(2,1)S(1)}, bf16[128,512]{1,0:T(8,128)(2,1)S(1)}, u32[]{:S(2)}, u32[]{:S(2)}) collective-permute-start(bf16[128,512]{1,0:T(8,128)(2,1)S(1)} %product_back.1.refs_0_), channel_id=1, source_target_pairs={{0,24},{4,28},{8,16},{12,20},{16,8},{20,12},{24,0},{28,4},{1,25},{... | collective-permute-start | bytes 393224 | tf_op jit(solution)/shard_map/ppermute | solution.py:41
  102.1 9.8 %collective-permute-start.38 = (bf16[192,2048]{1,0:T(8,128)(2,1)S(1)}, bf16[192,2048]{1,0:T(8,128)(2,1)S(1)}, u32[]{:S(2)}, u32[]{:S(2)}) collective-permute-start(bf16[192,2048]{1,0:T(8,128)(2,1)S(1)} %pad_maximum_fusion.refs_2_), channel_id=1, source_target_pairs={{0,1},{1,0},{2,3},{3,2},{4,5},{5,4},{6,7},{7,6},{8,9},{9,8},{10,11... | collective-permute-start | bytes 2359304 | tf_op jit(solution)/shard_map/ppermute | solution.py:41
  102.7 7.0 %collective-permute-start.33 = (bf16[64,2048]{1,0:T(8,128)(2,1)S(1)}, bf16[64,2048]{1,0:T(8,128)(2,1)S(1)}, u32[]{:S(2)}, u32[]{:S(2)}) collective-permute-start(bf16[64,2048]{1,0:T(8,128)(2,1)S(1)} %get-tuple-element.211), channel_id=1, source_target_pairs={{0,1},{1,0},{2,3},{3,2},{4,5},{5,4},{6,7},{7,6},{8,9},{9,8},{10,11... | collective-permute-start | bytes 786440 | tf_op jit(solution)/shard_map/ppermute | solution.py:41
  109.1 6.5 %collective-permute-start.37 = (bf16[192,2048]{1,0:T(8,128)(2,1)S(1)}, bf16[192,2048]{1,0:T(8,128)(2,1)S(1)}, u32[]{:S(2)}, u32[]{:S(2)}) collective-permute-start(bf16[192,2048]{1,0:T(8,128)(2,1)S(1)} %constant_dynamic-update-slice_fusion.5.refs_0_), channel_id=1, source_target_pairs={{0,1},{1,0},{2,3},{3,2},{4,5},{5,4},{6,7},{7,6},{8,9},{9,8},{10,11... | collective-permute-start | bytes 2359304 | tf_op jit(solution)/shard_map/ppermute | solution.py:41
  109.1 6.4 %collective-permute-start.28 = (bf16[128,512]{1,0:T(8,128)(2,1)S(1)}, bf16[128,512]{1,0:T(8,128)(2,1)S(1)}, u32[]{:S(2)}, u32[]{:S(2)}) collective-permute-start(bf16[128,512]{1,0:T(8,128)(2,1)S(1)} %collective-permute-done.27.refs_2_), channel_id=1, source_target_pairs={{0,4},{4,0},{8,12},{12,8},{16,20},{20,16},{24,28},{28,24},{1,5},{5... | collective-permute-start | bytes 393224 | tf_op jit(solution)/shard_map/ppermute | solution.py:41
  109.8 20.0 %collective-permute-start.34 = (bf16[64,2048]{1,0:T(8,128)(2,1)S(1)}, bf16[64,2048]{1,0:T(8,128)(2,1)S(1)}, u32[]{:S(2)}, u32[]{:S(2)}) collective-permute-start(bf16[64,2048]{1,0:T(8,128)(2,1)S(1)} %add_convert_fusion.1.low), channel_id=1, source_target_pairs={{0,2},{1,3},{2,0},{3,1},{4,6},{5,7},{6,4},{7,5},{8,10},{9,11},{10,... | collective-permute-start | bytes 786440 | tf_op jit(solution)/shard_map/ppermute | solution.py:41
  110.8 32.0 %collective-permute-start.40 = (bf16[96,2048]{1,0:T(8,128)(2,1)S(1)}, bf16[96,2048]{1,0:T(8,128)(2,1)S(1)}, u32[]{:S(2)}, u32[]{:S(2)}) collective-permute-start(bf16[96,2048]{1,0:T(8,128)(2,1)S(1)} %collective-permute-done.36), channel_id=1, source_target_pairs={{0,2},{1,3},{2,0},{3,1},{4,6},{5,7},{6,4},{7,5},{8,10},{9,11},{10,... | collective-permute-start | bytes 1179656 | tf_op jit(solution)/shard_map/ppermute | solution.py:41
  111.9 17.9 %collective-permute-start.26 = (bf16[128,512]{1,0:T(8,128)(2,1)S(1)}, bf16[128,512]{1,0:T(8,128)(2,1)S(1)}, u32[]{:S(2)}, u32[]{:S(2)}) collective-permute-start(bf16[128,512]{1,0:T(8,128)(2,1)S(1)} %product_back.1.refs_0_), channel_id=1, source_target_pairs={{0,4},{4,0},{8,12},{12,8},{16,20},{20,16},{24,28},{28,24},{1,5},{5... | collective-permute-start | bytes 393224 | tf_op jit(solution)/shard_map/ppermute | solution.py:41
  115.5 14.3 %collective-permute-start.30 = (bf16[128,512]{1,0:T(8,128)(2,1)S(1)}, bf16[128,512]{1,0:T(8,128)(2,1)S(1)}, u32[]{:S(2)}, u32[]{:S(2)}) collective-permute-start(bf16[128,512]{1,0:T(8,128)(2,1)S(1)} %collective-permute-done.29.refs_4_), channel_id=1, source_target_pairs={{0,4},{4,0},{8,12},{12,8},{16,20},{20,16},{24,28},{28,24},{1,5},{5... | collective-permute-start | bytes 393224 | tf_op jit(solution)/shard_map/ppermute | solution.py:41
  115.5 14.2 %collective-permute-start.32 = (bf16[128,512]{1,0:T(8,128)(2,1)S(1)}, bf16[128,512]{1,0:T(8,128)(2,1)S(1)}, u32[]{:S(2)}, u32[]{:S(2)}) collective-permute-start(bf16[128,512]{1,0:T(8,128)(2,1)S(1)} %collective-permute-done.31.refs_6_), channel_id=1, source_target_pairs={{0,4},{4,0},{8,12},{12,8},{16,20},{20,16},{24,28},{28,24},{1,5},{5... | collective-permute-start | bytes 393224 | tf_op jit(solution)/shard_map/ppermute | solution.py:41
  129.8 13.1 %collective-permute-start.39 = (bf16[64,2048]{1,0:T(8,128)(2,1)S(1)}, bf16[64,2048]{1,0:T(8,128)(2,1)S(1)}, u32[]{:S(2)}, u32[]{:S(2)}) collective-permute-start(bf16[64,2048]{1,0:T(8,128)(2,1)S(1)} %get-tuple-element.234), channel_id=1, source_target_pairs={{0,4},{4,0},{8,12},{12,8},{16,20},{20,16},{24,28},{28,24},{1,5},{5... | collective-permute-start | bytes 786440 | tf_op jit(solution)/shard_map/ppermute | solution.py:41
  130.0 12.9 %collective-permute-start.43 = (bf16[2,72,256]{2,1,0:T(8,128)(2,1)S(1)}, bf16[2,72,256]{2,1,0:T(8,128)(2,1)S(1)}, u32[]{:S(2)}, u32[]{:S(2)}) collective-permute-start(bf16[2,72,256]{2,1,0:T(8,128)(2,1)S(1)} %get-tuple-element.239), channel_id=1, source_target_pairs={{0,24},{4,28},{8,16},{12,20},{16,8},{20,12},{24,0},{28,4},{1,25},{... | collective-permute-start | bytes 221192 | tf_op jit(solution)/shard_map/ppermute | solution.py:41
  132.4 10.5 %collective-permute-start.42 = (bf16[2,72,256]{2,1,0:T(8,128)(2,1)S(1)}, bf16[2,72,256]{2,1,0:T(8,128)(2,1)S(1)}, u32[]{:S(2)}, u32[]{:S(2)}) collective-permute-start(bf16[2,72,256]{2,1,0:T(8,128)(2,1)S(1)} %get-tuple-element.238), channel_id=1, source_target_pairs={{0,16},{4,20},{8,24},{12,28},{16,0},{20,4},{24,8},{28,12},{1,17},{... | collective-permute-start | bytes 221192 | tf_op jit(solution)/shard_map/ppermute | solution.py:41
  133.7 9.2 %collective-permute-start.41 = (bf16[2,72,256]{2,1,0:T(8,128)(2,1)S(1)}, bf16[2,72,256]{2,1,0:T(8,128)(2,1)S(1)}, u32[]{:S(2)}, u32[]{:S(2)}) collective-permute-start(bf16[2,72,256]{2,1,0:T(8,128)(2,1)S(1)} %get-tuple-element.237), channel_id=1, source_target_pairs={{0,8},{4,12},{8,0},{12,4},{16,24},{20,28},{24,16},{28,20},{1,9},{5... | collective-permute-start | bytes 221192 | tf_op jit(solution)/shard_map/ppermute | solution.py:41
  146.7 9.0 %collective-permute-start.45 = (bf16[64,2048]{1,0:T(8,128)(2,1)S(1)}, bf16[64,2048]{1,0:T(8,128)(2,1)S(1)}, u32[]{:S(2)}, u32[]{:S(2)}) collective-permute-start(bf16[64,2048]{1,0:T(8,128)(2,1)S(1)} %add_convert_fusion.low), channel_id=1, source_target_pairs={{0,2},{1,3},{2,0},{3,1},{4,6},{5,7},{6,4},{7,5},{8,10},{9,11},{10,... | collective-permute-start | bytes 786440 | tf_op jit(solution)/shard_map/ppermute | solution.py:41
  148.1 6.9 %collective-permute-start.47 = (bf16[72,256]{1,0:T(8,128)(2,1)S(1)}, bf16[72,256]{1,0:T(8,128)(2,1)S(1)}, u32[]{:S(2)}, u32[]{:S(2)}) collective-permute-start(bf16[72,256]{1,0:T(8,128)(2,1)S(1)} %get-tuple-element.328), channel_id=1, source_target_pairs={{0,4},{4,0},{8,12},{12,8},{16,20},{20,16},{24,28},{28,24},{1,5},{5... | collective-permute-start | bytes 110600 | tf_op jit(solution)/shard_map/ppermute | solution.py:41
  149.7 5.2 %collective-permute-start.48 = (bf16[72,256]{1,0:T(8,128)(2,1)S(1)}, bf16[72,256]{1,0:T(8,128)(2,1)S(1)}, u32[]{:S(2)}, u32[]{:S(2)}) collective-permute-start(bf16[72,256]{1,0:T(8,128)(2,1)S(1)} %get-tuple-element.326), channel_id=1, source_target_pairs={{0,4},{4,0},{8,12},{12,8},{16,20},{20,16},{24,28},{28,24},{1,5},{5... | collective-permute-start | bytes 110600 | tf_op jit(solution)/shard_map/ppermute | solution.py:41
  150.1 4.8 %collective-permute-start.49 = (bf16[72,256]{1,0:T(8,128)(2,1)S(1)}, bf16[72,256]{1,0:T(8,128)(2,1)S(1)}, u32[]{:S(2)}, u32[]{:S(2)}) collective-permute-start(bf16[72,256]{1,0:T(8,128)(2,1)S(1)} %get-tuple-element.324), channel_id=1, source_target_pairs={{0,4},{4,0},{8,12},{12,8},{16,20},{20,16},{24,28},{28,24},{1,5},{5... | collective-permute-start | bytes 110600 | tf_op jit(solution)/shard_map/ppermute | solution.py:41
  151.8 4.0 %collective-permute-start.46 = (bf16[72,256]{1,0:T(8,128)(2,1)S(1)}, bf16[72,256]{1,0:T(8,128)(2,1)S(1)}, u32[]{:S(2)}, u32[]{:S(2)}) collective-permute-start(bf16[72,256]{1,0:T(8,128)(2,1)S(1)} %get-tuple-element.330), channel_id=1, source_target_pairs={{0,4},{4,0},{8,12},{12,8},{16,20},{20,16},{24,28},{28,24},{1,5},{5... | collective-permute-start | bytes 110600 | tf_op jit(solution)/shard_map/ppermute | solution.py:41
  155.7 4.2 %collective-permute-start.53 = (bf16[192,2048]{1,0:T(8,128)(2,1)S(1)}, bf16[192,2048]{1,0:T(8,128)(2,1)S(1)}, u32[]{:S(2)}, u32[]{:S(2)}) collective-permute-start(bf16[192,2048]{1,0:T(8,128)(2,1)S(1)} %pad_maximum_fusion.1.refs_2_), channel_id=1, source_target_pairs={{0,1},{1,0},{2,3},{3,2},{4,5},{5,4},{6,7},{7,6},{8,9},{9,8},{10,11... | collective-permute-start | bytes 2359304 | tf_op jit(solution)/shard_map/ppermute | solution.py:41
  155.7 4.2 %collective-permute-start.56 = (bf16[192,2048]{1,0:T(8,128)(2,1)S(1)}, bf16[192,2048]{1,0:T(8,128)(2,1)S(1)}, u32[]{:S(2)}, u32[]{:S(2)}) collective-permute-start(bf16[192,2048]{1,0:T(8,128)(2,1)S(1)} %collective-permute-done.19.refs_6_), channel_id=1, source_target_pairs={{0,1},{1,0},{2,3},{3,2},{4,5},{5,4},{6,7},{7,6},{8,9},{9,8},{10,11... | collective-permute-start | bytes 2359304 | tf_op jit(solution)/shard_map/ppermute | solution.py:41
  175.0 4.3 %collective-permute-start.57 = (bf16[8,72,256]{2,1,0:T(8,128)(2,1)S(1)}, bf16[8,72,256]{2,1,0:T(8,128)(2,1)S(1)}, u32[]{:S(2)}, u32[]{:S(2)}) collective-permute-start(bf16[8,72,256]{2,1,0:T(8,128)(2,1)S(1)} %constant_dynamic-update-slice_fusion.9.came_a), channel_id=1, source_target_pairs={{0,1},{1,0},{2,3},{3,2},{4,5},{5,4},{6,7},{7,6},{8,9},{9,8},{10,11... | collective-permute-start | bytes 884744 | tf_op jit(solution)/shard_map/ppermute | solution.py:41
  (30 other events, 213.2 us)

commit v10 on v9

--- a/solution.py
+++ b/solution.py
@@ -513,10 +513,9 @@
 
 def gelu_parts(value):
     rate = math.sqrt(2 / math.pi)
-    square = value * value
-    bent = jnp.tanh(value * (rate + (rate * 0.044715) * square))
-    upper = 0.5 * (1 + bent)
-    slope = upper + (0.5 * value) * (1 - bent * bent) * (rate + (rate * 3 * 0.044715) * square)
+    bend = value * (rate + (rate * 0.044715) * (value * value))
+    upper = 0.5 + 0.5 * jnp.tanh(bend)
+    slope = upper + (upper * (1 - upper)) * (6 * bend - (4 * rate) * value)
     return value * upper, slope
 
 

time: 181 us -> 180 us (level)
  no operation moved by 1% of the time
where the time goes in v10:
time: 180 us
  Pallas kernels  80.8 us (45%)
  starting transfers between devices  58.3 us (32%)
  waiting for transfers between devices  36.2 us (20%)
  local copies, waits for them, and re-layouts  2.22 us (1%)
    ppermute x59, starting transfers between devices, swap(): return lax.ppermute(value, axis, [(i, i ^ bit) for i in range(size)])  58.3 us
    ppermute x59, waiting for transfers between devices, swap(): return lax.ppermute(value, axis, [(i, i ^ bit) for i in range(size)])  36.2 us
    pallas_call x2, Pallas kernels, feed_all(): pl.pallas_call(partial(all_kernel, count=count), grid_spec=pltpu.Prefetch...  26.8 us
    pallas_call x1, Pallas kernels, attend_all(): pl.pallas_call(partial(all_forward_kernel, groups=groups, scale=1.0 / mat...  9.35 us
    pallas_call x1, Pallas kernels, attend_back(): pl.pallas_call(partial(backward_kernel, count=count, groups=groups, scale...  8.36 us
    pallas_call x5, Pallas kernels, project_rows(): pl.pallas_call(partial(rows_kernel, count=len(weights)), out_shape=[jax.S...  7.65 us
    pallas_call x1, Pallas kernels, feed_own(): pl.pallas_call(own_kernel, in_specs=[WHOLE] * 3, out_specs=[WHOLE] * 4, o...  5.36 us
  transfers between devices with their start and end apart: 59, of which 23 were waited for; matrix products, arithmetic and copies ran while one was open for 1% of the time, Pallas kernels for 34%

profile of v10, /device:TPU:0, one launch (start us, length us, event | category | flops | bytes accessed | tf_op | source)
XLA Modules:
  0.0 180.2 jit_solution(13657893697661429260)
XLA Ops:
  2.2 3.1 %collective-permute-start = (bf16[32,2048]{1,0:T(8,128)(2,1)S(1)}, bf16[32,2048]{1,0:T(8,128)(2,1)S(1)}, u32[]{:S(2)}, u32[]{:S(2)}) collective-permute-start(bf16[32,2048]{1,0:T(8,128)(2,1)S(1)} %constant_dynamic-slice_fusion.4), channel_id=1, source_target_pairs={{0,8},{4,12},{8,0},{12,4},{16,24},{20,28},{24,16},{28,20},{1,9},{5... | collective-permute-start | bytes 393224 | tf_op jit(solution)/shard_map/ppermute | solution.py:41
  5.2 2.6 %collective-permute-start.2 = (bf16[32,2048]{1,0:T(8,128)(2,1)S(1)}, bf16[32,2048]{1,0:T(8,128)(2,1)S(1)}, u32[]{:S(2)}, u32[]{:S(2)}) collective-permute-start(bf16[32,2048]{1,0:T(8,128)(2,1)S(1)} %constant_dynamic-slice_fusion.4), channel_id=1, source_target_pairs={{0,16},{4,20},{8,24},{12,28},{16,0},{20,4},{24,8},{28,12},{1,17},{... | collective-permute-start | bytes 393224 | tf_op jit(solution)/shard_map/ppermute | solution.py:41
  7.8 2.4 %collective-permute-done = bf16[32,2048]{1,0:T(8,128)(2,1)S(1)} collective-permute-done((bf16[32,2048]{1,0:T(8,128)(2,1)S(1)}, bf16[32,2048]{1,0:T(8,128)(2,1)S(1)}, u32[]{:S(2)}, u32[]{:S(2)}) %collective-permute-start) | collective-permute-done | bytes 131104 | tf_op jit(solution)/shard_map/ppermute | solution.py:41
  10.3 1.7 collective-permute-start.1
  12.0 1.5 collective-permute-start.6
  14.1 2.4 %tables.1 = (s32[512,1]{1,0:T(8,128)}, s32[512,1]{1,0:T(8,128)}, s32[512,1]{1,0:T(8,128)}, s32[512,1]{1,0:T(8,128)}, s32[1,1024]{1,0:T(1,128)}, /*index=5*/s32[1,128]{1,0:T(1,128)}, s32[128,1]{1,0:T(8,128)}) custom-call(s32[2]{0:T(128)} %pad_add_fusion.index, s32[1,8]{1,0:T(1,128)} %frames.1, s32[1,8]{1,0:T(1,128)} %texts.1, s32[1,8]{1,0:T(1,128)} %actions.1), custom_call_target="tpu_custom_call" | custom-call | flops 10485 | bytes 10485 | tf_op jit(solution)/shard_map/tables/pallas_call | solution.py:206
  18.2 1.5 collective-permute-start.3
  20.2 1.6 collective-permute-start.7
  23.2 1.6 collective-permute-start.8
  24.8 1.5 collective-permute-start.9
  26.2 3.3 %collective-permute-done.7.refs_4_ = bf16[64,2048]{1,0:T(8,128)(2,1)S(1)} collective-permute-done((bf16[64,2048]{1,0:T(8,128)(2,1)S(1)}, bf16[64,2048]{1,0:T(8,128)(2,1)S(1)}, u32[]{:S(2)}, u32[]{:S(2)}) %collective-permute-start.7) | collective-permute-done | bytes 262176 | tf_op jit(solution)/shard_map/ppermute | solution.py:41
  29.5 1.5 collective-permute-start.10
  31.0 1.4 collective-permute-start.11
  32.5 1.5 collective-permute-start.12
  36.3 2.5 %norm_pieces.1 = bf16[8,8,8,2048]{3,2,1,0:T(8,128)(2,1)S(1)} custom-call(s32[1]{0:T(128)} %bitcast.11.refs_0_, bf16[64,2048]{1,0:T(8,128)(2,1)S(1)} %bitcast.78, bf16[64,2048]{1,0:T(8,128)(2,1)S(1)} %collective-permute-done.6.refs_2_, bf16[64,2048]{1,0:T(8,128)(2,1)S(1)} %pad_maximum_fusion.6.refs_3_, bf16[64,2048]{1,0:T(8,128)(2,1)S(1)} %collective-permute-done.7.refs_4_, ...), custom_call_target="tpu_custom_call" | custom-call | flops 104857 | bytes 41943 | tf_op jit(solution)/shard_map/norm_pieces/pallas_call | solution.py:360
  40.9 1.5 collective-permute-start.14
  42.5 2.3 %project_rows.6 = (bf16[512,512]{1,0:T(8,128)(2,1)S(1)}, bf16[512,512]{1,0:T(8,128)(2,1)S(1)}) custom-call(bf16[512,2048]{1,0:T(8,128)(2,1)S(1)} %bitcast.72, bf16[2048,512]{1,0:T(8,128)(2,1)S(1)} %copy-done.1, bf16[2048,512]{1,0:T(8,128)(2,1)S(1)} %copy-done.2), custom_call_target="tpu_custom_call" | custom-call | flops 21474836 | bytes 20971 | tf_op jit(solution)/shard_map/project_rows/pallas_call | solution.py:234
  44.9 2.4 %project_rows.7 = (bf16[512,512]{1,0:T(8,128)(2,1)S(1)}, bf16[512,512]{1,0:T(8,128)(2,1)S(1)}) custom-call(bf16[512,2048]{1,0:T(8,128)(2,1)S(1)} %collective-permute-done.13.refs_0_.refs_1_, bf16[2048,512]{1,0:T(8,128)(2,1)S(1)} %copy-done.1, bf16[2048,512]{1,0:T(8,128)(2,1)S(1)} %copy-done.2), custom_call_target="tpu_custom_call" | custom-call | flops 21474836 | bytes 20971 | tf_op jit(solution)/shard_map/project_rows/pallas_call | solution.py:234
  47.3 1.9 %attend.1.refs_0_ = bf16[128,512]{1,0:T(8,128)(2,1)S(1)} custom-call(bf16[128,512]{1,0:T(8,128)(2,1)S(1)} %project_rows.5.query, bf16[512,512]{1,0:T(8,128)(2,1)S(1)} %get-tuple-element.173.key_a.refs_2_.refs_10_, bf16[512,512]{1,0:T(8,128)(2,1)S(1)} %get-tuple-element.174.key_b.refs_3_.refs_11_, ...), custom_call_target="tpu_custom_call" | custom-call | flops 2684354 | bytes 20971 | tf_op jit(solution)/shard_map/attend/pallas_call | solution.py:823
  49.4 2.0 %collective-permute-done.15 = bf16[96,2048]{1,0:T(8,128)(2,1)S(1)} collective-permute-done((bf16[96,2048]{1,0:T(8,128)(2,1)S(1)}, bf16[96,2048]{1,0:T(8,128)(2,1)S(1)}, u32[]{:S(2)}, u32[]{:S(2)}) %collective-permute-start.15) | collective-permute-done | bytes 393248 | tf_op jit(solution)/shard_map/ppermute | solution.py:41
  52.0 1.6 collective-permute-start.19
  55.1 3.5 %grad_activated.1 = f32[128,2048]{1,0:T(8,128)S(1)} custom-call(bf16[128,2048]{1,0:T(8,128)(2,1)S(1)} %pad_maximum_fusion.3.grad.refs_7_, bf16[2048,2048]{1,0:T(8,128)(2,1)S(1)} %bitcast.68), custom_call_target="tpu_custom_call" | custom-call | flops 10737418 | bytes 83886 | tf_op jit(solution)/shard_map/grad_activated/pallas_call | solution.py:575
  62.5 1.5 collective-permute-done.18
  64.1 5.4 %feed_own.1 = (bf16[128,2048]{1,0:T(8,128)(2,1)S(1)}, bf16[128,2048]{1,0:T(8,128)(2,1)S(1)}, f32[64,2048]{1,0:T(8,128)S(1)}, bf16[64,2048]{1,0:T(8,128)(2,1)S(1)}) custom-call(bf16[128,2048]{1,0:T(8,128)(2,1)S(1)} %constant_dynamic-update-slice_fusion.lifted.refs_6_, bf16[2048,2048]{1,0:T(8,128)(2,1)S(1)} %bitcast.70, f32[128,2048]{1,0:T(8,128)S(1)} %grad_activated.1), custom_call_target="tpu_custom_call" | custom-call | flops 21474836 | bytes 83886 | tf_op jit(solution)/shard_map/feed_own/pallas_call | solution.py:549
  69.5 2.5 %collective-permute-done.19.refs_6_ = bf16[192,2048]{1,0:T(8,128)(2,1)S(1)} collective-permute-done((bf16[192,2048]{1,0:T(8,128)(2,1)S(1)}, bf16[192,2048]{1,0:T(8,128)(2,1)S(1)}, u32[]{:S(2)}, u32[]{:S(2)}) %collective-permute-start.19) | collective-permute-done | bytes 786464 | tf_op jit(solution)/shard_map/ppermute | solution.py:41
  71.9 1.5 collective-permute-done.20
  74.7 1.9 %collective-permute-start.22 = (bf16[32,2048]{1,0:T(8,128)(2,1)S(1)}, bf16[32,2048]{1,0:T(8,128)(2,1)S(1)}, u32[]{:S(2)}, u32[]{:S(2)}) collective-permute-start(bf16[32,2048]{1,0:T(8,128)(2,1)S(1)} %constant_dynamic-slice_fusion), channel_id=1, source_target_pairs={{0,8},{4,12},{8,0},{12,4},{16,24},{20,28},{24,16},{28,20},{1,9},{5... | collective-permute-start | bytes 393224 | tf_op jit(solution)/shard_map/ppermute | solution.py:41
  77.9 1.4 collective-permute-start.24
  79.3 9.3 %attend_all.1 = (bf16[512,512]{1,0:T(8,128)(2,1)S(1)}, bf16[512,512]{1,0:T(8,128)(2,1)S(1)}, bf16[4,2560,256]{2,1,0:T(8,128)(2,1)}) custom-call(bf16[512,512]{1,0:T(8,128)(2,1)S(1)} %project_rows.8.refs_0_.refs_8_, bf16[512,512]{1,0:T(8,128)(2,1)S(1)} %project_rows.9.refs_1_.refs_9_, bf16[512,512]{1,0:T(8,128)(2,1)S(1)} %get-tuple-element.173.key_a.refs_2_.refs_10_, ...), custom_call_target="tpu_custom_call" | custom-call | flops 21474836 | bytes 41943 | tf_op jit(solution)/shard_map/attend_all/pallas_call | solution.py:915
  91.4 1.5 collective-permute-start.36
  93.9 2.4 %collective-permute-start.27 = (bf16[128,512]{1,0:T(8,128)(2,1)S(1)}, bf16[128,512]{1,0:T(8,128)(2,1)S(1)}, u32[]{:S(2)}, u32[]{:S(2)}) collective-permute-start(bf16[128,512]{1,0:T(8,128)(2,1)S(1)} %product_back.1.refs_0_), channel_id=1, source_target_pairs={{0,8},{4,12},{8,0},{12,4},{16,24},{20,28},{24,16},{28,20},{1,9},{5... | collective-permute-start | bytes 393224 | tf_op jit(solution)/shard_map/ppermute | solution.py:41
  96.2 1.5 collective-permute-start.29
  97.7 1.4 collective-permute-start.31
  99.1 2.0 %down_own.1 = (f32[64,2048]{1,0:T(8,128)S(1)}, bf16[64,2048]{1,0:T(8,128)(2,1)S(1)}) custom-call(bf16[128,2048]{1,0:T(8,128)(2,1)S(1)} %get-tuple-element.209.rows.refs_8_, bf16[2048,2048]{1,0:T(8,128)(2,1)S(1)} %bitcast.68), custom_call_target="tpu_custom_call" | custom-call | flops 10737418 | bytes 83886 | tf_op jit(solution)/shard_map/down_own/pallas_call | solution.py:295
  102.7 6.3 %collective-permute-done.29.refs_4_ = bf16[128,512]{1,0:T(8,128)(2,1)S(1)} collective-permute-done((bf16[128,512]{1,0:T(8,128)(2,1)S(1)}, bf16[128,512]{1,0:T(8,128)(2,1)S(1)}, u32[]{:S(2)}, u32[]{:S(2)}) %collective-permute-start.29) | collective-permute-done | bytes 131104 | tf_op jit(solution)/shard_map/ppermute | solution.py:41
  111.9 1.5 collective-permute-start.26
  113.4 2.1 %collective-permute-done.28.refs_3_ = bf16[128,512]{1,0:T(8,128)(2,1)S(1)} collective-permute-done((bf16[128,512]{1,0:T(8,128)(2,1)S(1)}, bf16[128,512]{1,0:T(8,128)(2,1)S(1)}, u32[]{:S(2)}, u32[]{:S(2)}) %collective-permute-start.28) | collective-permute-done | bytes 131104 | tf_op jit(solution)/shard_map/ppermute | solution.py:41
  115.5 2.0 %collective-permute-start.32 = (bf16[128,512]{1,0:T(8,128)(2,1)S(1)}, bf16[128,512]{1,0:T(8,128)(2,1)S(1)}, u32[]{:S(2)}, u32[]{:S(2)}) collective-permute-start(bf16[128,512]{1,0:T(8,128)(2,1)S(1)} %collective-permute-done.31.refs_6_), channel_id=1, source_target_pairs={{0,4},{4,0},{8,12},{12,8},{16,20},{20,16},{24,28},{28,24},{1,5},{5... | collective-permute-start | bytes 393224 | tf_op jit(solution)/shard_map/ppermute | solution.py:41
  117.5 12.0 %feed_all.2 = (bf16[256,2048]{1,0:T(8,128)(2,1)}, bf16[2048,256]{1,0:T(8,128)(2,1)}) custom-call(s32[1]{0:T(128)} %bitcast.5.index, bf16[192,2048]{1,0:T(8,128)(2,1)S(1)} %constant_dynamic-update-slice_fusion.5.refs_0_, bf16[192,2048]{1,0:T(8,128)(2,1)S(1)} %collective-permute-done.37.refs_1_, bf16[192,2048]{1,0:T(8,128)(2,1)S(1)} %pad_maximum_fusion.refs_2_, ...), custom_call_target="tpu_custom_call" | custom-call | flops 72477576 | bytes 199229 | tf_op jit(solution)/shard_map/feed_all/pallas_call | solution.py:665
  129.7 2.4 %collective-permute-start.43 = (bf16[2,72,256]{2,1,0:T(8,128)(2,1)S(1)}, bf16[2,72,256]{2,1,0:T(8,128)(2,1)S(1)}, u32[]{:S(2)}, u32[]{:S(2)}) collective-permute-start(bf16[2,72,256]{2,1,0:T(8,128)(2,1)S(1)} %get-tuple-element.239), channel_id=1, source_target_pairs={{0,24},{4,28},{8,16},{12,20},{16,8},{20,12},{24,0},{28,4},{1,25},{... | collective-permute-start | bytes 221192 | tf_op jit(solution)/shard_map/ppermute | solution.py:41
  134.1 8.4 %attend_back.1 = (bf16[512,512]{1,0:T(8,128)(2,1)S(1)}, bf16[512,512]{1,0:T(8,128)(2,1)S(1)}, bf16[512,512]{1,0:T(8,128)(2,1)S(1)}, bf16[512,512]{1,0:T(8,128)(2...) custom-call(bf16[128,512]{1,0:T(8,128)(2,1)S(1)} %product_back.1.ref, ...), custom_call_target="tpu_custom_call" | custom-call | flops 42949672 | bytes 136314 | tf_op jit(solution)/shard_map/attend_back/pallas_call | solution.py:1031
  142.6 2.1 %product_halves.3 = (f32[64,2048]{1,0:T(8,128)S(1)}, bf16[64,2048]{1,0:T(8,128)(2,1)S(1)}) custom-call(bf16[128,512]{1,0:T(8,128)(2,1)S(1)} %get-tuple-element.240.refs_0_, bf16[128,512]{1,0:T(8,128)(2,1)S(1)} %get-tuple-element.241.refs_1_, bf16[128,512]{1,0:T(8,128)(2,1)S(1)} %get-tuple-element.242.refs_2_, bf16[2048,512]{1,0:T(8,128)(2,1)S(1)} %copy-done, ...), custom_call_target="tpu_custom_call" | custom-call | flops 8053063 | bytes 62914 | tf_op jit(solution)/shard_map/product_halves/pallas_call | solution.py:270
  144.8 1.5 collective-permute-done.44
  147.8 1.7 collective-permute-start.47
  149.8 1.7 collective-permute-start.49
  151.8 2.8 %project.1 = (f32[256,512]{1,0:T(8,128)}, f32[256,512]{1,0:T(8,128)}, f32[256,512]{1,0:T(8,128)}, f32[3,256]{1,0:T(4,128)S(1)}) custom-call(s32[1]{0:T(128)} %bitcast.5.index, bf16[512,2048]{1,0:T(8,128)(2,1)S(1)} %bitcast.74, bf16[512,2048]{1,0:T(8,128)(2,1)S(1)} %collective-permute-done.13.refs_0_.refs_1_, ...), custom_call_target="tpu_custom_call" | custom-call | flops 16106127 | bytes 47185 | tf_op jit(solution)/shard_map/project/pallas_call | solution.py:721
  157.4 2.2 %collective-permute-done.54 = f32[3,256]{1,0:T(4,128)S(1)} collective-permute-done((f32[3,256]{1,0:T(4,128)S(1)}, f32[3,256]{1,0:T(4,128)S(1)}, u32[]{:S(2)}, u32[]{:S(2)}) %collective-permute-start.54) | collective-permute-done | bytes 3104 | tf_op jit(solution)/shard_map/ppermute | solution.py:41
  159.6 14.8 %feed_all.3 = (f32[256,2048]{1,0:T(8,128)}, f32[2048,256]{1,0:T(8,128)}) custom-call(s32[1]{0:T(128)} %bitcast.5.index, bf16[64,2048]{1,0:T(8,128)(2,1)S(1)} %collective-permute-done.39.refs_0_, bf16[64,2048]{1,0:T(8,128)(2,1)S(1)} %collective-permute-done.52.refs_1_, bf16[192,2048]{1,0:T(8,128)(2,1)S(1)} %pad_maximum_fusion.1.refs_2_, ...), custom_call_target="tpu_custom_call" | custom-call | flops 96636768 | bytes 209715 | tf_op jit(solution)/shard_map/feed_all/pallas_call | solution.py:665
  (180 shorter events, 39.7 us)
Async XLA Ops:
  2.2 8.1 %collective-permute-start = (bf16[32,2048]{1,0:T(8,128)(2,1)S(1)}, bf16[32,2048]{1,0:T(8,128)(2,1)S(1)}, u32[]{:S(2)}, u32[]{:S(2)}) collective-permute-start(bf16[32,2048]{1,0:T(8,128)(2,1)S(1)} %constant_dynamic-slice_fusion.4), channel_id=1, source_target_pairs={{0,8},{4,12},{8,0},{12,4},{16,24},{20,28},{24,16},{28,20},{1,9},{5... | collective-permute-start | bytes 393224 | tf_op jit(solution)/shard_map/ppermute | solution.py:41
  5.2 12.9 %collective-permute-start.2 = (bf16[32,2048]{1,0:T(8,128)(2,1)S(1)}, bf16[32,2048]{1,0:T(8,128)(2,1)S(1)}, u32[]{:S(2)}, u32[]{:S(2)}) collective-permute-start(bf16[32,2048]{1,0:T(8,128)(2,1)S(1)} %constant_dynamic-slice_fusion.4), channel_id=1, source_target_pairs={{0,16},{4,20},{8,24},{12,28},{16,0},{20,4},{24,8},{28,12},{1,17},{... | collective-permute-start | bytes 393224 | tf_op jit(solution)/shard_map/ppermute | solution.py:41
  7.8 11.8 %collective-permute-start.4 = (bf16[32,2048]{1,0:T(8,128)(2,1)S(1)}, bf16[32,2048]{1,0:T(8,128)(2,1)S(1)}, u32[]{:S(2)}, u32[]{:S(2)}) collective-permute-start(bf16[32,2048]{1,0:T(8,128)(2,1)S(1)} %constant_dynamic-slice_fusion.4), channel_id=1, source_target_pairs={{0,24},{4,28},{8,16},{12,20},{16,8},{20,12},{24,0},{28,4},{1,25},{... | collective-permute-start | bytes 393224 | tf_op jit(solution)/shard_map/ppermute | solution.py:41
  10.3 9.9 %collective-permute-start.1 = (bf16[32,2048]{1,0:T(8,128)(2,1)S(1)}, bf16[32,2048]{1,0:T(8,128)(2,1)S(1)}, u32[]{:S(2)}, u32[]{:S(2)}) collective-permute-start(bf16[32,2048]{1,0:T(8,128)(2,1)S(1)} %collective-permute-done), channel_id=1, source_target_pairs={{0,2},{1,3},{2,0},{3,1},{4,6},{5,7},{6,4},{7,5},{8,10},{9,11},{10,... | collective-permute-start | bytes 393224 | tf_op jit(solution)/shard_map/ppermute | solution.py:41
  12.0 20.5 %collective-permute-start.6 = (bf16[64,2048]{1,0:T(8,128)(2,1)S(1)}, bf16[64,2048]{1,0:T(8,128)(2,1)S(1)}, u32[]{:S(2)}, u32[]{:S(2)}) collective-permute-start(bf16[64,2048]{1,0:T(8,128)(2,1)S(1)} %bitcast.76), channel_id=1, source_target_pairs={{0,4},{4,0},{8,12},{12,8},{16,20},{20,16},{24,28},{28,24},{1,5},{5... | collective-permute-start | bytes 786440 | tf_op jit(solution)/shard_map/ppermute | solution.py:41
  18.2 5.0 %collective-permute-start.3 = (bf16[32,2048]{1,0:T(8,128)(2,1)S(1)}, bf16[32,2048]{1,0:T(8,128)(2,1)S(1)}, u32[]{:S(2)}, u32[]{:S(2)}) collective-permute-start(bf16[32,2048]{1,0:T(8,128)(2,1)S(1)} %collective-permute-done.2), channel_id=1, source_target_pairs={{0,2},{1,3},{2,0},{3,1},{4,6},{5,7},{6,4},{7,5},{8,10},{9,11},{10,... | collective-permute-start | bytes 393224 | tf_op jit(solution)/shard_map/ppermute | solution.py:41
  19.7 5.1 %collective-permute-start.5 = (bf16[32,2048]{1,0:T(8,128)(2,1)S(1)}, bf16[32,2048]{1,0:T(8,128)(2,1)S(1)}, u32[]{:S(2)}, u32[]{:S(2)}) collective-permute-start(bf16[32,2048]{1,0:T(8,128)(2,1)S(1)} %collective-permute-done.4), channel_id=1, source_target_pairs={{0,2},{1,3},{2,0},{3,1},{4,6},{5,7},{6,4},{7,5},{8,10},{9,11},{10,... | collective-permute-start | bytes 393224 | tf_op jit(solution)/shard_map/ppermute | solution.py:41
  20.2 9.3 %collective-permute-start.7 = (bf16[64,2048]{1,0:T(8,128)(2,1)S(1)}, bf16[64,2048]{1,0:T(8,128)(2,1)S(1)}, u32[]{:S(2)}, u32[]{:S(2)}) collective-permute-start(bf16[64,2048]{1,0:T(8,128)(2,1)S(1)} %pad_maximum_fusion.6.refs_3_), channel_id=1, source_target_pairs={{0,4},{4,0},{8,12},{12,8},{16,20},{20,16},{24,28},{28,24},{1,5},{5... | collective-permute-start | bytes 786440 | tf_op jit(solution)/shard_map/ppermute | solution.py:41
  23.2 11.9 %collective-permute-start.8 = (bf16[64,2048]{1,0:T(8,128)(2,1)S(1)}, bf16[64,2048]{1,0:T(8,128)(2,1)S(1)}, u32[]{:S(2)}, u32[]{:S(2)}) collective-permute-start(bf16[64,2048]{1,0:T(8,128)(2,1)S(1)} %pad_maximum_fusion.7.refs_5_), channel_id=1, source_target_pairs={{0,4},{4,0},{8,12},{12,8},{16,20},{20,16},{24,28},{28,24},{1,5},{5... | collective-permute-start | bytes 786440 | tf_op jit(solution)/shard_map/ppermute | solution.py:41
  24.8 11.5 %collective-permute-start.9 = (bf16[64,2048]{1,0:T(8,128)(2,1)S(1)}, bf16[64,2048]{1,0:T(8,128)(2,1)S(1)}, u32[]{:S(2)}, u32[]{:S(2)}) collective-permute-start(bf16[64,2048]{1,0:T(8,128)(2,1)S(1)} %pad_maximum_fusion.8.refs_7_), channel_id=1, source_target_pairs={{0,4},{4,0},{8,12},{12,8},{16,20},{20,16},{24,28},{28,24},{1,5},{5... | collective-permute-start | bytes 786440 | tf_op jit(solution)/shard_map/ppermute | solution.py:41
  29.5 9.3 %collective-permute-start.10 = (bf16[32,2048]{1,0:T(8,128)(2,1)S(1)}, bf16[32,2048]{1,0:T(8,128)(2,1)S(1)}, u32[]{:S(2)}, u32[]{:S(2)}) collective-permute-start(bf16[32,2048]{1,0:T(8,128)(2,1)S(1)} %constant_dynamic-slice_fusion.2), channel_id=1, source_target_pairs={{0,8},{4,12},{8,0},{12,4},{16,24},{20,28},{24,16},{28,20},{1,9},{5... | collective-permute-start | bytes 393224 | tf_op jit(solution)/shard_map/ppermute | solution.py:41
  31.0 8.7 %collective-permute-start.11 = (bf16[32,2048]{1,0:T(8,128)(2,1)S(1)}, bf16[32,2048]{1,0:T(8,128)(2,1)S(1)}, u32[]{:S(2)}, u32[]{:S(2)}) collective-permute-start(bf16[32,2048]{1,0:T(8,128)(2,1)S(1)} %constant_dynamic-slice_fusion.2), channel_id=1, source_target_pairs={{0,16},{4,20},{8,24},{12,28},{16,0},{20,4},{24,8},{28,12},{1,17},{... | collective-permute-start | bytes 393224 | tf_op jit(solution)/shard_map/ppermute | solution.py:41
  32.5 7.2 %collective-permute-start.12 = (bf16[32,2048]{1,0:T(8,128)(2,1)S(1)}, bf16[32,2048]{1,0:T(8,128)(2,1)S(1)}, u32[]{:S(2)}, u32[]{:S(2)}) collective-permute-start(bf16[32,2048]{1,0:T(8,128)(2,1)S(1)} %constant_dynamic-slice_fusion.2), channel_id=1, source_target_pairs={{0,24},{4,28},{8,16},{12,20},{16,8},{20,12},{24,0},{28,4},{1,25},{... | collective-permute-start | bytes 393224 | tf_op jit(solution)/shard_map/ppermute | solution.py:41
  39.7 5.1 %collective-permute-start.13 = (bf16[512,2048]{1,0:T(8,128)(2,1)S(1)}, bf16[512,2048]{1,0:T(8,128)(2,1)S(1)}, u32[]{:S(2)}, u32[]{:S(2)}) collective-permute-start(bf16[512,2048]{1,0:T(8,128)(2,1)S(1)} %bitcast.71), channel_id=1, source_target_pairs={{0,1},{1,0},{2,3},{3,2},{4,5},{5,4},{6,7},{7,6},{8,9},{9,8},{10,11... | collective-permute-start | bytes 6291464 | tf_op jit(solution)/shard_map/ppermute | solution.py:41
  39.8 11.6 %collective-permute-start.15 = (bf16[96,2048]{1,0:T(8,128)(2,1)S(1)}, bf16[96,2048]{1,0:T(8,128)(2,1)S(1)}, u32[]{:S(2)}, u32[]{:S(2)}) collective-permute-start(bf16[96,2048]{1,0:T(8,128)(2,1)S(1)} %pad_maximum_fusion.5), channel_id=1, source_target_pairs={{0,2},{1,3},{2,0},{3,1},{4,6},{5,7},{6,4},{7,5},{8,10},{9,11},{10,... | collective-permute-start | bytes 1179656 | tf_op jit(solution)/shard_map/ppermute | solution.py:41
  40.9 8.4 %collective-permute-start.14 = (bf16[64,2048]{1,0:T(8,128)(2,1)S(1)}, bf16[64,2048]{1,0:T(8,128)(2,1)S(1)}, u32[]{:S(2)}, u32[]{:S(2)}) collective-permute-start(bf16[64,2048]{1,0:T(8,128)(2,1)S(1)} %bitcast.84), channel_id=1, source_target_pairs={{0,4},{4,0},{8,12},{12,8},{16,20},{20,16},{24,28},{28,24},{1,5},{5... | collective-permute-start | bytes 786440 | tf_op jit(solution)/shard_map/ppermute | solution.py:41
  52.0 20.0 %collective-permute-start.19 = (bf16[192,2048]{1,0:T(8,128)(2,1)S(1)}, bf16[192,2048]{1,0:T(8,128)(2,1)S(1)}, u32[]{:S(2)}, u32[]{:S(2)}) collective-permute-start(bf16[192,2048]{1,0:T(8,128)(2,1)S(1)} %pad_maximum_fusion.refs_2_), channel_id=1, source_target_pairs={{0,4},{4,0},{8,12},{12,8},{16,20},{20,16},{24,28},{28,24},{1,5},{5... | collective-permute-start | bytes 2359304 | tf_op jit(solution)/shard_map/ppermute | solution.py:41
  53.6 8.4 %collective-permute-start.17 = (bf16[64,2048]{1,0:T(8,128)(2,1)S(1)}, bf16[64,2048]{1,0:T(8,128)(2,1)S(1)}, u32[]{:S(2)}, u32[]{:S(2)}) collective-permute-start(bf16[64,2048]{1,0:T(8,128)(2,1)S(1)} %add_convert_fusion.3.low), channel_id=1, source_target_pairs={{0,2},{1,3},{2,0},{3,1},{4,6},{5,7},{6,4},{7,5},{8,10},{9,11},{10,... | collective-permute-start | bytes 786440 | tf_op jit(solution)/shard_map/ppermute | solution.py:41
  73.5 16.1 %collective-permute-start.21 = (bf16[64,2048]{1,0:T(8,128)(2,1)S(1)}, bf16[64,2048]{1,0:T(8,128)(2,1)S(1)}, u32[]{:S(2)}, u32[]{:S(2)}) collective-permute-start(bf16[64,2048]{1,0:T(8,128)(2,1)S(1)} %add_convert_fusion.2.low), channel_id=1, source_target_pairs={{0,2},{1,3},{2,0},{3,1},{4,6},{5,7},{6,4},{7,5},{8,10},{9,11},{10,... | collective-permute-start | bytes 786440 | tf_op jit(solution)/shard_map/ppermute | solution.py:41
  74.7 14.0 %collective-permute-start.22 = (bf16[32,2048]{1,0:T(8,128)(2,1)S(1)}, bf16[32,2048]{1,0:T(8,128)(2,1)S(1)}, u32[]{:S(2)}, u32[]{:S(2)}) collective-permute-start(bf16[32,2048]{1,0:T(8,128)(2,1)S(1)} %constant_dynamic-slice_fusion), channel_id=1, source_target_pairs={{0,8},{4,12},{8,0},{12,4},{16,24},{20,28},{24,16},{28,20},{1,9},{5... | collective-permute-start | bytes 393224 | tf_op jit(solution)/shard_map/ppermute | solution.py:41
  76.7 12.9 %collective-permute-start.23 = (bf16[32,2048]{1,0:T(8,128)(2,1)S(1)}, bf16[32,2048]{1,0:T(8,128)(2,1)S(1)}, u32[]{:S(2)}, u32[]{:S(2)}) collective-permute-start(bf16[32,2048]{1,0:T(8,128)(2,1)S(1)} %constant_dynamic-slice_fusion), channel_id=1, source_target_pairs={{0,16},{4,20},{8,24},{12,28},{16,0},{20,4},{24,8},{28,12},{1,17},{... | collective-permute-start | bytes 393224 | tf_op jit(solution)/shard_map/ppermute | solution.py:41
  77.9 11.6 %collective-permute-start.24 = (bf16[32,2048]{1,0:T(8,128)(2,1)S(1)}, bf16[32,2048]{1,0:T(8,128)(2,1)S(1)}, u32[]{:S(2)}, u32[]{:S(2)}) collective-permute-start(bf16[32,2048]{1,0:T(8,128)(2,1)S(1)} %constant_dynamic-slice_fusion), channel_id=1, source_target_pairs={{0,24},{4,28},{8,16},{12,20},{16,8},{20,12},{24,0},{28,4},{1,25},{... | collective-permute-start | bytes 393224 | tf_op jit(solution)/shard_map/ppermute | solution.py:41
  90.5 11.6 %collective-permute-start.35 = (bf16[96,2048]{1,0:T(8,128)(2,1)S(1)}, bf16[96,2048]{1,0:T(8,128)(2,1)S(1)}, u32[]{:S(2)}, u32[]{:S(2)}) collective-permute-start(bf16[96,2048]{1,0:T(8,128)(2,1)S(1)} %get-tuple-element.318), channel_id=1, source_target_pairs={{0,2},{1,3},{2,0},{3,1},{4,6},{5,7},{6,4},{7,5},{8,10},{9,11},{10,... | collective-permute-start | bytes 1179656 | tf_op jit(solution)/shard_map/ppermute | solution.py:41
  91.4 11.2 %collective-permute-start.36 = (bf16[96,2048]{1,0:T(8,128)(2,1)S(1)}, bf16[96,2048]{1,0:T(8,128)(2,1)S(1)}, u32[]{:S(2)}, u32[]{:S(2)}) collective-permute-start(bf16[96,2048]{1,0:T(8,128)(2,1)S(1)} %get-tuple-element.318), channel_id=1, source_target_pairs={{0,4},{4,0},{8,12},{12,8},{16,20},{20,16},{24,28},{28,24},{1,5},{5... | collective-permute-start | bytes 1179656 | tf_op jit(solution)/shard_map/ppermute | solution.py:41
  93.9 8.8 %collective-permute-start.27 = (bf16[128,512]{1,0:T(8,128)(2,1)S(1)}, bf16[128,512]{1,0:T(8,128)(2,1)S(1)}, u32[]{:S(2)}, u32[]{:S(2)}) collective-permute-start(bf16[128,512]{1,0:T(8,128)(2,1)S(1)} %product_back.1.refs_0_), channel_id=1, source_target_pairs={{0,8},{4,12},{8,0},{12,4},{16,24},{20,28},{24,16},{28,20},{1,9},{5... | collective-permute-start | bytes 393224 | tf_op jit(solution)/shard_map/ppermute | solution.py:41
  96.2 12.8 %collective-permute-start.29 = (bf16[128,512]{1,0:T(8,128)(2,1)S(1)}, bf16[128,512]{1,0:T(8,128)(2,1)S(1)}, u32[]{:S(2)}, u32[]{:S(2)}) collective-permute-start(bf16[128,512]{1,0:T(8,128)(2,1)S(1)} %product_back.1.refs_0_), channel_id=1, source_target_pairs={{0,16},{4,20},{8,24},{12,28},{16,0},{20,4},{24,8},{28,12},{1,17},{... | collective-permute-start | bytes 393224 | tf_op jit(solution)/shard_map/ppermute | solution.py:41
  97.7 11.3 %collective-permute-start.31 = (bf16[128,512]{1,0:T(8,128)(2,1)S(1)}, bf16[128,512]{1,0:T(8,128)(2,1)S(1)}, u32[]{:S(2)}, u32[]{:S(2)}) collective-permute-start(bf16[128,512]{1,0:T(8,128)(2,1)S(1)} %product_back.1.refs_0_), channel_id=1, source_target_pairs={{0,24},{4,28},{8,16},{12,20},{16,8},{20,12},{24,0},{28,4},{1,25},{... | collective-permute-start | bytes 393224 | tf_op jit(solution)/shard_map/ppermute | solution.py:41
  102.1 9.8 %collective-permute-start.38 = (bf16[192,2048]{1,0:T(8,128)(2,1)S(1)}, bf16[192,2048]{1,0:T(8,128)(2,1)S(1)}, u32[]{:S(2)}, u32[]{:S(2)}) collective-permute-start(bf16[192,2048]{1,0:T(8,128)(2,1)S(1)} %pad_maximum_fusion.refs_2_), channel_id=1, source_target_pairs={{0,1},{1,0},{2,3},{3,2},{4,5},{5,4},{6,7},{7,6},{8,9},{9,8},{10,11... | collective-permute-start | bytes 2359304 | tf_op jit(solution)/shard_map/ppermute | solution.py:41
  102.7 7.0 %collective-permute-start.33 = (bf16[64,2048]{1,0:T(8,128)(2,1)S(1)}, bf16[64,2048]{1,0:T(8,128)(2,1)S(1)}, u32[]{:S(2)}, u32[]{:S(2)}) collective-permute-start(bf16[64,2048]{1,0:T(8,128)(2,1)S(1)} %get-tuple-element.211), channel_id=1, source_target_pairs={{0,1},{1,0},{2,3},{3,2},{4,5},{5,4},{6,7},{7,6},{8,9},{9,8},{10,11... | collective-permute-start | bytes 786440 | tf_op jit(solution)/shard_map/ppermute | solution.py:41
  109.1 6.5 %collective-permute-start.37 = (bf16[192,2048]{1,0:T(8,128)(2,1)S(1)}, bf16[192,2048]{1,0:T(8,128)(2,1)S(1)}, u32[]{:S(2)}, u32[]{:S(2)}) collective-permute-start(bf16[192,2048]{1,0:T(8,128)(2,1)S(1)} %constant_dynamic-update-slice_fusion.5.refs_0_), channel_id=1, source_target_pairs={{0,1},{1,0},{2,3},{3,2},{4,5},{5,4},{6,7},{7,6},{8,9},{9,8},{10,11... | collective-permute-start | bytes 2359304 | tf_op jit(solution)/shard_map/ppermute | solution.py:41
  109.1 6.4 %collective-permute-start.28 = (bf16[128,512]{1,0:T(8,128)(2,1)S(1)}, bf16[128,512]{1,0:T(8,128)(2,1)S(1)}, u32[]{:S(2)}, u32[]{:S(2)}) collective-permute-start(bf16[128,512]{1,0:T(8,128)(2,1)S(1)} %collective-permute-done.27.refs_2_), channel_id=1, source_target_pairs={{0,4},{4,0},{8,12},{12,8},{16,20},{20,16},{24,28},{28,24},{1,5},{5... | collective-permute-start | bytes 393224 | tf_op jit(solution)/shard_map/ppermute | solution.py:41
  109.8 19.7 %collective-permute-start.34 = (bf16[64,2048]{1,0:T(8,128)(2,1)S(1)}, bf16[64,2048]{1,0:T(8,128)(2,1)S(1)}, u32[]{:S(2)}, u32[]{:S(2)}) collective-permute-start(bf16[64,2048]{1,0:T(8,128)(2,1)S(1)} %add_convert_fusion.1.low), channel_id=1, source_target_pairs={{0,2},{1,3},{2,0},{3,1},{4,6},{5,7},{6,4},{7,5},{8,10},{9,11},{10,... | collective-permute-start | bytes 786440 | tf_op jit(solution)/shard_map/ppermute | solution.py:41
  110.8 31.7 %collective-permute-start.40 = (bf16[96,2048]{1,0:T(8,128)(2,1)S(1)}, bf16[96,2048]{1,0:T(8,128)(2,1)S(1)}, u32[]{:S(2)}, u32[]{:S(2)}) collective-permute-start(bf16[96,2048]{1,0:T(8,128)(2,1)S(1)} %collective-permute-done.36), channel_id=1, source_target_pairs={{0,2},{1,3},{2,0},{3,1},{4,6},{5,7},{6,4},{7,5},{8,10},{9,11},{10,... | collective-permute-start | bytes 1179656 | tf_op jit(solution)/shard_map/ppermute | solution.py:41
  111.9 17.6 %collective-permute-start.26 = (bf16[128,512]{1,0:T(8,128)(2,1)S(1)}, bf16[128,512]{1,0:T(8,128)(2,1)S(1)}, u32[]{:S(2)}, u32[]{:S(2)}) collective-permute-start(bf16[128,512]{1,0:T(8,128)(2,1)S(1)} %product_back.1.refs_0_), channel_id=1, source_target_pairs={{0,4},{4,0},{8,12},{12,8},{16,20},{20,16},{24,28},{28,24},{1,5},{5... | collective-permute-start | bytes 393224 | tf_op jit(solution)/shard_map/ppermute | solution.py:41
  115.5 14.0 %collective-permute-start.30 = (bf16[128,512]{1,0:T(8,128)(2,1)S(1)}, bf16[128,512]{1,0:T(8,128)(2,1)S(1)}, u32[]{:S(2)}, u32[]{:S(2)}) collective-permute-start(bf16[128,512]{1,0:T(8,128)(2,1)S(1)} %collective-permute-done.29.refs_4_), channel_id=1, source_target_pairs={{0,4},{4,0},{8,12},{12,8},{16,20},{20,16},{24,28},{28,24},{1,5},{5... | collective-permute-start | bytes 393224 | tf_op jit(solution)/shard_map/ppermute | solution.py:41
  115.5 13.9 %collective-permute-start.32 = (bf16[128,512]{1,0:T(8,128)(2,1)S(1)}, bf16[128,512]{1,0:T(8,128)(2,1)S(1)}, u32[]{:S(2)}, u32[]{:S(2)}) collective-permute-start(bf16[128,512]{1,0:T(8,128)(2,1)S(1)} %collective-permute-done.31.refs_6_), channel_id=1, source_target_pairs={{0,4},{4,0},{8,12},{12,8},{16,20},{20,16},{24,28},{28,24},{1,5},{5... | collective-permute-start | bytes 393224 | tf_op jit(solution)/shard_map/ppermute | solution.py:41
  129.5 13.1 %collective-permute-start.39 = (bf16[64,2048]{1,0:T(8,128)(2,1)S(1)}, bf16[64,2048]{1,0:T(8,128)(2,1)S(1)}, u32[]{:S(2)}, u32[]{:S(2)}) collective-permute-start(bf16[64,2048]{1,0:T(8,128)(2,1)S(1)} %get-tuple-element.234), channel_id=1, source_target_pairs={{0,4},{4,0},{8,12},{12,8},{16,20},{20,16},{24,28},{28,24},{1,5},{5... | collective-permute-start | bytes 786440 | tf_op jit(solution)/shard_map/ppermute | solution.py:41
  129.7 12.9 %collective-permute-start.43 = (bf16[2,72,256]{2,1,0:T(8,128)(2,1)S(1)}, bf16[2,72,256]{2,1,0:T(8,128)(2,1)S(1)}, u32[]{:S(2)}, u32[]{:S(2)}) collective-permute-start(bf16[2,72,256]{2,1,0:T(8,128)(2,1)S(1)} %get-tuple-element.239), channel_id=1, source_target_pairs={{0,24},{4,28},{8,16},{12,20},{16,8},{20,12},{24,0},{28,4},{1,25},{... | collective-permute-start | bytes 221192 | tf_op jit(solution)/shard_map/ppermute | solution.py:41
  132.1 10.5 %collective-permute-start.42 = (bf16[2,72,256]{2,1,0:T(8,128)(2,1)S(1)}, bf16[2,72,256]{2,1,0:T(8,128)(2,1)S(1)}, u32[]{:S(2)}, u32[]{:S(2)}) collective-permute-start(bf16[2,72,256]{2,1,0:T(8,128)(2,1)S(1)} %get-tuple-element.238), channel_id=1, source_target_pairs={{0,16},{4,20},{8,24},{12,28},{16,0},{20,4},{24,8},{28,12},{1,17},{... | collective-permute-start | bytes 221192 | tf_op jit(solution)/shard_map/ppermute | solution.py:41
  133.4 9.2 %collective-permute-start.41 = (bf16[2,72,256]{2,1,0:T(8,128)(2,1)S(1)}, bf16[2,72,256]{2,1,0:T(8,128)(2,1)S(1)}, u32[]{:S(2)}, u32[]{:S(2)}) collective-permute-start(bf16[2,72,256]{2,1,0:T(8,128)(2,1)S(1)} %get-tuple-element.237), channel_id=1, source_target_pairs={{0,8},{4,12},{8,0},{12,4},{16,24},{20,28},{24,16},{28,20},{1,9},{5... | collective-permute-start | bytes 221192 | tf_op jit(solution)/shard_map/ppermute | solution.py:41
  146.4 9.0 %collective-permute-start.45 = (bf16[64,2048]{1,0:T(8,128)(2,1)S(1)}, bf16[64,2048]{1,0:T(8,128)(2,1)S(1)}, u32[]{:S(2)}, u32[]{:S(2)}) collective-permute-start(bf16[64,2048]{1,0:T(8,128)(2,1)S(1)} %add_convert_fusion.low), channel_id=1, source_target_pairs={{0,2},{1,3},{2,0},{3,1},{4,6},{5,7},{6,4},{7,5},{8,10},{9,11},{10,... | collective-permute-start | bytes 786440 | tf_op jit(solution)/shard_map/ppermute | solution.py:41
  147.8 6.9 %collective-permute-start.47 = (bf16[72,256]{1,0:T(8,128)(2,1)S(1)}, bf16[72,256]{1,0:T(8,128)(2,1)S(1)}, u32[]{:S(2)}, u32[]{:S(2)}) collective-permute-start(bf16[72,256]{1,0:T(8,128)(2,1)S(1)} %get-tuple-element.328), channel_id=1, source_target_pairs={{0,4},{4,0},{8,12},{12,8},{16,20},{20,16},{24,28},{28,24},{1,5},{5... | collective-permute-start | bytes 110600 | tf_op jit(solution)/shard_map/ppermute | solution.py:41
  149.4 5.2 %collective-permute-start.48 = (bf16[72,256]{1,0:T(8,128)(2,1)S(1)}, bf16[72,256]{1,0:T(8,128)(2,1)S(1)}, u32[]{:S(2)}, u32[]{:S(2)}) collective-permute-start(bf16[72,256]{1,0:T(8,128)(2,1)S(1)} %get-tuple-element.326), channel_id=1, source_target_pairs={{0,4},{4,0},{8,12},{12,8},{16,20},{20,16},{24,28},{28,24},{1,5},{5... | collective-permute-start | bytes 110600 | tf_op jit(solution)/shard_map/ppermute | solution.py:41
  149.8 4.8 %collective-permute-start.49 = (bf16[72,256]{1,0:T(8,128)(2,1)S(1)}, bf16[72,256]{1,0:T(8,128)(2,1)S(1)}, u32[]{:S(2)}, u32[]{:S(2)}) collective-permute-start(bf16[72,256]{1,0:T(8,128)(2,1)S(1)} %get-tuple-element.324), channel_id=1, source_target_pairs={{0,4},{4,0},{8,12},{12,8},{16,20},{20,16},{24,28},{28,24},{1,5},{5... | collective-permute-start | bytes 110600 | tf_op jit(solution)/shard_map/ppermute | solution.py:41
  151.5 4.0 %collective-permute-start.46 = (bf16[72,256]{1,0:T(8,128)(2,1)S(1)}, bf16[72,256]{1,0:T(8,128)(2,1)S(1)}, u32[]{:S(2)}, u32[]{:S(2)}) collective-permute-start(bf16[72,256]{1,0:T(8,128)(2,1)S(1)} %get-tuple-element.330), channel_id=1, source_target_pairs={{0,4},{4,0},{8,12},{12,8},{16,20},{20,16},{24,28},{28,24},{1,5},{5... | collective-permute-start | bytes 110600 | tf_op jit(solution)/shard_map/ppermute | solution.py:41
  155.4 4.2 %collective-permute-start.53 = (bf16[192,2048]{1,0:T(8,128)(2,1)S(1)}, bf16[192,2048]{1,0:T(8,128)(2,1)S(1)}, u32[]{:S(2)}, u32[]{:S(2)}) collective-permute-start(bf16[192,2048]{1,0:T(8,128)(2,1)S(1)} %pad_maximum_fusion.1.refs_2_), channel_id=1, source_target_pairs={{0,1},{1,0},{2,3},{3,2},{4,5},{5,4},{6,7},{7,6},{8,9},{9,8},{10,11... | collective-permute-start | bytes 2359304 | tf_op jit(solution)/shard_map/ppermute | solution.py:41
  155.4 4.2 %collective-permute-start.56 = (bf16[192,2048]{1,0:T(8,128)(2,1)S(1)}, bf16[192,2048]{1,0:T(8,128)(2,1)S(1)}, u32[]{:S(2)}, u32[]{:S(2)}) collective-permute-start(bf16[192,2048]{1,0:T(8,128)(2,1)S(1)} %collective-permute-done.19.refs_6_), channel_id=1, source_target_pairs={{0,1},{1,0},{2,3},{3,2},{4,5},{5,4},{6,7},{7,6},{8,9},{9,8},{10,11... | collective-permute-start | bytes 2359304 | tf_op jit(solution)/shard_map/ppermute | solution.py:41
  174.6 4.3 %collective-permute-start.57 = (bf16[8,72,256]{2,1,0:T(8,128)(2,1)S(1)}, bf16[8,72,256]{2,1,0:T(8,128)(2,1)S(1)}, u32[]{:S(2)}, u32[]{:S(2)}) collective-permute-start(bf16[8,72,256]{2,1,0:T(8,128)(2,1)S(1)} %constant_dynamic-update-slice_fusion.9.came_a), channel_id=1, source_target_pairs={{0,1},{1,0},{2,3},{3,2},{4,5},{5,4},{6,7},{7,6},{8,9},{9,8},{10,11... | collective-permute-start | bytes 884744 | tf_op jit(solution)/shard_map/ppermute | solution.py:41
  (30 other events, 212.6 us)
